TPU v7x, 32 devices: a whole 2x2x4 slice. The times are simulated.
32 devices in a mesh: dp: 8 (over z, x), tensor: 4 (over y, core).
Axes of the slice: x: 2, y: 2, z: 4, core: 2. Of those that a mesh axis runs over, the one named last changes fastest.
Arguments:
- patches: bfloat16 [24, 2048, 1024], P('dp', 'tensor'), may hold values from -6 to 6
- cotangent: bfloat16 [24, 2048, 1024], P('dp', 'tensor'), may hold values from -6 to 6
- empty_slots: int32 [8], replicated, may hold values from 0 to 2
- dataset_id: int32 [24], replicated, may hold values from 0 to 5
- dataset_weight: int32 [6], replicated, may hold values from 1 to 8
- query_key_value_weight: bfloat16 [3, 1024, 1024], P(None, None, 'tensor'), may hold values from -0.25 to 0.25
- qv_bias: float32 [2, 1024], P(None, 'tensor'), may hold values from -3 to 3
- output_projection_weight: bfloat16 [1024, 1024], P('tensor'), may hold values from -0.75 to 0.75
- out_bias: float32 [1024], replicated, may hold values from -2 to 2
- up_projection_weight: bfloat16 [1024, 4096], P(None, 'tensor'), may hold values from -0.1875 to 0.1875
- up_bias: float32 [4096], P('tensor'), may hold values from -2 to 2
- down_projection_weight: bfloat16 [4096, 1024], P('tensor'), may hold values from -0.09375 to 0.09375
- down_bias: float32 [1024], replicated, may hold values from -2 to 2
- attn_gain: float32 [1024], replicated, may hold values from 0.5 to 1.5
- attn_shift: float32 [1024], replicated, may hold values from -1.5 to 1.5
- mlp_gain: float32 [1024], replicated, may hold values from 0.5 to 1.5
- mlp_shift: float32 [1024], replicated, may hold values from -1.5 to 1.5
Outputs:
- block_out: bfloat16 [24, 2048, 1024], P('dp', 'tensor')
- grad_patches: bfloat16 [24, 2048, 1024], P('dp', 'tensor')
- grad_qkv_weight: float32 [3, 1024, 1024], P(None, None, 'tensor')
- grad_qv_bias: float32 [2, 1024], P(None, 'tensor')
- grad_out_weight: float32 [1024, 1024], P('tensor')
- grad_out_bias: float32 [1024], replicated
- grad_up_weight: float32 [1024, 4096], P(None, 'tensor')
- grad_up_bias: float32 [4096], P('tensor')
- grad_down_weight: float32 [4096, 1024], P('tensor')
- grad_down_bias: float32 [1024], replicated
- grad_attn_gain: float32 [1024], replicated
- grad_attn_shift: float32 [1024], replicated
- sensitivity_feedforward_scale: float32 [1024], replicated
- grad_mlp_shift: float32 [1024], replicated
All inputs are finite; a program needn't handle non-finite values.
Results may differ from a plain program's by a relative error of at most 0.02.
Values may be sent and summed in bfloat16 or wider, within the bound.
No kernel may reach another device: no remote copies, remote signals or barrier semaphores. Data moves between devices by JAX's collectives and lax.ppermute only.
A program may use at most 256 MiB of HBM per device.

v0:
```python
import jax
import jax.numpy as jnp
from jax import lax
from jax.sharding import PartitionSpec as P

HD = 64


epsilon = 1e-05


def norm_rows(source, norm_gain, norm_shift):
    row_mean = jnp.mean(source, axis=-1, keepdims=True)
    centred = source - row_mean
    spread = jnp.mean(centred * centred, axis=-1, keepdims=True)
    return centred * lax.rsqrt(spread + epsilon) * norm_gain + norm_shift


def gelu_exact(pre_act):
    return jax.nn.gelu(pre_act, approximate=False)


def split_heads(array, head_count):
    return array.reshape(array.shape[0], array.shape[1], head_count, HD)


def attend_item(operands):
    queries, key_rows, values = operands
    length, head_count, head_size = queries.shape
    qblock = min(512, length)
    score_scale = head_size ** (-0.5)
    blocks = queries.reshape(length // qblock, qblock, head_count, head_size)

    def one_block(query_block):
        scores = (
            jnp.einsum("qhd,khd->hqk", query_block, key_rows, preferred_element_type=jnp.float32)
            * score_scale
        )
        row_top = jnp.max(scores, axis=-1, keepdims=True)
        exp_scores = jnp.exp(scores - row_top)
        row_total = jnp.sum(exp_scores, axis=-1, keepdims=True)
        attn_weights = (exp_scores / row_total).astype(jnp.bfloat16)
        attended = jnp.einsum(
            "hqk,khd->qhd", attn_weights, values, preferred_element_type=jnp.float32
        )
        return (attended.astype(jnp.bfloat16), (row_top + jnp.log(row_total))[:, :, 0])

    attended, log_total = lax.map(one_block, blocks)
    return (attended.reshape(length, head_count, head_size), log_total)


def attend_back(operands):
    queries, key_rows, values, grad_attended, log_total = operands
    length, head_count, head_size = queries.shape
    qblock = min(512, length)
    score_scale = head_size ** (-0.5)
    query_blocks = queries.reshape(length // qblock, qblock, head_count, head_size)
    grad_blocks = grad_attended.reshape(length // qblock, qblock, head_count, head_size)

    def one_block(carried, block_in):
        query_block, grad_block, lse_block = block_in
        scores = (
            jnp.einsum("qhd,khd->hqk", query_block, key_rows, preferred_element_type=jnp.float32)
            * score_scale
        )
        attn_weights = jnp.exp(scores - lse_block[:, :, None])
        grad_weights = jnp.einsum(
            "qhd,khd->hqk", grad_block, values, preferred_element_type=jnp.float32
        )
        grad_scores = attn_weights * (
            grad_weights - jnp.sum(attn_weights * grad_weights, axis=-1, keepdims=True)
        )
        grad_low = grad_scores.astype(jnp.bfloat16)
        sensitivity_questions = (
            jnp.einsum("hqk,khd->qhd", grad_low, key_rows, preferred_element_type=jnp.float32)
            * score_scale
        )
        key_acc = (
            carried[0]
            + jnp.einsum("hqk,qhd->khd", grad_low, query_block, preferred_element_type=jnp.float32)
            * score_scale
        )
        value_acc = carried[1] + jnp.einsum(
            "hqk,qhd->khd",
            attn_weights.astype(jnp.bfloat16),
            grad_block,
            preferred_element_type=jnp.float32,
        )
        return ((key_acc, value_acc), sensitivity_questions)

    zero_acc = jnp.zeros((length, head_count, head_size), jnp.float32)
    (grad_keys, grad_values), grad_queries = lax.scan(
        one_block, (zero_acc, zero_acc), (query_blocks, grad_blocks, log_total)
    )
    return (grad_queries.reshape(length, head_count, head_size), grad_keys, grad_values)


def shards(
    patches,
    cotangent,
    empty_slots,
    dataset_id,
    dataset_weight,
    query_key_value_weight,
    qv_bias,
    output_projection_weight,
    out_bias,
    up_projection_weight,
    up_bias,
    down_projection_weight,
    down_bias,
    attn_gain,
    attn_shift,
    mlp_gain,
    mlp_shift,
):
    number_format = jnp.float32
    half_type = jnp.bfloat16
    slot_count = patches.shape[0]
    group_slots = empty_slots.shape[0]
    slot_index = jnp.arange(group_slots * slot_count, dtype=jnp.int32) % slot_count
    filled = jnp.repeat(slot_count - empty_slots, slot_count)
    valid_all = (slot_index < filled).astype(number_format)
    table_hits = (
        dataset_id[:, None] == jnp.arange(dataset_weight.shape[0], dtype=jnp.int32)[None, :]
    )
    numerator = jnp.sum(jnp.where(table_hits, dataset_weight[None, :], 0), axis=1).astype(
        number_format
    )
    total_items = jnp.sum(valid_all)
    total_weight = jnp.sum(valid_all * numerator)
    multiplier_whole = valid_all * numerator * total_items / total_weight
    own_start = lax.axis_index("dp") * slot_count
    own_scale = lax.dynamic_slice_in_dim(multiplier_whole, own_start, slot_count)
    own_valid = lax.dynamic_slice_in_dim(valid_all, own_start, slot_count)
    inputs = patches.astype(number_format)
    normed = norm_rows(inputs, attn_gain, attn_shift).astype(half_type)
    normalized_every = lax.all_gather(normed, "tensor", axis=1, tiled=True)
    local_width = query_key_value_weight.shape[2]
    head_count = local_width // HD
    projected_rows = jnp.einsum(
        "owz,gzh->gowh",
        normalized_every,
        query_key_value_weight,
        preferred_element_type=number_format,
    )
    queries = split_heads((projected_rows[0] + qv_bias[0]).astype(half_type), head_count)
    key_rows = split_heads(projected_rows[1].astype(half_type), head_count)
    values = split_heads((projected_rows[2] + qv_bias[1]).astype(half_type), head_count)
    attended, log_total = lax.map(attend_item, (queries, key_rows, values))
    attended_matrix = attended.reshape(slot_count, attended.shape[1], local_width)
    attn_part = jnp.einsum(
        "ifz,zp->ifp",
        attended_matrix,
        output_projection_weight,
        preferred_element_type=number_format,
    )
    attn_rows = lax.psum_scatter(
        attn_part.astype(jnp.bfloat16), "tensor", scatter_dimension=1, tiled=True
    ).astype(jnp.float32)
    residual = inputs + attn_rows + out_bias
    normed_mlp = norm_rows(residual, mlp_gain, mlp_shift).astype(half_type)
    cot_scaled = cotangent.astype(number_format) * own_scale[:, None, None]
    cot_low = cot_scaled.astype(half_type)
    normalized_perceptron_every = lax.all_gather(normed_mlp, "tensor", axis=1, tiled=True)
    hidden_pre = (
        jnp.einsum(
            "jzb,bu->jzu",
            normalized_perceptron_every,
            up_projection_weight,
            preferred_element_type=number_format,
        )
        + up_bias
    )
    gelu_out, gelu_back = jax.vjp(gelu_exact, hidden_pre)
    latent_activations = gelu_out.astype(half_type)
    perceptron_portion = jnp.einsum(
        "vuc,cy->vuy",
        latent_activations,
        down_projection_weight,
        preferred_element_type=number_format,
    )
    mlp_rows = lax.psum_scatter(
        perceptron_portion.astype(jnp.bfloat16), "tensor", scatter_dimension=1, tiled=True
    ).astype(jnp.float32)
    output = ((residual + mlp_rows + down_bias) * own_valid[:, None, None]).astype(half_type)
    adjoint_for_each_layer = lax.all_gather(cot_low, "tensor", axis=1, tiled=True)
    hidden_gradient = jnp.einsum(
        "eph,wh->epw",
        adjoint_for_each_layer,
        down_projection_weight,
        preferred_element_type=number_format,
    )
    preactivation_gradient = gelu_back(hidden_gradient)[0].astype(half_type)
    down_gradient = jnp.einsum(
        "wuf,wul->fl",
        latent_activations,
        adjoint_for_each_layer,
        preferred_element_type=number_format,
    )
    up_gradient = jnp.einsum(
        "eug,eut->gt",
        normalized_perceptron_every,
        preactivation_gradient,
        preferred_element_type=number_format,
    )
    grad_up_bias = jnp.sum(preactivation_gradient.astype(number_format), axis=(0, 1))
    norm_portion = jnp.einsum(
        "jmn,hn->jmh",
        preactivation_gradient,
        up_projection_weight,
        preferred_element_type=number_format,
    )
    grad_normed_mlp = lax.psum_scatter(
        norm_portion.astype(jnp.bfloat16), "tensor", scatter_dimension=1, tiled=True
    ).astype(jnp.float32)
    mlp_norm_back = jax.vjp(norm_rows, residual, mlp_gain, mlp_shift)[1]
    grad_resid_norm, sensitivity_feedforward_scale, grad_mlp_shift = mlp_norm_back(grad_normed_mlp)
    grad_residual = cot_scaled + grad_resid_norm
    grad_out_bias = jnp.sum(grad_residual, axis=(0, 1))
    grad_down_bias = jnp.sum(cot_scaled, axis=(0, 1))
    residual_gradient_every = lax.all_gather(
        grad_residual.astype(half_type), "tensor", axis=1, tiled=True
    )
    grad_attended = jnp.einsum(
        "xmn,wn->xmw",
        residual_gradient_every,
        output_projection_weight,
        preferred_element_type=number_format,
    ).astype(half_type)
    grad_out = jnp.einsum(
        "ift,ifr->tr",
        attended_matrix,
        residual_gradient_every,
        preferred_element_type=number_format,
    )
    grad_queries, grad_keys, grad_values = lax.map(
        attend_back, (queries, key_rows, values, split_heads(grad_attended, head_count), log_total)
    )
    flat_shape = (slot_count, grad_queries.shape[1], local_width)
    projection_gradient = jnp.stack(
        [
            grad_queries.reshape(flat_shape).astype(half_type),
            grad_keys.reshape(flat_shape).astype(half_type),
            grad_values.reshape(flat_shape).astype(half_type),
        ]
    )
    query_key_value_gradient = jnp.einsum(
        "ktr,jktq->jrq", normalized_every, projection_gradient, preferred_element_type=number_format
    )
    grad_qv = jnp.stack(
        [
            jnp.sum(projection_gradient[0].astype(number_format), axis=(0, 1)),
            jnp.sum(projection_gradient[2].astype(number_format), axis=(0, 1)),
        ]
    )
    normed_part = jnp.einsum(
        "vbmk,vxk->bmx",
        projection_gradient,
        query_key_value_weight,
        preferred_element_type=number_format,
    )
    grad_normed = lax.psum_scatter(
        normed_part.astype(jnp.bfloat16), "tensor", scatter_dimension=1, tiled=True
    ).astype(jnp.float32)
    attn_norm_back = jax.vjp(norm_rows, inputs, attn_gain, attn_shift)[1]
    grad_input_norm, grad_attn_gain, grad_attn_shift = attn_norm_back(grad_normed)
    grad_inputs = (grad_residual + grad_input_norm).astype(half_type)
    summed = (
        lax.psum(query_key_value_gradient.astype(jnp.bfloat16), "dp").astype(jnp.float32),
        lax.psum(grad_qv.astype(jnp.bfloat16), "dp").astype(jnp.float32),
        lax.psum(grad_out.astype(jnp.bfloat16), "dp").astype(jnp.float32),
        lax.psum(up_gradient.astype(jnp.bfloat16), "dp").astype(jnp.float32),
        lax.psum(grad_up_bias.astype(jnp.bfloat16), "dp").astype(jnp.float32),
        lax.psum(down_gradient.astype(jnp.bfloat16), "dp").astype(jnp.float32),
    )
    small_sums = lax.psum(
        (
            grad_attn_gain,
            grad_attn_shift,
            sensitivity_feedforward_scale,
            grad_mlp_shift,
            grad_out_bias,
            grad_down_bias,
        ),
        ("dp", "tensor"),
    )
    return (
        output,
        grad_inputs,
        summed[0] / total_items,
        summed[1] / total_items,
        summed[2] / total_items,
        small_sums[4] / total_items,
        summed[3] / total_items,
        summed[4] / total_items,
        summed[5] / total_items,
        small_sums[5] / total_items,
        small_sums[0] / total_items,
        small_sums[1] / total_items,
        small_sums[2] / total_items,
        small_sums[3] / total_items,
    )


def solution(mesh):
    placed = (
        P("dp", "tensor", None),
        P("dp", "tensor", None),
        P(),
        P(),
        P(),
        P(None, None, "tensor"),
        P(None, "tensor"),
        P("tensor", None),
        P(),
        P(None, "tensor"),
        P("tensor"),
        P("tensor", None),
        P(),
        P(),
        P(),
        P(),
        P(),
    )
    return jax.shard_map(
        shards,
        mesh=mesh,
        in_specs=placed,
        out_specs=(
            P("dp", "tensor", None),
            P("dp", "tensor", None),
            P(None, None, "tensor"),
            P(None, "tensor"),
            P("tensor", None),
            P(),
            P(None, "tensor"),
            P("tensor"),
            P("tensor", None),
            P(),
            P(),
            P(),
            P(),
            P(),
        ),
        check_vma=False,
    )
```

profile of v0, /device:TPU:0, one launch (start us, length us, event | category | flops | bytes accessed | tf_op | source)
XLA Modules:
  0.0 1974.1 jit_solution(18060391247935320922)
XLA Ops:
  16.7 84.7 %all-gather.5.cloned.1.call-done = bf16[3,2048,1024]{2,1,0:T(8,128)(2,1)} async-done(((bf16[3,512,1024]{2,1,0:T(8,128)(2,1)}), bf16[3,2048,1024]{2,1,0:T(8,128)(2,1)}) %all-gather.5.cloned.1.call-update) | async-done | bytes 12582928 | tf_op jit(solution)/shard_map/all_gather | solution.py:138
  144.1 192.9 %while.54 = (s32[]{:T(128)}, bf16[3,2048,4,64]{1,3,2,0:T(8,128)(2,1)}, f32[3,4,4,512]{3,2,1,0:T(4,128)}, bf16[3,2048,4,64]{1,3,2,0:T(8,128)(2,1)}, bf16[3,2048,4...) while((s32[]{:T(128)}, ...), condition=%wide.region_7.8_spmd, body=%wide.region_2.7_spmd.sunk | while | flops 1111619584 | bytes 74055984 | solution.py:150
  152.4 47.4 %while.57 = (s32[]{:T(128)}, bf16[4,512,4,64]{1,3,2,0:T(8,128)(2,1)}, f32[4,4,512]{2,1,0:T(4,128)S(1)}, bf16[4,512,4,64]{1,3,2,0:T(8,128)(2,1)}, bf16[2048,4,64]...) while((s32[]{:T(128)}, bf16[4,512,4,64]{1,3,2,0:T(8,128)(2,1)}, ...), condition=%wide.region_6.6_spmd, body=%wide.region_3.5_spmd.sunk | while | flops 1111619584 | bytes 57213052 | solution.py:48
  216.6 47.4 %while.57 = (s32[]{:T(128)}, bf16[4,512,4,64]{1,3,2,0:T(8,128)(2,1)}, f32[4,4,512]{2,1,0:T(4,128)S(1)}, bf16[4,512,4,64]{1,3,2,0:T(8,128)(2,1)}, bf16[2048,4,64]...) while((s32[]{:T(128)}, bf16[4,512,4,64]{1,3,2,0:T(8,128)(2,1)}, ...), condition=%wide.region_6.6_spmd, body=%wide.region_3.5_spmd.sunk | while | flops 1111619584 | bytes 57213052 | solution.py:48
  280.8 47.4 %while.57 = (s32[]{:T(128)}, bf16[4,512,4,64]{1,3,2,0:T(8,128)(2,1)}, f32[4,4,512]{2,1,0:T(4,128)S(1)}, bf16[4,512,4,64]{1,3,2,0:T(8,128)(2,1)}, bf16[2048,4,64]...) while((s32[]{:T(128)}, bf16[4,512,4,64]{1,3,2,0:T(8,128)(2,1)}, ...), condition=%wide.region_6.6_spmd, body=%wide.region_3.5_spmd.sunk | while | flops 1111619584 | bytes 57213052 | solution.py:48
  347.1 99.1 %reduce-scatter.5.cloned.1.call-done = bf16[3,512,1024]{2,1,0:T(8,128)(2,1)} async-done(((bf16[3,2048,1024]{2,1,0:T(8,128)(2,1)}), bf16[3,512,1024]{2,1,0:T(8,128)(2,1)}) %reduce-scatter.5.cloned.1.call-update) | async-done | bytes 3145744 | tf_op jit(solution)/shard_map/reduce_scatter | solution.py:158
  465.1 73.9 %all-gather.7.cloned.1.call-done = bf16[3,2048,1024]{2,1,0:T(8,128)(2,1)} async-done(((bf16[3,512,1024]{2,1,0:T(8,128)(2,1)}), bf16[3,2048,1024]{2,1,0:T(8,128)(2,1)}) %all-gather.7.cloned.1.call-update) | async-done | bytes 12582928 | tf_op jit(solution)/shard_map/all_gather | solution.py:165
  539.1 29.6 %fusion.72 = (u8[2048,1024]{1,0:T(8,128)(4,1)}, u8[2048,1024]{1,0:T(8,128)(4,1)}, f32[3,2048,1024]{2,1,0:T(8,128)}) fusion(f32[1024]{0:T(1024)S(1)} %copy-done.41, bf16[3,2048,1024]{2,1,0:T(8,128)(2,1)} %all-gather.7.cloned.1.call-done, bf16[1024,1024]{1,0:T(8,128)(2,1)S(1)} %copy-done), kind=kOutput, calls=%fused_computation.128 | convolution fusion | flops 12968787968 | bytes 44044288 | tf_op jit(solution)/shard_map/jzb,bu->jzu/dot_general | solution.py:167
  568.7 61.6 %multiply_convert_fusion.1 = (bf16[3,2048,1024]{2,1,0:T(8,128)(2,1)}, f32[3,2048,1024]{2,1,0:T(8,128)}) fusion(f32[3,2048,1024]{2,1,0:T(8,128)} %get-tuple-element.412, f32[1024]{0:T(1024)S(1)} %copy-done.41, u8[2048,1024]{1,0:T(8,128)(4,1)} %get-tuple-element.313, u8[2048,1024]{1,0:T(8,128)(4,1)} %get-tuple-element.312), kind=kLoop, calls=%fused_computation.67 | loop fusion | flops 446693376 | bytes 67112960 | tf_op jit(solution)/shard_map/convert_element_type | solution.py:176
  630.3 32.6 %fusion.103 = (bf16[1024]{0:T(1024)(128)(2,1)}, bf16[3,2048,1024]{2,1,0:T(8,128)(2,1)}) fusion(f32[3,2048,1024]{2,1,0:T(8,128)} %get-tuple-element.399, bf16[3,2048,1024]{2,1,0:T(8,128)(2,1)} %all-gather.9.cloned.1.call-done, bf16[1024,1024]{1,0:T(8,128)(2,1)} %param.36, f32[3,2048,1024]{2,1,0:T(8,128)} %get-tuple-element.412, f32[1024]{0:T(1024)S(1)} %copy-done.41), kind=kOutput, calls=%fused_computation.192 | convolution fusion | flops 12985564160 | bytes 77600768 | tf_op jit(solution)/shard_map/eph,wh->epw/dot_general | solution.py:188
  662.9 20.4 %convolution_convert_fusion = bf16[3,2048,1024]{2,1,0:T(8,128)(2,1)} fusion(bf16[3,2048,1024]{2,1,0:T(8,128)(2,1)} %get-tuple-element.414, bf16[1024,1024]{1,0:T(8,128)(2,1)S(1)} %copy-done), kind=kOutput, calls=%fused_computation.105 | convolution fusion | flops 12891193344 | bytes 27262976 | tf_op jit(solution)/shard_map/jmn,hn->jmh/dot_general | solution.py:208
  684.8 21.3 %convolution_convert_fusion.1 = bf16[3,2048,1024]{2,1,0:T(8,128)(2,1)} fusion(bf16[3,2048,1024]{2,1,0:T(8,128)(2,1)} %get-tuple-element.398, bf16[1024,1024]{1,0:T(8,128)(2,1)S(1)} %copy-done.47), kind=kOutput, calls=%fused_computation.106 | convolution fusion | flops 12891193344 | bytes 27262976 | tf_op jit(solution)/shard_map/vuc,cy->vuy/dot_general | solution.py:177
  706.3 76.2 %reduce-scatter.9.cloned.1.call-done = bf16[3,512,1024]{2,1,0:T(8,128)(2,1)} async-done(((bf16[3,2048,1024]{2,1,0:T(8,128)(2,1)}), bf16[3,512,1024]{2,1,0:T(8,128)(2,1)}) %reduce-scatter.9.cloned.1.call-update) | async-done | bytes 3145744 | tf_op jit(solution)/shard_map/reduce_scatter | solution.py:214
  795.7 88.3 %reduce-scatter.7.cloned.1.call-done = bf16[3,512,1024]{2,1,0:T(8,128)(2,1)} async-done(((bf16[3,2048,1024]{2,1,0:T(8,128)(2,1)}), bf16[3,512,1024]{2,1,0:T(8,128)(2,1)}) %reduce-scatter.7.cloned.1.call-update) | async-done | bytes 3145744 | tf_op jit(solution)/shard_map/reduce_scatter | solution.py:183
  899.3 19.5 bitcast_convert_fusion.1
  937.8 43.7 %all-gather.11.cloned.1.call-done = bf16[3,2048,1024]{2,1,0:T(8,128)(2,1)} async-done(((bf16[3,512,1024]{2,1,0:T(8,128)(2,1)}), bf16[3,2048,1024]{2,1,0:T(8,128)(2,1)}) %all-gather.11.cloned.1.call-update) | async-done | bytes 12582928 | tf_op jit(solution)/shard_map/all_gather | solution.py:222
  995.9 553.7 %while.56 = (s32[]{:T(128)}, bf16[3,2048,4,64]{1,3,2,0:T(8,128)(2,1)}, bf16[3,2048,4,64]{1,3,2,0:T(8,128)(2,1)}, bf16[3,2048,4,64]{1,3,2,0:T(8,128)(2,1)}, bf16[...) while((s32[]{:T(128)}, ...), condition=%wide.region_22.23_spmd, body=%wide.region_18.22_spmd.sunk | while | flops 2737436672 | bytes 246014544 | solution.py:237
  1010.8 158.2 %while.58 = (s32[]{:T(128)}, f32[2048,4,64]{0,2,1:T(8,128)}, f32[2048,4,64]{0,2,1:T(8,128)}, bf16[4,512,4,64]{1,3,2,0:T(8,128)(2,1)}, bf16[4,512,4,64]{1,3,2,0:T...) while((s32[]{:T(128)}, f32[2048,4,64]{0,2,1:T(8,128)}, ...), condition=%wide.region_21.21_spmd.clone, body=%wide.region_19.20_spmd.clone.sunk | while | flops 2737436672 | bytes 206102832 | solution.py:92
  1195.3 158.2 %while.58 = (s32[]{:T(128)}, f32[2048,4,64]{0,2,1:T(8,128)}, f32[2048,4,64]{0,2,1:T(8,128)}, bf16[4,512,4,64]{1,3,2,0:T(8,128)(2,1)}, bf16[4,512,4,64]{1,3,2,0:T...) while((s32[]{:T(128)}, f32[2048,4,64]{0,2,1:T(8,128)}, ...), condition=%wide.region_21.21_spmd.clone, body=%wide.region_19.20_spmd.clone.sunk | while | flops 2737436672 | bytes 206102832 | solution.py:92
  1379.8 158.2 %while.58 = (s32[]{:T(128)}, f32[2048,4,64]{0,2,1:T(8,128)}, f32[2048,4,64]{0,2,1:T(8,128)}, bf16[4,512,4,64]{1,3,2,0:T(8,128)(2,1)}, bf16[4,512,4,64]{1,3,2,0:T...) while((s32[]{:T(128)}, f32[2048,4,64]{0,2,1:T(8,128)}, ...), condition=%wide.region_21.21_spmd.clone, body=%wide.region_19.20_spmd.clone.sunk | while | flops 2737436672 | bytes 206102832 | solution.py:92
  1609.1 22.8 %all-reduce.1 = (bf16[2,256]{1,0:T(2,128)(2,1)S(1)}, bf16[1024]{0:T(1024)(128)(2,1)S(1)}) all-reduce(bf16[2,256]{1,0:T(2,128)(2,1)S(1)} %pad_maximum_fusion.7, bf16[1024]{0:T(1024)(128)(2,1)S(1)} %copy-done.45), channel_id=1, replica_groups=mesh['dp'=8,'tensor'=4] {'dp'}, use_global_device_ids=true, to_apply=%region_29.30 | all-reduce | flops 1536 | bytes 6144 | tf_op jit(solution)/shard_map/psum | solution.py:271
  1634.4 167.8 %all-reduce.5.cloned.1.call-done = (bf16[3,1024,256]{1,2,0:T(8,128)(2,1)}, bf16[256,1024]{1,0:T(8,128)(2,1)}, bf16[1024,1024]{1,0:T(8,128)(2,1)}, bf16[1024,1024]{1,0:T(8,128)(2,1)}) async-done(((bf16[3,1024,256]{1,2,0:T(8,128)(2,1)}, bf16[256,1024]{1,0:T(8,128)(2,1)}, bf16[1024,1024]{1,0:T(8,128)(2,1)}, bf16[1024,1024]{1,0:T(8,128)(2,1)}), (bf16[3,1024,256]{1,2,0:T(8,128)(2,1)}, ...) | async-done | bytes 6291472 | tf_op jit(solution)/shard_map/psum | solution.py:270
  1821.7 81.2 %reduce-scatter.11.cloned.1.call-done = bf16[3,512,1024]{2,1,0:T(8,128)(2,1)} async-done(((bf16[3,2048,1024]{2,1,0:T(8,128)(2,1)}), bf16[3,512,1024]{2,1,0:T(8,128)(2,1)}) %reduce-scatter.11.cloned.1.call-update) | async-done | bytes 3145744 | tf_op jit(solution)/shard_map/reduce_scatter | solution.py:263
  1912.9 39.7 %all-reduce = (f32[1024]{0:T(1024)S(1)}, f32[1024]{0:T(1024)S(1)}, f32[1024]{0:T(1024)S(1)}, f32[1024]{0:T(1024)S(1)}, f32[1024]{0:T(1024)S(1)}, /*index=5*/f32[1024]{0:T(1024)S(1)}) all-reduce(f32[1024]{0:T(1024)S(1)} %copy-done.37, f32[1024]{0:T(1024)S(1)} %copy-done.38, ...), channel_id=1, replica_groups=mesh['dp'=8,'tensor'=4] {'dp','tensor'}, use_global_device_ids=true, to_apply=%region_32.33 | all-reduce | flops 6144 | bytes 49152 | tf_op jit(solution)/shard_map/psum | solution.py:277
  (542 shorter events, 995.2 us)
Async XLA Ops:
  7.2 531.9 %copy-start = (bf16[1024,1024]{1,0:T(8,128)(2,1)S(1)}, bf16[1024,1024]{1,0:T(8,128)(2,1)}, u32[]{:S(2)}) copy-start(bf16[1024,1024]{1,0:T(8,128)(2,1)} %param.34) | copy-start | bytes 6291460
  7.2 94.1 %all-gather.5.cloned.1.call-start = ((), (), s32[]{:S(2)}) async-start(), calls=%async_computation.4 | async-start | bytes 15728640 | tf_op jit(solution)/shard_map/all_gather | solution.py:138
  16.4 429.9 %reduce-scatter.5.cloned.1.call-start = ((), (), s32[]{:S(2)}) async-start(), calls=%async_computation.5 | async-start | bytes 15728640 | tf_op jit(solution)/shard_map/reduce_scatter | solution.py:158
  347.0 99.2 %copy-start.23 = (f32[1024]{0:T(1024)S(1)}, f32[1024]{0:T(1024)}, u32[]{:S(2)}) copy-start(f32[1024]{0:T(1024)} %param.33) | copy-start | bytes 12292
  347.1 106.7 %copy-start.32 = (f32[1024]{0:T(1024)S(1)}, f32[1024]{0:T(1024)}, u32[]{:S(2)}) copy-start(f32[1024]{0:T(1024)} %param.40) | copy-start | bytes 12292
  347.1 106.7 %copy-start.39 = (f32[1024]{0:T(1024)S(1)}, f32[1024]{0:T(1024)}, u32[]{:S(2)}) copy-start(f32[1024]{0:T(1024)} %param.41) | copy-start | bytes 12292
  347.1 192.0 %all-gather.7.cloned.1.call-start = ((), (), s32[]{:S(2)}) async-start(), calls=%async_computation.6 | async-start | bytes 15728640 | tf_op jit(solution)/shard_map/all_gather | solution.py:165
  456.8 173.5 %all-gather.9.cloned.1.call-start = ((), (), s32[]{:S(2)}) async-start(), calls=%async_computation.8 | async-start | bytes 15728640 | tf_op jit(solution)/shard_map/all_gather | solution.py:187
  460.3 108.4 %copy-start.43 = (f32[3]{0:T(128)}, f32[3]{0:T(128)S(1)}, u32[]{:S(2)}) copy-start(f32[3]{0:T(128)S(1)} %dynamic_slice.47) | copy-start | bytes 40
  465.1 317.4 %reduce-scatter.9.cloned.1.call-start = ((), (), s32[]{:S(2)}) async-start(), calls=%async_computation.9 | async-start | bytes 15728640 | tf_op jit(solution)/shard_map/reduce_scatter | solution.py:214
  683.3 200.7 %reduce-scatter.7.cloned.1.call-start = ((), (), s32[]{:S(2)}) async-start(), calls=%async_computation.7 | async-start | bytes 15728640 | tf_op jit(solution)/shard_map/reduce_scatter | solution.py:183
  706.2 275.4 %all-gather.11.cloned.1.call-start = ((), (), s32[]{:S(2)}) async-start(), calls=%async_computation.10 | async-start | bytes 15728640 | tf_op jit(solution)/shard_map/all_gather | solution.py:222
  788.4 95.6 %copy-start.42 = (f32[1024]{0:T(1024)S(1)}, f32[1024]{0:T(1024)}, u32[]{:S(2)}) copy-start(f32[1024]{0:T(1024)} %param.37) | copy-start | bytes 12292
  788.4 95.6 %copy-start.44 = (f32[3]{0:T(128)S(1)}, f32[3]{0:T(128)}, u32[]{:S(2)}) copy-start(f32[3]{0:T(128)} %copy-done.43) | copy-start | bytes 40
  899.2 902.9 %all-reduce.5.cloned.1.call-start = ((), (), s32[]{:S(2)}) async-start(), calls=%async_computation.12 | async-start | bytes 12582912 | tf_op jit(solution)/shard_map/psum | solution.py:270
  1587.3 315.7 %reduce-scatter.11.cloned.1.call-start = ((), (), s32[]{:S(2)}) async-start(), calls=%async_computation.11 | async-start | bytes 15728640 | tf_op jit(solution)/shard_map/reduce_scatter | solution.py:263
  1812.1 90.8 %copy-start.22 = (f32[3,512]{1,0:T(4,128)S(1)}, f32[3,512]{1,0:T(4,128)}, u32[]{:S(2)}) copy-start(f32[3,512]{1,0:T(4,128)} %copy-done.21) | copy-start | bytes 18436
  1812.1 90.8 %copy-start.34 = (f32[1024]{0:T(1024)S(1)}, f32[1024]{0:T(1024)}, u32[]{:S(2)}) copy-start(f32[1024]{0:T(1024)} %param.38) | copy-start | bytes 12292
  1818.0 89.3 %copy-start.29 = (f32[3,512]{1,0:T(4,128)S(1)}, f32[3,512]{1,0:T(4,128)}, u32[]{:S(2)}) copy-start(f32[3,512]{1,0:T(4,128)} %copy-done.28) | copy-start | bytes 18436
  1818.0 89.4 %copy-start.25 = (f32[3,512]{1,0:T(4,128)S(1)}, f32[3,512]{1,0:T(4,128)}, u32[]{:S(2)}) copy-start(f32[3,512]{1,0:T(4,128)} %copy-done.24) | copy-start | bytes 18436
  1821.7 91.2 %copy-start.35 = (f32[1024]{0:T(1024)S(1)}, f32[1024]{0:T(1024)}, u32[]{:S(2)}) copy-start(f32[1024]{0:T(1024)} %get-tuple-element.318) | copy-start | bytes 12292
  1821.7 91.2 %copy-start.36 = (f32[1024]{0:T(1024)S(1)}, f32[1024]{0:T(1024)}, u32[]{:S(2)}) copy-start(f32[1024]{0:T(1024)} %get-tuple-element.314) | copy-start | bytes 12292
  1821.7 91.2 %copy-start.37 = (f32[1024]{0:T(1024)S(1)}, f32[1024]{0:T(1024)}, u32[]{:S(2)}) copy-start(f32[1024]{0:T(1024)} %get-tuple-element.396) | copy-start | bytes 12292
  1821.7 91.2 %copy-start.38 = (f32[1024]{0:T(1024)S(1)}, f32[1024]{0:T(1024)}, u32[]{:S(2)}) copy-start(f32[1024]{0:T(1024)} %get-tuple-element.411) | copy-start | bytes 12292
  (105 other events, 966.3 us)
Sparse Core Ops, SparseCore 0:
  16.5 84.7 all-gather.4
  347.2 99.0 reduce-scatter.4
  456.9 82.0 all-gather.6
  540.5 82.0 all-gather.8
  683.4 99.0 reduce-scatter.8
  785.0 99.0 reduce-scatter.6
  899.4 82.1 all-gather.10
  1587.4 214.7 all-reduce.4
  1804.9 97.9 reduce-scatter.10
where the time goes:
time: 1990 us; the launch traced here: 1970 us
  waiting for transfers between devices  715 us (36%)
  matrix products  649 us (33%)
  other arithmetic  334 us (17%)
  local copies, waits for them, and re-layouts  196 us (10%)
  blocking collectives  62.6 us (3%)
    psum x1, waiting for transfers between devices, shards(): lax.psum(query_key_value_gradient.astype(jnp.bfloat16), 'dp')  168 us
    convert_element_type x12, other arithmetic, one_block(): grad_low = grad_scores.astype(jnp.bfloat16)  127 us
    dot_general x12, matrix products, one_block(): jnp.einsum('qhd,khd->hqk', grad_block, values, preferred_element_type=jnp...  113 us
    reduce_scatter x1, waiting for transfers between devices, shards(): lax.psum_scatter(attn_part.astype(jnp.bfloat16), 'tensor', scatter_dimens...  99.1 us
    reduce_scatter x1, waiting for transfers between devices, shards(): lax.psum_scatter(perceptron_portion.astype(jnp.bfloat16), 'tensor', scatt...  88.3 us
    all_gather x1, waiting for transfers between devices, shards(): normalized_every = lax.all_gather(normed, 'tensor', axis=1, tiled=True)  84.7 us
    dot_general x12, matrix products, one_block(): jnp.einsum('hqk,khd->qhd', grad_low, key_rows, preferred_element_type=jnp...  82.8 us
    dot_general x24, matrix products, one_block(): jnp.einsum('qhd,khd->hqk', query_block, key_rows, preferred_element_type=...  82.5 us
  transfers between devices with their start and end apart: 9, of which 8 were waited for; matrix products, arithmetic and copies ran while one was open for 11% of the time, Pallas kernels for 0%

commit v1 on v0

v1 whole, which is shorter than its diff:
```python
import jax
import jax.numpy as jnp
from jax import lax
from jax.experimental import pallas as pl
from jax.experimental.pallas import tpu as pltpu
from jax.sharding import PartitionSpec as P

HD = 64
SCORE_SCALE = HD ** (-0.5)
LOG2E = 1.4426950408889634
SQRT_HALF = 0.7071067811865476
INV_SQRT_2PI = 0.3989422804014327
epsilon = 1e-05
f32 = jnp.float32
bf16 = jnp.bfloat16
VMEM_LIMIT = 60 << 20
COST_SCALE = 64


def nn(a, b):
    return lax.dot_general(a, b, (((1,), (0,)), ((), ())), preferred_element_type=f32)


def nt(a, b):
    return lax.dot_general(a, b, (((1,), (1,)), ((), ())), preferred_element_type=f32)


def tn(a, b):
    return lax.dot_general(a, b, (((0,), (0,)), ((), ())), preferred_element_type=f32)


def tie(first, second):
    return lax.optimization_barrier((first, second))


def largest_block(extent, limit):
    block = min(extent, limit)
    while extent % block:
        block //= 2
    return block


def norm_rows(source, norm_gain, norm_shift):
    row_mean = jnp.mean(source, axis=-1, keepdims=True)
    centred = source - row_mean
    spread = jnp.mean(centred * centred, axis=-1, keepdims=True)
    return centred * lax.rsqrt(spread + epsilon) * norm_gain + norm_shift


def attend(qkv):
    _, length, width = qkv.shape
    lanes = min(128, width)
    heads = lanes // HD
    qblock = largest_block(length, 1024)
    to_log2 = SCORE_SCALE * LOG2E

    def body(q_ref, k_ref, v_ref, out_ref, lse_ref):
        queries = q_ref[...]
        keys = k_ref[...]
        values_t = v_ref[...].T
        lane = lax.broadcasted_iota(jnp.int32, (1, lanes), 1)
        outs = []
        for h in range(heads):
            own = queries
            if heads > 1:
                own = jnp.where(lane // HD == h, queries, jnp.zeros_like(queries))
            scores = nt(keys, own)
            top = jnp.max(scores, axis=0, keepdims=True)
            exp_scores = jnp.exp2((scores - top) * to_log2)
            total = jnp.sum(exp_scores, axis=0, keepdims=True)
            outs.append(nn(values_t[h * HD : (h + 1) * HD, :], exp_scores.astype(bf16)) / total)
            lse_ref[h : h + 1, :] = top * to_log2 + jnp.log2(total)
        out_ref[...] = jnp.concatenate(outs, axis=0).T.astype(bf16)

    pairs = width // lanes
    return pl.pallas_call(
        body,
        grid=(pairs, length // qblock),
        in_specs=[
            pl.BlockSpec((None, qblock, lanes), lambda h, j: (0, j, h)),
            pl.BlockSpec((None, length, lanes), lambda h, j: (1, 0, h)),
            pl.BlockSpec((None, length, lanes), lambda h, j: (2, 0, h)),
        ],
        out_specs=[
            pl.BlockSpec((qblock, lanes), lambda h, j: (j, h)),
            pl.BlockSpec((None, heads, qblock), lambda h, j: (h, 0, j)),
        ],
        out_shape=[
            jax.ShapeDtypeStruct((length, width), bf16),
            jax.ShapeDtypeStruct((pairs, heads, length), f32),
        ],
        compiler_params=pltpu.CompilerParams(vmem_limit_bytes=VMEM_LIMIT),
        cost_estimate=pl.CostEstimate(
            flops=8 * length * length * width // COST_SCALE,
            transcendentals=0,
            bytes_accessed=length * width,
        ),
        name="attend",
    )(qkv, qkv, qkv)


def attend_back(qkv, attended, grad_attended, lse):
    _, length, width = qkv.shape
    lanes = min(128, width)
    heads = lanes // HD
    kblock = largest_block(length, 512)
    kblocks = length // kblock
    to_log2 = SCORE_SCALE * LOG2E

    def body(q_ref, k_ref, v_ref, out_ref, grad_ref, lse_ref, dqkv_ref, dq_acc, row_dot):
        kb = pl.program_id(1)
        queries = q_ref[...]
        grads = grad_ref[...]
        keys = k_ref[...]
        values = v_ref[...]
        keys_t = keys.T
        lane = lax.broadcasted_iota(jnp.int32, (1, lanes), 1)

        @pl.when(kb == 0)
        def _():
            product = out_ref[...].astype(f32) * grads.astype(f32)
            high = product.astype(bf16)
            rest = (product - high.astype(f32)).astype(bf16)
            pick = lax.broadcasted_iota(jnp.int32, (8, lanes), 0)
            mask = (lax.broadcasted_iota(jnp.int32, (8, lanes), 1) // HD == pick).astype(f32).astype(bf16)
            row_dot[...] = nt(mask, high) + nt(mask, rest)

        dk = None
        dv = None
        dqs = []
        for h in range(heads):
            own_q = queries
            own_g = grads
            if heads > 1:
                mine = lane // HD == h
                own_q = jnp.where(mine, queries, jnp.zeros_like(queries))
                own_g = jnp.where(mine, grads, jnp.zeros_like(grads))
            scores = nt(keys, own_q)
            weights = jnp.exp2(scores * to_log2 - lse_ref[h : h + 1, :])
            grad_weights = nt(values, own_g)
            grad_scores = (weights * (grad_weights - row_dot[h : h + 1, :])).astype(bf16)
            dv_h = nn(weights.astype(bf16), own_g)
            dk_h = nn(grad_scores, own_q)
            dv = dv_h if dv is None else dv + dv_h
            dk = dk_h if dk is None else dk + dk_h
            dqs.append(nn(keys_t[h * HD : (h + 1) * HD, :], grad_scores))
        rows = pl.ds(pl.multiple_of(kb * kblock, kblock), kblock)
        dqkv_ref[1, rows, :] = (dk * SCORE_SCALE).astype(bf16)
        dqkv_ref[2, rows, :] = dv.astype(bf16)
        dq = jnp.concatenate(dqs, axis=0)
        if kblocks == 1:
            dqkv_ref[0] = (dq * SCORE_SCALE).T.astype(bf16)
            return

        @pl.when(kb == 0)
        def _():
            dq_acc[...] = dq

        @pl.when((kb > 0) & (kb < kblocks - 1))
        def _():
            dq_acc[...] += dq

        @pl.when(kb == kblocks - 1)
        def _():
            dqkv_ref[0] = ((dq_acc[...] + dq) * SCORE_SCALE).T.astype(bf16)

    pairs = width // lanes
    return pl.pallas_call(
        body,
        grid=(pairs, kblocks),
        in_specs=[
            pl.BlockSpec((None, length, lanes), lambda h, kb: (0, 0, h)),
            pl.BlockSpec((None, kblock, lanes), lambda h, kb: (1, kb, h)),
            pl.BlockSpec((None, kblock, lanes), lambda h, kb: (2, kb, h)),
            pl.BlockSpec((length, lanes), lambda h, kb: (0, h)),
            pl.BlockSpec((length, lanes), lambda h, kb: (0, h)),
            pl.BlockSpec((None, heads, length), lambda h, kb: (h, 0, 0)),
        ],
        out_specs=pl.BlockSpec((3, length, lanes), lambda h, kb: (0, 0, h)),
        out_shape=jax.ShapeDtypeStruct((3, length, width), bf16),
        scratch_shapes=[pltpu.VMEM((lanes, length), f32), pltpu.VMEM((8, length), f32)],
        compiler_params=pltpu.CompilerParams(vmem_limit_bytes=VMEM_LIMIT),
        cost_estimate=pl.CostEstimate(
            flops=20 * length * length * width // COST_SCALE,
            transcendentals=0,
            bytes_accessed=length * width,
        ),
        name="attend_back",
    )(qkv, qkv, qkv, attended, grad_attended, lse)


def mlp_forward(normed, up, up_bias, down, total):
    rows, model = normed.shape
    units = up.shape[1]
    block = largest_block(rows, 512)
    first = total is None

    def body(*refs):
        if first:
            x_ref, up_ref, bias_ref, down_ref, hidden_ref, slope_ref, sum_ref = refs
        else:
            x_ref, up_ref, bias_ref, down_ref, before_ref, hidden_ref, slope_ref, sum_ref = refs
        part = largest_block(units, 256)
        for j in range(units // part):
            cols = slice(j * part, (j + 1) * part)
            pre = nn(x_ref[...], up_ref[:, cols]) + bias_ref[:, cols]
            cdf = 0.5 + 0.5 * lax.erf(pre * SQRT_HALF)
            density = jnp.exp2(pre * pre * (-0.5 * LOG2E)) * INV_SQRT_2PI
            hidden_ref[:, cols] = (pre * cdf).astype(bf16)
            slope_ref[:, cols] = (cdf + pre * density).astype(bf16)
        out = nn(hidden_ref[...], down_ref[...])
        sum_ref[...] = out if first else before_ref[...] + out

    row_spec = pl.BlockSpec((block, model), lambda i: (i, 0))
    unit_spec = pl.BlockSpec((block, units), lambda i: (i, 0))
    in_specs = [
        row_spec,
        pl.BlockSpec((model, units), lambda i: (0, 0)),
        pl.BlockSpec((1, units), lambda i: (0, 0)),
        pl.BlockSpec((units, model), lambda i: (0, 0)),
    ]
    operands = [normed, up, up_bias, down]
    if not first:
        in_specs.append(row_spec)
        operands.append(total)
    return pl.pallas_call(
        body,
        grid=(rows // block,),
        in_specs=in_specs,
        out_specs=[unit_spec, unit_spec, row_spec],
        out_shape=[
            jax.ShapeDtypeStruct((rows, units), bf16),
            jax.ShapeDtypeStruct((rows, units), bf16),
            jax.ShapeDtypeStruct((rows, model), f32),
        ],
        input_output_aliases={} if first else {4: 2},
        compiler_params=pltpu.CompilerParams(vmem_limit_bytes=VMEM_LIMIT),
        cost_estimate=pl.CostEstimate(
            flops=4 * rows * model * units // COST_SCALE,
            transcendentals=0,
            bytes_accessed=rows * units,
        ),
        name="mlp_forward",
    )(*operands)


def mlp_backward(cot, down, slope, up, total):
    rows, model = cot.shape
    units = up.shape[1]
    block = largest_block(rows, 512)
    first = total is None

    def body(*refs):
        if first:
            cot_ref, down_ref, slope_ref, up_ref, grad_ref, bias_ref, sum_ref = refs
        else:
            cot_ref, down_ref, slope_ref, up_ref, before_ref, grad_ref, bias_ref, sum_ref = refs
        part = largest_block(units, 256)

        @pl.when(pl.program_id(0) == 0)
        def _():
            bias_ref[...] = jnp.zeros_like(bias_ref)

        for j in range(units // part):
            cols = slice(j * part, (j + 1) * part)
            grad = nt(cot_ref[...], down_ref[cols, :]) * slope_ref[:, cols].astype(f32)
            low = grad.astype(bf16)
            grad_ref[:, cols] = low
            bias_ref[:, cols] += jnp.sum(low.astype(f32), axis=0, keepdims=True)
        out = nt(grad_ref[...], up_ref[...])
        sum_ref[...] = out if first else before_ref[...] + out

    row_spec = pl.BlockSpec((block, model), lambda i: (i, 0))
    unit_spec = pl.BlockSpec((block, units), lambda i: (i, 0))
    in_specs = [
        row_spec,
        pl.BlockSpec((units, model), lambda i: (0, 0)),
        unit_spec,
        pl.BlockSpec((model, units), lambda i: (0, 0)),
    ]
    operands = [cot, down, slope, up]
    if not first:
        in_specs.append(row_spec)
        operands.append(total)
    return pl.pallas_call(
        body,
        grid=(rows // block,),
        in_specs=in_specs,
        out_specs=[unit_spec, pl.BlockSpec((1, units), lambda i: (0, 0)), row_spec],
        out_shape=[
            jax.ShapeDtypeStruct((rows, units), bf16),
            jax.ShapeDtypeStruct((1, units), f32),
            jax.ShapeDtypeStruct((rows, model), f32),
        ],
        input_output_aliases={} if first else {4: 2},
        compiler_params=pltpu.CompilerParams(vmem_limit_bytes=VMEM_LIMIT),
        cost_estimate=pl.CostEstimate(
            flops=4 * rows * model * units // COST_SCALE,
            transcendentals=0,
            bytes_accessed=rows * units,
        ),
        name="mlp_backward",
    )(*operands)


def project_back(normed, dqkv, weight, before, last):
    rows, model = normed.shape
    width = weight.shape[2]
    block = largest_block(rows, 512)
    steps = rows // block
    first = before is None

    def kernel(*refs):
        normed_ref, dqkv_ref, weight_ref = refs[:3]
        rest = refs[3:]
        if not first:
            wgrad_before, column_before = rest[:2]
            rest = rest[2:]
        row_ref, wgrad_ref, column_ref = rest[:3]
        step = pl.program_id(0)

        @pl.when(step == 0)
        def _():
            if first:
                wgrad_ref[...] = jnp.zeros_like(wgrad_ref)
                column_ref[...] = jnp.zeros_like(column_ref)
            else:
                wgrad_ref[...] = wgrad_before[...]
                column_ref[...] = column_before[...]

        row_grad = nt(dqkv_ref[0], weight_ref[0])
        for c in range(1, 3):
            row_grad = row_grad + nt(dqkv_ref[c], weight_ref[c])
        row_ref[...] = row_grad.astype(bf16)
        for c in range(3):
            wgrad_ref[c] += tn(normed_ref[...], dqkv_ref[c])
            column_ref[c : c + 1, :] += jnp.sum(dqkv_ref[c].astype(f32), axis=0, keepdims=True)
        if last:
            low_ref = rest[3]

            @pl.when(step == steps - 1)
            def _():
                low_ref[:, :model, :] = wgrad_ref[...].astype(bf16)
                for c in range(3):
                    row = jnp.broadcast_to(column_ref[c : c + 1, :], (16, width))
                    low_ref[c, model:, :] = row.astype(bf16)

    whole = pl.BlockSpec((3, model, width), lambda i: (0, 0, 0))
    columns = pl.BlockSpec((8, width), lambda i: (0, 0))
    row_spec = pl.BlockSpec((block, model), lambda i: (i, 0))
    operands = [normed, dqkv, weight]
    in_specs = [row_spec, pl.BlockSpec((3, block, width), lambda i: (0, i, 0)), whole]
    if not first:
        operands += list(before)
        in_specs += [whole, columns]
    out_specs = [row_spec, whole, columns]
    out_shape = [
        jax.ShapeDtypeStruct((rows, model), bf16),
        jax.ShapeDtypeStruct((3, model, width), f32),
        jax.ShapeDtypeStruct((8, width), f32),
    ]
    if last:
        out_specs.append(pl.BlockSpec((3, model + 16, width), lambda i: (0, 0, 0)))
        out_shape.append(jax.ShapeDtypeStruct((3, model + 16, width), bf16))
    return pl.pallas_call(
        kernel,
        grid=(steps,),
        in_specs=in_specs,
        out_specs=out_specs,
        out_shape=out_shape,
        input_output_aliases={} if first else {3: 1, 4: 2},
        compiler_params=pltpu.CompilerParams(vmem_limit_bytes=VMEM_LIMIT),
        cost_estimate=pl.CostEstimate(
            flops=12 * rows * model * width // COST_SCALE,
            transcendentals=0,
            bytes_accessed=rows * width,
        ),
        name="project_back",
    )(*operands)


def make_shards(tensor_size, group_size):
    square = tensor_size == 4

    def swap(value, bits):
        return lax.ppermute(value, "tensor", [(i, i ^ bits) for i in range(tensor_size)])

    def gather_far(own):
        return swap(own, 2) if square else lax.all_gather(own, "tensor")

    def gather_near(own, far):
        if not square:
            return [far[i] for i in range(tensor_size)]
        return [own, swap(own, 1), far, swap(far, 1)]

    def exchange_blocks(blocks):
        if not square:
            moved = lax.all_to_all(jnp.stack(blocks), "tensor", 0, 0)
            return [moved[i] for i in range(tensor_size)]
        return [blocks[0], swap(blocks[1], 1), swap(blocks[2], 2), swap(blocks[3], 3)]

    def sum_near(blocks, anchor):
        if not square:
            return (jnp.stack(blocks), None), anchor
        anchor, (near_own, near_far) = tie(anchor, (swap(blocks[1], 1), swap(blocks[3], 1)))
        far = (blocks[2].astype(f32) + near_far.astype(f32)).astype(blocks[2].dtype)
        return (blocks[0].astype(f32) + near_own.astype(f32), far), anchor

    def sum_far(stage, anchor):
        own, far = stage
        if not square:
            own = lax.psum_scatter(own, "tensor", scatter_dimension=0, tiled=False).astype(f32)
            anchor, own = tie(anchor, own)
            return own, anchor
        anchor, received = tie(anchor, swap(far, 2))
        return own + received.astype(f32), anchor

    steps = []
    for axis, size in (("tensor", tensor_size), ("dp", group_size)):
        bit = 1
        while bit < size:
            steps.append((axis, [(i, i ^ bit) for i in range(size)]))
            bit *= 2
    tensor_steps = [step for step in steps if step[0] == "tensor"]

    def sum_step(value, step, anchor):
        anchor, received = tie(anchor, lax.ppermute(value, step[0], step[1]))
        return value + received, anchor

    def in_order(stacked):
        if not square:
            return stacked
        own = lax.axis_index("tensor")
        return jnp.concatenate(
            [lax.dynamic_slice_in_dim(stacked, own ^ i, 1, axis=0) for i in range(tensor_size)], axis=0
        )

    def shards(
        patches,
        cotangent,
        empty_slots,
        dataset_id,
        dataset_weight,
        query_key_value_weight,
        qv_bias,
        output_projection_weight,
        out_bias,
        up_projection_weight,
        up_bias,
        down_projection_weight,
        down_bias,
        attn_gain,
        attn_shift,
        mlp_gain,
        mlp_shift,
    ):
        slot_count, own_rows, model = patches.shape
        width = query_key_value_weight.shape[2]
        group_slots = empty_slots.shape[0]
        slot_index = jnp.arange(group_slots * slot_count, dtype=jnp.int32) % slot_count
        filled = jnp.repeat(slot_count - empty_slots, slot_count)
        valid_all = (slot_index < filled).astype(f32)
        table_hits = dataset_id[:, None] == jnp.arange(dataset_weight.shape[0], dtype=jnp.int32)[None, :]
        numerator = jnp.sum(jnp.where(table_hits, dataset_weight[None, :], 0), axis=1).astype(f32)
        total_items = jnp.sum(valid_all)
        total_weight = jnp.sum(valid_all * numerator)
        multiplier_whole = valid_all * numerator * total_items / total_weight
        own_start = lax.axis_index("dp") * slot_count
        own_scale = lax.dynamic_slice_in_dim(multiplier_whole, own_start, slot_count)
        own_valid = lax.dynamic_slice_in_dim(valid_all, own_start, slot_count)
        row_scale = jnp.repeat(own_scale, own_rows)[:, None]
        row_valid = jnp.repeat(own_valid, own_rows)[:, None]
        all_rows = slot_count * own_rows

        inputs = patches.astype(f32)
        normed = norm_rows(inputs, attn_gain, attn_shift).astype(bf16)
        proj_bias = jnp.stack([qv_bias[0], jnp.zeros_like(qv_bias[0]), qv_bias[1]])[:, None, :]

        bias_row = up_bias[None, :]
        bias_far = gather_far(bias_row)
        normed = [normed[i] for i in range(slot_count)]
        normed_far = [gather_far(normed[0])]
        qkvs, attended, lses, attended_rows, normed_every = [], [], [], [], []
        for i in range(slot_count):
            if i + 1 < slot_count:
                if i == 0:
                    normed_far[0], normed[1] = tie(normed_far[0], normed[1])
                normed_far.append(gather_far(normed[i + 1]))
            every = jnp.concatenate(gather_near(normed[i], normed_far[i]), axis=0)
            if i == slot_count - 1:
                every, (up_far, out_far) = tie(every, (up_far, out_far))
            else:
                every = lax.optimization_barrier(every)
            qkv = (
                jnp.einsum("wz,gzh->gwh", every, query_key_value_weight, preferred_element_type=f32) + proj_bias
            ).astype(bf16)
            if i == 0:
                qkv, (out_own, up_own, ahead) = tie(
                    qkv, (output_projection_weight, up_projection_weight, normed[min(2, slot_count - 1)])
                )
                if slot_count > 2:
                    normed[2] = ahead
                out_far = gather_far(out_own)
                up_far = gather_far(up_own)
            if i == 0:
                qkv, bias_far = tie(qkv, bias_far)
            out, lse = attend(qkv)
            if i == 0:
                out, down_own = tie(out, down_projection_weight)
                down_far = gather_far(down_own)
            if i == slot_count - 1:
                out, down_far = tie(out, down_far)
            moved = exchange_blocks([out[b * own_rows : (b + 1) * own_rows] for b in range(tensor_size)])
            normed_every.append(every)
            qkvs.append(qkv)
            attended.append(out)
            lses.append(lse)
            attended_rows.append(jnp.concatenate(moved, axis=1))
        attended_rows = jnp.concatenate(attended_rows, axis=0)
        out_weight = jnp.concatenate(gather_near(out_own, out_far), axis=0)
        attended_rows, out_weight = tie(attended_rows, out_weight)
        bias_blocks = gather_near(bias_row, bias_far)
        up_blocks = gather_near(up_own, up_far)
        down_blocks = gather_near(down_own, down_far)

        flat_inputs = inputs.reshape(all_rows, model)
        residual = flat_inputs + nn(attended_rows, out_weight) + out_bias
        normed_mlp = norm_rows(residual, mlp_gain, mlp_shift).astype(bf16)
        cot_scaled = cotangent.astype(f32).reshape(all_rows, model) * row_scale
        cot_low = cot_scaled.astype(bf16)

        total = None
        hiddens, slopes = [], []
        for b in range(tensor_size):
            hidden, slope, total = mlp_forward(normed_mlp, up_blocks[b], bias_blocks[b], down_blocks[b], total)
            hiddens.append(hidden)
            slopes.append(slope)
        output = ((residual + total + down_bias) * row_valid).astype(bf16)

        down_grads = [tn(hidden, cot_low).astype(bf16) for hidden in hiddens]
        cot_back, down_grads = tie(cot_low, down_grads)

        total = None
        pre_grads, bias_grads = [], []
        for b in range(tensor_size):
            pre_grad, bias_grad, total = mlp_backward(cot_back, down_blocks[b], slopes[b], up_blocks[b], total)
            if b == 0:
                down_stage, total = sum_near(down_grads, total)
            pre_grads.append(pre_grad)
            bias_grads.append(bias_grad)
        down_sum, total = sum_far(down_stage, total)
        down_all = lax.psum(down_sum.astype(bf16), "dp")
        mlp_norm_back = jax.vjp(norm_rows, residual, mlp_gain, mlp_shift)[1]
        grad_resid_norm, grad_mlp_gain, grad_mlp_shift = mlp_norm_back(total)
        grad_residual = cot_scaled + grad_resid_norm
        grad_out_bias = jnp.sum(grad_residual, axis=0)
        grad_down_bias = jnp.sum(cot_scaled, axis=0)
        grad_res_low = grad_residual.astype(bf16)
        grad_attended_rows = nt(grad_res_low, out_weight).astype(bf16)
        grad_attended_rows, (pre_grads, grad_res_wide) = tie(grad_attended_rows, (pre_grads, grad_res_low))

        grad_attended = []
        for i in range(slot_count):
            rows = grad_attended_rows[i * own_rows : (i + 1) * own_rows]
            moved = exchange_blocks([rows[:, b * width : (b + 1) * width] for b in range(tensor_size)])
            grad_attended.append(jnp.concatenate(moved, axis=0))

        up_grads = [tn(normed_mlp, pre_grad).astype(bf16) for pre_grad in pre_grads]
        out_grads = tn(attended_rows, grad_res_wide).astype(bf16)
        out_grads = [out_grads[b * width : (b + 1) * width] for b in range(tensor_size)]

        up_stage, grad_attended[0] = sum_near(up_grads, grad_attended[0])
        out_stage, grad_attended[0] = sum_near(out_grads, grad_attended[0])
        small_rows = jnp.stack([grad_mlp_gain, grad_mlp_shift, grad_out_bias, grad_down_bias])
        bias_rows = in_order(jnp.concatenate(bias_grads, axis=0))
        smalls = jnp.concatenate([small_rows.reshape(-1), bias_rows.reshape(-1)]).reshape(-1, 128)
        waiting = list(steps)

        weights_wide = query_key_value_weight.astype(f32)
        sums = None
        grad_normed = []
        for i in range(slot_count):
            last = i == slot_count - 1
            dqkv = attend_back(qkvs[i], attended[i], grad_attended[i], lses[i])
            if i == 0:
                up_sum, dqkv = sum_far(up_stage, dqkv)
                out_sum, dqkv = sum_far(out_stage, dqkv)
                dqkv, down_all = tie(dqkv, down_all)
                up_sum, down_all = tie(up_sum, down_all)
                up_all = lax.psum((up_sum.astype(bf16), out_sum.astype(bf16)), "dp")
            if last:
                dqkv, up_all = tie(dqkv, up_all)
            if waiting:
                smalls, dqkv = sum_step(smalls, waiting.pop(0), dqkv)
            results = project_back(normed_every[i], dqkv, query_key_value_weight, sums, last)
            partial, sums = results[0], results[1:3]
            while waiting and (last or len(waiting) % 2):
                smalls, partial = sum_step(smalls, waiting.pop(0), partial)
            if last:
                qkv_all = lax.psum(results[3], "dp")
            grad_normed.append([partial[b * own_rows : (b + 1) * own_rows] for b in range(tensor_size)])
        for i in range(slot_count):
            anchor = inputs[i]
            stage, anchor = sum_near(grad_normed[i], anchor)
            grad_normed[i] = sum_far(stage, anchor)[0]
        grad_normed, qkv_all = tie(jnp.stack(grad_normed), qkv_all)
        attn_norm_back = jax.vjp(lambda v: norm_rows(v, attn_gain, attn_shift), inputs)[1]
        grad_inputs = (
            grad_residual.reshape(slot_count, own_rows, model) + attn_norm_back(grad_normed)[0]
        ).astype(bf16)
        weight_grad = qkv_all[:, :model].astype(f32)
        columns = qkv_all[:, model].astype(f32)
        raw = jnp.stack(
            [
                jnp.sum(weight_grad * weights_wide, axis=(0, 2)),
                jnp.sum(columns[:, None, :] * weights_wide, axis=(0, 2)),
            ]
        )
        for step in tensor_steps:
            raw = raw + lax.ppermute(raw, step[0], step[1])
        up_all, out_all = [value.astype(f32) for value in up_all]
        down_all = down_all.astype(f32)
        inverse = 1.0 / total_items
        smalls = smalls.reshape(-1) * inverse
        small_rows = smalls[: 4 * model].reshape(4, model)
        units = up_bias.shape[0]
        bias_all = lax.dynamic_slice_in_dim(smalls[4 * model :], lax.axis_index("tensor") * units, units)
        shift_all = raw[1] * inverse
        gain_all = (raw[0] * inverse - attn_shift * shift_all) / attn_gain
        columns = columns * inverse
        return (
            output.reshape(patches.shape),
            grad_inputs,
            weight_grad * inverse,
            jnp.stack([columns[0], columns[2]]),
            out_all * inverse,
            small_rows[2],
            up_all * inverse,
            bias_all,
            down_all * inverse,
            small_rows[3],
            gain_all,
            shift_all,
            small_rows[0],
            small_rows[1],
        )

    return shards


def solution(mesh):
    items = P("dp", "tensor", None)
    return jax.shard_map(
        make_shards(mesh.shape["tensor"], mesh.shape["dp"]),
        mesh=mesh,
        in_specs=(
            items,
            items,
            P(),
            P(),
            P(),
            P(None, None, "tensor"),
            P(None, "tensor"),
            P("tensor", None),
            P(),
            P(None, "tensor"),
            P("tensor"),
            P("tensor", None),
            P(),
            P(),
            P(),
            P(),
            P(),
        ),
        out_specs=(
            items,
            items,
            P(None, None, "tensor"),
            P(None, "tensor"),
            P("tensor", None),
            P(),
            P(None, "tensor"),
            P("tensor"),
            P("tensor", None),
            P(),
            P(),
            P(),
            P(),
            P(),
        ),
        check_vma=False,
    )
```

time: 1990 us -> 882 us (0.44)
  matrix products: 649 us -> 72.4 us
  waiting for transfers between devices: 715 us -> 210 us
  Pallas kernels: 0 us -> 367 us
  other arithmetic: 334 us -> 136 us
  local copies, waits for them, and re-layouts: 196 us -> 32.4 us
  blocking collectives: 62.6 us -> 0 us
  starting transfers between devices: 0.78 us -> 39.1 us
    dot_general x96 -> x14, matrix products: 649 us -> 72.4 us  [the longest x9 50.1 us: tn(): lax.dot_general(a, b, (((0,), (0,)), ((), ())), preferred_element_type=f32)]
    pallas_call x0 -> x17, Pallas kernels: none -> 367 us  [the longest x3 147 us: attend_back(): pl.pallas_call(body, grid=(pairs, kblocks), in_specs=[pl.BlockSpec((None,...]
    reduce_scatter x4 -> x0, waiting for transfers between devices: 345 us -> none  [the longest x1 99.1 us: shards(): lax.psum_scatter(attn_part.astype(jnp.bfloat16), 'tensor', scatter_dimens...]
    all_gather x4 -> x0, waiting for transfers between devices: 202 us -> none  [the longest x1 84.7 us: shards(): normalized_every = lax.all_gather(normed, 'tensor', axis=1, tiled=True)]
    convert_element_type x20 -> x15, other arithmetic: 217 us -> 38.4 us  [the longest x6 18.3 us: sum_near(): far = (blocks[2].astype(f32) + near_far.astype(f32)).astype(blocks[2].dtype)]
    ppermute x0 -> x64, waiting for transfers between devices: none -> 130 us  [the longest x57 129 us: swap(): lax.ppermute(value, 'tensor', [(i, i ^ bits) for i in range(tensor_size)])]
    psum x1 -> x3, waiting for transfers between devices: 168 us -> 79.4 us  [the longest x1 56 us: shards(): qkv_all = lax.psum(results[3], 'dp')]
    psum x2 -> x0, blocking collectives: 62.6 us -> none  [the longest x1 39.7 us: shards(): lax.psum((grad_attn_gain, grad_attn_shift, sensitivity_feedforward_scale,...]
  transfers between devices with their start and end apart: 9 -> 67, of which waited for: 8 -> 19; matrix products, arithmetic and copies ran while one was open for 11% -> 19% of each run, Pallas kernels for 0% -> 40%
where the time goes in v1:
time: 882 us; the launch traced here: 873 us
  Pallas kernels  367 us (42%)
  waiting for transfers between devices  210 us (24%)
  other arithmetic  136 us (15%)
  matrix products  72.4 us (8%)
  starting transfers between devices  39.1 us (4%)
  local copies, waits for them, and re-layouts  32.4 us (4%)
  between operations  16 us (2%)
    pallas_call x3, Pallas kernels, attend_back(): pl.pallas_call(body, grid=(pairs, kblocks), in_specs=[pl.BlockSpec((None,...  147 us
    ppermute x57, waiting for transfers between devices, swap(): lax.ppermute(value, 'tensor', [(i, i ^ bits) for i in range(tensor_size)])  129 us
    pallas_call x3, Pallas kernels, attend(): pl.pallas_call(body, grid=(pairs, length // qblock), in_specs=[pl.BlockSp...  76.1 us
    psum x1, waiting for transfers between devices, shards(): qkv_all = lax.psum(results[3], 'dp')  56 us
    pallas_call x4, Pallas kernels, mlp_forward(): pl.pallas_call(body, grid=(rows // block,), in_specs=in_specs, out_specs=...  53.7 us
    pallas_call x4, Pallas kernels, mlp_backward(): pl.pallas_call(body, grid=(rows // block,), in_specs=in_specs, out_specs=...  52.2 us
    dot_general x9, matrix products, tn(): lax.dot_general(a, b, (((0,), (0,)), ((), ())), preferred_element_type=f32)  50.1 us
    pallas_call x3, Pallas kernels, project_back(): pl.pallas_call(kernel, grid=(steps,), in_specs=in_specs, out_specs=out_sp...  38 us
  transfers between devices with their start and end apart: 67, of which 19 were waited for; matrix products, arithmetic and copies ran while one was open for 19% of the time, Pallas kernels for 40%

profile of v1, /device:TPU:0, one launch (start us, length us, event | category | flops | bytes accessed | tf_op | source)
XLA Modules:
  0.0 872.8 jit_solution(5095008108178029465)
XLA Ops:
  18.3 23.5 %collective-permute-done.1 = bf16[512,1024]{1,0:T(8,128)(2,1)} collective-permute-done((bf16[512,1024]{1,0:T(8,128)(2,1)}, bf16[512,1024]{1,0:T(8,128)(2,1)}, u32[]{:S(2)}, u32[]{:S(2)}) %collective-permute-start.1) | collective-permute-done | bytes 1048608 | tf_op jit(solution)/shard_map/ppermute | solution.py:386
  47.3 22.0 %collective-permute-done.8 = bf16[512,1024]{1,0:T(8,128)(2,1)} collective-permute-done((bf16[512,1024]{1,0:T(8,128)(2,1)}, bf16[512,1024]{1,0:T(8,128)(2,1)}, u32[]{:S(2)}, u32[]{:S(2)}) %collective-permute-start.8) | collective-permute-done | bytes 1048608 | tf_op jit(solution)/shard_map/ppermute | solution.py:386
  79.1 25.3 %attend.3 = (bf16[2048,256]{1,0:T(8,128)(2,1)}, f32[2,2,2048]{2,1,0:T(2,128)}) custom-call(bf16[3,2048,256]{2,1,0:T(8,128)(2,1)} %fusion.10.q_ref.k_ref.v_ref, bf16[3,2048,256]{2,1,0:T(8,128)(2,1)} %fusion.10.q_ref.k_ref.v_ref, bf16[3,2048,256]{2,1,0:T(8,128)(2,1)} %fusion.10.q_ref.k_ref.v_ref), custom_call_target="tpu_custom_call" | custom-call | flops 134217728 | bytes 524288 | tf_op jit(solution)/shard_map/attend/pallas_call | solution.py:76
  117.7 25.6 %attend.4 = (bf16[2048,256]{1,0:T(8,128)(2,1)}, f32[2,2,2048]{2,1,0:T(2,128)}) custom-call(bf16[3,2048,256]{2,1,0:T(8,128)(2,1)} %fusion.11.q_ref.k_ref.v_ref, bf16[3,2048,256]{2,1,0:T(8,128)(2,1)} %fusion.11.q_ref.k_ref.v_ref, bf16[3,2048,256]{2,1,0:T(8,128)(2,1)} %fusion.11.q_ref.k_ref.v_ref), custom_call_target="tpu_custom_call" | custom-call | flops 134217728 | bytes 524288 | tf_op jit(solution)/shard_map/attend/pallas_call | solution.py:76
  161.7 25.2 %attend.5 = (bf16[2048,256]{1,0:T(8,128)(2,1)}, f32[2,2,2048]{2,1,0:T(2,128)}) custom-call(bf16[3,2048,256]{2,1,0:T(8,128)(2,1)} %fusion.12.q_ref.k_ref.v_ref, bf16[3,2048,256]{2,1,0:T(8,128)(2,1)} %fusion.12.q_ref.k_ref.v_ref, bf16[3,2048,256]{2,1,0:T(8,128)(2,1)} %fusion.12.q_ref.k_ref.v_ref), custom_call_target="tpu_custom_call" | custom-call | flops 134217728 | bytes 524288 | tf_op jit(solution)/shard_map/attend/pallas_call | solution.py:76
  186.9 14.5 %collective-permute-done.18.refs_3_.refs_1_ = bf16[1024,1024]{1,0:T(8,128)(2,1)} collective-permute-done((bf16[1024,1024]{1,0:T(8,128)(2,1)}, bf16[1024,1024]{1,0:T(8,128)(2,1)}, u32[]{:S(2)}, u32[]{:S(2)}) %collective-permute-start.18) | collective-permute-done | bytes 2097184 | tf_op jit(solution)/shard_map/ppermute | solution.py:386
  235.2 22.7 %maximum_maximum_fusion = bf16[1536,1024]{1,0:T(8,128)(2,1)S(1)} fusion(bf16[512,256]{1,0:T(8,128)(2,1)S(1)} %collective-permute-done.21, bf16[512,256]{1,0:T(8,128)(2,1)S(1)} %collective-permute-done.20, bf16[512,256]{1,0:T(8,128)(2,1)S(1)} %collective-permute-done.19, bf16[512,256]{1,0:T(8,128)(2,1)S(1)} %get-tuple-element.270, ...), kind=kLoop, calls=%fused_computation.46 | loop fusion | flops 37748736 | bytes 6291456 | tf_op jit(solution)/shard_map/concatenate | solution.py:519
  269.5 13.1 %mlp_forward.4 = (bf16[1536,1024]{1,0:T(8,128)(2,1)}, bf16[1536,1024]{1,0:T(8,128)(2,1)}, f32[1536,1024]{1,0:T(8,128)}) custom-call(bf16[1536,1024]{1,0:T(8,128)(2,1)} %add_convert_fusion.1.refs_0_, bf16[1024,1024]{1,0:T(8,128)(2,1)} %refs_3_.1, f32[1,1024]{1,0:T(1,128)} %bitcast.118, bf16[1024,1024]{1,0:T(8,128)(2,1)} %refs_1_.1), custom_call_target="tpu_custom_call" | custom-call | flops 100663296 | bytes 1572864 | tf_op jit(solution)/shard_map/mlp_forward/pallas_call | solution.py:226
  283.2 13.5 %mlp_forward.5 = (bf16[1536,1024]{1,0:T(8,128)(2,1)}, bf16[1536,1024]{1,0:T(8,128)(2,1)}, f32[1536,1024]{1,0:T(8,128)}) custom-call(bf16[1536,1024]{1,0:T(8,128)(2,1)} %add_convert_fusion.1.refs_0_, bf16[1024,1024]{1,0:T(8,128)(2,1)} %collective-permute-done.27.refs_1_.refs_3_, f32[1,1024]{1,0:T(1,128)} %copy-done.44, ...), custom_call_target="tpu_custom_call", output_to_operand_aliasing={{2}: (4, {})} | custom-call | flops 100663296 | bytes 1572864 | tf_op jit(solution)/shard_map/mlp_forward/pallas_call | solution.py:226
  296.7 13.5 %mlp_forward.6 = (bf16[1536,1024]{1,0:T(8,128)(2,1)}, bf16[1536,1024]{1,0:T(8,128)(2,1)}, f32[1536,1024]{1,0:T(8,128)}) custom-call(bf16[1536,1024]{1,0:T(8,128)(2,1)} %add_convert_fusion.1.refs_0_, bf16[1024,1024]{1,0:T(8,128)(2,1)} %collective-permute-done.16.refs_1_.refs_3_, f32[1,1024]{1,0:T(1,128)} %copy-done.43, ...), custom_call_target="tpu_custom_call", output_to_operand_aliasing={{2}: (4, {})} | custom-call | flops 100663296 | bytes 1572864 | tf_op jit(solution)/shard_map/mlp_forward/pallas_call | solution.py:226
  328.6 13.5 %mlp_forward.7 = (bf16[1536,1024]{1,0:T(8,128)(2,1)}, bf16[1536,1024]{1,0:T(8,128)(2,1)}, f32[1536,1024]{1,0:T(8,128)}) custom-call(bf16[1536,1024]{1,0:T(8,128)(2,1)} %add_convert_fusion.1.refs_0_, bf16[1024,1024]{1,0:T(8,128)(2,1)} %collective-permute-done.24.refs_1_.refs_3_, f32[1,1024]{1,0:T(1,128)} %copy-done.45, ...), custom_call_target="tpu_custom_call", output_to_operand_aliasing={{2}: (4, {})} | custom-call | flops 100663296 | bytes 1572864 | tf_op jit(solution)/shard_map/mlp_forward/pallas_call | solution.py:226
  350.2 11.7 %mlp_backward.4 = (bf16[1536,1024]{1,0:T(8,128)(2,1)}, f32[1,1024]{1,0:T(1,128)}, f32[1536,1024]{1,0:T(8,128)}) custom-call(bf16[1536,1024]{1,0:T(8,128)(2,1)} %fusion.1.refs_0_, bf16[1024,1024]{1,0:T(8,128)(2,1)} %refs_1_.1, bf16[1536,1024]{1,0:T(8,128)(2,1)} %get-tuple-element.152.refs_2_, bf16[1024,1024]{1,0:T(8,128)(2,1)} %refs_3_.1), custom_call_target="tpu_custom_call" | custom-call | flops 100663296 | bytes 1572864 | tf_op jit(solution)/shard_map/mlp_backward/pallas_call | solution.py:285
  366.9 13.6 %mlp_backward.5 = (bf16[1536,1024]{1,0:T(8,128)(2,1)}, f32[1,1024]{1,0:T(1,128)}, f32[1536,1024]{1,0:T(8,128)}) custom-call(bf16[1536,1024]{1,0:T(8,128)(2,1)} %fusion.1.refs_0_, bf16[1024,1024]{1,0:T(8,128)(2,1)} %collective-permute-done.29.refs_3_.refs_1_, bf16[1536,1024]{1,0:T(8,128)(2,1)} %get-tuple-element.151.refs_2_, ...), custom_call_target="tpu_custom_call", output_to_operand_aliasing={{2}: (4, {})} | custom-call | flops 100663296 | bytes 1572864 | tf_op jit(solution)/shard_map/mlp_backward/pallas_call | solution.py:285
  380.6 13.4 %mlp_backward.6 = (bf16[1536,1024]{1,0:T(8,128)(2,1)}, f32[1,1024]{1,0:T(1,128)}, f32[1536,1024]{1,0:T(8,128)}) custom-call(bf16[1536,1024]{1,0:T(8,128)(2,1)} %fusion.1.refs_0_, bf16[1024,1024]{1,0:T(8,128)(2,1)} %collective-permute-done.18.refs_3_.refs_1_, bf16[1536,1024]{1,0:T(8,128)(2,1)} %get-tuple-element.150.refs_2_, ...), custom_call_target="tpu_custom_call", output_to_operand_aliasing={{2}: (4, {})} | custom-call | flops 100663296 | bytes 1572864 | tf_op jit(solution)/shard_map/mlp_backward/pallas_call | solution.py:285
  394.0 13.5 %mlp_backward.7 = (bf16[1536,1024]{1,0:T(8,128)(2,1)}, f32[1,1024]{1,0:T(1,128)}, f32[1536,1024]{1,0:T(8,128)}) custom-call(bf16[1536,1024]{1,0:T(8,128)(2,1)} %fusion.1.refs_0_, bf16[1024,1024]{1,0:T(8,128)(2,1)} %collective-permute-done.26.refs_3_.refs_1_, bf16[1536,1024]{1,0:T(8,128)(2,1)} %get-tuple-element.149.refs_2_, ...), custom_call_target="tpu_custom_call", output_to_operand_aliasing={{2}: (4, {})} | custom-call | flops 100663296 | bytes 1572864 | tf_op jit(solution)/shard_map/mlp_backward/pallas_call | solution.py:285
  489.8 48.9 %attend_back.3.refs_1_ = bf16[3,2048,256]{2,1,0:T(8,128)(2,1)} custom-call(bf16[3,2048,256]{2,1,0:T(8,128)(2,1)} %fusion.10.q_ref.k_ref.v_ref, bf16[3,2048,256]{2,1,0:T(8,128)(2,1)} %fusion.10.q_ref.k_ref.v_ref, bf16[3,2048,256]{2,1,0:T(8,128)(2,1)} %fusion.10.q_ref.k_ref.v_ref, bf16[2048,256]{1,0:T(8,128)(2,1)} %get-tuple-element.124.out_ref, ...), custom_call_target="tpu_custom_call" | custom-call | flops 335544320 | bytes 524288 | tf_op jit(solution)/shard_map/attend_back/pallas_call | solution.py:168
  538.7 23.4 %all-reduce.5.cloned.1.call-done = bf16[1024,1024]{1,0:T(8,128)(2,1)} async-done(((bf16[1024,1024]{1,0:T(8,128)(2,1)}), bf16[1024,1024]{1,0:T(8,128)(2,1)}) %all-reduce.5.cloned.1.call-update) | async-done | bytes 2097168 | tf_op jit(solution)/shard_map/psum | solution.py:552
  574.4 12.1 %project_back.3 = (bf16[2048,1024]{1,0:T(8,128)(2,1)}, f32[3,1024,256]{2,1,0:T(8,128)}, f32[8,256]{1,0:T(8,128)}) custom-call(bf16[2048,1024]{1,0:T(8,128)(2,1)} %copy-done.13, bf16[3,2048,256]{2,1,0:T(8,128)(2,1)} %attend_back.3.refs_1_, bf16[3,1024,256]{2,1,0:T(8,128)(2,1)} %refs_2_.5), custom_call_target="tpu_custom_call" | custom-call | flops 100663296 | bytes 524288 | tf_op jit(solution)/shard_map/project_back/pallas_call | solution.py:365
  592.1 48.9 %attend_back.4.refs_1_ = bf16[3,2048,256]{2,1,0:T(8,128)(2,1)} custom-call(bf16[3,2048,256]{2,1,0:T(8,128)(2,1)} %fusion.11.q_ref.k_ref.v_ref, bf16[3,2048,256]{2,1,0:T(8,128)(2,1)} %fusion.11.q_ref.k_ref.v_ref, bf16[3,2048,256]{2,1,0:T(8,128)(2,1)} %fusion.11.q_ref.k_ref.v_ref, bf16[2048,256]{1,0:T(8,128)(2,1)} %get-tuple-element.126.out_ref, ...), custom_call_target="tpu_custom_call" | custom-call | flops 335544320 | bytes 524288 | tf_op jit(solution)/shard_map/attend_back/pallas_call | solution.py:168
  642.4 12.5 %project_back.4 = (bf16[2048,1024]{1,0:T(8,128)(2,1)}, f32[3,1024,256]{2,1,0:T(8,128)}, f32[8,256]{1,0:T(8,128)}) custom-call(bf16[2048,1024]{1,0:T(8,128)(2,1)} %copy-done.14, bf16[3,2048,256]{2,1,0:T(8,128)(2,1)} %attend_back.4.refs_1_, bf16[3,1024,256]{2,1,0:T(8,128)(2,1)} %refs_2_.5, ...), custom_call_target="tpu_custom_call", output_to_operand_aliasing={{1}: (3, {}), {2}: (4, {})} | custom-call | flops 100663296 | bytes 524288 | tf_op jit(solution)/shard_map/project_back/pallas_call | solution.py:365
  675.0 49.1 %attend_back.5.refs_1_ = bf16[3,2048,256]{2,1,0:T(8,128)(2,1)} custom-call(bf16[3,2048,256]{2,1,0:T(8,128)(2,1)} %fusion.12.q_ref.k_ref.v_ref, bf16[3,2048,256]{2,1,0:T(8,128)(2,1)} %fusion.12.q_ref.k_ref.v_ref, bf16[3,2048,256]{2,1,0:T(8,128)(2,1)} %fusion.12.q_ref.k_ref.v_ref, bf16[2048,256]{1,0:T(8,128)(2,1)} %get-tuple-element.133.out_ref, ...), custom_call_target="tpu_custom_call" | custom-call | flops 335544320 | bytes 524288 | tf_op jit(solution)/shard_map/attend_back/pallas_call | solution.py:168
  731.0 13.5 %project_back.5 = (bf16[2048,1024]{1,0:T(8,128)(2,1)}, f32[3,1024,256]{2,1,0:T(8,128)}, f32[8,256]{1,0:T(8,128)}, bf16[3,1040,256]{2,1,0:T(8,128)(2,1)}) custom-call(bf16[2048,1024]{1,0:T(8,128)(2,1)} %copy-done.12, bf16[3,2048,256]{2,1,0:T(8,128)(2,1)} %attend_back.5.refs_1_, ...), custom_call_target="tpu_custom_call", output_to_operand_aliasing={{1}: (3, {}), {2}: (4, {})} | custom-call | flops 100663296 | bytes 524288 | tf_op jit(solution)/shard_map/project_back/pallas_call | solution.py:365
  766.7 18.9 %collective-permute-done.61 = bf16[512,1024]{1,0:T(8,128)(2,1)S(1)} collective-permute-done((bf16[512,1024]{1,0:T(8,128)(2,1)S(1)}, bf16[512,1024]{1,0:T(8,128)(2,1)S(1)}, u32[]{:S(2)}, u32[]{:S(2)}) %collective-permute-start.61) | collective-permute-done | bytes 1048608 | tf_op jit(solution)/shard_map/ppermute | solution.py:386
  791.1 56.0 %all-reduce.7.cloned.1.call-done = bf16[3,1040,256]{2,1,0:T(8,128)(2,1)} async-done(((bf16[3,1040,256]{2,1,0:T(8,128)(2,1)}), bf16[3,1040,256]{2,1,0:T(8,128)(2,1)}) %all-reduce.7.cloned.1.call-update) | async-done | bytes 1597456 | tf_op jit(solution)/shard_map/psum | solution.py:600
  (381 shorter events, 309.1 us)
Async XLA Ops:
  7.2 554.8 %all-reduce.5.cloned.1.call-start = ((), (), s32[]{:S(2)}) async-start(), calls=%async_computation | async-start | bytes 4194304 | tf_op jit(solution)/shard_map/psum | solution.py:552
  44.3 62.1 %collective-permute-start.7 = (bf16[512,1024]{1,0:T(8,128)(2,1)}, bf16[512,1024]{1,0:T(8,128)(2,1)}, u32[]{:S(2)}, u32[]{:S(2)}) collective-permute-start(bf16[512,1024]{1,0:T(8,128)(2,1)} %get-tuple-element.125), channel_id=1, source_target_pairs={{0,1},{1,0},{2,3},{3,2},{4,5},{5,4},{6,7},{7,6},{8,9},{9,8},{10,11... | collective-permute-start | bytes 3145736 | tf_op jit(solution)/shard_map/ppermute | solution.py:386
  77.1 68.3 %collective-permute-start.13 = (bf16[512,1024]{1,0:T(8,128)(2,1)}, bf16[512,1024]{1,0:T(8,128)(2,1)}, u32[]{:S(2)}, u32[]{:S(2)}) collective-permute-start(bf16[512,1024]{1,0:T(8,128)(2,1)} %get-tuple-element.127), channel_id=1, source_target_pairs={{0,1},{1,0},{2,3},{3,2},{4,5},{5,4},{6,7},{7,6},{8,9},{9,8},{10,11... | collective-permute-start | bytes 3145736 | tf_op jit(solution)/shard_map/ppermute | solution.py:386
  77.4 79.1 %collective-permute-start.16 = (bf16[1024,1024]{1,0:T(8,128)(2,1)}, bf16[1024,1024]{1,0:T(8,128)(2,1)}, u32[]{:S(2)}, u32[]{:S(2)}) collective-permute-start(bf16[1024,1024]{1,0:T(8,128)(2,1)} %refs_3_.1), channel_id=1, source_target_pairs={{0,2},{1,3},{2,0},{3,1},{4,6},{5,7},{6,4},{7,5},{8,10},{9,11},{10,... | collective-permute-start | bytes 6291464 | tf_op jit(solution)/shard_map/ppermute | solution.py:386
  106.8 94.7 %collective-permute-start.18 = (bf16[1024,1024]{1,0:T(8,128)(2,1)}, bf16[1024,1024]{1,0:T(8,128)(2,1)}, u32[]{:S(2)}, u32[]{:S(2)}) collective-permute-start(bf16[1024,1024]{1,0:T(8,128)(2,1)} %refs_1_.1), channel_id=1, source_target_pairs={{0,2},{1,3},{2,0},{3,1},{4,6},{5,7},{6,4},{7,5},{8,10},{9,11},{10,... | collective-permute-start | bytes 6291464 | tf_op jit(solution)/shard_map/ppermute | solution.py:386
  145.4 60.8 %collective-permute-start.6 = (bf16[512,256]{1,0:T(8,128)(2,1)}, bf16[512,256]{1,0:T(8,128)(2,1)S(1)}, u32[]{:S(2)}, u32[]{:S(2)}) collective-permute-start(bf16[512,256]{1,0:T(8,128)(2,1)} %get-tuple-element.263), channel_id=1, source_target_pairs={{0,3},{1,2},{2,1},{3,0},{4,7},{5,6},{6,5},{7,4},{8,11},{9,10},{10,... | collective-permute-start | bytes 786440 | tf_op jit(solution)/shard_map/ppermute | solution.py:386
  145.4 67.3 %collective-permute-start.5 = (bf16[512,256]{1,0:T(8,128)(2,1)}, bf16[512,256]{1,0:T(8,128)(2,1)}, u32[]{:S(2)}, u32[]{:S(2)}) collective-permute-start(bf16[512,256]{1,0:T(8,128)(2,1)} %get-tuple-element.264), channel_id=1, source_target_pairs={{0,2},{1,3},{2,0},{3,1},{4,6},{5,7},{6,4},{7,5},{8,10},{9,11},{10,... | collective-permute-start | bytes 786440 | tf_op jit(solution)/shard_map/ppermute | solution.py:386
  156.5 56.2 %collective-permute-start.4 = (bf16[512,256]{1,0:T(8,128)(2,1)}, bf16[512,256]{1,0:T(8,128)(2,1)}, u32[]{:S(2)}, u32[]{:S(2)}) collective-permute-start(bf16[512,256]{1,0:T(8,128)(2,1)} %get-tuple-element.265), channel_id=1, source_target_pairs={{0,1},{1,0},{2,3},{3,2},{4,5},{5,4},{6,7},{7,6},{8,9},{9,8},{10,11... | collective-permute-start | bytes 786440 | tf_op jit(solution)/shard_map/ppermute | solution.py:386
  156.5 61.0 %collective-permute-start.12 = (bf16[512,256]{1,0:T(8,128)(2,1)}, bf16[512,256]{1,0:T(8,128)(2,1)}, u32[]{:S(2)}, u32[]{:S(2)}) collective-permute-start(bf16[512,256]{1,0:T(8,128)(2,1)} %get-tuple-element.267), channel_id=1, source_target_pairs={{0,3},{1,2},{2,1},{3,0},{4,7},{5,6},{6,5},{7,4},{8,11},{9,10},{10,... | collective-permute-start | bytes 786440 | tf_op jit(solution)/shard_map/ppermute | solution.py:386
  223.8 58.8 %collective-permute-start.28 = (f32[1,1024]{1,0:T(1,128)S(1)}, f32[1,1024]{1,0:T(1,128)S(1)}, u32[]{:S(2)}, u32[]{:S(2)}) collective-permute-start(f32[1,1024]{1,0:T(1,128)S(1)} %bitcast.120), channel_id=1, source_target_pairs={{0,1},{1,0},{2,3},{3,2},{4,5},{5,4},{6,7},{7,6},{8,9},{9,8},{10,11... | collective-permute-start | bytes 12296 | tf_op jit(solution)/shard_map/ppermute | solution.py:386
  228.7 54.0 %collective-permute-start.27 = (bf16[1024,1024]{1,0:T(8,128)(2,1)}, bf16[1024,1024]{1,0:T(8,128)(2,1)}, u32[]{:S(2)}, u32[]{:S(2)}) collective-permute-start(bf16[1024,1024]{1,0:T(8,128)(2,1)} %refs_3_.1), channel_id=1, source_target_pairs={{0,1},{1,0},{2,3},{3,2},{4,5},{5,4},{6,7},{7,6},{8,9},{9,8},{10,11... | collective-permute-start | bytes 6291464 | tf_op jit(solution)/shard_map/ppermute | solution.py:386
  258.0 70.0 %collective-permute-start.25 = (f32[1,1024]{1,0:T(1,128)S(1)}, f32[1,1024]{1,0:T(1,128)S(1)}, u32[]{:S(2)}, u32[]{:S(2)}) collective-permute-start(f32[1,1024]{1,0:T(1,128)S(1)} %collective-permute-done.3.refs_2_), channel_id=1, source_target_pairs={{0,1},{1,0},{2,3},{3,2},{4,5},{5,4},{6,7},{7,6},{8,9},{9,8},{10,11... | collective-permute-start | bytes 12296 | tf_op jit(solution)/shard_map/ppermute | solution.py:386
  258.0 70.0 %collective-permute-start.24 = (bf16[1024,1024]{1,0:T(8,128)(2,1)}, bf16[1024,1024]{1,0:T(8,128)(2,1)}, u32[]{:S(2)}, u32[]{:S(2)}) collective-permute-start(bf16[1024,1024]{1,0:T(8,128)(2,1)} %collective-permute-done.16.refs_1_.refs_3_), channel_id=1, source_target_pairs={{0,1},{1,0},{2,3},{3,2},{4,5},{5,4},{6,7},{7,6},{8,9},{9,8},{10,11... | collective-permute-start | bytes 6291464 | tf_op jit(solution)/shard_map/ppermute | solution.py:386
  459.7 264.4 %all-reduce.9.cloned.1.call-start = ((), (), s32[]{:S(2)}) async-start(), calls=%async_computation.2 | async-start | bytes 5242880 | tf_op jit(solution)/shard_map/psum | solution.py:590
  469.3 69.4 %collective-permute-start.40 = (bf16[1024,1024]{1,0:T(8,128)(2,1)}, bf16[1024,1024]{1,0:T(8,128)(2,1)}, u32[]{:S(2)}, u32[]{:S(2)}) collective-permute-start(bf16[1024,1024]{1,0:T(8,128)(2,1)} %add_convert_fusion.7), channel_id=1, source_target_pairs={{0,2},{1,3},{2,0},{3,1},{4,6},{5,7},{6,4},{7,5},{8,10},{9,11},{10,... | collective-permute-start | bytes 6291464 | tf_op jit(solution)/shard_map/ppermute | solution.py:386
  481.1 57.6 %collective-permute-start.41 = (bf16[256,1024]{1,0:T(8,128)(2,1)S(1)}, bf16[256,1024]{1,0:T(8,128)(2,1)}, u32[]{:S(2)}, u32[]{:S(2)}) collective-permute-start(bf16[256,1024]{1,0:T(8,128)(2,1)S(1)} %add_convert_fusion.13), channel_id=1, source_target_pairs={{0,2},{1,3},{2,0},{3,1},{4,6},{5,7},{6,4},{7,5},{8,10},{9,11},{10,... | collective-permute-start | bytes 1572872 | tf_op jit(solution)/shard_map/ppermute | solution.py:386
  570.2 276.9 %all-reduce.7.cloned.1.call-start = ((), (), s32[]{:S(2)}) async-start(), calls=%async_computation.1 | async-start | bytes 3194880 | tf_op jit(solution)/shard_map/psum | solution.py:600
  572.9 68.1 %collective-permute-start.49 = (f32[64,128]{1,0:T(8,128)S(1)}, f32[64,128]{1,0:T(8,128)S(1)}, u32[]{:S(2)}, u32[]{:S(2)}) collective-permute-start(f32[64,128]{1,0:T(8,128)S(1)} %add.245), channel_id=1, source_target_pairs={{0,2},{1,3},{2,0},{3,1},{4,6},{5,7},{6,4},{7,5},{8,10},{9,11},{10,... | collective-permute-start | bytes 98312 | tf_op jit(solution)/shard_map/ppermute | solution.py:427
  589.6 69.8 %collective-permute-start.43 = (bf16[512,1024]{1,0:T(8,128)(2,1)}, bf16[512,1024]{1,0:T(8,128)(2,1)}, u32[]{:S(2)}, u32[]{:S(2)}) collective-permute-start(bf16[512,1024]{1,0:T(8,128)(2,1)} %get-tuple-element.239), channel_id=1, source_target_pairs={{0,1},{1,0},{2,3},{3,2},{4,5},{5,4},{6,7},{7,6},{8,9},{9,8},{10,11... | collective-permute-start | bytes 3145736 | tf_op jit(solution)/shard_map/ppermute | solution.py:386
  589.8 71.3 %collective-permute-start.44 = (bf16[512,1024]{1,0:T(8,128)(2,1)}, bf16[512,1024]{1,0:T(8,128)(2,1)}, u32[]{:S(2)}, u32[]{:S(2)}) collective-permute-start(bf16[512,1024]{1,0:T(8,128)(2,1)} %get-tuple-element.238), channel_id=1, source_target_pairs={{0,1},{1,0},{2,3},{3,2},{4,5},{5,4},{6,7},{7,6},{8,9},{9,8},{10,11... | collective-permute-start | bytes 3145736 | tf_op jit(solution)/shard_map/ppermute | solution.py:386
  658.1 66.0 %collective-permute-start.51 = (bf16[512,1024]{1,0:T(8,128)(2,1)}, bf16[512,1024]{1,0:T(8,128)(2,1)}, u32[]{:S(2)}, u32[]{:S(2)}) collective-permute-start(bf16[512,1024]{1,0:T(8,128)(2,1)} %get-tuple-element.241), channel_id=1, source_target_pairs={{0,1},{1,0},{2,3},{3,2},{4,5},{5,4},{6,7},{7,6},{8,9},{9,8},{10,11... | collective-permute-start | bytes 3145736 | tf_op jit(solution)/shard_map/ppermute | solution.py:386
  658.1 66.0 %collective-permute-start.52 = (bf16[512,1024]{1,0:T(8,128)(2,1)}, bf16[512,1024]{1,0:T(8,128)(2,1)}, u32[]{:S(2)}, u32[]{:S(2)}) collective-permute-start(bf16[512,1024]{1,0:T(8,128)(2,1)} %get-tuple-element.240), channel_id=1, source_target_pairs={{0,1},{1,0},{2,3},{3,2},{4,5},{5,4},{6,7},{7,6},{8,9},{9,8},{10,11... | collective-permute-start | bytes 3145736 | tf_op jit(solution)/shard_map/ppermute | solution.py:386
  668.0 56.2 %collective-permute-start.57 = (f32[64,128]{1,0:T(8,128)S(1)}, f32[64,128]{1,0:T(8,128)S(1)}, u32[]{:S(2)}, u32[]{:S(2)}) collective-permute-start(f32[64,128]{1,0:T(8,128)S(1)} %add.254), channel_id=1, source_target_pairs={{0,8},{4,12},{8,0},{12,4},{16,24},{20,28},{24,16},{28,20},{1,9},{5... | collective-permute-start | bytes 98312 | tf_op jit(solution)/shard_map/ppermute | solution.py:427
  673.8 77.0 %collective-permute-start.45 = (bf16[512,1024]{1,0:T(8,128)(2,1)}, bf16[512,1024]{1,0:T(8,128)(2,1)}, u32[]{:S(2)}, u32[]{:S(2)}) collective-permute-start(bf16[512,1024]{1,0:T(8,128)(2,1)} %add_convert_fusion.11), channel_id=1, source_target_pairs={{0,2},{1,3},{2,0},{3,1},{4,6},{5,7},{6,4},{7,5},{8,10},{9,11},{10,... | collective-permute-start | bytes 3145736 | tf_op jit(solution)/shard_map/ppermute | solution.py:386
  (110 other events, 1667.6 us)
Sparse Core Ops, SparseCore 0:
  459.8 102.1 all-reduce.4
  570.4 115.3 all-reduce.8
  758.5 88.5 all-reduce.6

commit v2 on v1

--- a/solution.py
+++ b/solution.py
@@ -189,125 +189,388 @@
     )(qkv, qkv, qkv, attended, grad_attended, lse)
 
 
-def mlp_forward(normed, up, up_bias, down, total):
-    rows, model = normed.shape
-    units = up.shape[1]
-    block = largest_block(rows, 512)
-    first = total is None
+def hint(flops, size):
+    return pl.CostEstimate(flops=flops // COST_SCALE, transcendentals=0, bytes_accessed=size)
+
+
+def params():
+    return pltpu.CompilerParams(vmem_limit_bytes=VMEM_LIMIT)
+
+
+def norm_item(patches, item, norm_gain, norm_shift):
+    _, rows, model = patches.shape
+    block = largest_block(rows, 256)
+
+    def body(x_ref, gain_ref, shift_ref, out_ref):
+        out_ref[...] = norm_rows(x_ref[...].astype(f32), gain_ref[...], shift_ref[...]).astype(bf16)
+
+    vector = pl.BlockSpec((1, model), lambda i: (0, 0))
+    return pl.pallas_call(
+        body,
+        grid=(rows // block,),
+        in_specs=[pl.BlockSpec((None, block, model), lambda i: (item, i, 0)), vector, vector],
+        out_specs=pl.BlockSpec((block, model), lambda i: (i, 0)),
+        out_shape=jax.ShapeDtypeStruct((rows, model), bf16),
+        compiler_params=params(),
+        cost_estimate=hint(0, rows * model),
+        name="norm_item",
+    )(patches, norm_gain, norm_shift)
+
+
+def out_project(patches, item, heads, weight, out_bias, norm_gain, norm_shift, before):
+    slots, rows, model = patches.shape
+    block = largest_block(rows, 256)
+    steps = rows // block
+    count = len(heads)
 
     def body(*refs):
-        if first:
-            x_ref, up_ref, bias_ref, down_ref, hidden_ref, slope_ref, sum_ref = refs
-        else:
-            x_ref, up_ref, bias_ref, down_ref, before_ref, hidden_ref, slope_ref, sum_ref = refs
-        part = largest_block(units, 256)
-        for j in range(units // part):
-            cols = slice(j * part, (j + 1) * part)
-            pre = nn(x_ref[...], up_ref[:, cols]) + bias_ref[:, cols]
-            cdf = 0.5 + 0.5 * lax.erf(pre * SQRT_HALF)
-            density = jnp.exp2(pre * pre * (-0.5 * LOG2E)) * INV_SQRT_2PI
-            hidden_ref[:, cols] = (pre * cdf).astype(bf16)
-            slope_ref[:, cols] = (cdf + pre * density).astype(bf16)
-        out = nn(hidden_ref[...], down_ref[...])
-        sum_ref[...] = out if first else before_ref[...] + out
+        x_ref, weight_ref, bias_ref, gain_ref, shift_ref = refs[:5]
+        head_refs = refs[5 : 5 + count]
+        attended_ref, residual_ref, normed_ref = refs[-3:]
+        attended = [ref[...] for ref in head_refs]
+        attended = attended[0] if count == 1 else jnp.concatenate(attended, axis=1)
+        attended_ref[...] = attended
+        residual = x_ref[...].astype(f32) + nn(attended, weight_ref[...]) + bias_ref[...]
+        residual_ref[...] = residual
+        normed_ref[...] = norm_rows(residual, gain_ref[...], shift_ref[...]).astype(bf16)
+
+    vector = pl.BlockSpec((1, model), lambda i: (0, 0))
+    placed = pl.BlockSpec((block, model), lambda i: (item * steps + i, 0))
+    operands = [patches, weight, out_bias, norm_gain, norm_shift, *heads]
+    in_specs = [
+        pl.BlockSpec((None, block, model), lambda i: (item, i, 0)),
+        pl.BlockSpec((model, model), lambda i: (0, 0)),
+        vector,
+        vector,
+        vector,
+    ] + [pl.BlockSpec((block, head.shape[1]), lambda i: (i, 0)) for head in heads]
+    aliases = {}
+    if before is not None:
+        aliases = {len(operands) + k: k for k in range(3)}
+        operands += before
+        in_specs += [pl.BlockSpec(memory_space=pl.ANY)] * 3
+    return pl.pallas_call(
+        body,
+        grid=(steps,),
+        in_specs=in_specs,
+        out_specs=[placed] * 3,
+        out_shape=[jax.ShapeDtypeStruct((slots * rows, model), t) for t in (bf16, f32, bf16)],
+        input_output_aliases=aliases,
+        compiler_params=params(),
+        cost_estimate=hint(2 * rows * model * model, rows * model),
+        name="out_project",
+    )(*operands)
+
+
+def residual_back(total, residual, cotangent, scale, item, weight, norm_gain, low_before, pieces):
+    slots, rows, model = cotangent.shape
+    block = largest_block(rows, 256)
+    steps = rows // block
+    piece = model // pieces
+
+    def body(*refs):
+        total_ref, residual_ref, cot_ref, scale_ref, weight_ref, gain_ref = refs[:6]
+        outs = refs[6:] if low_before is None else refs[7:]
+        grad_ref, low_ref, sum_ref = outs[:3]
+        attended_refs = outs[3:]
+        residual = residual_ref[...]
+        centred = residual - jnp.mean(residual, axis=-1, keepdims=True)
+        rate = lax.rsqrt(jnp.mean(centred * centred, axis=-1, keepdims=True) + epsilon)
+        xhat = centred * rate
+        grad_normed = total_ref[...]
+        scaled = grad_normed * gain_ref[...]
+        inner = jnp.mean(scaled, axis=-1, keepdims=True)
+        outer = jnp.mean(scaled * xhat, axis=-1, keepdims=True)
+        cot = cot_ref[...].astype(f32) * scale_ref[item]
+        grad = cot + rate * (scaled - inner - xhat * outer)
+        grad_ref[...] = grad
+        low = grad.astype(bf16)
+        low_ref[...] = low
+
+        @pl.when(pl.program_id(0) == 0)
+        def _():
+            sum_ref[...] = jnp.zeros_like(sum_ref)
+
+        for k, value in enumerate((grad_normed * xhat, grad_normed, grad, cot)):
+            sum_ref[k : k + 1, :] += jnp.sum(value, axis=0, keepdims=True)
+        attended = nt(low, weight_ref[...]).astype(bf16)
+        for k in range(pieces):
+            attended_refs[k][...] = attended[:, k * piece : (k + 1) * piece]
 
     row_spec = pl.BlockSpec((block, model), lambda i: (i, 0))
-    unit_spec = pl.BlockSpec((block, units), lambda i: (i, 0))
+    placed = pl.BlockSpec((block, model), lambda i: (item * steps + i, 0))
+    operands = [total, residual, cotangent, scale, weight, norm_gain]
     in_specs = [
-        row_spec,
-        pl.BlockSpec((model, units), lambda i: (0, 0)),
-        pl.BlockSpec((1, units), lambda i: (0, 0)),
-        pl.BlockSpec((units, model), lambda i: (0, 0)),
+        placed,
+        placed,
+        pl.BlockSpec((None, block, model), lambda i: (item, i, 0)),
+        pl.BlockSpec(memory_space=pltpu.SMEM),
+        pl.BlockSpec((model, model), lambda i: (0, 0)),
+        pl.BlockSpec((1, model), lambda i: (0, 0)),
     ]
-    operands = [normed, up, up_bias, down]
-    if not first:
-        in_specs.append(row_spec)
-        operands.append(total)
+    aliases = {}
+    if low_before is not None:
+        aliases = {6: 1}
+        operands.append(low_before)
+        in_specs.append(pl.BlockSpec(memory_space=pl.ANY))
+    return pl.pallas_call(
+        body,
+        grid=(steps,),
+        in_specs=in_specs,
+        out_specs=[row_spec, placed, pl.BlockSpec((8, model), lambda i: (0, 0))]
+        + [pl.BlockSpec((block, piece), lambda i: (i, 0))] * pieces,
+        out_shape=[
+            jax.ShapeDtypeStruct((rows, model), f32),
+            jax.ShapeDtypeStruct((slots * rows, model), bf16),
+            jax.ShapeDtypeStruct((8, model), f32),
+        ]
+        + [jax.ShapeDtypeStruct((rows, piece), bf16)] * pieces,
+        input_output_aliases=aliases,
+        compiler_params=params(),
+        cost_estimate=hint(2 * rows * model * model, rows * model),
+        name="residual_back",
+    )(*operands)
+
+
+def input_back(terms, patches, item, grad_residual, norm_gain, before):
+    slots, rows, model = patches.shape
+    block = largest_block(rows, 256)
+    count = len(terms)
+
+    def body(*refs):
+        x_ref, grad_ref, gain_ref = refs[:3]
+        out_ref = refs[-1]
+        grad_normed = refs[3][...].astype(f32)
+        for k in range(1, count):
+            grad_normed = grad_normed + refs[3 + k][...].astype(f32)
+        source = x_ref[...].astype(f32)
+        centred = source - jnp.mean(source, axis=-1, keepdims=True)
+        rate = lax.rsqrt(jnp.mean(centred * centred, axis=-1, keepdims=True) + epsilon)
+        xhat = centred * rate
+        scaled = grad_normed * gain_ref[...]
+        inner = jnp.mean(scaled, axis=-1, keepdims=True)
+        outer = jnp.mean(scaled * xhat, axis=-1, keepdims=True)
+        out_ref[...] = (grad_ref[...] + rate * (scaled - inner - xhat * outer)).astype(bf16)
+
+    row_spec = pl.BlockSpec((block, model), lambda i: (i, 0))
+    placed = pl.BlockSpec((None, block, model), lambda i: (item, i, 0))
+    operands = [patches, grad_residual, norm_gain, *terms]
+    in_specs = [placed, row_spec, pl.BlockSpec((1, model), lambda i: (0, 0))] + [row_spec] * count
+    aliases = {}
+    if before is not None:
+        aliases = {len(operands): 0}
+        operands.append(before)
+        in_specs.append(pl.BlockSpec(memory_space=pl.ANY))
     return pl.pallas_call(
         body,
         grid=(rows // block,),
         in_specs=in_specs,
-        out_specs=[unit_spec, unit_spec, row_spec],
+        out_specs=placed,
+        out_shape=jax.ShapeDtypeStruct((slots, rows, model), bf16),
+        input_output_aliases=aliases,
+        compiler_params=params(),
+        cost_estimate=hint(0, rows * model),
+        name="input_back",
+    )(*operands)
+
+
+def mlp_forward(normed, cot, ups, biases, downs, total):
+    rows, model = normed.shape
+    count = len(ups)
+    units = ups[0].shape[1]
+    block = largest_block(rows, 512)
+    steps = rows // block
+    first = total is None
+
+    def body(*refs):
+        x_ref, cot_ref = refs[:2]
+        up_refs, bias_refs, down_refs = (refs[2 + k * count : 2 + (k + 1) * count] for k in range(3))
+        rest = refs[2 + 3 * count :]
+        if not first:
+            before_ref = rest[0]
+            rest = rest[1:]
+        slope_ref, sum_ref = rest[:2]
+        grad_refs = rest[2 : 2 + count]
+        hidden_ref, acc_ref = rest[2 + count :]
+        step = pl.program_id(0)
+        part = largest_block(units, 256)
+        for k in range(count):
+            for j in range(units // part):
+                cols = slice(j * part, (j + 1) * part)
+                wide = slice(k * units + j * part, k * units + (j + 1) * part)
+                pre = nn(x_ref[...], up_refs[k][:, cols]) + bias_refs[k][:, cols]
+                cdf = 0.5 + 0.5 * lax.erf(pre * SQRT_HALF)
+                density = jnp.exp2(pre * pre * (-0.5 * LOG2E)) * INV_SQRT_2PI
+                hidden_ref[:, wide] = (pre * cdf).astype(bf16)
+                slope_ref[:, wide] = (cdf + pre * density).astype(bf16)
+        out = None if first else before_ref[...]
+        for k in range(count):
+            hidden = hidden_ref[:, k * units : (k + 1) * units]
+            product = nn(hidden, down_refs[k][...])
+            out = product if out is None else out + product
+            grad = tn(hidden, cot_ref[...])
+
+            @pl.when(step == 0)
+            def _():
+                acc_ref[k] = grad
+
+            @pl.when(step > 0)
+            def _():
+                acc_ref[k] += grad
+
+        sum_ref[...] = out
+
+        @pl.when(step == steps - 1)
+        def _():
+            for k in range(count):
+                grad_refs[k][...] = acc_ref[k].astype(bf16)
+
+    row_spec = pl.BlockSpec((block, model), lambda i: (i, 0))
+    slope_spec = pl.BlockSpec((block, count * units), lambda i: (i, 0))
+    up_spec = pl.BlockSpec((model, units), lambda i: (0, 0), pipeline_mode=pl.Buffered(1))
+    down_spec = pl.BlockSpec((units, model), lambda i: (0, 0), pipeline_mode=pl.Buffered(1))
+    grad_spec = pl.BlockSpec((units, model), lambda i: (0, 0))
+    operands = [normed, cot, *ups, *biases, *downs]
+    in_specs = [row_spec, row_spec] + [up_spec] * count
+    in_specs += [pl.BlockSpec((1, units), lambda i: (0, 0))] * count + [down_spec] * count
+    aliases = {}
+    if not first:
+        aliases = {len(operands): 1}
+        operands.append(total)
+        in_specs.append(row_spec)
+    return pl.pallas_call(
+        body,
+        grid=(steps,),
+        in_specs=in_specs,
+        out_specs=[slope_spec, row_spec] + [grad_spec] * count,
         out_shape=[
-            jax.ShapeDtypeStruct((rows, units), bf16),
-            jax.ShapeDtypeStruct((rows, units), bf16),
+            jax.ShapeDtypeStruct((rows, count * units), bf16),
             jax.ShapeDtypeStruct((rows, model), f32),
-        ],
-        input_output_aliases={} if first else {4: 2},
-        compiler_params=pltpu.CompilerParams(vmem_limit_bytes=VMEM_LIMIT),
-        cost_estimate=pl.CostEstimate(
-            flops=4 * rows * model * units // COST_SCALE,
-            transcendentals=0,
-            bytes_accessed=rows * units,
-        ),
+        ]
+        + [jax.ShapeDtypeStruct((units, model), bf16)] * count,
+        scratch_shapes=[pltpu.VMEM((block, count * units), bf16), pltpu.VMEM((count, units, model), f32)],
+        input_output_aliases=aliases,
+        compiler_params=params(),
+        cost_estimate=hint(6 * rows * model * units * count, rows * units),
         name="mlp_forward",
     )(*operands)
 
 
-def mlp_backward(cot, down, slope, up, total):
+def mlp_backward(cot, slope, ups, downs, before, index, calls):
     rows, model = cot.shape
-    units = up.shape[1]
+    count = len(ups)
+    units = ups[0].shape[1]
     block = largest_block(rows, 512)
-    first = total is None
+    first = before is None
 
     def body(*refs):
-        if first:
-            cot_ref, down_ref, slope_ref, up_ref, grad_ref, bias_ref, sum_ref = refs
-        else:
-            cot_ref, down_ref, slope_ref, up_ref, before_ref, grad_ref, bias_ref, sum_ref = refs
-        part = largest_block(units, 256)
+        cot_ref, slope_ref = refs[:2]
+        up_refs, down_refs = refs[2 : 2 + count], refs[2 + count : 2 + 2 * count]
+        grad_ref, sum_ref, bias_ref = refs[-3:]
 
         @pl.when(pl.program_id(0) == 0)
         def _():
             bias_ref[...] = jnp.zeros_like(bias_ref)
 
-        for j in range(units // part):
-            cols = slice(j * part, (j + 1) * part)
-            grad = nt(cot_ref[...], down_ref[cols, :]) * slope_ref[:, cols].astype(f32)
-            low = grad.astype(bf16)
-            grad_ref[:, cols] = low
-            bias_ref[:, cols] += jnp.sum(low.astype(f32), axis=0, keepdims=True)
-        out = nt(grad_ref[...], up_ref[...])
-        sum_ref[...] = out if first else before_ref[...] + out
+        out = None if first else refs[3 + 2 * count][...]
+        part = largest_block(units, 512)
+        for k in range(count):
+            for j in range(units // part):
+                rows_of = slice(j * part, (j + 1) * part)
+                wide = slice(k * units + j * part, k * units + (j + 1) * part)
+                low = (nt(cot_ref[...], down_refs[k][rows_of, :]) * slope_ref[:, wide].astype(f32)).astype(bf16)
+                grad_ref[:, wide] = low
+                bias_ref[:, wide] += jnp.sum(low.astype(f32), axis=0, keepdims=True)
+            product = nt(grad_ref[:, k * units : (k + 1) * units], up_refs[k][...])
+            out = product if out is None else out + product
+        sum_ref[...] = out
 
     row_spec = pl.BlockSpec((block, model), lambda i: (i, 0))
-    unit_spec = pl.BlockSpec((block, units), lambda i: (i, 0))
-    in_specs = [
-        row_spec,
-        pl.BlockSpec((units, model), lambda i: (0, 0)),
-        unit_spec,
-        pl.BlockSpec((model, units), lambda i: (0, 0)),
-    ]
-    operands = [cot, down, slope, up]
+    slope_spec = pl.BlockSpec((block, count * units), lambda i: (i, 0))
+    up_spec = pl.BlockSpec((model, units), lambda i: (0, 0), pipeline_mode=pl.Buffered(1))
+    down_spec = pl.BlockSpec((units, model), lambda i: (0, 0), pipeline_mode=pl.Buffered(1))
+    operands = [cot, slope, *ups, *downs]
+    in_specs = [row_spec, slope_spec] + [up_spec] * count + [down_spec] * count
+    aliases = {}
     if not first:
-        in_specs.append(row_spec)
-        operands.append(total)
+        aliases = {len(operands): 0, len(operands) + 1: 1}
+        operands += before
+        in_specs += [pl.BlockSpec(memory_space=pl.ANY), row_spec]
     return pl.pallas_call(
         body,
         grid=(rows // block,),
         in_specs=in_specs,
-        out_specs=[unit_spec, pl.BlockSpec((1, units), lambda i: (0, 0)), row_spec],
+        out_specs=[
+            pl.BlockSpec((block, count * units), lambda i: (i, index)),
+            row_spec,
+            pl.BlockSpec((1, count * units), lambda i: (0, 0)),
+        ],
         out_shape=[
-            jax.ShapeDtypeStruct((rows, units), bf16),
-            jax.ShapeDtypeStruct((1, units), f32),
+            jax.ShapeDtypeStruct((rows, calls * count * units), bf16),
             jax.ShapeDtypeStruct((rows, model), f32),
+            jax.ShapeDtypeStruct((1, count * units), f32),
         ],
-        input_output_aliases={} if first else {4: 2},
-        compiler_params=pltpu.CompilerParams(vmem_limit_bytes=VMEM_LIMIT),
-        cost_estimate=pl.CostEstimate(
-            flops=4 * rows * model * units // COST_SCALE,
-            transcendentals=0,
-            bytes_accessed=rows * units,
-        ),
+        input_output_aliases=aliases,
+        compiler_params=params(),
+        cost_estimate=hint(4 * rows * model * units * count, rows * units),
         name="mlp_backward",
     )(*operands)
 
 
-def project_back(normed, dqkv, weight, before, last):
+def weight_back(normed, pre_grad, attended, grad_low, pieces):
+    rows, model = normed.shape
+    every = pre_grad.shape[1]
+    units = every // pieces
+    piece = model // pieces
+    block = largest_block(rows, 512)
+    steps = rows // block
+
+    def body(x_ref, pre_ref, attended_ref, grad_ref, *refs):
+        up_refs, out_refs = refs[:pieces], refs[pieces : 2 * pieces]
+        up_acc, out_acc = refs[2 * pieces :]
+        step = pl.program_id(0)
+
+        @pl.when(step == 0)
+        def _():
+            up_acc[...] = jnp.zeros_like(up_acc)
+            out_acc[...] = jnp.zeros_like(out_acc)
+
+        part = largest_block(every, 512)
+        for j in range(every // part):
+            cols = slice(j * part, (j + 1) * part)
+            up_acc[:, cols] += tn(x_ref[...], pre_ref[:, cols])
+        part = largest_block(model, 512)
+        for j in range(model // part):
+            cols = slice(j * part, (j + 1) * part)
+            out_acc[:, cols] += tn(attended_ref[...], grad_ref[:, cols])
+
+        @pl.when(step == steps - 1)
+        def _():
+            for k in range(pieces):
+                up_refs[k][...] = up_acc[:, k * units : (k + 1) * units].astype(bf16)
+                out_refs[k][...] = out_acc[k * piece : (k + 1) * piece, :].astype(bf16)
+
+    row_spec = pl.BlockSpec((block, model), lambda i: (i, 0))
+    return pl.pallas_call(
+        body,
+        grid=(steps,),
+        in_specs=[row_spec, pl.BlockSpec((block, every), lambda i: (i, 0)), row_spec, row_spec],
+        out_specs=[pl.BlockSpec((model, units), lambda i: (0, 0))] * pieces
+        + [pl.BlockSpec((piece, model), lambda i: (0, 0))] * pieces,
+        out_shape=[jax.ShapeDtypeStruct((model, units), bf16)] * pieces
+        + [jax.ShapeDtypeStruct((piece, model), bf16)] * pieces,
+        scratch_shapes=[pltpu.VMEM((model, every), f32), pltpu.VMEM((model, model), f32)],
+        compiler_params=params(),
+        cost_estimate=hint(2 * rows * model * (every + model), rows * model),
+        name="weight_back",
+    )(normed, pre_grad, attended, grad_low)
+
+
+def project_back(normed, dqkv, weight, before, last, pieces):
     rows, model = normed.shape
     width = weight.shape[2]
-    block = largest_block(rows, 512)
-    steps = rows // block
+    block = rows // pieces
+    steps = pieces
     first = before is None
 
     def kernel(*refs):
@@ -316,7 +579,8 @@
         if not first:
             wgrad_before, column_before = rest[:2]
             rest = rest[2:]
-        row_ref, wgrad_ref, column_ref = rest[:3]
+        row_refs, rest = rest[:pieces], rest[pieces:]
+        wgrad_ref, column_ref = rest[:2]
         step = pl.program_id(0)
 
         @pl.when(step == 0)
@@ -331,12 +595,18 @@
         row_grad = nt(dqkv_ref[0], weight_ref[0])
         for c in range(1, 3):
             row_grad = row_grad + nt(dqkv_ref[c], weight_ref[c])
-        row_ref[...] = row_grad.astype(bf16)
+        row_grad = row_grad.astype(bf16)
+        for k in range(pieces):
+
+            @pl.when(step == k)
+            def _():
+                row_refs[k][...] = row_grad
+
         for c in range(3):
             wgrad_ref[c] += tn(normed_ref[...], dqkv_ref[c])
             column_ref[c : c + 1, :] += jnp.sum(dqkv_ref[c].astype(f32), axis=0, keepdims=True)
         if last:
-            low_ref = rest[3]
+            low_ref = rest[2]
 
             @pl.when(step == steps - 1)
             def _():
@@ -353,9 +623,8 @@
     if not first:
         operands += list(before)
         in_specs += [whole, columns]
-    out_specs = [row_spec, whole, columns]
-    out_shape = [
-        jax.ShapeDtypeStruct((rows, model), bf16),
+    out_specs = [pl.BlockSpec((block, model), lambda i: (0, 0))] * pieces + [whole, columns]
+    out_shape = [jax.ShapeDtypeStruct((block, model), bf16)] * pieces + [
         jax.ShapeDtypeStruct((3, model, width), f32),
         jax.ShapeDtypeStruct((8, width), f32),
     ]
@@ -368,7 +637,7 @@
         in_specs=in_specs,
         out_specs=out_specs,
         out_shape=out_shape,
-        input_output_aliases={} if first else {3: 1, 4: 2},
+        input_output_aliases={} if first else {3: pieces, 4: pieces + 1},
         compiler_params=pltpu.CompilerParams(vmem_limit_bytes=VMEM_LIMIT),
         cost_estimate=pl.CostEstimate(
             flops=12 * rows * model * width // COST_SCALE,
@@ -401,19 +670,36 @@
 
     def sum_near(blocks, anchor):
         if not square:
-            return (jnp.stack(blocks), None), anchor
+            return (jnp.stack(blocks),), anchor
         anchor, (near_own, near_far) = tie(anchor, (swap(blocks[1], 1), swap(blocks[3], 1)))
         far = (blocks[2].astype(f32) + near_far.astype(f32)).astype(blocks[2].dtype)
-        return (blocks[0].astype(f32) + near_own.astype(f32), far), anchor
+        return (blocks[0], near_own, far), anchor
+
+    def sums_near(lists, anchor):
+        if not square:
+            return [sum_near(blocks, anchor)[0] for blocks in lists], anchor
+        moved = [(swap(blocks[1], 1), swap(blocks[3], 1)) for blocks in lists]
+        anchor, moved = tie(anchor, moved)
+        return [
+            (blocks[0], own, (blocks[2].astype(f32) + far.astype(f32)).astype(blocks[2].dtype))
+            for blocks, (own, far) in zip(lists, moved, strict=True)
+        ], anchor
+
+    def terms_far(stage, anchor):
+        if not square:
+            own = lax.psum_scatter(stage[0], "tensor", scatter_dimension=0, tiled=False)
+            anchor, own = tie(anchor, own)
+            return [own], anchor
+        own, near, far = stage
+        anchor, received = tie(anchor, swap(far, 2))
+        return [own, near, received], anchor
 
     def sum_far(stage, anchor):
-        own, far = stage
-        if not square:
-            own = lax.psum_scatter(own, "tensor", scatter_dimension=0, tiled=False).astype(f32)
-            anchor, own = tie(anchor, own)
-            return own, anchor
-        anchor, received = tie(anchor, swap(far, 2))
-        return own + received.astype(f32), anchor
+        terms, anchor = terms_far(stage, anchor)
+        total = terms[0].astype(f32)
+        for term in terms[1:]:
+            total = total + term.astype(f32)
+        return total.astype(terms[0].dtype), anchor
 
     steps = []
     for axis, size in (("tensor", tensor_size), ("dp", group_size)):
@@ -426,6 +712,37 @@
     def sum_step(value, step, anchor):
         anchor, received = tie(anchor, lax.ppermute(value, step[0], step[1]))
         return value + received, anchor
+
+    def ring_plan():
+        bits = [1 << k for k in range(group_size.bit_length() - 1)]
+        return [(bit, True) for bit in bits] + [(bit, False) for bit in reversed(bits)]
+
+    def ring_step(value, step, anchor):
+        bit, reducing = step
+        side = (lax.axis_index("dp") // bit) % 2
+        pairs = [(i, i ^ bit) for i in range(group_size)]
+        if reducing:
+            half = value.shape[0] // 2
+            sent = lax.dynamic_slice_in_dim(value, (1 - side) * half, half, axis=0)
+            anchor, received = tie(anchor, lax.ppermute(sent, "dp", pairs))
+            kept = lax.dynamic_slice_in_dim(value, side * half, half, axis=0)
+            return (kept.astype(f32) + received.astype(f32)).astype(value.dtype), anchor
+        anchor, received = tie(anchor, lax.ppermute(value, "dp", pairs))
+        return in_halves(value, received, side), anchor
+
+    def in_halves(own, other, side):
+        rows = own.shape[0]
+        whole = jnp.zeros((2 * rows,) + own.shape[1:], own.dtype)
+        whole = lax.dynamic_update_slice_in_dim(whole, own, side * rows, axis=0)
+        return lax.dynamic_update_slice_in_dim(whole, other, (1 - side) * rows, axis=0)
+
+    def fetch_half(own):
+        half = own.shape[0] // 2
+        side = lax.axis_index("dp") % 2
+        return swap(lax.dynamic_slice_in_dim(own, side * half, half, axis=0), 2)
+
+    def fetch_rest(half):
+        return lax.ppermute(half, "dp", [(i, i ^ 1) for i in range(group_size)])
 
     def in_order(stacked):
         if not square:
@@ -468,111 +785,130 @@
         own_start = lax.axis_index("dp") * slot_count
         own_scale = lax.dynamic_slice_in_dim(multiplier_whole, own_start, slot_count)
         own_valid = lax.dynamic_slice_in_dim(valid_all, own_start, slot_count)
+        all_rows = slot_count * own_rows
         row_scale = jnp.repeat(own_scale, own_rows)[:, None]
         row_valid = jnp.repeat(own_valid, own_rows)[:, None]
-        all_rows = slot_count * own_rows
-
-        inputs = patches.astype(f32)
-        normed = norm_rows(inputs, attn_gain, attn_shift).astype(bf16)
+        gain_row, shift_row, mlp_gain_row, mlp_shift_row, out_bias_row = (
+            value[None, :] for value in (attn_gain, attn_shift, mlp_gain, mlp_shift, out_bias)
+        )
         proj_bias = jnp.stack([qv_bias[0], jnp.zeros_like(qv_bias[0]), qv_bias[1]])[:, None, :]
-
         bias_row = up_bias[None, :]
+
+        dp_side = lax.axis_index("dp") % 2
+        fetch = fetch_half if square else gather_far
+        weights_near = ()
+        if square:
+            weights_near = tuple(
+                swap(value, 1) for value in (output_projection_weight, up_projection_weight, down_projection_weight)
+            )
+
+        normed = [norm_item(patches, 0, gain_row, shift_row)]
+        normed_far = [gather_far(normed[0])]
         bias_far = gather_far(bias_row)
-        normed = [normed[i] for i in range(slot_count)]
-        normed_far = [gather_far(normed[0])]
-        qkvs, attended, lses, attended_rows, normed_every = [], [], [], [], []
+        qkvs, attended, lses, heads_own, normed_every = [], [], [], [], []
         for i in range(slot_count):
             if i + 1 < slot_count:
                 if i == 0:
+                    normed += [norm_item(patches, k, gain_row, shift_row) for k in range(1, slot_count)]
                     normed_far[0], normed[1] = tie(normed_far[0], normed[1])
                 normed_far.append(gather_far(normed[i + 1]))
             every = jnp.concatenate(gather_near(normed[i], normed_far[i]), axis=0)
-            if i == slot_count - 1:
-                every, (up_far, out_far) = tie(every, (up_far, out_far))
-            else:
-                every = lax.optimization_barrier(every)
+            every = lax.optimization_barrier(every)
             qkv = (
                 jnp.einsum("wz,gzh->gwh", every, query_key_value_weight, preferred_element_type=f32) + proj_bias
             ).astype(bf16)
             if i == 0:
-                qkv, (out_own, up_own, ahead) = tie(
-                    qkv, (output_projection_weight, up_projection_weight, normed[min(2, slot_count - 1)])
-                )
-                if slot_count > 2:
-                    normed[2] = ahead
+                qkv, (up_own, weights_near, bias_far) = tie(qkv, (up_projection_weight, weights_near, bias_far))
+                up_far = fetch(up_own)
+            out, lse = attend(qkv)
+            if i + 1 < slot_count:
+                out, (normed[i + 1], normed_far[i + 1]) = tie(out, (normed[i + 1], normed_far[i + 1]))
+            if i == 0:
+                out, (down_own, out_own, up_far) = tie(out, (down_projection_weight, output_projection_weight, up_far))
+                down_far = fetch(down_own)
                 out_far = gather_far(out_own)
-                up_far = gather_far(up_own)
-            if i == 0:
-                qkv, bias_far = tie(qkv, bias_far)
-            out, lse = attend(qkv)
-            if i == 0:
-                out, down_own = tie(out, down_projection_weight)
-                down_far = gather_far(down_own)
+                if square:
+                    up_rest = fetch_rest(up_far)
+            if i == min(1, slot_count - 1) and square:
+                out, (down_far, up_rest) = tie(out, (down_far, up_rest))
+                up_far = in_halves(up_far, up_rest, dp_side)
+                up_diag = swap(up_far, 1)
+                down_rest = fetch_rest(down_far)
             if i == slot_count - 1:
-                out, down_far = tie(out, down_far)
-            moved = exchange_blocks([out[b * own_rows : (b + 1) * own_rows] for b in range(tensor_size)])
+                out, out_far = tie(out, out_far)
+                if square:
+                    out, (down_rest, up_diag) = tie(out, (down_rest, up_diag))
+                    down_far = in_halves(down_far, down_rest, dp_side)
+                    down_diag = swap(down_far, 1)
+            heads_own.append(exchange_blocks([out[b * own_rows : (b + 1) * own_rows] for b in range(tensor_size)]))
             normed_every.append(every)
             qkvs.append(qkv)
             attended.append(out)
             lses.append(lse)
-            attended_rows.append(jnp.concatenate(moved, axis=1))
-        attended_rows = jnp.concatenate(attended_rows, axis=0)
-        out_weight = jnp.concatenate(gather_near(out_own, out_far), axis=0)
-        attended_rows, out_weight = tie(attended_rows, out_weight)
+        if square:
+            out_weight = jnp.concatenate([out_own, weights_near[0], out_far, swap(out_far, 1)], axis=0)
+        else:
+            out_weight = jnp.concatenate(gather_near(out_own, out_far), axis=0)
+        rows_done = None
+        for i in range(slot_count):
+            heads = heads_own[i] if square else [jnp.concatenate(heads_own[i], axis=1)]
+            rows_done = out_project(
+                patches, i, heads, out_weight, out_bias_row, mlp_gain_row, mlp_shift_row, rows_done
+            )
+        attended_rows, residual, normed_mlp = rows_done
+        cot_low = (cotangent.astype(f32).reshape(all_rows, model) * row_scale).astype(bf16)
+
         bias_blocks = gather_near(bias_row, bias_far)
-        up_blocks = gather_near(up_own, up_far)
-        down_blocks = gather_near(down_own, down_far)
-
-        flat_inputs = inputs.reshape(all_rows, model)
-        residual = flat_inputs + nn(attended_rows, out_weight) + out_bias
-        normed_mlp = norm_rows(residual, mlp_gain, mlp_shift).astype(bf16)
-        cot_scaled = cotangent.astype(f32).reshape(all_rows, model) * row_scale
-        cot_low = cot_scaled.astype(bf16)
-
+        if square:
+            up_blocks = [up_own, weights_near[1], up_far, up_diag]
+            down_blocks = [down_own, weights_near[2], down_far, down_diag]
+        else:
+            up_blocks = gather_near(up_own, up_far)
+            down_blocks = gather_near(down_own, down_far)
+        calls = tensor_size // 2
         total = None
-        hiddens, slopes = [], []
-        for b in range(tensor_size):
-            hidden, slope, total = mlp_forward(normed_mlp, up_blocks[b], bias_blocks[b], down_blocks[b], total)
-            hiddens.append(hidden)
+        slopes, down_grads = [], []
+        for c in range(calls):
+            pair = slice(2 * c, 2 * c + 2)
+            slope, total, *grads = mlp_forward(
+                normed_mlp, cot_low, up_blocks[pair], bias_blocks[pair], down_blocks[pair], total
+            )
             slopes.append(slope)
+            down_grads += grads
         output = ((residual + total + down_bias) * row_valid).astype(bf16)
 
-        down_grads = [tn(hidden, cot_low).astype(bf16) for hidden in hiddens]
         cot_back, down_grads = tie(cot_low, down_grads)
-
-        total = None
-        pre_grads, bias_grads = [], []
-        for b in range(tensor_size):
-            pre_grad, bias_grad, total = mlp_backward(cot_back, down_blocks[b], slopes[b], up_blocks[b], total)
-            if b == 0:
-                down_stage, total = sum_near(down_grads, total)
-            pre_grads.append(pre_grad)
+        before = None
+        bias_grads = []
+        for c in range(calls):
+            pair = slice(2 * c, 2 * c + 2)
+            *before, bias_grad = mlp_backward(
+                cot_back, slopes[c], up_blocks[pair], down_blocks[pair], before, c, calls
+            )
             bias_grads.append(bias_grad)
-        down_sum, total = sum_far(down_stage, total)
-        down_all = lax.psum(down_sum.astype(bf16), "dp")
-        mlp_norm_back = jax.vjp(norm_rows, residual, mlp_gain, mlp_shift)[1]
-        grad_resid_norm, grad_mlp_gain, grad_mlp_shift = mlp_norm_back(total)
-        grad_residual = cot_scaled + grad_resid_norm
-        grad_out_bias = jnp.sum(grad_residual, axis=0)
-        grad_down_bias = jnp.sum(cot_scaled, axis=0)
-        grad_res_low = grad_residual.astype(bf16)
-        grad_attended_rows = nt(grad_res_low, out_weight).astype(bf16)
-        grad_attended_rows, (pre_grads, grad_res_wide) = tie(grad_attended_rows, (pre_grads, grad_res_low))
-
-        grad_attended = []
+            if c == 0:
+                down_stage, before = sum_near(down_grads, before)
+        down_sum, before = sum_far(down_stage, before)
+        ring = ring_plan()
+        pre_grad, total = before
+
+        grad_low = None
+        grad_residuals, grad_attended, sums = [], [], []
         for i in range(slot_count):
-            rows = grad_attended_rows[i * own_rows : (i + 1) * own_rows]
-            moved = exchange_blocks([rows[:, b * width : (b + 1) * width] for b in range(tensor_size)])
-            grad_attended.append(jnp.concatenate(moved, axis=0))
-
-        up_grads = [tn(normed_mlp, pre_grad).astype(bf16) for pre_grad in pre_grads]
-        out_grads = tn(attended_rows, grad_res_wide).astype(bf16)
-        out_grads = [out_grads[b * width : (b + 1) * width] for b in range(tensor_size)]
-
-        up_stage, grad_attended[0] = sum_near(up_grads, grad_attended[0])
-        out_stage, grad_attended[0] = sum_near(out_grads, grad_attended[0])
-        small_rows = jnp.stack([grad_mlp_gain, grad_mlp_shift, grad_out_bias, grad_down_bias])
-        bias_rows = in_order(jnp.concatenate(bias_grads, axis=0))
+            grad_residual, grad_low, item_sums, *pieces = residual_back(
+                total, residual, cotangent, own_scale, i, out_weight, mlp_gain_row, grad_low, tensor_size
+            )
+            grad_residuals.append(grad_residual)
+            sums.append(item_sums[:4])
+            grad_attended.append(exchange_blocks(pieces))
+        weight_grads = weight_back(normed_mlp, pre_grad, attended_rows, grad_low, tensor_size)
+        weight_grads, grad_attended[0] = tie(weight_grads, grad_attended[0])
+        down_sum, weight_grads = ring_step(down_sum, ring.pop(0), weight_grads)
+        up_grads, out_grads = weight_grads[:tensor_size], weight_grads[tensor_size:]
+
+        (up_stage, out_stage), grad_attended[0] = sums_near([up_grads, out_grads], grad_attended[0])
+        small_rows = sum(sums[1:], sums[0])
+        bias_rows = in_order(jnp.concatenate(bias_grads, axis=1).reshape(tensor_size, -1))
         smalls = jnp.concatenate([small_rows.reshape(-1), bias_rows.reshape(-1)]).reshape(-1, 128)
         waiting = list(steps)
 
@@ -581,33 +917,43 @@
         grad_normed = []
         for i in range(slot_count):
             last = i == slot_count - 1
-            dqkv = attend_back(qkvs[i], attended[i], grad_attended[i], lses[i])
+            dqkv = attend_back(qkvs[i], attended[i], jnp.concatenate(grad_attended[i], axis=0), lses[i])
+            if not last:
+                dqkv, grad_attended[i + 1] = tie(dqkv, grad_attended[i + 1])
+            if i >= 2:
+                grad_normed[i - 2], dqkv = terms_far(grad_normed[i - 2], dqkv)
+            if i >= 1:
+                grad_normed[i - 1], dqkv = sum_near(grad_normed[i - 1], dqkv)
             if i == 0:
                 up_sum, dqkv = sum_far(up_stage, dqkv)
                 out_sum, dqkv = sum_far(out_stage, dqkv)
-                dqkv, down_all = tie(dqkv, down_all)
-                up_sum, down_all = tie(up_sum, down_all)
-                up_all = lax.psum((up_sum.astype(bf16), out_sum.astype(bf16)), "dp")
+                up_all = lax.psum((up_sum, out_sum), "dp")
             if last:
                 dqkv, up_all = tie(dqkv, up_all)
             if waiting:
                 smalls, dqkv = sum_step(smalls, waiting.pop(0), dqkv)
-            results = project_back(normed_every[i], dqkv, query_key_value_weight, sums, last)
-            partial, sums = results[0], results[1:3]
+            if ring:
+                down_sum, dqkv = ring_step(down_sum, ring.pop(0), dqkv)
+            results = project_back(normed_every[i], dqkv, query_key_value_weight, sums, last, tensor_size)
+            partial, sums = results[:tensor_size], results[tensor_size : tensor_size + 2]
+            while ring and (last or len(ring) % 2 == 0):
+                down_sum, partial = ring_step(down_sum, ring.pop(0), partial)
             while waiting and (last or len(waiting) % 2):
                 smalls, partial = sum_step(smalls, waiting.pop(0), partial)
             if last:
-                qkv_all = lax.psum(results[3], "dp")
-            grad_normed.append([partial[b * own_rows : (b + 1) * own_rows] for b in range(tensor_size)])
+                qkv_all = lax.psum(results[-1], "dp")
+            grad_normed.append(partial)
+        grad_inputs = None
         for i in range(slot_count):
-            anchor = inputs[i]
-            stage, anchor = sum_near(grad_normed[i], anchor)
-            grad_normed[i] = sum_far(stage, anchor)[0]
-        grad_normed, qkv_all = tie(jnp.stack(grad_normed), qkv_all)
-        attn_norm_back = jax.vjp(lambda v: norm_rows(v, attn_gain, attn_shift), inputs)[1]
-        grad_inputs = (
-            grad_residual.reshape(slot_count, own_rows, model) + attn_norm_back(grad_normed)[0]
-        ).astype(bf16)
+            grad_residual = grad_residuals[i]
+            if i == slot_count - 1:
+                grad_normed[i], grad_residual = sum_near(grad_normed[i], grad_residual)
+            terms = grad_normed[i]
+            if i >= slot_count - 2:
+                terms, grad_residual = terms_far(terms, grad_residual)
+            if i == slot_count - 1:
+                grad_residual, qkv_all = tie(grad_residual, qkv_all)
+            grad_inputs = input_back(terms, patches, i, grad_residual, gain_row, grad_inputs)
         weight_grad = qkv_all[:, :model].astype(f32)
         columns = qkv_all[:, model].astype(f32)
         raw = jnp.stack(
@@ -619,7 +965,7 @@
         for step in tensor_steps:
             raw = raw + lax.ppermute(raw, step[0], step[1])
         up_all, out_all = [value.astype(f32) for value in up_all]
-        down_all = down_all.astype(f32)
+        down_all = down_sum.astype(f32)
         inverse = 1.0 / total_items
         smalls = smalls.reshape(-1) * inverse
         small_rows = smalls[: 4 * model].reshape(4, model)

time: 882 us -> 882 us (level)
  Pallas kernels: 367 us -> 466 us
  other arithmetic: 136 us -> 63.8 us
  matrix products: 72.4 us -> 14.2 us
  starting transfers between devices: 39.1 us -> 55.1 us
  waiting for transfers between devices: 210 us -> 222 us
    pallas_call x4 -> x15, Pallas kernels: 53.7 us -> 158 us  [the longest x2 71.8 us: mlp_forward(): pl.pallas_call(body, grid=(steps,), in_specs=in_specs, out_specs=[slope_s...]
    dot_general x11 -> x0, matrix products: 58.2 us -> none  [the longest x9 50.1 us: tn(): lax.dot_general(a, b, (((0,), (0,)), ((), ())), preferred_element_type=f32)]
    ppermute x57, waiting for transfers between devices: 129 us -> 173 us  [swap(): lax.ppermute(value, 'tensor', [(i, i ^ bits) for i in range(tensor_size)])]
    psum x3 -> x2, waiting for transfers between devices: 79.4 us -> 41 us  [the longest x1 41 us: shards(): qkv_all = lax.psum(results[-1], 'dp')]
    reduce_sum x9 -> x0, other arithmetic: 28.4 us -> none  [the longest x2 10.1 us: norm_rows(): return centred * lax.rsqrt(spread + epsilon) * norm_gain + norm_shift]
    concatenate x6 -> x4, other arithmetic: 29.8 us -> 6.57 us  [the longest x3 6.53 us: shards(): jnp.concatenate(grad_attended[i], axis=0)]
    ppermute x0 -> x8, starting transfers between devices: none -> 13.2 us  [the longest x3 4.98 us: ring_step(): anchor, received = tie(anchor, lax.ppermute(sent, 'dp', pairs))]
    another operation x5 -> x0, other arithmetic: 13 us -> none  [the longest x4 13 us: shards(): grad_normed, qkv_all = tie(jnp.stack(grad_normed), qkv_all)]
  transfers between devices with their start and end apart: 67 -> 74, of which waited for: 19 -> 19; matrix products, arithmetic and copies ran while one was open for 19% -> 10% of each run, Pallas kernels for 40% -> 47%
where the time goes in v2:
time: 882 us; the launch traced here: 873 us
  Pallas kernels  466 us (53%)
  waiting for transfers between devices  222 us (25%)
  other arithmetic  63.8 us (7%)
  starting transfers between devices  55.1 us (6%)
  local copies, waits for them, and re-layouts  35.1 us (4%)
  between operations  16.1 us (2%)
  matrix products  14.2 us (2%)
    ppermute x57, waiting for transfers between devices, swap(): lax.ppermute(value, 'tensor', [(i, i ^ bits) for i in range(tensor_size)])  173 us
    pallas_call x3, Pallas kernels, attend_back(): pl.pallas_call(body, grid=(pairs, kblocks), in_specs=[pl.BlockSpec((None,...  147 us
    pallas_call x3, Pallas kernels, attend(): pl.pallas_call(body, grid=(pairs, length // qblock), in_specs=[pl.BlockSp...  76.4 us
    pallas_call x2, Pallas kernels, mlp_forward(): pl.pallas_call(body, grid=(steps,), in_specs=in_specs, out_specs=[slope_s...  71.8 us
    pallas_call x3, Pallas kernels, project_back(): pl.pallas_call(kernel, grid=(steps,), in_specs=in_specs, out_specs=out_sp...  43.6 us
    pallas_call x2, Pallas kernels, mlp_backward(): pl.pallas_call(body, grid=(rows // block,), in_specs=in_specs, out_specs=...  41.7 us
    psum x1, waiting for transfers between devices, shards(): qkv_all = lax.psum(results[-1], 'dp')  41 us
    ppermute x57, starting transfers between devices, swap(): lax.ppermute(value, 'tensor', [(i, i ^ bits) for i in range(tensor_size)])  36.1 us
  transfers between devices with their start and end apart: 74, of which 19 were waited for; matrix products, arithmetic and copies ran while one was open for 10% of the time, Pallas kernels for 47%

profile of v2, /device:TPU:0, one launch (start us, length us, event | category | flops | bytes accessed | tf_op | source)
XLA Modules:
  0.0 873.1 jit_solution(10108833720623114348)
XLA Ops:
  15.6 20.8 %collective-permute-done.1 = bf16[512,1024]{1,0:T(8,128)(2,1)} collective-permute-done((bf16[512,1024]{1,0:T(8,128)(2,1)}, bf16[512,1024]{1,0:T(8,128)(2,1)}, u32[]{:S(2)}, u32[]{:S(2)}) %collective-permute-start.1) | collective-permute-done | bytes 1048608 | tf_op jit(solution)/shard_map/ppermute | solution.py:655
  49.9 25.3 %attend.3 = (bf16[2048,256]{1,0:T(8,128)(2,1)}, f32[2,2,2048]{2,1,0:T(2,128)}) custom-call(bf16[3,2048,256]{2,1,0:T(8,128)(2,1)} %fusion.9.q_ref.k_ref.v_ref, bf16[3,2048,256]{2,1,0:T(8,128)(2,1)} %fusion.9.q_ref.k_ref.v_ref, bf16[3,2048,256]{2,1,0:T(8,128)(2,1)} %fusion.9.q_ref.k_ref.v_ref), custom_call_target="tpu_custom_call" | custom-call | flops 134217728 | bytes 524288 | tf_op jit(solution)/shard_map/attend/pallas_call | solution.py:76
  84.9 19.5 %collective-permute-done.8 = bf16[512,1024]{1,0:T(8,128)(2,1)} collective-permute-done((bf16[512,1024]{1,0:T(8,128)(2,1)}, bf16[512,1024]{1,0:T(8,128)(2,1)}, u32[]{:S(2)}, u32[]{:S(2)}) %collective-permute-start.8) | collective-permute-done | bytes 1048608 | tf_op jit(solution)/shard_map/ppermute | solution.py:655
  113.4 25.5 %attend.4 = (bf16[2048,256]{1,0:T(8,128)(2,1)}, f32[2,2,2048]{2,1,0:T(2,128)}) custom-call(bf16[3,2048,256]{2,1,0:T(8,128)(2,1)} %fusion.10.q_ref.k_ref.v_ref, bf16[3,2048,256]{2,1,0:T(8,128)(2,1)} %fusion.10.q_ref.k_ref.v_ref, bf16[3,2048,256]{2,1,0:T(8,128)(2,1)} %fusion.10.q_ref.k_ref.v_ref), custom_call_target="tpu_custom_call" | custom-call | flops 134217728 | bytes 524288 | tf_op jit(solution)/shard_map/attend/pallas_call | solution.py:76
  163.3 25.6 %attend.5 = (bf16[2048,256]{1,0:T(8,128)(2,1)}, f32[2,2,2048]{2,1,0:T(2,128)}) custom-call(bf16[3,2048,256]{2,1,0:T(8,128)(2,1)} %fusion.11.q_ref.k_ref.v_ref, bf16[3,2048,256]{2,1,0:T(8,128)(2,1)} %fusion.11.q_ref.k_ref.v_ref, bf16[3,2048,256]{2,1,0:T(8,128)(2,1)} %fusion.11.q_ref.k_ref.v_ref), custom_call_target="tpu_custom_call" | custom-call | flops 134217728 | bytes 524288 | tf_op jit(solution)/shard_map/attend/pallas_call | solution.py:76
  242.2 35.2 %mlp_forward.2 = (bf16[1536,2048]{1,0:T(8,128)(2,1)}, f32[1536,1024]{1,0:T(8,128)}, bf16[1024,1024]{1,0:T(8,128)(2,1)}, bf16[1024,1024]{1,0:T(8,128)(2,1)}) custom-call(bf16[1536,1024]{1,0:T(8,128)(2,1)} %get-tuple-element.253.refs_0_.x_ref, bf16[1536,1024]{1,0:T(8,128)(2,1)} %fusion.refs_1_.refs_0_, bf16[1024,1024]{1,0:T(8,128)(2,1)} %refs_2_.7, ...), custom_call_target="tpu_custom_call" | custom-call | flops 301989888 | bytes 1572864 | tf_op jit(solution)/shard_map/mlp_forward/pallas_call | solution.py:441
  278.1 36.6 %mlp_forward.3 = (bf16[1536,2048]{1,0:T(8,128)(2,1)}, f32[1536,1024]{1,0:T(8,128)}, bf16[1024,1024]{1,0:T(8,128)(2,1)}, bf16[1024,1024]{1,0:T(8,128)(2,1)}) custom-call(bf16[1536,1024]{1,0:T(8,128)(2,1)} %get-tuple-element.253.refs_0_.x_ref, bf16[1536,1024]{1,0:T(8,128)(2,1)} %fusion.refs_1_.refs_0_, ...), custom_call_target="tpu_custom_call", output_to_operand_aliasing={{1}: (8, {})} | custom-call | flops 301989888 | bytes 1572864 | tf_op jit(solution)/shard_map/mlp_forward/pallas_call | solution.py:441
  315.3 20.5 %mlp_backward.2 = (bf16[1536,4096]{1,0:T(8,128)(2,1)}, f32[1536,1024]{1,0:T(8,128)}, f32[1,2048]{1,0:T(1,128)}) custom-call(bf16[1536,1024]{1,0:T(8,128)(2,1)} %fusion.refs_1_.refs_0_, bf16[1536,2048]{1,0:T(8,128)(2,1)} %get-tuple-element.267.refs_1_, bf16[1024,1024]{1,0:T(8,128)(2,1)} %refs_2_.7, bf16[1024,1024]{1,0:T(8,128)(2,1)} %collective-permute-done.4.refs_3_, ...), custom_call_target="tpu_custom_call" | custom-call | flops 201326592 | bytes 1572864 | tf_op jit(solution)/shard_map/mlp_backward/pallas_call | solution.py:499
  341.2 21.1 %mlp_backward.3 = (bf16[1536,4096]{1,0:T(8,128)(2,1)}, f32[1536,1024]{1,0:T(8,128)}, f32[1,2048]{1,0:T(1,128)}) custom-call(bf16[1536,1024]{1,0:T(8,128)(2,1)} %fusion.refs_1_.refs_0_, bf16[1536,2048]{1,0:T(8,128)(2,1)} %get-tuple-element.266.refs_1_, ...), custom_call_target="tpu_custom_call", output_to_operand_aliasing={{0}: (6, {}), {1}: (7, {})} | custom-call | flops 201326592 | bytes 1572864 | tf_op jit(solution)/shard_map/mlp_backward/pallas_call | solution.py:499
  362.3 25.5 %collective-permute-done.34 = bf16[1024,1024]{1,0:T(8,128)(2,1)S(1)} collective-permute-done((bf16[1024,1024]{1,0:T(8,128)(2,1)}, bf16[1024,1024]{1,0:T(8,128)(2,1)S(1)}, u32[]{:S(2)}, u32[]{:S(2)}) %collective-permute-start.34) | collective-permute-done | bytes 2097184 | tf_op jit(solution)/shard_map/ppermute | solution.py:655
  416.7 26.6 %weight_back.1 = (bf16[1024,1024]{1,0:T(8,128)(2,1)}, bf16[1024,1024]{1,0:T(8,128)(2,1)}, bf16[1024,1024]{1,0:T(8,128)(2,1)}, bf16[1024,1024]{1,0:T(8,128)(2,1)}...) custom-call(bf16[1536,1024]{1,0:T(8,128)(2,1)} %get-tuple-element.25, ...), custom_call_target="tpu_custom_call" | custom-call | flops 251658240 | bytes 1572864 | tf_op jit(solution)/shard_map/weight_back/pallas_call | solution.py:554
  444.5 7.1 collective-permute-done.41
  466.1 45.4 %collective-permute-done.44 = bf16[512,256]{1,0:T(8,128)(2,1)} collective-permute-done((bf16[512,256]{1,0:T(8,128)(2,1)}, bf16[512,256]{1,0:T(8,128)(2,1)}, u32[]{:S(2)}, u32[]{:S(2)}) %collective-permute-start.44) | collective-permute-done | bytes 262176 | tf_op jit(solution)/shard_map/ppermute | solution.py:655
  513.7 49.0 %attend_back.3.refs_1_ = bf16[3,2048,256]{2,1,0:T(8,128)(2,1)} custom-call(bf16[3,2048,256]{2,1,0:T(8,128)(2,1)} %fusion.9.q_ref.k_ref.v_ref, bf16[3,2048,256]{2,1,0:T(8,128)(2,1)} %fusion.9.q_ref.k_ref.v_ref, bf16[3,2048,256]{2,1,0:T(8,128)(2,1)} %fusion.9.q_ref.k_ref.v_ref, bf16[2048,256]{1,0:T(8,128)(2,1)} %get-tuple-element.245.out_ref, ...), custom_call_target="tpu_custom_call" | custom-call | flops 335544320 | bytes 524288 | tf_op jit(solution)/shard_map/attend_back/pallas_call | solution.py:168
  562.8 13.8 %project_back.3 = (bf16[512,1024]{1,0:T(8,128)(2,1)}, bf16[512,1024]{1,0:T(8,128)(2,1)}, bf16[512,1024]{1,0:T(8,128)(2,1)}, bf16[512,1024]{1,0:T(8,128)(2,1)}, f...) custom-call(bf16[2048,1024]{1,0:T(8,128)(2,1)} %copy-done.6, bf16[3,2048,256]{2,1,0:T(8,128)(2,1)} %attend_back.3.refs_1_, ...), custom_call_target="tpu_custom_call" | custom-call | flops 100663296 | bytes 524288 | tf_op jit(solution)/shard_map/project_back/pallas_call | solution.py:634
  584.8 7.5 collective-permute-done.53
  605.8 49.0 %attend_back.4.refs_1_ = bf16[3,2048,256]{2,1,0:T(8,128)(2,1)} custom-call(bf16[3,2048,256]{2,1,0:T(8,128)(2,1)} %fusion.10.q_ref.k_ref.v_ref, bf16[3,2048,256]{2,1,0:T(8,128)(2,1)} %fusion.10.q_ref.k_ref.v_ref, bf16[3,2048,256]{2,1,0:T(8,128)(2,1)} %fusion.10.q_ref.k_ref.v_ref, bf16[2048,256]{1,0:T(8,128)(2,1)} %get-tuple-element.244.out_ref, ...), custom_call_target="tpu_custom_call" | custom-call | flops 335544320 | bytes 524288 | tf_op jit(solution)/shard_map/attend_back/pallas_call | solution.py:168
  662.6 14.1 %project_back.4 = (bf16[512,1024]{1,0:T(8,128)(2,1)}, bf16[512,1024]{1,0:T(8,128)(2,1)}, bf16[512,1024]{1,0:T(8,128)(2,1)}, bf16[512,1024]{1,0:T(8,128)(2,1)}, f...) custom-call(bf16[2048,1024]{1,0:T(8,128)(2,1)} %copy-done.5, ...), custom_call_target="tpu_custom_call", output_to_operand_aliasing={{4}: (3, {}), {5}: (4, {})} | custom-call | flops 100663296 | bytes 524288 | tf_op jit(solution)/shard_map/project_back/pallas_call | solution.py:634
  682.1 49.1 %attend_back.5.refs_1_ = bf16[3,2048,256]{2,1,0:T(8,128)(2,1)} custom-call(bf16[3,2048,256]{2,1,0:T(8,128)(2,1)} %fusion.11.q_ref.k_ref.v_ref, bf16[3,2048,256]{2,1,0:T(8,128)(2,1)} %fusion.11.q_ref.k_ref.v_ref, bf16[3,2048,256]{2,1,0:T(8,128)(2,1)} %fusion.11.q_ref.k_ref.v_ref, bf16[2048,256]{1,0:T(8,128)(2,1)} %get-tuple-element.243.out_ref, ...), custom_call_target="tpu_custom_call" | custom-call | flops 335544320 | bytes 524288 | tf_op jit(solution)/shard_map/attend_back/pallas_call | solution.py:168
  732.4 15.7 %project_back.5 = (bf16[512,1024]{1,0:T(8,128)(2,1)}, bf16[512,1024]{1,0:T(8,128)(2,1)}, bf16[512,1024]{1,0:T(8,128)(2,1)}, bf16[512,1024]{1,0:T(8,128)(2,1)}, f...) custom-call(bf16[2048,1024]{1,0:T(8,128)(2,1)} %copy-done.4, ...), custom_call_target="tpu_custom_call", output_to_operand_aliasing={{4}: (3, {}), {5}: (4, {})} | custom-call | flops 100663296 | bytes 524288 | tf_op jit(solution)/shard_map/project_back/pallas_call | solution.py:634
  748.7 7.0 multiply_convert_fusion
  775.9 13.1 %collective-permute-done.69.refs_5_ = bf16[512,1024]{1,0:T(8,128)(2,1)S(1)} collective-permute-done((bf16[512,1024]{1,0:T(8,128)(2,1)S(1)}, bf16[512,1024]{1,0:T(8,128)(2,1)S(1)}, u32[]{:S(2)}, u32[]{:S(2)}) %collective-permute-start.69) | collective-permute-done | bytes 1048608 | tf_op jit(solution)/shard_map/ppermute | solution.py:655
  794.9 15.8 %collective-permute-done.68.refs_5_ = bf16[512,1024]{1,0:T(8,128)(2,1)} collective-permute-done((bf16[512,1024]{1,0:T(8,128)(2,1)}, bf16[512,1024]{1,0:T(8,128)(2,1)}, u32[]{:S(2)}, u32[]{:S(2)}) %collective-permute-start.68) | collective-permute-done | bytes 1048608 | tf_op jit(solution)/shard_map/ppermute | solution.py:655
  810.7 41.0 %all-reduce.4.cloned.1.call-done = bf16[3,1040,256]{2,1,0:T(8,128)(2,1)} async-done(((bf16[3,1040,256]{2,1,0:T(8,128)(2,1)}), bf16[3,1040,256]{2,1,0:T(8,128)(2,1)}) %all-reduce.4.cloned.1.call-update) | async-done | bytes 1597456 | tf_op jit(solution)/shard_map/psum | solution.py:944
  (396 shorter events, 246.9 us)
Async XLA Ops:
  7.2 724.1 %all-reduce.6.cloned.1.call-start = ((), (), s32[]{:S(2)}) async-start(), calls=%async_computation.1 | async-start | bytes 5242880 | tf_op jit(solution)/shard_map/psum | solution.py:930
  81.0 58.0 %collective-permute-start.11 = (bf16[512,1024]{1,0:T(8,128)(2,1)}, bf16[512,1024]{1,0:T(8,128)(2,1)}, u32[]{:S(2)}, u32[]{:S(2)}) collective-permute-start(bf16[512,1024]{1,0:T(8,128)(2,1)} %norm_item.5), channel_id=1, source_target_pairs={{0,2},{1,3},{2,0},{3,1},{4,6},{5,7},{6,4},{7,5},{8,10},{9,11},{10,... | collective-permute-start | bytes 3145736 | tf_op jit(solution)/shard_map/ppermute | solution.py:655
  195.2 82.3 %collective-permute-start.30 = (bf16[1024,1024]{1,0:T(8,128)(2,1)}, bf16[1024,1024]{1,0:T(8,128)(2,1)}, u32[]{:S(2)}, u32[]{:S(2)}) collective-permute-start(bf16[1024,1024]{1,0:T(8,128)(2,1)} %constant_dynamic-update-slice_fusion.12.refs_6_.refs_4_), channel_id=1, source_target_pairs={{0,1},{1,0},{2,3},{3,2},{4,5},{5,4},{6,7},{7,6},{8,9},{9,8},{10,11... | collective-permute-start | bytes 6291464 | tf_op jit(solution)/shard_map/ppermute | solution.py:655
  339.7 48.2 %collective-permute-start.34 = (bf16[1024,1024]{1,0:T(8,128)(2,1)}, bf16[1024,1024]{1,0:T(8,128)(2,1)S(1)}, u32[]{:S(2)}, u32[]{:S(2)}) collective-permute-start(bf16[1024,1024]{1,0:T(8,128)(2,1)} %add_convert_fusion.6), channel_id=1, source_target_pairs={{0,2},{1,3},{2,0},{3,1},{4,6},{5,7},{6,4},{7,5},{8,10},{9,11},{10,... | collective-permute-start | bytes 6291464 | tf_op jit(solution)/shard_map/ppermute | solution.py:655
  393.6 49.8 %collective-permute-start.38 = (bf16[512,1024]{1,0:T(8,128)(2,1)S(1)}, bf16[512,1024]{1,0:T(8,128)(2,1)}, u32[]{:S(2)}, u32[]{:S(2)}) collective-permute-start(bf16[512,1024]{1,0:T(8,128)(2,1)S(1)} %constant_dynamic-slice_fusion.6), channel_id=1, source_target_pairs={{0,4},{4,0},{8,12},{12,8},{16,20},{20,16},{24,28},{28,24},{1,5},{5... | collective-permute-start | bytes 3145736 | tf_op jit(solution)/shard_map/ppermute | solution.py:727
  401.0 42.4 %collective-permute-start.35 = (bf16[512,256]{1,0:T(8,128)(2,1)}, bf16[512,256]{1,0:T(8,128)(2,1)S(1)}, u32[]{:S(2)}, u32[]{:S(2)}) collective-permute-start(bf16[512,256]{1,0:T(8,128)(2,1)} %get-tuple-element.294), channel_id=1, source_target_pairs={{0,1},{1,0},{2,3},{3,2},{4,5},{5,4},{6,7},{7,6},{8,9},{9,8},{10,11... | collective-permute-start | bytes 786440 | tf_op jit(solution)/shard_map/ppermute | solution.py:655
  457.0 105.7 %collective-permute-start.49 = (bf16[1024,1024]{1,0:T(8,128)(2,1)}, bf16[1024,1024]{1,0:T(8,128)(2,1)}, u32[]{:S(2)}, u32[]{:S(2)}) collective-permute-start(bf16[1024,1024]{1,0:T(8,128)(2,1)} %add_convert_fusion.4), channel_id=1, source_target_pairs={{0,2},{1,3},{2,0},{3,1},{4,6},{5,7},{6,4},{7,5},{8,10},{9,11},{10,... | collective-permute-start | bytes 6291464 | tf_op jit(solution)/shard_map/ppermute | solution.py:655
  459.1 52.4 %collective-permute-start.44 = (bf16[512,256]{1,0:T(8,128)(2,1)}, bf16[512,256]{1,0:T(8,128)(2,1)}, u32[]{:S(2)}, u32[]{:S(2)}) collective-permute-start(bf16[512,256]{1,0:T(8,128)(2,1)} %get-tuple-element.323), channel_id=1, source_target_pairs={{0,2},{1,3},{2,0},{3,1},{4,6},{5,7},{6,4},{7,5},{8,10},{9,11},{10,... | collective-permute-start | bytes 786440 | tf_op jit(solution)/shard_map/ppermute | solution.py:655
  461.2 101.6 %collective-permute-start.52 = (bf16[256,1024]{1,0:T(8,128)(2,1)S(1)}, bf16[256,1024]{1,0:T(8,128)(2,1)S(1)}, u32[]{:S(2)}, u32[]{:S(2)}) collective-permute-start(bf16[256,1024]{1,0:T(8,128)(2,1)S(1)} %constant_dynamic-slice_fusion.1), channel_id=1, source_target_pairs={{0,8},{4,12},{8,0},{12,4},{16,24},{20,28},{24,16},{28,20},{1,9},{5... | collective-permute-start | bytes 1572872 | tf_op jit(solution)/shard_map/ppermute | solution.py:727
  464.3 98.4 %collective-permute-start.50 = (bf16[256,1024]{1,0:T(8,128)(2,1)S(1)}, bf16[256,1024]{1,0:T(8,128)(2,1)S(1)}, u32[]{:S(2)}, u32[]{:S(2)}) collective-permute-start(bf16[256,1024]{1,0:T(8,128)(2,1)S(1)} %add_convert_fusion.13), channel_id=1, source_target_pairs={{0,2},{1,3},{2,0},{3,1},{4,6},{5,7},{6,4},{7,5},{8,10},{9,11},{10,... | collective-permute-start | bytes 1572872 | tf_op jit(solution)/shard_map/ppermute | solution.py:655
  466.0 96.7 %collective-permute-start.45 = (bf16[512,256]{1,0:T(8,128)(2,1)}, bf16[512,256]{1,0:T(8,128)(2,1)S(1)}, u32[]{:S(2)}, u32[]{:S(2)}) collective-permute-start(bf16[512,256]{1,0:T(8,128)(2,1)} %get-tuple-element.324), channel_id=1, source_target_pairs={{0,3},{1,2},{2,1},{3,0},{4,7},{5,6},{6,5},{7,4},{8,11},{9,10},{10,... | collective-permute-start | bytes 786440 | tf_op jit(solution)/shard_map/ppermute | solution.py:655
  511.5 51.3 %collective-permute-start.51 = (f32[64,128]{1,0:T(8,128)S(1)}, f32[64,128]{1,0:T(8,128)S(1)}, u32[]{:S(2)}, u32[]{:S(2)}) collective-permute-start(f32[64,128]{1,0:T(8,128)S(1)} %constant_dynamic-update-slice_fusion.4), channel_id=1, source_target_pairs={{0,1},{1,0},{2,3},{3,2},{4,5},{5,4},{6,7},{7,6},{8,9},{9,8},{10,11... | collective-permute-start | bytes 98312 | tf_op jit(solution)/shard_map/ppermute | solution.py:713
  592.3 62.5 %collective-permute-start.54 = (bf16[512,1024]{1,0:T(8,128)(2,1)}, bf16[512,1024]{1,0:T(8,128)(2,1)S(1)}, u32[]{:S(2)}, u32[]{:S(2)}) collective-permute-start(bf16[512,1024]{1,0:T(8,128)(2,1)} %get-tuple-element.361), channel_id=1, source_target_pairs={{0,1},{1,0},{2,3},{3,2},{4,5},{5,4},{6,7},{7,6},{8,9},{9,8},{10,11... | collective-permute-start | bytes 3145736 | tf_op jit(solution)/shard_map/ppermute | solution.py:655
  592.3 62.5 %collective-permute-start.55 = (bf16[512,1024]{1,0:T(8,128)(2,1)}, bf16[512,1024]{1,0:T(8,128)(2,1)S(1)}, u32[]{:S(2)}, u32[]{:S(2)}) collective-permute-start(bf16[512,1024]{1,0:T(8,128)(2,1)} %get-tuple-element.362), channel_id=1, source_target_pairs={{0,1},{1,0},{2,3},{3,2},{4,5},{5,4},{6,7},{7,6},{8,9},{9,8},{10,11... | collective-permute-start | bytes 3145736 | tf_op jit(solution)/shard_map/ppermute | solution.py:655
  593.9 257.8 %all-reduce.4.cloned.1.call-start = ((), (), s32[]{:S(2)}) async-start(), calls=%async_computation | async-start | bytes 3194880 | tf_op jit(solution)/shard_map/psum | solution.py:944
  595.7 59.1 %collective-permute-start.48 = (bf16[512,256]{1,0:T(8,128)(2,1)}, bf16[512,256]{1,0:T(8,128)(2,1)}, u32[]{:S(2)}, u32[]{:S(2)}) collective-permute-start(bf16[512,256]{1,0:T(8,128)(2,1)} %get-tuple-element.333), channel_id=1, source_target_pairs={{0,3},{1,2},{2,1},{3,0},{4,7},{5,6},{6,5},{7,4},{8,11},{9,10},{10,... | collective-permute-start | bytes 786440 | tf_op jit(solution)/shard_map/ppermute | solution.py:655
  597.0 57.8 %collective-permute-start.57 = (f32[64,128]{1,0:T(8,128)S(1)}, f32[64,128]{1,0:T(8,128)S(1)}, u32[]{:S(2)}, u32[]{:S(2)}) collective-permute-start(f32[64,128]{1,0:T(8,128)S(1)} %add.234), channel_id=1, source_target_pairs={{0,2},{1,3},{2,0},{3,1},{4,6},{5,7},{6,4},{7,5},{8,10},{9,11},{10,... | collective-permute-start | bytes 98312 | tf_op jit(solution)/shard_map/ppermute | solution.py:713
  603.6 51.3 %collective-permute-start.58 = (bf16[128,1024]{1,0:T(8,128)(2,1)}, bf16[128,1024]{1,0:T(8,128)(2,1)S(1)}, u32[]{:S(2)}, u32[]{:S(2)}) collective-permute-start(bf16[128,1024]{1,0:T(8,128)(2,1)} %get-tuple-element.435), channel_id=1, source_target_pairs={{0,16},{4,20},{8,24},{12,28},{16,0},{20,4},{24,8},{28,12},{1,17},{... | collective-permute-start | bytes 786440 | tf_op jit(solution)/shard_map/ppermute | solution.py:730
  661.0 70.1 %collective-permute-start.56 = (bf16[512,1024]{1,0:T(8,128)(2,1)S(1)}, bf16[512,1024]{1,0:T(8,128)(2,1)}, u32[]{:S(2)}, u32[]{:S(2)}) collective-permute-start(bf16[512,1024]{1,0:T(8,128)(2,1)S(1)} %add_convert_fusion.9), channel_id=1, source_target_pairs={{0,2},{1,3},{2,0},{3,1},{4,6},{5,7},{6,4},{7,5},{8,10},{9,11},{10,... | collective-permute-start | bytes 3145736 | tf_op jit(solution)/shard_map/ppermute | solution.py:655
  676.8 54.4 %collective-permute-start.61 = (bf16[512,1024]{1,0:T(8,128)(2,1)}, bf16[512,1024]{1,0:T(8,128)(2,1)}, u32[]{:S(2)}, u32[]{:S(2)}) collective-permute-start(bf16[512,1024]{1,0:T(8,128)(2,1)} %get-tuple-element.382), channel_id=1, source_target_pairs={{0,1},{1,0},{2,3},{3,2},{4,5},{5,4},{6,7},{7,6},{8,9},{9,8},{10,11... | collective-permute-start | bytes 3145736 | tf_op jit(solution)/shard_map/ppermute | solution.py:655
  676.9 54.3 %collective-permute-start.62 = (bf16[512,1024]{1,0:T(8,128)(2,1)}, bf16[512,1024]{1,0:T(8,128)(2,1)S(1)}, u32[]{:S(2)}, u32[]{:S(2)}) collective-permute-start(bf16[512,1024]{1,0:T(8,128)(2,1)} %get-tuple-element.383), channel_id=1, source_target_pairs={{0,1},{1,0},{2,3},{3,2},{4,5},{5,4},{6,7},{7,6},{8,9},{9,8},{10,11... | collective-permute-start | bytes 3145736 | tf_op jit(solution)/shard_map/ppermute | solution.py:655
  678.7 53.7 %collective-permute-start.64 = (bf16[512,1024]{1,0:T(8,128)(2,1)S(1)}, bf16[512,1024]{1,0:T(8,128)(2,1)}, u32[]{:S(2)}, u32[]{:S(2)}) collective-permute-start(bf16[512,1024]{1,0:T(8,128)(2,1)S(1)} %constant_dynamic-update-slice_fusion.8), channel_id=1, source_target_pairs={{0,4},{4,0},{8,12},{12,8},{16,20},{20,16},{24,28},{28,24},{1,5},{5... | collective-permute-start | bytes 3145736 | tf_op jit(solution)/shard_map/ppermute | solution.py:730
  679.3 52.0 %collective-permute-start.63 = (f32[64,128]{1,0:T(8,128)S(1)}, f32[64,128]{1,0:T(8,128)S(1)}, u32[]{:S(2)}, u32[]{:S(2)}) collective-permute-start(f32[64,128]{1,0:T(8,128)S(1)} %add.242), channel_id=1, source_target_pairs={{0,8},{4,12},{8,0},{12,4},{16,24},{20,28},{24,16},{28,20},{1,9},{5... | collective-permute-start | bytes 98312 | tf_op jit(solution)/shard_map/ppermute | solution.py:713
  767.6 43.2 %collective-permute-start.68 = (bf16[512,1024]{1,0:T(8,128)(2,1)}, bf16[512,1024]{1,0:T(8,128)(2,1)}, u32[]{:S(2)}, u32[]{:S(2)}) collective-permute-start(bf16[512,1024]{1,0:T(8,128)(2,1)} %add_convert_fusion.8), channel_id=1, source_target_pairs={{0,2},{1,3},{2,0},{3,1},{4,6},{5,7},{6,4},{7,5},{8,10},{9,11},{10,... | collective-permute-start | bytes 3145736 | tf_op jit(solution)/shard_map/ppermute | solution.py:655
  (123 other events, 2036.2 us)
Sparse Core Ops, SparseCore 0:
  594.1 132.6 all-reduce.5
  761.3 90.3 all-reduce.3

commit v3 on v2

--- a/solution.py
+++ b/solution.py
@@ -217,33 +217,34 @@
     )(patches, norm_gain, norm_shift)
 
 
-def out_project(patches, item, heads, weight, out_bias, norm_gain, norm_shift, before):
+def out_project(patches, item, place, heads, weight, out_bias, norm_gain, norm_shift, before):
     slots, rows, model = patches.shape
     block = largest_block(rows, 256)
     steps = rows // block
-    count = len(heads)
+    count, _, width = heads.shape
 
     def body(*refs):
-        x_ref, weight_ref, bias_ref, gain_ref, shift_ref = refs[:5]
-        head_refs = refs[5 : 5 + count]
+        place_ref, x_ref, weight_ref, bias_ref, gain_ref, shift_ref, head_ref = refs[:7]
         attended_ref, residual_ref, normed_ref = refs[-3:]
-        attended = [ref[...] for ref in head_refs]
-        attended = attended[0] if count == 1 else jnp.concatenate(attended, axis=1)
-        attended_ref[...] = attended
+        for k in range(count):
+            attended_ref[:, k * width : (k + 1) * width] = head_ref[place_ref[0] ^ k]
+        attended = attended_ref[...]
         residual = x_ref[...].astype(f32) + nn(attended, weight_ref[...]) + bias_ref[...]
         residual_ref[...] = residual
         normed_ref[...] = norm_rows(residual, gain_ref[...], shift_ref[...]).astype(bf16)
 
     vector = pl.BlockSpec((1, model), lambda i: (0, 0))
     placed = pl.BlockSpec((block, model), lambda i: (item * steps + i, 0))
-    operands = [patches, weight, out_bias, norm_gain, norm_shift, *heads]
+    operands = [place, patches, weight, out_bias, norm_gain, norm_shift, heads]
     in_specs = [
+        pl.BlockSpec(memory_space=pltpu.SMEM),
         pl.BlockSpec((None, block, model), lambda i: (item, i, 0)),
         pl.BlockSpec((model, model), lambda i: (0, 0)),
         vector,
         vector,
         vector,
-    ] + [pl.BlockSpec((block, head.shape[1]), lambda i: (i, 0)) for head in heads]
+        pl.BlockSpec((count, block, width), lambda i: (0, i, 0)),
+    ]
     aliases = {}
     if before is not None:
         aliases = {len(operands) + k: k for k in range(3)}
@@ -262,17 +263,15 @@
     )(*operands)
 
 
-def residual_back(total, residual, cotangent, scale, item, weight, norm_gain, low_before, pieces):
+def residual_back(total, residual, cotangent, scale, item, place, weight, norm_gain, low_before, pieces):
     slots, rows, model = cotangent.shape
     block = largest_block(rows, 256)
     steps = rows // block
     piece = model // pieces
 
     def body(*refs):
-        total_ref, residual_ref, cot_ref, scale_ref, weight_ref, gain_ref = refs[:6]
-        outs = refs[6:] if low_before is None else refs[7:]
-        grad_ref, low_ref, sum_ref = outs[:3]
-        attended_refs = outs[3:]
+        place_ref, total_ref, residual_ref, cot_ref, scale_ref, weight_ref, gain_ref = refs[:7]
+        grad_ref, low_ref, sum_ref, attended_ref = refs[-4:]
         residual = residual_ref[...]
         centred = residual - jnp.mean(residual, axis=-1, keepdims=True)
         rate = lax.rsqrt(jnp.mean(centred * centred, axis=-1, keepdims=True) + epsilon)
@@ -295,12 +294,13 @@
             sum_ref[k : k + 1, :] += jnp.sum(value, axis=0, keepdims=True)
         attended = nt(low, weight_ref[...]).astype(bf16)
         for k in range(pieces):
-            attended_refs[k][...] = attended[:, k * piece : (k + 1) * piece]
+            attended_ref[place_ref[0] ^ k] = attended[:, k * piece : (k + 1) * piece]
 
     row_spec = pl.BlockSpec((block, model), lambda i: (i, 0))
     placed = pl.BlockSpec((block, model), lambda i: (item * steps + i, 0))
-    operands = [total, residual, cotangent, scale, weight, norm_gain]
+    operands = [place, total, residual, cotangent, scale, weight, norm_gain]
     in_specs = [
+        pl.BlockSpec(memory_space=pltpu.SMEM),
         placed,
         placed,
         pl.BlockSpec((None, block, model), lambda i: (item, i, 0)),
@@ -310,21 +310,25 @@
     ]
     aliases = {}
     if low_before is not None:
-        aliases = {6: 1}
+        aliases = {7: 1}
         operands.append(low_before)
         in_specs.append(pl.BlockSpec(memory_space=pl.ANY))
     return pl.pallas_call(
         body,
         grid=(steps,),
         in_specs=in_specs,
-        out_specs=[row_spec, placed, pl.BlockSpec((8, model), lambda i: (0, 0))]
-        + [pl.BlockSpec((block, piece), lambda i: (i, 0))] * pieces,
+        out_specs=[
+            row_spec,
+            placed,
+            pl.BlockSpec((8, model), lambda i: (0, 0)),
+            pl.BlockSpec((pieces, block, piece), lambda i: (0, i, 0)),
+        ],
         out_shape=[
             jax.ShapeDtypeStruct((rows, model), f32),
             jax.ShapeDtypeStruct((slots * rows, model), bf16),
             jax.ShapeDtypeStruct((8, model), f32),
-        ]
-        + [jax.ShapeDtypeStruct((rows, piece), bf16)] * pieces,
+            jax.ShapeDtypeStruct((pieces, rows, piece), bf16),
+        ],
         input_output_aliases=aliases,
         compiler_params=params(),
         cost_estimate=hint(2 * rows * model * model, rows * model),
@@ -566,7 +570,7 @@
     )(normed, pre_grad, attended, grad_low)
 
 
-def project_back(normed, dqkv, weight, before, last, pieces):
+def project_back(place, normed, dqkv, weight, before, last, pieces):
     rows, model = normed.shape
     width = weight.shape[2]
     block = rows // pieces
@@ -574,8 +578,8 @@
     first = before is None
 
     def kernel(*refs):
-        normed_ref, dqkv_ref, weight_ref = refs[:3]
-        rest = refs[3:]
+        place_ref, normed_ref, dqkv_ref, weight_ref = refs[:4]
+        rest = refs[4:]
         if not first:
             wgrad_before, column_before = rest[:2]
             rest = rest[2:]
@@ -598,7 +602,7 @@
         row_grad = row_grad.astype(bf16)
         for k in range(pieces):
 
-            @pl.when(step == k)
+            @pl.when(step == place_ref[0] ^ k)
             def _():
                 row_refs[k][...] = row_grad
 
@@ -618,8 +622,8 @@
     whole = pl.BlockSpec((3, model, width), lambda i: (0, 0, 0))
     columns = pl.BlockSpec((8, width), lambda i: (0, 0))
     row_spec = pl.BlockSpec((block, model), lambda i: (i, 0))
-    operands = [normed, dqkv, weight]
-    in_specs = [row_spec, pl.BlockSpec((3, block, width), lambda i: (0, i, 0)), whole]
+    operands = [place, normed, dqkv, weight]
+    in_specs = [pl.BlockSpec(memory_space=pltpu.SMEM), row_spec, pl.BlockSpec((3, block, width), lambda i: (0, i, 0)), whole]
     if not first:
         operands += list(before)
         in_specs += [whole, columns]
@@ -637,7 +641,7 @@
         in_specs=in_specs,
         out_specs=out_specs,
         out_shape=out_shape,
-        input_output_aliases={} if first else {3: pieces, 4: pieces + 1},
+        input_output_aliases={} if first else {4: pieces, 5: pieces + 1},
         compiler_params=pltpu.CompilerParams(vmem_limit_bytes=VMEM_LIMIT),
         cost_estimate=pl.CostEstimate(
             flops=12 * rows * model * width // COST_SCALE,
@@ -662,11 +666,8 @@
             return [far[i] for i in range(tensor_size)]
         return [own, swap(own, 1), far, swap(far, 1)]
 
-    def exchange_blocks(blocks):
-        if not square:
-            moved = lax.all_to_all(jnp.stack(blocks), "tensor", 0, 0)
-            return [moved[i] for i in range(tensor_size)]
-        return [blocks[0], swap(blocks[1], 1), swap(blocks[2], 2), swap(blocks[3], 3)]
+    def exchange(stacked):
+        return lax.all_to_all(stacked, "tensor", 0, 0)
 
     def sum_near(blocks, anchor):
         if not square:
@@ -795,6 +796,9 @@
         bias_row = up_bias[None, :]
 
         dp_side = lax.axis_index("dp") % 2
+        place = jnp.zeros((1,), jnp.int32)
+        if square:
+            place = place + lax.axis_index("tensor")
         fetch = fetch_half if square else gather_far
         weights_near = ()
         if square:
@@ -802,18 +806,20 @@
                 swap(value, 1) for value in (output_projection_weight, up_projection_weight, down_projection_weight)
             )
 
-        normed = [norm_item(patches, 0, gain_row, shift_row)]
-        normed_far = [gather_far(normed[0])]
+        def gather_rows(own):
+            return lax.all_gather(own, "tensor", axis=0, tiled=True)
+
+        normed = [norm_item(patches, i, gain_row, shift_row) for i in range(slot_count)]
+        every = gather_rows(normed[0])
         bias_far = gather_far(bias_row)
         qkvs, attended, lses, heads_own, normed_every = [], [], [], [], []
         for i in range(slot_count):
-            if i + 1 < slot_count:
-                if i == 0:
-                    normed += [norm_item(patches, k, gain_row, shift_row) for k in range(1, slot_count)]
-                    normed_far[0], normed[1] = tie(normed_far[0], normed[1])
-                normed_far.append(gather_far(normed[i + 1]))
-            every = jnp.concatenate(gather_near(normed[i], normed_far[i]), axis=0)
-            every = lax.optimization_barrier(every)
+            last = i == slot_count - 1
+            normed_every.append(every)
+            following = None
+            if not last:
+                every, following = tie(every, normed[i + 1])
+                following = gather_rows(following)
             qkv = (
                 jnp.einsum("wz,gzh->gwh", every, query_key_value_weight, preferred_element_type=f32) + proj_bias
             ).astype(bf16)
@@ -821,39 +827,45 @@
                 qkv, (up_own, weights_near, bias_far) = tie(qkv, (up_projection_weight, weights_near, bias_far))
                 up_far = fetch(up_own)
             out, lse = attend(qkv)
-            if i + 1 < slot_count:
-                out, (normed[i + 1], normed_far[i + 1]) = tie(out, (normed[i + 1], normed_far[i + 1]))
             if i == 0:
-                out, (down_own, out_own, up_far) = tie(out, (down_projection_weight, output_projection_weight, up_far))
+                out, (following, down_own, out_own, up_far) = tie(
+                    out, (following, down_projection_weight, output_projection_weight, up_far)
+                )
                 down_far = fetch(down_own)
                 out_far = gather_far(out_own)
                 if square:
                     up_rest = fetch_rest(up_far)
-            if i == min(1, slot_count - 1) and square:
-                out, (down_far, up_rest) = tie(out, (down_far, up_rest))
-                up_far = in_halves(up_far, up_rest, dp_side)
-                up_diag = swap(up_far, 1)
-                down_rest = fetch_rest(down_far)
-            if i == slot_count - 1:
-                out, out_far = tie(out, out_far)
+            elif not last:
+                out, (following, heads_own[-1], out_far, down_far) = tie(
+                    out, (following, heads_own[-1], out_far, down_far)
+                )
                 if square:
-                    out, (down_rest, up_diag) = tie(out, (down_rest, up_diag))
+                    out, up_rest = tie(out, up_rest)
+                    up_far = in_halves(up_far, up_rest, dp_side)
+                    up_diag = swap(up_far, 1)
+                    down_rest = fetch_rest(down_far)
+                    out_diag = swap(out_far, 1)
+            if last:
+                out, heads_own[-1] = tie(out, heads_own[-1])
+                if square:
+                    out, (down_rest, up_diag, out_diag) = tie(out, (down_rest, up_diag, out_diag))
                     down_far = in_halves(down_far, down_rest, dp_side)
                     down_diag = swap(down_far, 1)
-            heads_own.append(exchange_blocks([out[b * own_rows : (b + 1) * own_rows] for b in range(tensor_size)]))
-            normed_every.append(every)
+            heads_own.append(exchange(out.reshape(tensor_size, own_rows, width)))
             qkvs.append(qkv)
             attended.append(out)
             lses.append(lse)
+            every = following
         if square:
-            out_weight = jnp.concatenate([out_own, weights_near[0], out_far, swap(out_far, 1)], axis=0)
+            out_weight = jnp.concatenate([out_own, weights_near[0], out_far, out_diag], axis=0)
         else:
             out_weight = jnp.concatenate(gather_near(out_own, out_far), axis=0)
         rows_done = None
         for i in range(slot_count):
-            heads = heads_own[i] if square else [jnp.concatenate(heads_own[i], axis=1)]
+            if i == slot_count - 1:
+                rows_done, heads_own[i] = tie(rows_done, heads_own[i])
             rows_done = out_project(
-                patches, i, heads, out_weight, out_bias_row, mlp_gain_row, mlp_shift_row, rows_done
+                patches, i, place, heads_own[i], out_weight, out_bias_row, mlp_gain_row, mlp_shift_row, rows_done
             )
         attended_rows, residual, normed_mlp = rows_done
         cot_low = (cotangent.astype(f32).reshape(all_rows, model) * row_scale).astype(bf16)
@@ -888,22 +900,21 @@
             bias_grads.append(bias_grad)
             if c == 0:
                 down_stage, before = sum_near(down_grads, before)
-        down_sum, before = sum_far(down_stage, before)
         ring = ring_plan()
         pre_grad, total = before
 
         grad_low = None
         grad_residuals, grad_attended, sums = [], [], []
         for i in range(slot_count):
-            grad_residual, grad_low, item_sums, *pieces = residual_back(
-                total, residual, cotangent, own_scale, i, out_weight, mlp_gain_row, grad_low, tensor_size
+            grad_residual, grad_low, item_sums, pieces = residual_back(
+                total, residual, cotangent, own_scale, i, place, out_weight, mlp_gain_row, grad_low, tensor_size
             )
             grad_residuals.append(grad_residual)
             sums.append(item_sums[:4])
-            grad_attended.append(exchange_blocks(pieces))
+            grad_attended.append(exchange(pieces))
         weight_grads = weight_back(normed_mlp, pre_grad, attended_rows, grad_low, tensor_size)
-        weight_grads, grad_attended[0] = tie(weight_grads, grad_attended[0])
-        down_sum, weight_grads = ring_step(down_sum, ring.pop(0), weight_grads)
+        weight_grads, grad_attended[:2] = tie(weight_grads, grad_attended[:2])
+        down_sum, weight_grads = sum_far(down_stage, weight_grads)
         up_grads, out_grads = weight_grads[:tensor_size], weight_grads[tensor_size:]
 
         (up_stage, out_stage), grad_attended[0] = sums_near([up_grads, out_grads], grad_attended[0])
@@ -917,8 +928,8 @@
         grad_normed = []
         for i in range(slot_count):
             last = i == slot_count - 1
-            dqkv = attend_back(qkvs[i], attended[i], jnp.concatenate(grad_attended[i], axis=0), lses[i])
-            if not last:
+            dqkv = attend_back(qkvs[i], attended[i], grad_attended[i].reshape(-1, width), lses[i])
+            if 1 <= i < slot_count - 1:
                 dqkv, grad_attended[i + 1] = tie(dqkv, grad_attended[i + 1])
             if i >= 2:
                 grad_normed[i - 2], dqkv = terms_far(grad_normed[i - 2], dqkv)
@@ -930,16 +941,16 @@
                 up_all = lax.psum((up_sum, out_sum), "dp")
             if last:
                 dqkv, up_all = tie(dqkv, up_all)
-            if waiting:
+            if waiting and i > 0:
                 smalls, dqkv = sum_step(smalls, waiting.pop(0), dqkv)
             if ring:
                 down_sum, dqkv = ring_step(down_sum, ring.pop(0), dqkv)
-            results = project_back(normed_every[i], dqkv, query_key_value_weight, sums, last, tensor_size)
+            results = project_back(place, normed_every[i], dqkv, query_key_value_weight, sums, last, tensor_size)
             partial, sums = results[:tensor_size], results[tensor_size : tensor_size + 2]
-            while ring and (last or len(ring) % 2 == 0):
+            if waiting:
+                smalls, partial = sum_step(smalls, waiting.pop(0), partial)
+            if ring and not last:
                 down_sum, partial = ring_step(down_sum, ring.pop(0), partial)
-            while waiting and (last or len(waiting) % 2):
-                smalls, partial = sum_step(smalls, waiting.pop(0), partial)
             if last:
                 qkv_all = lax.psum(results[-1], "dp")
             grad_normed.append(partial)
@@ -954,6 +965,10 @@
             if i == slot_count - 1:
                 grad_residual, qkv_all = tie(grad_residual, qkv_all)
             grad_inputs = input_back(terms, patches, i, grad_residual, gain_row, grad_inputs)
+        for step in ring:
+            down_sum = ring_step(down_sum, step, place)[0]
+        for step in waiting:
+            smalls = sum_step(smalls, step, place)[0]
         weight_grad = qkv_all[:, :model].astype(f32)
         columns = qkv_all[:, model].astype(f32)
         raw = jnp.stack(

time: 882 us -> 834 us (0.946)
  waiting for transfers between devices: 222 us -> 177 us
  other arithmetic: 63.8 us -> 52.7 us
    ppermute x57 -> x30, waiting for transfers between devices: 173 us -> 72.1 us  [swap(): lax.ppermute(value, 'tensor', [(i, i ^ bits) for i in range(tensor_size)])]
    all_gather x0 -> x3, waiting for transfers between devices: none -> 36.1 us  [gather_rows(): return lax.all_gather(own, 'tensor', axis=0, tiled=True)]
    all_to_all x0 -> x6, starting transfers between devices: none -> 22.8 us  [exchange(): return lax.all_to_all(stacked, 'tensor', 0, 0)]
    ppermute x57 -> x30, starting transfers between devices: 36.1 us -> 15.6 us  [swap(): lax.ppermute(value, 'tensor', [(i, i ^ bits) for i in range(tensor_size)])]
    all_to_all x0 -> x6, waiting for transfers between devices: none -> 18.6 us  [exchange(): return lax.all_to_all(stacked, 'tensor', 0, 0)]
    concatenate x6 -> x0, other arithmetic: 12.6 us -> none  [the longest x3 6.53 us: shards(): jnp.concatenate(grad_attended[i], axis=0)]
  transfers between devices with their start and end apart: 74 -> 56, of which waited for: 19 -> 14; matrix products, arithmetic and copies ran while one was open for 10% -> 10% of each run, Pallas kernels for 47% -> 52%
where the time goes in v3:
time: 834 us; the launch traced here: 825 us
  Pallas kernels  465 us (56%)
  waiting for transfers between devices  177 us (21%)
  starting transfers between devices  56.9 us (7%)
  other arithmetic  52.7 us (6%)
  local copies, waits for them, and re-layouts  34.7 us (4%)
  matrix products  22.7 us (3%)
  between operations  15.6 us (2%)
    pallas_call x3, Pallas kernels, attend_back(): pl.pallas_call(body, grid=(pairs, kblocks), in_specs=[pl.BlockSpec((None,...  147 us
    pallas_call x3, Pallas kernels, attend(): pl.pallas_call(body, grid=(pairs, length // qblock), in_specs=[pl.BlockSp...  75.7 us
    ppermute x30, waiting for transfers between devices, swap(): lax.ppermute(value, 'tensor', [(i, i ^ bits) for i in range(tensor_size)])  72.1 us
    pallas_call x2, Pallas kernels, mlp_forward(): pl.pallas_call(body, grid=(steps,), in_specs=in_specs, out_specs=[slope_s...  71.7 us
    pallas_call x3, Pallas kernels, project_back(): pl.pallas_call(kernel, grid=(steps,), in_specs=in_specs, out_specs=out_sp...  43.7 us
    psum x1, waiting for transfers between devices, shards(): qkv_all = lax.psum(results[-1], 'dp')  43.6 us
    pallas_call x2, Pallas kernels, mlp_backward(): pl.pallas_call(body, grid=(rows // block,), in_specs=in_specs, out_specs=...  41.7 us
    all_gather x3, waiting for transfers between devices, gather_rows(): return lax.all_gather(own, 'tensor', axis=0, tiled=True)  36.1 us
  transfers between devices with their start and end apart: 56, of which 14 were waited for; matrix products, arithmetic and copies ran while one was open for 10% of the time, Pallas kernels for 52%

profile of v3, /device:TPU:0, one launch (start us, length us, event | category | flops | bytes accessed | tf_op | source)
XLA Modules:
  0.0 825.0 jit_solution(6712290378575492410)
XLA Ops:
  12.8 34.6 %all-gather.4.cloned.1.call-done.refs_1_ = bf16[2048,1024]{1,0:T(8,128)(2,1)} async-done(((bf16[512,1024]{1,0:T(8,128)(2,1)}), bf16[2048,1024]{1,0:T(8,128)(2,1)}) %all-gather.4.cloned.1.call-update) | async-done | bytes 4194320 | tf_op jit(solution)/shard_map/all_gather | solution.py:810
  48.7 7.4 fusion.9.q_ref.k_ref.v_ref
  61.5 25.2 %attend.3 = (bf16[2048,256]{1,0:T(8,128)(2,1)}, f32[2,2,2048]{2,1,0:T(2,128)}) custom-call(bf16[3,2048,256]{2,1,0:T(8,128)(2,1)} %fusion.9.q_ref.k_ref.v_ref, bf16[3,2048,256]{2,1,0:T(8,128)(2,1)} %fusion.9.q_ref.k_ref.v_ref, bf16[3,2048,256]{2,1,0:T(8,128)(2,1)} %fusion.9.q_ref.k_ref.v_ref), custom_call_target="tpu_custom_call" | custom-call | flops 134217728 | bytes 524288 | tf_op jit(solution)/shard_map/attend/pallas_call | solution.py:76
  86.7 18.0 %collective-permute-done.4 = bf16[512,1024]{1,0:T(8,128)(2,1)} collective-permute-done((bf16[512,1024]{1,0:T(8,128)(2,1)S(1)}, bf16[512,1024]{1,0:T(8,128)(2,1)}, u32[]{:S(2)}, u32[]{:S(2)}) %collective-permute-start.4) | collective-permute-done | bytes 1048608 | tf_op jit(solution)/shard_map/ppermute | solution.py:659
  115.9 8.0 fusion.10.q_ref.k_ref.v_ref
  123.9 25.2 %attend.4 = (bf16[2048,256]{1,0:T(8,128)(2,1)}, f32[2,2,2048]{2,1,0:T(2,128)}) custom-call(bf16[3,2048,256]{2,1,0:T(8,128)(2,1)} %fusion.10.q_ref.k_ref.v_ref, bf16[3,2048,256]{2,1,0:T(8,128)(2,1)} %fusion.10.q_ref.k_ref.v_ref, bf16[3,2048,256]{2,1,0:T(8,128)(2,1)} %fusion.10.q_ref.k_ref.v_ref), custom_call_target="tpu_custom_call" | custom-call | flops 134217728 | bytes 524288 | tf_op jit(solution)/shard_map/attend/pallas_call | solution.py:76
  153.0 26.0 %collective-permute-done.5 = bf16[256,1024]{1,0:T(8,128)(2,1)} collective-permute-done((bf16[256,1024]{1,0:T(8,128)(2,1)S(1)}, bf16[256,1024]{1,0:T(8,128)(2,1)}, u32[]{:S(2)}, u32[]{:S(2)}) %collective-permute-start.5) | collective-permute-done | bytes 524320 | tf_op jit(solution)/shard_map/ppermute | solution.py:659
  188.0 7.3 fusion.11.q_ref.k_ref.v_ref
  195.3 25.2 %attend.5 = (bf16[2048,256]{1,0:T(8,128)(2,1)}, f32[2,2,2048]{2,1,0:T(2,128)}) custom-call(bf16[3,2048,256]{2,1,0:T(8,128)(2,1)} %fusion.11.q_ref.k_ref.v_ref, bf16[3,2048,256]{2,1,0:T(8,128)(2,1)} %fusion.11.q_ref.k_ref.v_ref, bf16[3,2048,256]{2,1,0:T(8,128)(2,1)} %fusion.11.q_ref.k_ref.v_ref), custom_call_target="tpu_custom_call" | custom-call | flops 134217728 | bytes 524288 | tf_op jit(solution)/shard_map/attend/pallas_call | solution.py:76
  259.8 35.0 %mlp_forward.2 = (bf16[1536,2048]{1,0:T(8,128)(2,1)}, f32[1536,1024]{1,0:T(8,128)}, bf16[1024,1024]{1,0:T(8,128)(2,1)}, bf16[1024,1024]{1,0:T(8,128)(2,1)}) custom-call(bf16[1536,1024]{1,0:T(8,128)(2,1)} %get-tuple-element.244.refs_0_.x_ref, bf16[1536,1024]{1,0:T(8,128)(2,1)} %fusion.refs_1_.refs_0_, bf16[1024,1024]{1,0:T(8,128)(2,1)} %refs_2_.1, ...), custom_call_target="tpu_custom_call" | custom-call | flops 301989888 | bytes 1572864 | tf_op jit(solution)/shard_map/mlp_forward/pallas_call | solution.py:445
  295.4 36.7 %mlp_forward.3 = (bf16[1536,2048]{1,0:T(8,128)(2,1)}, f32[1536,1024]{1,0:T(8,128)}, bf16[1024,1024]{1,0:T(8,128)(2,1)}, bf16[1024,1024]{1,0:T(8,128)(2,1)}) custom-call(bf16[1536,1024]{1,0:T(8,128)(2,1)} %get-tuple-element.244.refs_0_.x_ref, bf16[1536,1024]{1,0:T(8,128)(2,1)} %fusion.refs_1_.refs_0_, ...), custom_call_target="tpu_custom_call", output_to_operand_aliasing={{1}: (8, {})} | custom-call | flops 301989888 | bytes 1572864 | tf_op jit(solution)/shard_map/mlp_forward/pallas_call | solution.py:445
  332.7 20.5 %mlp_backward.2 = (bf16[1536,4096]{1,0:T(8,128)(2,1)}, f32[1536,1024]{1,0:T(8,128)}, f32[1,2048]{1,0:T(1,128)}) custom-call(bf16[1536,1024]{1,0:T(8,128)(2,1)} %fusion.refs_1_.refs_0_, bf16[1536,2048]{1,0:T(8,128)(2,1)} %get-tuple-element.258.refs_1_, bf16[1024,1024]{1,0:T(8,128)(2,1)} %refs_2_.1, bf16[1024,1024]{1,0:T(8,128)(2,1)} %collective-permute-done.1.refs_3_, ...), custom_call_target="tpu_custom_call" | custom-call | flops 201326592 | bytes 1572864 | tf_op jit(solution)/shard_map/mlp_backward/pallas_call | solution.py:503
  358.8 21.1 %mlp_backward.3 = (bf16[1536,4096]{1,0:T(8,128)(2,1)}, f32[1536,1024]{1,0:T(8,128)}, f32[1,2048]{1,0:T(1,128)}) custom-call(bf16[1536,1024]{1,0:T(8,128)(2,1)} %fusion.refs_1_.refs_0_, bf16[1536,2048]{1,0:T(8,128)(2,1)} %get-tuple-element.257.refs_1_, ...), custom_call_target="tpu_custom_call", output_to_operand_aliasing={{0}: (6, {}), {1}: (7, {})} | custom-call | flops 201326592 | bytes 1572864 | tf_op jit(solution)/shard_map/mlp_backward/pallas_call | solution.py:503
  397.8 18.6 %all-to-all-done.3 = bf16[4,512,256]{2,1,0:T(8,128)(2,1)S(1)} async-done(((bf16[4,512,256]{2,1,0:T(8,128)(2,1)}), bf16[4,512,256]{2,1,0:T(8,128)(2,1)S(1)}, u32[]{:S(2)}, u32[]{:S(2)}) %all-to-all-start.3) | async-done | bytes 1048608 | tf_op jit(solution)/shard_map/all_to_all | solution.py:670
  427.1 26.6 %weight_back.1 = (bf16[1024,1024]{1,0:T(8,128)(2,1)}, bf16[1024,1024]{1,0:T(8,128)(2,1)}, bf16[1024,1024]{1,0:T(8,128)(2,1)}, bf16[1024,1024]{1,0:T(8,128)(2,1)}...) custom-call(bf16[1536,1024]{1,0:T(8,128)(2,1)} %get-tuple-element.24, ...), custom_call_target="tpu_custom_call" | custom-call | flops 251658240 | bytes 1572864 | tf_op jit(solution)/shard_map/weight_back/pallas_call | solution.py:558
  475.6 48.9 %attend_back.5.refs_2_ = bf16[3,2048,256]{2,1,0:T(8,128)(2,1)} custom-call(bf16[3,2048,256]{2,1,0:T(8,128)(2,1)} %fusion.9.q_ref.k_ref.v_ref, bf16[3,2048,256]{2,1,0:T(8,128)(2,1)} %fusion.9.q_ref.k_ref.v_ref, bf16[3,2048,256]{2,1,0:T(8,128)(2,1)} %fusion.9.q_ref.k_ref.v_ref, bf16[2048,256]{1,0:T(8,128)(2,1)} %get-tuple-element.218.out_ref, ...), custom_call_target="tpu_custom_call" | custom-call | flops 335544320 | bytes 524288 | tf_op jit(solution)/shard_map/attend_back/pallas_call | solution.py:168
  530.3 13.7 %project_back.3 = (bf16[512,1024]{1,0:T(8,128)(2,1)}, bf16[512,1024]{1,0:T(8,128)(2,1)}, bf16[512,1024]{1,0:T(8,128)(2,1)}, bf16[512,1024]{1,0:T(8,128)(2,1)}, f...) custom-call(s32[1]{0:T(128)} %bitcast.refs_0_, bf16[2048,1024]{1,0:T(8,128)(2,1)} %all-gather.4.cloned.1.call-done.refs_1_, ...), custom_call_target="tpu_custom_call" | custom-call | flops 100663296 | bytes 524288 | tf_op jit(solution)/shard_map/project_back/pallas_call | solution.py:638
  560.9 48.9 %attend_back.3.refs_2_ = bf16[3,2048,256]{2,1,0:T(8,128)(2,1)} custom-call(bf16[3,2048,256]{2,1,0:T(8,128)(2,1)} %fusion.10.q_ref.k_ref.v_ref, bf16[3,2048,256]{2,1,0:T(8,128)(2,1)} %fusion.10.q_ref.k_ref.v_ref, bf16[3,2048,256]{2,1,0:T(8,128)(2,1)} %fusion.10.q_ref.k_ref.v_ref, bf16[2048,256]{1,0:T(8,128)(2,1)} %get-tuple-element.225.out_ref, ...), custom_call_target="tpu_custom_call" | custom-call | flops 335544320 | bytes 524288 | tf_op jit(solution)/shard_map/attend_back/pallas_call | solution.py:168
  614.2 14.2 %project_back.4 = (bf16[512,1024]{1,0:T(8,128)(2,1)}, bf16[512,1024]{1,0:T(8,128)(2,1)}, bf16[512,1024]{1,0:T(8,128)(2,1)}, bf16[512,1024]{1,0:T(8,128)(2,1)}, f...) custom-call(s32[1]{0:T(128)} %bitcast.refs_0_, ...), custom_call_target="tpu_custom_call", output_to_operand_aliasing={{4}: (4, {}), {5}: (5, {})} | custom-call | flops 100663296 | bytes 524288 | tf_op jit(solution)/shard_map/project_back/pallas_call | solution.py:638
  631.1 7.3 multiply_convert_fusion
  638.4 49.1 %attend_back.4.refs_2_ = bf16[3,2048,256]{2,1,0:T(8,128)(2,1)} custom-call(bf16[3,2048,256]{2,1,0:T(8,128)(2,1)} %fusion.11.q_ref.k_ref.v_ref, bf16[3,2048,256]{2,1,0:T(8,128)(2,1)} %fusion.11.q_ref.k_ref.v_ref, bf16[3,2048,256]{2,1,0:T(8,128)(2,1)} %fusion.11.q_ref.k_ref.v_ref, bf16[2048,256]{1,0:T(8,128)(2,1)} %get-tuple-element.238.out_ref, ...), custom_call_target="tpu_custom_call" | custom-call | flops 335544320 | bytes 524288 | tf_op jit(solution)/shard_map/attend_back/pallas_call | solution.py:168
  695.6 15.8 %project_back.5 = (bf16[512,1024]{1,0:T(8,128)(2,1)}, bf16[512,1024]{1,0:T(8,128)(2,1)}, bf16[512,1024]{1,0:T(8,128)(2,1)}, bf16[512,1024]{1,0:T(8,128)(2,1)}, f...) custom-call(s32[1]{0:T(128)} %bitcast.refs_0_, ...), custom_call_target="tpu_custom_call", output_to_operand_aliasing={{4}: (4, {}), {5}: (5, {})} | custom-call | flops 100663296 | bytes 524288 | tf_op jit(solution)/shard_map/project_back/pallas_call | solution.py:638
  722.2 17.0 %collective-permute-done.41.refs_5_ = bf16[512,1024]{1,0:T(8,128)(2,1)S(1)} collective-permute-done((bf16[512,1024]{1,0:T(8,128)(2,1)S(1)}, bf16[512,1024]{1,0:T(8,128)(2,1)S(1)}, u32[]{:S(2)}, u32[]{:S(2)}) %collective-permute-start.41) | collective-permute-done | bytes 1048608 | tf_op jit(solution)/shard_map/ppermute | solution.py:659
  760.4 43.6 %all-reduce.4.cloned.1.call-done = bf16[3,1040,256]{2,1,0:T(8,128)(2,1)} async-done(((bf16[3,1040,256]{2,1,0:T(8,128)(2,1)}), bf16[3,1040,256]{2,1,0:T(8,128)(2,1)}) %all-reduce.4.cloned.1.call-update) | async-done | bytes 1597456 | tf_op jit(solution)/shard_map/psum | solution.py:955
  (300 shorter events, 215.3 us)
Async XLA Ops:
  9.9 96.3 %all-gather.6.cloned.1.call-start = ((), (), s32[]{:S(2)}) async-start(), calls=%async_computation.7 | async-start | bytes 5242880 | tf_op jit(solution)/shard_map/all_gather | solution.py:810
  47.4 131.7 %all-gather.8.cloned.1.call-start = ((), (), s32[]{:S(2)}) async-start(), calls=%async_computation.8 | async-start | bytes 5242880 | tf_op jit(solution)/shard_map/all_gather | solution.py:810
  108.5 70.6 %collective-permute-start.6 = (bf16[512,1024]{1,0:T(8,128)(2,1)}, bf16[512,1024]{1,0:T(8,128)(2,1)}, u32[]{:S(2)}, u32[]{:S(2)}) collective-permute-start(bf16[512,1024]{1,0:T(8,128)(2,1)} %constant_dynamic-slice_fusion.7), channel_id=1, source_target_pairs={{0,2},{1,3},{2,0},{3,1},{4,6},{5,7},{6,4},{7,5},{8,10},{9,11},{10,... | collective-permute-start | bytes 3145736 | tf_op jit(solution)/shard_map/ppermute | solution.py:659
  108.5 70.6 %collective-permute-start.7 = (bf16[512,1024]{1,0:T(8,128)(2,1)}, bf16[512,1024]{1,0:T(8,128)(2,1)}, u32[]{:S(2)}, u32[]{:S(2)}) collective-permute-start(bf16[512,1024]{1,0:T(8,128)(2,1)} %collective-permute-done.4), channel_id=1, source_target_pairs={{0,4},{4,0},{8,12},{12,8},{16,20},{20,16},{24,28},{28,24},{1,5},{5... | collective-permute-start | bytes 3145736 | tf_op jit(solution)/shard_map/ppermute | solution.py:746
  110.1 69.0 %all-to-all-start = ((bf16[4,512,256]{2,1,0:T(8,128)(2,1)}), bf16[4,512,256]{2,1,0:T(8,128)(2,1)S(1)}, u32[]{:S(2)}, u32[]{:S(2)}) async-start(bf16[4,512,256]{2,1,0:T(8,128)(2,1)} %bitcast.8), calls=%async_computation | async-start | bytes 2097152 | tf_op jit(solution)/shard_map/all_to_all | solution.py:670
  113.8 65.3 %collective-permute-start.5 = (bf16[256,1024]{1,0:T(8,128)(2,1)S(1)}, bf16[256,1024]{1,0:T(8,128)(2,1)}, u32[]{:S(2)}, u32[]{:S(2)}) collective-permute-start(bf16[256,1024]{1,0:T(8,128)(2,1)S(1)} %copy-done.20), channel_id=1, source_target_pairs={{0,2},{1,3},{2,0},{3,1},{4,6},{5,7},{6,4},{7,5},{8,10},{9,11},{10,... | collective-permute-start | bytes 1572872 | tf_op jit(solution)/shard_map/ppermute | solution.py:659
  183.3 75.8 %collective-permute-start.13 = (f32[1,1024]{1,0:T(1,128)S(1)}, f32[1,1024]{1,0:T(1,128)S(1)}, u32[]{:S(2)}, u32[]{:S(2)}) collective-permute-start(f32[1,1024]{1,0:T(1,128)S(1)} %bitcast.101), channel_id=1, source_target_pairs={{0,1},{1,0},{2,3},{3,2},{4,5},{5,4},{6,7},{7,6},{8,9},{9,8},{10,11... | collective-permute-start | bytes 12296 | tf_op jit(solution)/shard_map/ppermute | solution.py:659
  228.0 66.9 %collective-permute-start.12 = (bf16[1024,1024]{1,0:T(8,128)(2,1)}, bf16[1024,1024]{1,0:T(8,128)(2,1)}, u32[]{:S(2)}, u32[]{:S(2)}) collective-permute-start(bf16[1024,1024]{1,0:T(8,128)(2,1)} %constant_dynamic-update-slice_fusion.12.refs_6_.refs_4_), channel_id=1, source_target_pairs={{0,1},{1,0},{2,3},{3,2},{4,5},{5,4},{6,7},{7,6},{8,9},{9,8},{10,11... | collective-permute-start | bytes 6291464 | tf_op jit(solution)/shard_map/ppermute | solution.py:659
  237.8 57.0 %collective-permute-start.11 = (f32[1,1024]{1,0:T(1,128)S(1)}, f32[1,1024]{1,0:T(1,128)S(1)}, u32[]{:S(2)}, u32[]{:S(2)}) collective-permute-start(f32[1,1024]{1,0:T(1,128)S(1)} %collective-permute-done.3.refs_4_), channel_id=1, source_target_pairs={{0,1},{1,0},{2,3},{3,2},{4,5},{5,4},{6,7},{7,6},{8,9},{9,8},{10,11... | collective-permute-start | bytes 12296 | tf_op jit(solution)/shard_map/ppermute | solution.py:659
  357.1 96.6 %collective-permute-start.16 = (bf16[1024,1024]{1,0:T(8,128)(2,1)}, bf16[1024,1024]{1,0:T(8,128)(2,1)}, u32[]{:S(2)}, u32[]{:S(2)}) collective-permute-start(bf16[1024,1024]{1,0:T(8,128)(2,1)} %add_convert_fusion.6), channel_id=1, source_target_pairs={{0,2},{1,3},{2,0},{3,1},{4,6},{5,7},{6,4},{7,5},{8,10},{9,11},{10,... | collective-permute-start | bytes 6291464 | tf_op jit(solution)/shard_map/ppermute | solution.py:659
  419.9 267.7 %all-reduce.6.cloned.1.call-start = ((), (), s32[]{:S(2)}) async-start(), calls=%async_computation.10 | async-start | bytes 5242880 | tf_op jit(solution)/shard_map/psum | solution.py:941
  466.8 57.8 %collective-permute-start.21 = (bf16[1024,1024]{1,0:T(8,128)(2,1)}, bf16[1024,1024]{1,0:T(8,128)(2,1)}, u32[]{:S(2)}, u32[]{:S(2)}) collective-permute-start(bf16[1024,1024]{1,0:T(8,128)(2,1)} %add_convert_fusion.5), channel_id=1, source_target_pairs={{0,2},{1,3},{2,0},{3,1},{4,6},{5,7},{6,4},{7,5},{8,10},{9,11},{10,... | collective-permute-start | bytes 6291464 | tf_op jit(solution)/shard_map/ppermute | solution.py:659
  472.6 53.7 %collective-permute-start.23 = (bf16[512,1024]{1,0:T(8,128)(2,1)S(1)}, bf16[512,1024]{1,0:T(8,128)(2,1)}, u32[]{:S(2)}, u32[]{:S(2)}) collective-permute-start(bf16[512,1024]{1,0:T(8,128)(2,1)S(1)} %constant_dynamic-slice_fusion.6), channel_id=1, source_target_pairs={{0,4},{4,0},{8,12},{12,8},{16,20},{20,16},{24,28},{28,24},{1,5},{5... | collective-permute-start | bytes 3145736 | tf_op jit(solution)/shard_map/ppermute | solution.py:728
  549.2 60.7 %collective-permute-start.26 = (bf16[512,1024]{1,0:T(8,128)(2,1)}, bf16[512,1024]{1,0:T(8,128)(2,1)}, u32[]{:S(2)}, u32[]{:S(2)}) collective-permute-start(bf16[512,1024]{1,0:T(8,128)(2,1)} %get-tuple-element.330), channel_id=1, source_target_pairs={{0,1},{1,0},{2,3},{3,2},{4,5},{5,4},{6,7},{7,6},{8,9},{9,8},{10,11... | collective-permute-start | bytes 3145736 | tf_op jit(solution)/shard_map/ppermute | solution.py:659
  549.5 60.3 %collective-permute-start.27 = (bf16[512,1024]{1,0:T(8,128)(2,1)}, bf16[512,1024]{1,0:T(8,128)(2,1)}, u32[]{:S(2)}, u32[]{:S(2)}) collective-permute-start(bf16[512,1024]{1,0:T(8,128)(2,1)} %get-tuple-element.331), channel_id=1, source_target_pairs={{0,1},{1,0},{2,3},{3,2},{4,5},{5,4},{6,7},{7,6},{8,9},{9,8},{10,11... | collective-permute-start | bytes 3145736 | tf_op jit(solution)/shard_map/ppermute | solution.py:659
  551.8 58.0 %all-to-all-start.5 = ((bf16[4,512,256]{2,1,0:T(8,128)(2,1)}), bf16[4,512,256]{2,1,0:T(8,128)(2,1)S(1)}, u32[]{:S(2)}, u32[]{:S(2)}) async-start(bf16[4,512,256]{2,1,0:T(8,128)(2,1)} %get-tuple-element.284), calls=%async_computation.5 | async-start | bytes 2097152 | tf_op jit(solution)/shard_map/all_to_all | solution.py:670
  555.3 248.6 %all-reduce.4.cloned.1.call-start = ((), (), s32[]{:S(2)}) async-start(), calls=%async_computation.9 | async-start | bytes 3194880 | tf_op jit(solution)/shard_map/psum | solution.py:955
  555.7 54.2 %collective-permute-start.30 = (bf16[128,1024]{1,0:T(8,128)(2,1)S(1)}, bf16[128,1024]{1,0:T(8,128)(2,1)S(1)}, u32[]{:S(2)}, u32[]{:S(2)}) collective-permute-start(bf16[128,1024]{1,0:T(8,128)(2,1)S(1)} %constant_dynamic-slice_fusion), channel_id=1, source_target_pairs={{0,16},{4,20},{8,24},{12,28},{16,0},{20,4},{24,8},{28,12},{1,17},{... | collective-permute-start | bytes 786440 | tf_op jit(solution)/shard_map/ppermute | solution.py:728
  558.2 51.7 %collective-permute-start.29 = (f32[64,128]{1,0:T(8,128)S(1)}, f32[64,128]{1,0:T(8,128)S(1)}, u32[]{:S(2)}, u32[]{:S(2)}) collective-permute-start(f32[64,128]{1,0:T(8,128)S(1)} %add.234), channel_id=1, source_target_pairs={{0,2},{1,3},{2,0},{3,1},{4,6},{5,7},{6,4},{7,5},{8,10},{9,11},{10,... | collective-permute-start | bytes 98312 | tf_op jit(solution)/shard_map/ppermute | solution.py:714
  614.1 73.4 %collective-permute-start.28 = (bf16[512,1024]{1,0:T(8,128)(2,1)}, bf16[512,1024]{1,0:T(8,128)(2,1)}, u32[]{:S(2)}, u32[]{:S(2)}) collective-permute-start(bf16[512,1024]{1,0:T(8,128)(2,1)} %add_convert_fusion.9), channel_id=1, source_target_pairs={{0,2},{1,3},{2,0},{3,1},{4,6},{5,7},{6,4},{7,5},{8,10},{9,11},{10,... | collective-permute-start | bytes 3145736 | tf_op jit(solution)/shard_map/ppermute | solution.py:659
  628.4 59.2 %collective-permute-start.35 = (f32[64,128]{1,0:T(8,128)S(1)}, f32[64,128]{1,0:T(8,128)S(1)}, u32[]{:S(2)}, u32[]{:S(2)}) collective-permute-start(f32[64,128]{1,0:T(8,128)S(1)} %add.246), channel_id=1, source_target_pairs={{0,8},{4,12},{8,0},{12,4},{16,24},{20,28},{24,16},{28,20},{1,9},{5... | collective-permute-start | bytes 98312 | tf_op jit(solution)/shard_map/ppermute | solution.py:714
  629.1 58.4 %collective-permute-start.33 = (bf16[512,1024]{1,0:T(8,128)(2,1)}, bf16[512,1024]{1,0:T(8,128)(2,1)}, u32[]{:S(2)}, u32[]{:S(2)}) collective-permute-start(bf16[512,1024]{1,0:T(8,128)(2,1)} %get-tuple-element.351), channel_id=1, source_target_pairs={{0,1},{1,0},{2,3},{3,2},{4,5},{5,4},{6,7},{7,6},{8,9},{9,8},{10,11... | collective-permute-start | bytes 3145736 | tf_op jit(solution)/shard_map/ppermute | solution.py:659
  629.1 58.4 %collective-permute-start.34 = (bf16[512,1024]{1,0:T(8,128)(2,1)}, bf16[512,1024]{1,0:T(8,128)(2,1)S(1)}, u32[]{:S(2)}, u32[]{:S(2)}) collective-permute-start(bf16[512,1024]{1,0:T(8,128)(2,1)} %get-tuple-element.352), channel_id=1, source_target_pairs={{0,1},{1,0},{2,3},{3,2},{4,5},{5,4},{6,7},{7,6},{8,9},{9,8},{10,11... | collective-permute-start | bytes 3145736 | tf_op jit(solution)/shard_map/ppermute | solution.py:659
  629.6 65.2 %collective-permute-start.36 = (bf16[256,1024]{1,0:T(8,128)(2,1)S(1)}, bf16[256,1024]{1,0:T(8,128)(2,1)S(1)}, u32[]{:S(2)}, u32[]{:S(2)}) collective-permute-start(bf16[256,1024]{1,0:T(8,128)(2,1)S(1)} %constant_dynamic-update-slice_fusion.10), channel_id=1, source_target_pairs={{0,8},{4,12},{8,0},{12,4},{16,24},{20,28},{24,16},{28,20},{1,9},{5... | collective-permute-start | bytes 1572872 | tf_op jit(solution)/shard_map/ppermute | solution.py:731
  (78 other events, 1338.4 us)
Sparse Core Ops, SparseCore 0:
  10.1 37.1 all-gather.3
  49.5 56.6 all-gather.5
  108.3 57.1 all-gather.7
  551.9 135.6 all-reduce.5
  711.6 92.3 all-reduce.3

commit v4 on v3

--- a/solution.py
+++ b/solution.py
@@ -99,9 +99,10 @@
     )(qkv, qkv, qkv)
 
 
-def attend_back(qkv, attended, grad_attended, lse):
+def attend_back(qkv, attended, grad_attended, item, lse):
     _, length, width = qkv.shape
     lanes = min(128, width)
+    shards_of = grad_attended.shape[0]
     heads = lanes // HD
     kblock = largest_block(length, 512)
     kblocks = length // kblock
@@ -110,7 +111,7 @@
     def body(q_ref, k_ref, v_ref, out_ref, grad_ref, lse_ref, dqkv_ref, dq_acc, row_dot):
         kb = pl.program_id(1)
         queries = q_ref[...]
-        grads = grad_ref[...]
+        grads = grad_ref[...].reshape(length, lanes)
         keys = k_ref[...]
         values = v_ref[...]
         keys_t = keys.T
@@ -173,7 +174,7 @@
             pl.BlockSpec((None, kblock, lanes), lambda h, kb: (1, kb, h)),
             pl.BlockSpec((None, kblock, lanes), lambda h, kb: (2, kb, h)),
             pl.BlockSpec((length, lanes), lambda h, kb: (0, h)),
-            pl.BlockSpec((length, lanes), lambda h, kb: (0, h)),
+            pl.BlockSpec((shards_of, length // shards_of, lanes), lambda h, kb: (0, item, h)),
             pl.BlockSpec((None, heads, length), lambda h, kb: (h, 0, 0)),
         ],
         out_specs=pl.BlockSpec((3, length, lanes), lambda h, kb: (0, 0, h)),
@@ -263,7 +264,7 @@
     )(*operands)
 
 
-def residual_back(total, residual, cotangent, scale, item, place, weight, norm_gain, low_before, pieces):
+def residual_back(total, residual, cotangent, scale, place, weight, norm_gain, pieces):
     slots, rows, model = cotangent.shape
     block = largest_block(rows, 256)
     steps = rows // block
@@ -280,7 +281,7 @@
         scaled = grad_normed * gain_ref[...]
         inner = jnp.mean(scaled, axis=-1, keepdims=True)
         outer = jnp.mean(scaled * xhat, axis=-1, keepdims=True)
-        cot = cot_ref[...].astype(f32) * scale_ref[item]
+        cot = cot_ref[...].astype(f32) * scale_ref[pl.program_id(0) // steps]
         grad = cot + rate * (scaled - inner - xhat * outer)
         grad_ref[...] = grad
         low = grad.astype(bf16)
@@ -297,43 +298,34 @@
             attended_ref[place_ref[0] ^ k] = attended[:, k * piece : (k + 1) * piece]
 
     row_spec = pl.BlockSpec((block, model), lambda i: (i, 0))
-    placed = pl.BlockSpec((block, model), lambda i: (item * steps + i, 0))
-    operands = [place, total, residual, cotangent, scale, weight, norm_gain]
-    in_specs = [
-        pl.BlockSpec(memory_space=pltpu.SMEM),
-        placed,
-        placed,
-        pl.BlockSpec((None, block, model), lambda i: (item, i, 0)),
-        pl.BlockSpec(memory_space=pltpu.SMEM),
-        pl.BlockSpec((model, model), lambda i: (0, 0)),
-        pl.BlockSpec((1, model), lambda i: (0, 0)),
-    ]
-    aliases = {}
-    if low_before is not None:
-        aliases = {7: 1}
-        operands.append(low_before)
-        in_specs.append(pl.BlockSpec(memory_space=pl.ANY))
     return pl.pallas_call(
         body,
-        grid=(steps,),
-        in_specs=in_specs,
+        grid=(slots * steps,),
+        in_specs=[
+            pl.BlockSpec(memory_space=pltpu.SMEM),
+            row_spec,
+            row_spec,
+            pl.BlockSpec((None, block, model), lambda i: (i // steps, i % steps, 0)),
+            pl.BlockSpec(memory_space=pltpu.SMEM),
+            pl.BlockSpec((model, model), lambda i: (0, 0)),
+            pl.BlockSpec((1, model), lambda i: (0, 0)),
+        ],
         out_specs=[
             row_spec,
-            placed,
+            row_spec,
             pl.BlockSpec((8, model), lambda i: (0, 0)),
             pl.BlockSpec((pieces, block, piece), lambda i: (0, i, 0)),
         ],
         out_shape=[
-            jax.ShapeDtypeStruct((rows, model), f32),
+            jax.ShapeDtypeStruct((slots * rows, model), f32),
             jax.ShapeDtypeStruct((slots * rows, model), bf16),
             jax.ShapeDtypeStruct((8, model), f32),
-            jax.ShapeDtypeStruct((pieces, rows, piece), bf16),
+            jax.ShapeDtypeStruct((pieces, slots * rows, piece), bf16),
         ],
-        input_output_aliases=aliases,
         compiler_params=params(),
-        cost_estimate=hint(2 * rows * model * model, rows * model),
+        cost_estimate=hint(2 * slots * rows * model * model, rows * model),
         name="residual_back",
-    )(*operands)
+    )(place, total, residual, cotangent, scale, weight, norm_gain)
 
 
 def input_back(terms, patches, item, grad_residual, norm_gain, before):
@@ -359,7 +351,9 @@
     row_spec = pl.BlockSpec((block, model), lambda i: (i, 0))
     placed = pl.BlockSpec((None, block, model), lambda i: (item, i, 0))
     operands = [patches, grad_residual, norm_gain, *terms]
-    in_specs = [placed, row_spec, pl.BlockSpec((1, model), lambda i: (0, 0))] + [row_spec] * count
+    steps = rows // block
+    grad_spec = pl.BlockSpec((block, model), lambda i: (item * steps + i, 0))
+    in_specs = [placed, grad_spec, pl.BlockSpec((1, model), lambda i: (0, 0))] + [row_spec] * count
     aliases = {}
     if before is not None:
         aliases = {len(operands): 0}
@@ -460,8 +454,32 @@
     )(*operands)
 
 
+def cot_back(cot, downs):
+    rows, model = cot.shape
+    count = len(downs)
+    units = downs[0].shape[0]
+    block = largest_block(rows, 512)
+
+    def body(cot_ref, *refs):
+        for k in range(count):
+            refs[count][:, k * units : (k + 1) * units] = nt(cot_ref[...], refs[k][...]).astype(bf16)
+
+    return pl.pallas_call(
+        body,
+        grid=(rows // block,),
+        in_specs=[pl.BlockSpec((block, model), lambda i: (i, 0))]
+        + [pl.BlockSpec((units, model), lambda i: (0, 0))] * count,
+        out_specs=pl.BlockSpec((block, count * units), lambda i: (i, 0)),
+        out_shape=jax.ShapeDtypeStruct((rows, count * units), bf16),
+        compiler_params=params(),
+        cost_estimate=hint(2 * rows * model * units * count, rows * units),
+        name="cot_back",
+    )(cot, *downs)
+
+
 def mlp_backward(cot, slope, ups, downs, before, index, calls):
-    rows, model = cot.shape
+    rows, _ = cot.shape
+    model = ups[0].shape[0]
     count = len(ups)
     units = ups[0].shape[1]
     block = largest_block(rows, 512)
@@ -469,20 +487,24 @@
 
     def body(*refs):
         cot_ref, slope_ref = refs[:2]
-        up_refs, down_refs = refs[2 : 2 + count], refs[2 + count : 2 + 2 * count]
+        up_refs, down_refs = refs[2 : 2 + count], refs[2 + count : 2 + count + len(downs)]
         grad_ref, sum_ref, bias_ref = refs[-3:]
 
         @pl.when(pl.program_id(0) == 0)
         def _():
             bias_ref[...] = jnp.zeros_like(bias_ref)
 
-        out = None if first else refs[3 + 2 * count][...]
+        out = None if first else refs[3 + count + len(downs)][...]
         part = largest_block(units, 512)
         for k in range(count):
             for j in range(units // part):
                 rows_of = slice(j * part, (j + 1) * part)
                 wide = slice(k * units + j * part, k * units + (j + 1) * part)
-                low = (nt(cot_ref[...], down_refs[k][rows_of, :]) * slope_ref[:, wide].astype(f32)).astype(bf16)
+                if downs:
+                    product = nt(cot_ref[...], down_refs[k][rows_of, :])
+                else:
+                    product = cot_ref[:, wide].astype(f32)
+                low = (product * slope_ref[:, wide].astype(f32)).astype(bf16)
                 grad_ref[:, wide] = low
                 bias_ref[:, wide] += jnp.sum(low.astype(f32), axis=0, keepdims=True)
             product = nt(grad_ref[:, k * units : (k + 1) * units], up_refs[k][...])
@@ -494,7 +516,7 @@
     up_spec = pl.BlockSpec((model, units), lambda i: (0, 0), pipeline_mode=pl.Buffered(1))
     down_spec = pl.BlockSpec((units, model), lambda i: (0, 0), pipeline_mode=pl.Buffered(1))
     operands = [cot, slope, *ups, *downs]
-    in_specs = [row_spec, slope_spec] + [up_spec] * count + [down_spec] * count
+    in_specs = [row_spec if downs else slope_spec, slope_spec] + [up_spec] * count + [down_spec] * len(downs)
     aliases = {}
     if not first:
         aliases = {len(operands): 0, len(operands) + 1: 1}
@@ -708,7 +730,6 @@
         while bit < size:
             steps.append((axis, [(i, i ^ bit) for i in range(size)]))
             bit *= 2
-    tensor_steps = [step for step in steps if step[0] == "tensor"]
 
     def sum_step(value, step, anchor):
         anchor, received = tie(anchor, lax.ppermute(value, step[0], step[1]))
@@ -812,6 +833,11 @@
         normed = [norm_item(patches, i, gain_row, shift_row) for i in range(slot_count)]
         every = gather_rows(normed[0])
         bias_far = gather_far(bias_row)
+        cot_low = (cotangent.astype(f32).reshape(all_rows, model) * row_scale).astype(bf16)
+        early = None
+        if square:
+            early = cot_back(cot_low, [down_projection_weight, weights_near[2]])
+            every, early = tie(every, early)
         qkvs, attended, lses, heads_own, normed_every = [], [], [], [], []
         for i in range(slot_count):
             last = i == slot_count - 1
@@ -824,40 +850,30 @@
                 jnp.einsum("wz,gzh->gwh", every, query_key_value_weight, preferred_element_type=f32) + proj_bias
             ).astype(bf16)
             if i == 0:
-                qkv, (up_own, weights_near, bias_far) = tie(qkv, (up_projection_weight, weights_near, bias_far))
+                qkv, (weights_near, bias_far) = tie(qkv, (weights_near, bias_far))
+            out, lse = attend(qkv)
+            if not last:
+                out, following = tie(out, following)
+            if i == 0:
+                out, (up_own, down_own, out_own) = tie(
+                    out, (up_projection_weight, down_projection_weight, output_projection_weight)
+                )
+                out_far = gather_far(out_own)
                 up_far = fetch(up_own)
-            out, lse = attend(qkv)
-            if i == 0:
-                out, (following, down_own, out_own, up_far) = tie(
-                    out, (following, down_projection_weight, output_projection_weight, up_far)
-                )
                 down_far = fetch(down_own)
-                out_far = gather_far(out_own)
-                if square:
-                    up_rest = fetch_rest(up_far)
-            elif not last:
-                out, (following, heads_own[-1], out_far, down_far) = tie(
-                    out, (following, heads_own[-1], out_far, down_far)
-                )
-                if square:
-                    out, up_rest = tie(out, up_rest)
-                    up_far = in_halves(up_far, up_rest, dp_side)
-                    up_diag = swap(up_far, 1)
-                    down_rest = fetch_rest(down_far)
-                    out_diag = swap(out_far, 1)
+            else:
+                out, heads_own[-1] = tie(out, heads_own[-1])
             if last:
-                out, heads_own[-1] = tie(out, heads_own[-1])
-                if square:
-                    out, (down_rest, up_diag, out_diag) = tie(out, (down_rest, up_diag, out_diag))
-                    down_far = in_halves(down_far, down_rest, dp_side)
-                    down_diag = swap(down_far, 1)
+                out, (out_far, up_far, down_far) = tie(out, (out_far, up_far, down_far))
             heads_own.append(exchange(out.reshape(tensor_size, own_rows, width)))
             qkvs.append(qkv)
             attended.append(out)
             lses.append(lse)
             every = following
         if square:
-            out_weight = jnp.concatenate([out_own, weights_near[0], out_far, out_diag], axis=0)
+            up_rest = fetch_rest(up_far)
+            down_rest = fetch_rest(down_far)
+            out_weight = jnp.concatenate([out_own, weights_near[0], out_far, swap(out_far, 1)], axis=0)
         else:
             out_weight = jnp.concatenate(gather_near(out_own, out_far), axis=0)
         rows_done = None
@@ -867,13 +883,18 @@
             rows_done = out_project(
                 patches, i, place, heads_own[i], out_weight, out_bias_row, mlp_gain_row, mlp_shift_row, rows_done
             )
+        if square:
+            rows_done, (up_rest, down_rest) = tie(rows_done, (up_rest, down_rest))
+            up_far = in_halves(up_far, up_rest, dp_side)
+            down_far = in_halves(down_far, down_rest, dp_side)
+            up_diag = swap(up_far, 1)
+            down_diag = swap(down_far, 1)
         attended_rows, residual, normed_mlp = rows_done
-        cot_low = (cotangent.astype(f32).reshape(all_rows, model) * row_scale).astype(bf16)
 
         bias_blocks = gather_near(bias_row, bias_far)
         if square:
-            up_blocks = [up_own, weights_near[1], up_far, up_diag]
-            down_blocks = [down_own, weights_near[2], down_far, down_diag]
+            up_blocks = [up_own, weights_near[1]]
+            down_blocks = [down_own, weights_near[2]]
         else:
             up_blocks = gather_near(up_own, up_far)
             down_blocks = gather_near(down_own, down_far)
@@ -882,6 +903,10 @@
         slopes, down_grads = [], []
         for c in range(calls):
             pair = slice(2 * c, 2 * c + 2)
+            if c == 1 and square:
+                total, moved = tie(total, (up_far, up_diag, down_far, down_diag))
+                up_blocks += moved[:2]
+                down_blocks += moved[2:]
             slope, total, *grads = mlp_forward(
                 normed_mlp, cot_low, up_blocks[pair], bias_blocks[pair], down_blocks[pair], total
             )
@@ -889,38 +914,35 @@
             down_grads += grads
         output = ((residual + total + down_bias) * row_valid).astype(bf16)
 
-        cot_back, down_grads = tie(cot_low, down_grads)
+        cot_late, down_grads = tie(cot_low, down_grads)
         before = None
         bias_grads = []
         for c in range(calls):
             pair = slice(2 * c, 2 * c + 2)
-            *before, bias_grad = mlp_backward(
-                cot_back, slopes[c], up_blocks[pair], down_blocks[pair], before, c, calls
-            )
+            if c == 0 and square:
+                *before, bias_grad = mlp_backward(early, slopes[c], up_blocks[pair], [], before, c, calls)
+            else:
+                *before, bias_grad = mlp_backward(
+                    cot_late, slopes[c], up_blocks[pair], down_blocks[pair], before, c, calls
+                )
             bias_grads.append(bias_grad)
             if c == 0:
                 down_stage, before = sum_near(down_grads, before)
         ring = ring_plan()
         pre_grad, total = before
 
-        grad_low = None
-        grad_residuals, grad_attended, sums = [], [], []
-        for i in range(slot_count):
-            grad_residual, grad_low, item_sums, pieces = residual_back(
-                total, residual, cotangent, own_scale, i, place, out_weight, mlp_gain_row, grad_low, tensor_size
-            )
-            grad_residuals.append(grad_residual)
-            sums.append(item_sums[:4])
-            grad_attended.append(exchange(pieces))
+        grad_residual, grad_low, small_rows, pieces = residual_back(
+            total, residual, cotangent, own_scale, place, out_weight, mlp_gain_row, tensor_size
+        )
+        down_sum, pieces = sum_far(down_stage, pieces)
+        grad_attended = exchange(pieces)
         weight_grads = weight_back(normed_mlp, pre_grad, attended_rows, grad_low, tensor_size)
-        weight_grads, grad_attended[:2] = tie(weight_grads, grad_attended[:2])
-        down_sum, weight_grads = sum_far(down_stage, weight_grads)
+        weight_grads, grad_attended = tie(weight_grads, grad_attended)
         up_grads, out_grads = weight_grads[:tensor_size], weight_grads[tensor_size:]
 
-        (up_stage, out_stage), grad_attended[0] = sums_near([up_grads, out_grads], grad_attended[0])
-        small_rows = sum(sums[1:], sums[0])
+        (up_stage, out_stage), grad_attended = sums_near([up_grads, out_grads], grad_attended)
         bias_rows = in_order(jnp.concatenate(bias_grads, axis=1).reshape(tensor_size, -1))
-        smalls = jnp.concatenate([small_rows.reshape(-1), bias_rows.reshape(-1)]).reshape(-1, 128)
+        smalls = jnp.concatenate([small_rows[:4].reshape(-1), bias_rows.reshape(-1)]).reshape(-1, 128)
         waiting = list(steps)
 
         weights_wide = query_key_value_weight.astype(f32)
@@ -928,9 +950,7 @@
         grad_normed = []
         for i in range(slot_count):
             last = i == slot_count - 1
-            dqkv = attend_back(qkvs[i], attended[i], grad_attended[i].reshape(-1, width), lses[i])
-            if 1 <= i < slot_count - 1:
-                dqkv, grad_attended[i + 1] = tie(dqkv, grad_attended[i + 1])
+            dqkv = attend_back(qkvs[i], attended[i], grad_attended, i, lses[i])
             if i >= 2:
                 grad_normed[i - 2], dqkv = terms_far(grad_normed[i - 2], dqkv)
             if i >= 1:
@@ -952,11 +972,19 @@
             if ring and not last:
                 down_sum, partial = ring_step(down_sum, ring.pop(0), partial)
             if last:
-                qkv_all = lax.psum(results[-1], "dp")
+                grad_residual, qkv_low = tie(grad_residual, results[-1])
+                qkv_all = lax.psum(qkv_low, "dp")
+                raw = jnp.stack(
+                    [
+                        jnp.sum(sums[0] * weights_wide, axis=(0, 2)),
+                        jnp.sum(sums[1][:3, None, :] * weights_wide, axis=(0, 2)),
+                    ]
+                )
+                for step in steps:
+                    raw = raw + lax.ppermute(raw, step[0], step[1])
             grad_normed.append(partial)
         grad_inputs = None
         for i in range(slot_count):
-            grad_residual = grad_residuals[i]
             if i == slot_count - 1:
                 grad_normed[i], grad_residual = sum_near(grad_normed[i], grad_residual)
             terms = grad_normed[i]
@@ -971,14 +999,6 @@
             smalls = sum_step(smalls, step, place)[0]
         weight_grad = qkv_all[:, :model].astype(f32)
         columns = qkv_all[:, model].astype(f32)
-        raw = jnp.stack(
-            [
-                jnp.sum(weight_grad * weights_wide, axis=(0, 2)),
-                jnp.sum(columns[:, None, :] * weights_wide, axis=(0, 2)),
-            ]
-        )
-        for step in tensor_steps:
-            raw = raw + lax.ppermute(raw, step[0], step[1])
         up_all, out_all = [value.astype(f32) for value in up_all]
         down_all = down_sum.astype(f32)
         inverse = 1.0 / total_items

time: 834 us -> 797 us (0.956)
  waiting for transfers between devices: 177 us -> 153 us
    ppermute x30, waiting for transfers between devices: 72.1 us -> 33.7 us  [swap(): lax.ppermute(value, 'tensor', [(i, i ^ bits) for i in range(tensor_size)])]
    ppermute x2 -> x5, waiting for transfers between devices: 1.12 us -> 24.4 us  [shards(): raw = raw + lax.ppermute(raw, step[0], step[1])]
    psum x1, waiting for transfers between devices: 43.6 us -> 23.3 us  [shards(): qkv_all = lax.psum(qkv_low, 'dp')]
    ppermute x2, waiting for transfers between devices: 0.01 us -> 17.2 us  [fetch_rest(): return lax.ppermute(half, 'dp', [(i, i ^ 1) for i in range(group_size)])]
    all_to_all x6 -> x4, starting transfers between devices: 22.8 us -> 15.8 us  [exchange(): return lax.all_to_all(stacked, 'tensor', 0, 0)]
    pallas_call x3 -> x2, Pallas kernels: 21.3 us -> 26.7 us  [the longest x1 14.9 us: residual_back(): pl.pallas_call(body, grid=(slots * steps,), in_specs=[pl.BlockSpec(memory...]
    all_to_all x6 -> x4, waiting for transfers between devices: 18.6 us -> 22 us  [exchange(): return lax.all_to_all(stacked, 'tensor', 0, 0)]
  transfers between devices with their start and end apart: 56 -> 57, of which waited for: 14 -> 17; matrix products, arithmetic and copies ran while one was open for 10% -> 10% of each run, Pallas kernels for 52% -> 51%
where the time goes in v4:
time: 797 us; the launch traced here: 792 us
  Pallas kernels  465 us (58%)
  waiting for transfers between devices  153 us (19%)
  other arithmetic  56.5 us (7%)
  starting transfers between devices  52.9 us (7%)
  local copies, waits for them, and re-layouts  30.4 us (4%)
  matrix products  19.3 us (2%)
  between operations  15.7 us (2%)
    pallas_call x3, Pallas kernels, attend_back(): pl.pallas_call(body, grid=(pairs, kblocks), in_specs=[pl.BlockSpec((None,...  148 us
    pallas_call x3, Pallas kernels, attend(): pl.pallas_call(body, grid=(pairs, length // qblock), in_specs=[pl.BlockSp...  76 us
    pallas_call x2, Pallas kernels, mlp_forward(): pl.pallas_call(body, grid=(steps,), in_specs=in_specs, out_specs=[slope_s...  71.8 us
    pallas_call x3, Pallas kernels, project_back(): pl.pallas_call(kernel, grid=(steps,), in_specs=in_specs, out_specs=out_sp...  43 us
    pallas_call x2, Pallas kernels, mlp_backward(): pl.pallas_call(body, grid=(rows // block,), in_specs=in_specs, out_specs=...  34.7 us
    ppermute x30, waiting for transfers between devices, swap(): lax.ppermute(value, 'tensor', [(i, i ^ bits) for i in range(tensor_size)])  33.7 us
    all_gather x3, waiting for transfers between devices, gather_rows(): return lax.all_gather(own, 'tensor', axis=0, tiled=True)  31.6 us
    pallas_call x1, Pallas kernels, weight_back(): pl.pallas_call(body, grid=(steps,), in_specs=[row_spec, pl.BlockSpec((blo...  26.4 us
  transfers between devices with their start and end apart: 57, of which 17 were waited for; matrix products, arithmetic and copies ran while one was open for 10% of the time, Pallas kernels for 51%

profile of v4, /device:TPU:0, one launch (start us, length us, event | category | flops | bytes accessed | tf_op | source)
XLA Modules:
  0.0 792.3 jit_solution(5945421620314565307)
XLA Ops:
  20.5 11.8 %cot_back.1.refs_0_ = bf16[1536,2048]{1,0:T(8,128)(2,1)} custom-call(bf16[1536,1024]{1,0:T(8,128)(2,1)} %fusion.cot_ref.refs_1_.refs_0_, bf16[1024,1024]{1,0:T(8,128)(2,1)} %refs_6_, bf16[1024,1024]{1,0:T(8,128)(2,1)} %collective-permute-done.refs_1_.refs_7_), custom_call_target="tpu_custom_call" | custom-call | flops 100663296 | bytes 1572864 | tf_op jit(solution)/shard_map/cot_back/pallas_call | solution.py:467
  32.3 15.1 %all-gather.4.cloned.1.call-done.refs_1_ = bf16[2048,1024]{1,0:T(8,128)(2,1)} async-done(((bf16[512,1024]{1,0:T(8,128)(2,1)}), bf16[2048,1024]{1,0:T(8,128)(2,1)}) %all-gather.4.cloned.1.call-update) | async-done | bytes 4194320 | tf_op jit(solution)/shard_map/all_gather | solution.py:831
  58.7 25.5 %attend.3 = (bf16[2048,256]{1,0:T(8,128)(2,1)}, f32[2,2,2048]{2,1,0:T(2,128)}) custom-call(bf16[3,2048,256]{2,1,0:T(8,128)(2,1)} %fusion.9.q_ref.k_ref.v_ref, bf16[3,2048,256]{2,1,0:T(8,128)(2,1)} %fusion.9.q_ref.k_ref.v_ref, bf16[3,2048,256]{2,1,0:T(8,128)(2,1)} %fusion.9.q_ref.k_ref.v_ref), custom_call_target="tpu_custom_call" | custom-call | flops 134217728 | bytes 524288 | tf_op jit(solution)/shard_map/attend/pallas_call | solution.py:76
  101.6 25.2 %attend.4 = (bf16[2048,256]{1,0:T(8,128)(2,1)}, f32[2,2,2048]{2,1,0:T(2,128)}) custom-call(bf16[3,2048,256]{2,1,0:T(8,128)(2,1)} %fusion.10.q_ref.k_ref.v_ref, bf16[3,2048,256]{2,1,0:T(8,128)(2,1)} %fusion.10.q_ref.k_ref.v_ref, bf16[3,2048,256]{2,1,0:T(8,128)(2,1)} %fusion.10.q_ref.k_ref.v_ref), custom_call_target="tpu_custom_call" | custom-call | flops 134217728 | bytes 524288 | tf_op jit(solution)/shard_map/attend/pallas_call | solution.py:76
  126.8 16.5 %all-gather.8.cloned.1.call-done.refs_1_ = bf16[2048,1024]{1,0:T(8,128)(2,1)} async-done(((bf16[512,1024]{1,0:T(8,128)(2,1)}), bf16[2048,1024]{1,0:T(8,128)(2,1)}) %all-gather.8.cloned.1.call-update) | async-done | bytes 4194320 | tf_op jit(solution)/shard_map/all_gather | solution.py:831
  155.5 25.2 %attend.5 = (bf16[2048,256]{1,0:T(8,128)(2,1)}, f32[2,2,2048]{2,1,0:T(2,128)}) custom-call(bf16[3,2048,256]{2,1,0:T(8,128)(2,1)} %fusion.11.q_ref.k_ref.v_ref, bf16[3,2048,256]{2,1,0:T(8,128)(2,1)} %fusion.11.q_ref.k_ref.v_ref, bf16[3,2048,256]{2,1,0:T(8,128)(2,1)} %fusion.11.q_ref.k_ref.v_ref), custom_call_target="tpu_custom_call" | custom-call | flops 134217728 | bytes 524288 | tf_op jit(solution)/shard_map/attend/pallas_call | solution.py:76
  180.7 11.6 %all-to-all-done.1.refs_6_ = bf16[4,512,256]{2,1,0:T(8,128)(2,1)S(1)} async-done(((bf16[4,512,256]{2,1,0:T(8,128)(2,1)}), bf16[4,512,256]{2,1,0:T(8,128)(2,1)S(1)}, u32[]{:S(2)}, u32[]{:S(2)}) %all-to-all-start.1) | async-done | bytes 1048608 | tf_op jit(solution)/shard_map/all_to_all | solution.py:692
  222.6 17.2 %collective-permute-done.9 = bf16[512,1024]{1,0:T(8,128)(2,1)} collective-permute-done((bf16[512,1024]{1,0:T(8,128)(2,1)}, bf16[512,1024]{1,0:T(8,128)(2,1)}, u32[]{:S(2)}, u32[]{:S(2)}) %collective-permute-start.9) | collective-permute-done | bytes 1048608 | tf_op jit(solution)/shard_map/ppermute | solution.py:767
  248.7 35.1 %mlp_forward.2 = (bf16[1536,2048]{1,0:T(8,128)(2,1)}, f32[1536,1024]{1,0:T(8,128)}, bf16[1024,1024]{1,0:T(8,128)(2,1)}, bf16[1024,1024]{1,0:T(8,128)(2,1)}) custom-call(bf16[1536,1024]{1,0:T(8,128)(2,1)} %get-tuple-element.242.refs_0_.x_ref, bf16[1536,1024]{1,0:T(8,128)(2,1)} %fusion.cot_ref.refs_1_.refs_0_, bf16[1024,1024]{1,0:T(8,128)(2,1)} %refs_2_.1, ...), custom_call_target="tpu_custom_call" | custom-call | flops 301989888 | bytes 1572864 | tf_op jit(solution)/shard_map/mlp_forward/pallas_call | solution.py:439
  284.4 36.7 %mlp_forward.3 = (bf16[1536,2048]{1,0:T(8,128)(2,1)}, f32[1536,1024]{1,0:T(8,128)}, bf16[1024,1024]{1,0:T(8,128)(2,1)}, bf16[1024,1024]{1,0:T(8,128)(2,1)}) custom-call(bf16[1536,1024]{1,0:T(8,128)(2,1)} %get-tuple-element.242.refs_0_.x_ref, bf16[1536,1024]{1,0:T(8,128)(2,1)} %fusion.cot_ref.refs_1_.refs_0_, ...), custom_call_target="tpu_custom_call", output_to_operand_aliasing={{1}: (8, {})} | custom-call | flops 301989888 | bytes 1572864 | tf_op jit(solution)/shard_map/mlp_forward/pallas_call | solution.py:439
  321.7 13.5 %mlp_backward.2 = (bf16[1536,4096]{1,0:T(8,128)(2,1)}, f32[1536,1024]{1,0:T(8,128)}, f32[1,2048]{1,0:T(1,128)}) custom-call(bf16[1536,2048]{1,0:T(8,128)(2,1)} %cot_back.1.refs_0_, bf16[1536,2048]{1,0:T(8,128)(2,1)} %get-tuple-element.262.refs_1_, bf16[1024,1024]{1,0:T(8,128)(2,1)} %refs_2_.1, bf16[1024,1024]{1,0:T(8,128)(2,1)} %collective-permute-done.2.refs_3_), custom_call_target="tpu_custom_call" | custom-call | flops 201326592 | bytes 1572864 | tf_op jit(solution)/shard_map/mlp_backward/pallas_call | solution.py:525
  339.7 21.2 %mlp_backward.3 = (bf16[1536,4096]{1,0:T(8,128)(2,1)}, f32[1536,1024]{1,0:T(8,128)}, f32[1,2048]{1,0:T(1,128)}) custom-call(bf16[1536,1024]{1,0:T(8,128)(2,1)} %fusion.cot_ref.refs_1_.refs_0_, bf16[1536,2048]{1,0:T(8,128)(2,1)} %get-tuple-element.260.refs_1_, bf16[1024,1024]{1,0:T(8,128)(2,1)} %copy-done.6, ...), custom_call_target="tpu_custom_call", output_to_operand_aliasing={{0}: (6, {}), {1}: (7, {})} | custom-call | flops 201326592 | bytes 1572864 | tf_op jit(solution)/shard_map/mlp_backward/pallas_call | solution.py:525
  360.9 14.9 %residual_back.1 = (f32[1536,1024]{1,0:T(8,128)}, bf16[1536,1024]{1,0:T(8,128)(2,1)}, f32[8,1024]{1,0:T(8,128)}, bf16[4,1536,256]{2,1,0:T(8,128)(2,1)}) custom-call(s32[1]{0:T(128)} %bitcast.refs_0_, f32[1536,1024]{1,0:T(8,128)} %get-tuple-element.269.refs_1_, f32[1536,1024]{1,0:T(8,128)} %get-tuple-element.241.refs_2_, bf16[3,512,1024]{2,1,0:T(8,128)(2,1)} %refs_3_.4, ...), custom_call_target="tpu_custom_call" | custom-call | flops 50331648 | bytes 524288 | tf_op jit(solution)/shard_map/residual_back/pallas_call | solution.py:301
  375.8 11.4 %collective-permute-done.16 = bf16[1024,1024]{1,0:T(8,128)(2,1)} collective-permute-done((bf16[1024,1024]{1,0:T(8,128)(2,1)}, bf16[1024,1024]{1,0:T(8,128)(2,1)}, u32[]{:S(2)}, u32[]{:S(2)}) %collective-permute-start.16) | collective-permute-done | bytes 2097184 | tf_op jit(solution)/shard_map/ppermute | solution.py:681
  391.0 26.4 %weight_back.1 = (bf16[1024,1024]{1,0:T(8,128)(2,1)}, bf16[1024,1024]{1,0:T(8,128)(2,1)}, bf16[1024,1024]{1,0:T(8,128)(2,1)}, bf16[1024,1024]{1,0:T(8,128)(2,1)}...) custom-call(bf16[1536,1024]{1,0:T(8,128)(2,1)} %get-tuple-element.24, ...), custom_call_target="tpu_custom_call" | custom-call | flops 251658240 | bytes 1572864 | tf_op jit(solution)/shard_map/weight_back/pallas_call | solution.py:580
  417.4 10.4 %all-to-all-done.3.grad_ref = bf16[4,1536,256]{2,1,0:T(8,128)(2,1)S(1)} async-done(((bf16[4,1536,256]{2,1,0:T(8,128)(2,1)}), bf16[4,1536,256]{2,1,0:T(8,128)(2,1)S(1)}, u32[]{:S(2)}, u32[]{:S(2)}) %all-to-all-start.3) | async-done | bytes 3145760 | tf_op jit(solution)/shard_map/all_to_all | solution.py:692
  449.6 49.3 %attend_back.4.refs_2_ = bf16[3,2048,256]{2,1,0:T(8,128)(2,1)} custom-call(bf16[3,2048,256]{2,1,0:T(8,128)(2,1)} %fusion.9.q_ref.k_ref.v_ref, bf16[3,2048,256]{2,1,0:T(8,128)(2,1)} %fusion.9.q_ref.k_ref.v_ref, bf16[3,2048,256]{2,1,0:T(8,128)(2,1)} %fusion.9.q_ref.k_ref.v_ref, bf16[2048,256]{1,0:T(8,128)(2,1)} %get-tuple-element.217.out_ref, ...), custom_call_target="tpu_custom_call" | custom-call | flops 335544320 | bytes 524288 | tf_op jit(solution)/shard_map/attend_back/pallas_call | solution.py:169
  504.2 13.2 %project_back.3 = (bf16[512,1024]{1,0:T(8,128)(2,1)}, bf16[512,1024]{1,0:T(8,128)(2,1)}, bf16[512,1024]{1,0:T(8,128)(2,1)}, bf16[512,1024]{1,0:T(8,128)(2,1)}, f...) custom-call(s32[1]{0:T(128)} %bitcast.refs_0_, bf16[2048,1024]{1,0:T(8,128)(2,1)} %all-gather.4.cloned.1.call-done.refs_1_, ...), custom_call_target="tpu_custom_call" | custom-call | flops 100663296 | bytes 524288 | tf_op jit(solution)/shard_map/project_back/pallas_call | solution.py:660
  529.3 49.7 %attend_back.5.refs_2_ = bf16[3,2048,256]{2,1,0:T(8,128)(2,1)} custom-call(bf16[3,2048,256]{2,1,0:T(8,128)(2,1)} %fusion.10.q_ref.k_ref.v_ref, bf16[3,2048,256]{2,1,0:T(8,128)(2,1)} %fusion.10.q_ref.k_ref.v_ref, bf16[3,2048,256]{2,1,0:T(8,128)(2,1)} %fusion.10.q_ref.k_ref.v_ref, bf16[2048,256]{1,0:T(8,128)(2,1)} %get-tuple-element.218.out_ref, ...), custom_call_target="tpu_custom_call" | custom-call | flops 335544320 | bytes 524288 | tf_op jit(solution)/shard_map/attend_back/pallas_call | solution.py:169
  585.2 14.1 %project_back.4 = (bf16[512,1024]{1,0:T(8,128)(2,1)}, bf16[512,1024]{1,0:T(8,128)(2,1)}, bf16[512,1024]{1,0:T(8,128)(2,1)}, bf16[512,1024]{1,0:T(8,128)(2,1)}, f...) custom-call(s32[1]{0:T(128)} %bitcast.refs_0_, ...), custom_call_target="tpu_custom_call", output_to_operand_aliasing={{4}: (4, {}), {5}: (5, {})} | custom-call | flops 100663296 | bytes 524288 | tf_op jit(solution)/shard_map/project_back/pallas_call | solution.py:660
  607.8 49.1 %attend_back.3.refs_2_ = bf16[3,2048,256]{2,1,0:T(8,128)(2,1)} custom-call(bf16[3,2048,256]{2,1,0:T(8,128)(2,1)} %fusion.11.q_ref.k_ref.v_ref, bf16[3,2048,256]{2,1,0:T(8,128)(2,1)} %fusion.11.q_ref.k_ref.v_ref, bf16[3,2048,256]{2,1,0:T(8,128)(2,1)} %fusion.11.q_ref.k_ref.v_ref, bf16[2048,256]{1,0:T(8,128)(2,1)} %get-tuple-element.231.out_ref, ...), custom_call_target="tpu_custom_call" | custom-call | flops 335544320 | bytes 524288 | tf_op jit(solution)/shard_map/attend_back/pallas_call | solution.py:169
  661.7 15.7 %project_back.5 = (bf16[512,1024]{1,0:T(8,128)(2,1)}, bf16[512,1024]{1,0:T(8,128)(2,1)}, bf16[512,1024]{1,0:T(8,128)(2,1)}, bf16[512,1024]{1,0:T(8,128)(2,1)}, f...) custom-call(s32[1]{0:T(128)} %bitcast.refs_0_, ...), custom_call_target="tpu_custom_call", output_to_operand_aliasing={{4}: (4, {}), {5}: (5, {})} | custom-call | flops 100663296 | bytes 524288 | tf_op jit(solution)/shard_map/project_back/pallas_call | solution.py:660
  690.8 14.4 %collective-permute-done.44 = f32[2,1024]{1,0:T(2,128)S(1)} collective-permute-done((f32[2,1024]{1,0:T(2,128)S(1)}, f32[2,1024]{1,0:T(2,128)S(1)}, u32[]{:S(2)}, u32[]{:S(2)}) %collective-permute-start.44) | collective-permute-done | bytes 8224 | tf_op jit(solution)/shard_map/ppermute | solution.py:984
  752.8 23.3 %all-reduce.4.cloned.1.call-done = bf16[3,1040,256]{2,1,0:T(8,128)(2,1)} async-done(((bf16[3,1040,256]{2,1,0:T(8,128)(2,1)}), bf16[3,1040,256]{2,1,0:T(8,128)(2,1)}) %all-reduce.4.cloned.1.call-update) | async-done | bytes 1597456 | tf_op jit(solution)/shard_map/psum | solution.py:976
  (304 shorter events, 229.9 us)
Async XLA Ops:
  10.1 74.1 %all-gather.6.cloned.1.call-start = ((), (), s32[]{:S(2)}) async-start(), calls=%async_computation.5 | async-start | bytes 5242880 | tf_op jit(solution)/shard_map/all_gather | solution.py:831
  47.4 95.9 %all-gather.8.cloned.1.call-start = ((), (), s32[]{:S(2)}) async-start(), calls=%async_computation.6 | async-start | bytes 5242880 | tf_op jit(solution)/shard_map/all_gather | solution.py:831
  84.2 59.0 %all-to-all-start = ((bf16[4,512,256]{2,1,0:T(8,128)(2,1)}), bf16[4,512,256]{2,1,0:T(8,128)(2,1)S(1)}, u32[]{:S(2)}, u32[]{:S(2)}) async-start(bf16[4,512,256]{2,1,0:T(8,128)(2,1)} %bitcast.59), calls=%async_computation | async-start | bytes 2097152 | tf_op jit(solution)/shard_map/all_to_all | solution.py:692
  90.4 101.9 %collective-permute-start.5 = (bf16[512,1024]{1,0:T(8,128)(2,1)}, bf16[512,1024]{1,0:T(8,128)(2,1)}, u32[]{:S(2)}, u32[]{:S(2)}) collective-permute-start(bf16[512,1024]{1,0:T(8,128)(2,1)} %constant_dynamic-slice_fusion.8), channel_id=1, source_target_pairs={{0,2},{1,3},{2,0},{3,1},{4,6},{5,7},{6,4},{7,5},{8,10},{9,11},{10,... | collective-permute-start | bytes 3145736 | tf_op jit(solution)/shard_map/ppermute | solution.py:681
  94.8 97.5 %collective-permute-start.6 = (bf16[512,1024]{1,0:T(8,128)(2,1)}, bf16[512,1024]{1,0:T(8,128)(2,1)}, u32[]{:S(2)}, u32[]{:S(2)}) collective-permute-start(bf16[512,1024]{1,0:T(8,128)(2,1)} %constant_dynamic-slice_fusion.7), channel_id=1, source_target_pairs={{0,2},{1,3},{2,0},{3,1},{4,6},{5,7},{6,4},{7,5},{8,10},{9,11},{10,... | collective-permute-start | bytes 3145736 | tf_op jit(solution)/shard_map/ppermute | solution.py:681
  99.5 92.8 %collective-permute-start.4 = (bf16[256,1024]{1,0:T(8,128)(2,1)S(1)}, bf16[256,1024]{1,0:T(8,128)(2,1)}, u32[]{:S(2)}, u32[]{:S(2)}) collective-permute-start(bf16[256,1024]{1,0:T(8,128)(2,1)S(1)} %copy-done.21), channel_id=1, source_target_pairs={{0,2},{1,3},{2,0},{3,1},{4,6},{5,7},{6,4},{7,5},{8,10},{9,11},{10,... | collective-permute-start | bytes 1572872 | tf_op jit(solution)/shard_map/ppermute | solution.py:681
  144.3 48.0 %all-to-all-start.1 = ((bf16[4,512,256]{2,1,0:T(8,128)(2,1)}), bf16[4,512,256]{2,1,0:T(8,128)(2,1)S(1)}, u32[]{:S(2)}, u32[]{:S(2)}) async-start(bf16[4,512,256]{2,1,0:T(8,128)(2,1)} %bitcast.58), calls=%async_computation.1 | async-start | bytes 2097152 | tf_op jit(solution)/shard_map/all_to_all | solution.py:692
  194.1 45.7 %collective-permute-start.9 = (bf16[512,1024]{1,0:T(8,128)(2,1)}, bf16[512,1024]{1,0:T(8,128)(2,1)}, u32[]{:S(2)}, u32[]{:S(2)}) collective-permute-start(bf16[512,1024]{1,0:T(8,128)(2,1)} %collective-permute-done.6), channel_id=1, source_target_pairs={{0,4},{4,0},{8,12},{12,8},{16,20},{20,16},{24,28},{28,24},{1,5},{5... | collective-permute-start | bytes 3145736 | tf_op jit(solution)/shard_map/ppermute | solution.py:767
  339.1 48.2 %collective-permute-start.16 = (bf16[1024,1024]{1,0:T(8,128)(2,1)}, bf16[1024,1024]{1,0:T(8,128)(2,1)}, u32[]{:S(2)}, u32[]{:S(2)}) collective-permute-start(bf16[1024,1024]{1,0:T(8,128)(2,1)} %add_convert_fusion.6), channel_id=1, source_target_pairs={{0,2},{1,3},{2,0},{3,1},{4,6},{5,7},{6,4},{7,5},{8,10},{9,11},{10,... | collective-permute-start | bytes 6291464 | tf_op jit(solution)/shard_map/ppermute | solution.py:681
  391.0 269.5 %all-reduce.6.cloned.1.call-start = ((), (), s32[]{:S(2)}) async-start(), calls=%async_computation.8 | async-start | bytes 5242880 | tf_op jit(solution)/shard_map/psum | solution.py:961
  440.7 58.2 %collective-permute-start.21 = (bf16[1024,1024]{1,0:T(8,128)(2,1)}, bf16[1024,1024]{1,0:T(8,128)(2,1)}, u32[]{:S(2)}, u32[]{:S(2)}) collective-permute-start(bf16[1024,1024]{1,0:T(8,128)(2,1)} %add_convert_fusion.5), channel_id=1, source_target_pairs={{0,2},{1,3},{2,0},{3,1},{4,6},{5,7},{6,4},{7,5},{8,10},{9,11},{10,... | collective-permute-start | bytes 6291464 | tf_op jit(solution)/shard_map/ppermute | solution.py:681
  444.9 55.1 %collective-permute-start.23 = (bf16[512,1024]{1,0:T(8,128)(2,1)S(1)}, bf16[512,1024]{1,0:T(8,128)(2,1)}, u32[]{:S(2)}, u32[]{:S(2)}) collective-permute-start(bf16[512,1024]{1,0:T(8,128)(2,1)S(1)} %constant_dynamic-slice_fusion.6), channel_id=1, source_target_pairs={{0,4},{4,0},{8,12},{12,8},{16,20},{20,16},{24,28},{28,24},{1,5},{5... | collective-permute-start | bytes 3145736 | tf_op jit(solution)/shard_map/ppermute | solution.py:749
  447.7 52.3 %collective-permute-start.22 = (bf16[256,1024]{1,0:T(8,128)(2,1)}, bf16[256,1024]{1,0:T(8,128)(2,1)}, u32[]{:S(2)}, u32[]{:S(2)}) collective-permute-start(bf16[256,1024]{1,0:T(8,128)(2,1)} %add_convert_fusion.13), channel_id=1, source_target_pairs={{0,2},{1,3},{2,0},{3,1},{4,6},{5,7},{6,4},{7,5},{8,10},{9,11},{10,... | collective-permute-start | bytes 1572872 | tf_op jit(solution)/shard_map/ppermute | solution.py:681
  522.5 56.4 %collective-permute-start.26 = (bf16[512,1024]{1,0:T(8,128)(2,1)}, bf16[512,1024]{1,0:T(8,128)(2,1)S(1)}, u32[]{:S(2)}, u32[]{:S(2)}) collective-permute-start(bf16[512,1024]{1,0:T(8,128)(2,1)} %get-tuple-element.318), channel_id=1, source_target_pairs={{0,1},{1,0},{2,3},{3,2},{4,5},{5,4},{6,7},{7,6},{8,9},{9,8},{10,11... | collective-permute-start | bytes 3145736 | tf_op jit(solution)/shard_map/ppermute | solution.py:681
  522.9 56.1 %collective-permute-start.27 = (bf16[512,1024]{1,0:T(8,128)(2,1)}, bf16[512,1024]{1,0:T(8,128)(2,1)}, u32[]{:S(2)}, u32[]{:S(2)}) collective-permute-start(bf16[512,1024]{1,0:T(8,128)(2,1)} %get-tuple-element.319), channel_id=1, source_target_pairs={{0,1},{1,0},{2,3},{3,2},{4,5},{5,4},{6,7},{7,6},{8,9},{9,8},{10,11... | collective-permute-start | bytes 3145736 | tf_op jit(solution)/shard_map/ppermute | solution.py:681
  525.2 250.8 %all-reduce.4.cloned.1.call-start = ((), (), s32[]{:S(2)}) async-start(), calls=%async_computation.7 | async-start | bytes 3194880 | tf_op jit(solution)/shard_map/psum | solution.py:976
  525.6 53.4 %collective-permute-start.30 = (bf16[128,1024]{1,0:T(8,128)(2,1)S(1)}, bf16[128,1024]{1,0:T(8,128)(2,1)S(1)}, u32[]{:S(2)}, u32[]{:S(2)}) collective-permute-start(bf16[128,1024]{1,0:T(8,128)(2,1)S(1)} %constant_dynamic-slice_fusion), channel_id=1, source_target_pairs={{0,16},{4,20},{8,24},{12,28},{16,0},{20,4},{24,8},{28,12},{1,17},{... | collective-permute-start | bytes 786440 | tf_op jit(solution)/shard_map/ppermute | solution.py:749
  528.0 50.9 %collective-permute-start.29 = (f32[64,128]{1,0:T(8,128)S(1)}, f32[64,128]{1,0:T(8,128)S(1)}, u32[]{:S(2)}, u32[]{:S(2)}) collective-permute-start(f32[64,128]{1,0:T(8,128)S(1)} %add.235), channel_id=1, source_target_pairs={{0,2},{1,3},{2,0},{3,1},{4,6},{5,7},{6,4},{7,5},{8,10},{9,11},{10,... | collective-permute-start | bytes 98312 | tf_op jit(solution)/shard_map/ppermute | solution.py:735
  583.5 77.0 %collective-permute-start.28 = (bf16[512,1024]{1,0:T(8,128)(2,1)S(1)}, bf16[512,1024]{1,0:T(8,128)(2,1)}, u32[]{:S(2)}, u32[]{:S(2)}) collective-permute-start(bf16[512,1024]{1,0:T(8,128)(2,1)S(1)} %add_convert_fusion.9), channel_id=1, source_target_pairs={{0,2},{1,3},{2,0},{3,1},{4,6},{5,7},{6,4},{7,5},{8,10},{9,11},{10,... | collective-permute-start | bytes 3145736 | tf_op jit(solution)/shard_map/ppermute | solution.py:681
  599.3 61.2 %collective-permute-start.33 = (bf16[512,1024]{1,0:T(8,128)(2,1)}, bf16[512,1024]{1,0:T(8,128)(2,1)}, u32[]{:S(2)}, u32[]{:S(2)}) collective-permute-start(bf16[512,1024]{1,0:T(8,128)(2,1)} %get-tuple-element.339), channel_id=1, source_target_pairs={{0,1},{1,0},{2,3},{3,2},{4,5},{5,4},{6,7},{7,6},{8,9},{9,8},{10,11... | collective-permute-start | bytes 3145736 | tf_op jit(solution)/shard_map/ppermute | solution.py:681
  599.3 61.1 %collective-permute-start.34 = (bf16[512,1024]{1,0:T(8,128)(2,1)}, bf16[512,1024]{1,0:T(8,128)(2,1)}, u32[]{:S(2)}, u32[]{:S(2)}) collective-permute-start(bf16[512,1024]{1,0:T(8,128)(2,1)} %get-tuple-element.340), channel_id=1, source_target_pairs={{0,1},{1,0},{2,3},{3,2},{4,5},{5,4},{6,7},{7,6},{8,9},{9,8},{10,11... | collective-permute-start | bytes 3145736 | tf_op jit(solution)/shard_map/ppermute | solution.py:681
  599.9 61.0 %collective-permute-start.36 = (bf16[256,1024]{1,0:T(8,128)(2,1)S(1)}, bf16[256,1024]{1,0:T(8,128)(2,1)S(1)}, u32[]{:S(2)}, u32[]{:S(2)}) collective-permute-start(bf16[256,1024]{1,0:T(8,128)(2,1)S(1)} %constant_dynamic-update-slice_fusion.10), channel_id=1, source_target_pairs={{0,8},{4,12},{8,0},{12,4},{16,24},{20,28},{24,16},{28,20},{1,9},{5... | collective-permute-start | bytes 1572872 | tf_op jit(solution)/shard_map/ppermute | solution.py:752
  680.5 46.1 %collective-permute-start.37 = (bf16[512,1024]{1,0:T(8,128)(2,1)}, bf16[512,1024]{1,0:T(8,128)(2,1)}, u32[]{:S(2)}, u32[]{:S(2)}) collective-permute-start(bf16[512,1024]{1,0:T(8,128)(2,1)} %add_convert_fusion.8), channel_id=1, source_target_pairs={{0,2},{1,3},{2,0},{3,1},{4,6},{5,7},{6,4},{7,5},{8,10},{9,11},{10,... | collective-permute-start | bytes 3145736 | tf_op jit(solution)/shard_map/ppermute | solution.py:681
  686.9 44.6 %collective-permute-start.42 = (bf16[512,1024]{1,0:T(8,128)(2,1)}, bf16[512,1024]{1,0:T(8,128)(2,1)}, u32[]{:S(2)}, u32[]{:S(2)}) collective-permute-start(bf16[512,1024]{1,0:T(8,128)(2,1)} %constant_dynamic-update-slice_fusion.8), channel_id=1, source_target_pairs={{0,4},{4,0},{8,12},{12,8},{16,20},{20,16},{24,28},{28,24},{1,5},{5... | collective-permute-start | bytes 3145736 | tf_op jit(solution)/shard_map/ppermute | solution.py:752
  (79 other events, 1267.5 us)
Sparse Core Ops, SparseCore 0:
  10.2 37.1 all-gather.3
  49.5 34.4 all-gather.5
  86.2 57.0 all-gather.7
  525.3 132.0 all-reduce.5
  683.7 92.3 all-reduce.3

commit v5 on v4

--- a/solution.py
+++ b/solution.py
@@ -51,7 +51,7 @@
     _, length, width = qkv.shape
     lanes = min(128, width)
     heads = lanes // HD
-    qblock = largest_block(length, 1024)
+    qblock = largest_block(length, 2048)
     to_log2 = SCORE_SCALE * LOG2E
 
     def body(q_ref, k_ref, v_ref, out_ref, lse_ref):
@@ -104,7 +104,7 @@
     lanes = min(128, width)
     shards_of = grad_attended.shape[0]
     heads = lanes // HD
-    kblock = largest_block(length, 512)
+    kblock = largest_block(length, 1024)
     kblocks = length // kblock
     to_log2 = SCORE_SCALE * LOG2E
 
@@ -598,6 +598,7 @@
     block = rows // pieces
     steps = pieces
     first = before is None
+    given = 0 if last else pieces
 
     def kernel(*refs):
         place_ref, normed_ref, dqkv_ref, weight_ref = refs[:4]
@@ -605,7 +606,7 @@
         if not first:
             wgrad_before, column_before = rest[:2]
             rest = rest[2:]
-        row_refs, rest = rest[:pieces], rest[pieces:]
+        row_refs, rest = rest[:given], rest[given:]
         wgrad_ref, column_ref = rest[:2]
         step = pl.program_id(0)
 
@@ -618,15 +619,16 @@
                 wgrad_ref[...] = wgrad_before[...]
                 column_ref[...] = column_before[...]
 
-        row_grad = nt(dqkv_ref[0], weight_ref[0])
-        for c in range(1, 3):
-            row_grad = row_grad + nt(dqkv_ref[c], weight_ref[c])
-        row_grad = row_grad.astype(bf16)
-        for k in range(pieces):
-
-            @pl.when(step == place_ref[0] ^ k)
-            def _():
-                row_refs[k][...] = row_grad
+        if not last:
+            row_grad = nt(dqkv_ref[0], weight_ref[0])
+            for c in range(1, 3):
+                row_grad = row_grad + nt(dqkv_ref[c], weight_ref[c])
+            row_grad = row_grad.astype(bf16)
+            for k in range(pieces):
+
+                @pl.when(step == place_ref[0] ^ k)
+                def _():
+                    row_refs[k][...] = row_grad
 
         for c in range(3):
             wgrad_ref[c] += tn(normed_ref[...], dqkv_ref[c])
@@ -649,8 +651,8 @@
     if not first:
         operands += list(before)
         in_specs += [whole, columns]
-    out_specs = [pl.BlockSpec((block, model), lambda i: (0, 0))] * pieces + [whole, columns]
-    out_shape = [jax.ShapeDtypeStruct((block, model), bf16)] * pieces + [
+    out_specs = [pl.BlockSpec((block, model), lambda i: (0, 0))] * given + [whole, columns]
+    out_shape = [jax.ShapeDtypeStruct((block, model), bf16)] * given + [
         jax.ShapeDtypeStruct((3, model, width), f32),
         jax.ShapeDtypeStruct((8, width), f32),
     ]
@@ -663,7 +665,7 @@
         in_specs=in_specs,
         out_specs=out_specs,
         out_shape=out_shape,
-        input_output_aliases={} if first else {4: pieces, 5: pieces + 1},
+        input_output_aliases={} if first else {4: given, 5: given + 1},
         compiler_params=pltpu.CompilerParams(vmem_limit_bytes=VMEM_LIMIT),
         cost_estimate=pl.CostEstimate(
             flops=12 * rows * model * width // COST_SCALE,
@@ -672,6 +674,38 @@
         ),
         name="project_back",
     )(*operands)
+
+
+def project_rows(place, dqkv, weight, pieces):
+    _, rows, width = dqkv.shape
+    model = weight.shape[1]
+    block = rows // pieces
+
+    def kernel(place_ref, dqkv_ref, weight_ref, *row_refs):
+        row_grad = nt(dqkv_ref[0], weight_ref[0])
+        for c in range(1, 3):
+            row_grad = row_grad + nt(dqkv_ref[c], weight_ref[c])
+        row_grad = row_grad.astype(bf16)
+        for k in range(pieces):
+
+            @pl.when(pl.program_id(0) == place_ref[0] ^ k)
+            def _():
+                row_refs[k][...] = row_grad
+
+    return pl.pallas_call(
+        kernel,
+        grid=(pieces,),
+        in_specs=[
+            pl.BlockSpec(memory_space=pltpu.SMEM),
+            pl.BlockSpec((3, block, width), lambda i: (0, i, 0)),
+            pl.BlockSpec((3, model, width), lambda i: (0, 0, 0)),
+        ],
+        out_specs=[pl.BlockSpec((block, model), lambda i: (0, 0))] * pieces,
+        out_shape=[jax.ShapeDtypeStruct((block, model), bf16)] * pieces,
+        compiler_params=params(),
+        cost_estimate=hint(6 * rows * model * width, rows * width),
+        name="project_rows",
+    )(place, dqkv, weight)
 
 
 def make_shards(tensor_size, group_size):
@@ -854,17 +888,17 @@
             out, lse = attend(qkv)
             if not last:
                 out, following = tie(out, following)
-            if i == 0:
+            if i > 0:
+                out, heads_own[-1] = tie(out, heads_own[-1])
+            if i == min(1, slot_count - 1):
                 out, (up_own, down_own, out_own) = tie(
                     out, (up_projection_weight, down_projection_weight, output_projection_weight)
                 )
                 out_far = gather_far(out_own)
                 up_far = fetch(up_own)
                 down_far = fetch(down_own)
-            else:
-                out, heads_own[-1] = tie(out, heads_own[-1])
             if last:
-                out, (out_far, up_far, down_far) = tie(out, (out_far, up_far, down_far))
+                out, (out_far, up_far) = tie(out, (out_far, up_far))
             heads_own.append(exchange(out.reshape(tensor_size, own_rows, width)))
             qkvs.append(qkv)
             attended.append(out)
@@ -872,23 +906,21 @@
             every = following
         if square:
             up_rest = fetch_rest(up_far)
-            down_rest = fetch_rest(down_far)
             out_weight = jnp.concatenate([out_own, weights_near[0], out_far, swap(out_far, 1)], axis=0)
         else:
             out_weight = jnp.concatenate(gather_near(out_own, out_far), axis=0)
         rows_done = None
         for i in range(slot_count):
             if i == slot_count - 1:
-                rows_done, heads_own[i] = tie(rows_done, heads_own[i])
+                rows_done, (heads_own[i], down_far) = tie(rows_done, (heads_own[i], down_far))
             rows_done = out_project(
                 patches, i, place, heads_own[i], out_weight, out_bias_row, mlp_gain_row, mlp_shift_row, rows_done
             )
         if square:
-            rows_done, (up_rest, down_rest) = tie(rows_done, (up_rest, down_rest))
+            down_rest = fetch_rest(down_far)
+            rows_done, up_rest = tie(rows_done, up_rest)
             up_far = in_halves(up_far, up_rest, dp_side)
-            down_far = in_halves(down_far, down_rest, dp_side)
             up_diag = swap(up_far, 1)
-            down_diag = swap(down_far, 1)
         attended_rows, residual, normed_mlp = rows_done
 
         bias_blocks = gather_near(bias_row, bias_far)
@@ -904,9 +936,10 @@
         for c in range(calls):
             pair = slice(2 * c, 2 * c + 2)
             if c == 1 and square:
-                total, moved = tie(total, (up_far, up_diag, down_far, down_diag))
-                up_blocks += moved[:2]
-                down_blocks += moved[2:]
+                total, (up_diag, down_rest) = tie(total, (up_diag, down_rest))
+                down_far = in_halves(down_far, down_rest, dp_side)
+                up_blocks += [up_far, up_diag]
+                down_blocks += [down_far, swap(down_far, 1)]
             slope, total, *grads = mlp_forward(
                 normed_mlp, cot_low, up_blocks[pair], bias_blocks[pair], down_blocks[pair], total
             )
@@ -953,7 +986,7 @@
             dqkv = attend_back(qkvs[i], attended[i], grad_attended, i, lses[i])
             if i >= 2:
                 grad_normed[i - 2], dqkv = terms_far(grad_normed[i - 2], dqkv)
-            if i >= 1:
+            if i >= 1 and not last:
                 grad_normed[i - 1], dqkv = sum_near(grad_normed[i - 1], dqkv)
             if i == 0:
                 up_sum, dqkv = sum_far(up_stage, dqkv)
@@ -966,14 +999,19 @@
             if ring:
                 down_sum, dqkv = ring_step(down_sum, ring.pop(0), dqkv)
             results = project_back(place, normed_every[i], dqkv, query_key_value_weight, sums, last, tensor_size)
-            partial, sums = results[:tensor_size], results[tensor_size : tensor_size + 2]
-            if waiting:
-                smalls, partial = sum_step(smalls, waiting.pop(0), partial)
-            if ring and not last:
-                down_sum, partial = ring_step(down_sum, ring.pop(0), partial)
-            if last:
-                grad_residual, qkv_low = tie(grad_residual, results[-1])
+            if not last:
+                partial, sums = results[:tensor_size], results[tensor_size:]
+                if waiting:
+                    smalls, partial = sum_step(smalls, waiting.pop(0), partial)
+                if ring:
+                    down_sum, partial = ring_step(down_sum, ring.pop(0), partial)
+            else:
+                *sums, qkv_low = results
+                qkv_low, (dqkv, grad_residual) = tie(qkv_low, (dqkv, grad_residual))
                 qkv_all = lax.psum(qkv_low, "dp")
+                partial = project_rows(place, dqkv, query_key_value_weight, tensor_size)
+                if i >= 1:
+                    grad_normed[i - 1], partial = sum_near(grad_normed[i - 1], partial)
                 raw = jnp.stack(
                     [
                         jnp.sum(sums[0] * weights_wide, axis=(0, 2)),
@@ -990,9 +1028,8 @@
             terms = grad_normed[i]
             if i >= slot_count - 2:
                 terms, grad_residual = terms_far(terms, grad_residual)
-            if i == slot_count - 1:
-                grad_residual, qkv_all = tie(grad_residual, qkv_all)
             grad_inputs = input_back(terms, patches, i, grad_residual, gain_row, grad_inputs)
+        grad_inputs, qkv_all = tie(grad_inputs, qkv_all)
         for step in ring:
             down_sum = ring_step(down_sum, step, place)[0]
         for step in waiting:

time: 797 us -> 760 us (0.954)
  waiting for transfers between devices: 153 us -> 124 us
  Pallas kernels: 465 us -> 457 us
    ppermute x5, waiting for transfers between devices: 24.4 us -> 4.59 us  [shards(): raw = raw + lax.ppermute(raw, step[0], step[1])]
    ppermute x30, waiting for transfers between devices: 33.7 us -> 52.1 us  [swap(): lax.ppermute(value, 'tensor', [(i, i ^ bits) for i in range(tensor_size)])]
    ppermute x2, waiting for transfers between devices: 17.2 us -> 0.01 us  [fetch_rest(): return lax.ppermute(half, 'dp', [(i, i ^ 1) for i in range(group_size)])]
    pallas_call x0 -> x1, Pallas kernels: none -> 8.3 us  [project_rows(): pl.pallas_call(kernel, grid=(pieces,), in_specs=[pl.BlockSpec(memory_spac...]
    all_gather x3, waiting for transfers between devices: 31.6 us -> 23.3 us  [gather_rows(): return lax.all_gather(own, 'tensor', axis=0, tiled=True)]
  transfers between devices with their start and end apart: 57 -> 57, of which waited for: 17 -> 21; matrix products, arithmetic and copies ran while one was open for 10% -> 11% of each run, Pallas kernels for 51% -> 56%
where the time goes in v5:
time: 760 us; the launch traced here: 752 us
  Pallas kernels  457 us (60%)
  waiting for transfers between devices  124 us (16%)
  other arithmetic  56.8 us (7%)
  starting transfers between devices  49.7 us (7%)
  local copies, waits for them, and re-layouts  26.5 us (3%)
  matrix products  21.9 us (3%)
  between operations  15.6 us (2%)
    pallas_call x3, Pallas kernels, attend_back(): pl.pallas_call(body, grid=(pairs, kblocks), in_specs=[pl.BlockSpec((None,...  141 us
    pallas_call x3, Pallas kernels, attend(): pl.pallas_call(body, grid=(pairs, length // qblock), in_specs=[pl.BlockSp...  72.4 us
    pallas_call x2, Pallas kernels, mlp_forward(): pl.pallas_call(body, grid=(steps,), in_specs=in_specs, out_specs=[slope_s...  71.4 us
    ppermute x30, waiting for transfers between devices, swap(): lax.ppermute(value, 'tensor', [(i, i ^ bits) for i in range(tensor_size)])  52.1 us
    pallas_call x3, Pallas kernels, project_back(): pl.pallas_call(kernel, grid=(steps,), in_specs=in_specs, out_specs=out_sp...  38.1 us
    pallas_call x2, Pallas kernels, mlp_backward(): pl.pallas_call(body, grid=(rows // block,), in_specs=in_specs, out_specs=...  35 us
    pallas_call x1, Pallas kernels, weight_back(): pl.pallas_call(body, grid=(steps,), in_specs=[row_spec, pl.BlockSpec((blo...  26.4 us
    all_gather x3, waiting for transfers between devices, gather_rows(): return lax.all_gather(own, 'tensor', axis=0, tiled=True)  23.3 us
  transfers between devices with their start and end apart: 57, of which 21 were waited for; matrix products, arithmetic and copies ran while one was open for 11% of the time, Pallas kernels for 56%

profile of v5, /device:TPU:0, one launch (start us, length us, event | category | flops | bytes accessed | tf_op | source)
XLA Modules:
  0.0 752.2 jit_solution(16023613117170933109)
XLA Ops:
  20.5 11.8 %cot_back.1.refs_0_ = bf16[1536,2048]{1,0:T(8,128)(2,1)} custom-call(bf16[1536,1024]{1,0:T(8,128)(2,1)} %fusion.cot_ref.refs_1_.refs_0_, bf16[1024,1024]{1,0:T(8,128)(2,1)} %refs_6_, bf16[1024,1024]{1,0:T(8,128)(2,1)} %collective-permute-done.refs_1_.refs_7_), custom_call_target="tpu_custom_call" | custom-call | flops 100663296 | bytes 1572864 | tf_op jit(solution)/shard_map/cot_back/pallas_call | solution.py:467
  32.3 15.1 %all-gather.4.cloned.1.call-done.refs_1_ = bf16[2048,1024]{1,0:T(8,128)(2,1)} async-done(((bf16[512,1024]{1,0:T(8,128)(2,1)}), bf16[2048,1024]{1,0:T(8,128)(2,1)}) %all-gather.4.cloned.1.call-update) | async-done | bytes 4194320 | tf_op jit(solution)/shard_map/all_gather | solution.py:865
  58.5 24.2 %attend.3 = (bf16[2048,256]{1,0:T(8,128)(2,1)}, f32[2,2,2048]{2,1,0:T(2,128)}) custom-call(bf16[3,2048,256]{2,1,0:T(8,128)(2,1)} %fusion.9.q_ref.k_ref.v_ref, bf16[3,2048,256]{2,1,0:T(8,128)(2,1)} %fusion.9.q_ref.k_ref.v_ref, bf16[3,2048,256]{2,1,0:T(8,128)(2,1)} %fusion.9.q_ref.k_ref.v_ref), custom_call_target="tpu_custom_call" | custom-call | flops 134217728 | bytes 524288 | tf_op jit(solution)/shard_map/attend/pallas_call | solution.py:76
  94.9 24.3 %attend.4 = (bf16[2048,256]{1,0:T(8,128)(2,1)}, f32[2,2,2048]{2,1,0:T(2,128)}) custom-call(bf16[3,2048,256]{2,1,0:T(8,128)(2,1)} %fusion.10.q_ref.k_ref.v_ref, bf16[3,2048,256]{2,1,0:T(8,128)(2,1)} %fusion.10.q_ref.k_ref.v_ref, bf16[3,2048,256]{2,1,0:T(8,128)(2,1)} %fusion.10.q_ref.k_ref.v_ref), custom_call_target="tpu_custom_call" | custom-call | flops 134217728 | bytes 524288 | tf_op jit(solution)/shard_map/attend/pallas_call | solution.py:76
  144.5 23.8 %attend.5 = (bf16[2048,256]{1,0:T(8,128)(2,1)}, f32[2,2,2048]{2,1,0:T(2,128)}) custom-call(bf16[3,2048,256]{2,1,0:T(8,128)(2,1)} %fusion.11.q_ref.k_ref.v_ref, bf16[3,2048,256]{2,1,0:T(8,128)(2,1)} %fusion.11.q_ref.k_ref.v_ref, bf16[3,2048,256]{2,1,0:T(8,128)(2,1)} %fusion.11.q_ref.k_ref.v_ref), custom_call_target="tpu_custom_call" | custom-call | flops 134217728 | bytes 524288 | tf_op jit(solution)/shard_map/attend/pallas_call | solution.py:76
  168.3 9.2 %collective-permute-done.4 = bf16[256,1024]{1,0:T(8,128)(2,1)} collective-permute-done((bf16[256,1024]{1,0:T(8,128)(2,1)S(1)}, bf16[256,1024]{1,0:T(8,128)(2,1)}, u32[]{:S(2)}, u32[]{:S(2)}) %collective-permute-start.4) | collective-permute-done | bytes 524320 | tf_op jit(solution)/shard_map/ppermute | solution.py:715
  201.1 9.5 %all-to-all-done.2.refs_6_ = bf16[4,512,256]{2,1,0:T(8,128)(2,1)} async-done(((bf16[4,512,256]{2,1,0:T(8,128)(2,1)}), bf16[4,512,256]{2,1,0:T(8,128)(2,1)}, u32[]{:S(2)}, u32[]{:S(2)}) %all-to-all-start.2) | async-done | bytes 1048608 | tf_op jit(solution)/shard_map/all_to_all | solution.py:726
  223.4 34.9 %mlp_forward.2 = (bf16[1536,2048]{1,0:T(8,128)(2,1)}, f32[1536,1024]{1,0:T(8,128)}, bf16[1024,1024]{1,0:T(8,128)(2,1)}, bf16[1024,1024]{1,0:T(8,128)(2,1)}) custom-call(bf16[1536,1024]{1,0:T(8,128)(2,1)} %get-tuple-element.238.refs_0_.x_ref, bf16[1536,1024]{1,0:T(8,128)(2,1)} %fusion.cot_ref.refs_1_.refs_0_, bf16[1024,1024]{1,0:T(8,128)(2,1)} %refs_2_.1, ...), custom_call_target="tpu_custom_call" | custom-call | flops 301989888 | bytes 1572864 | tf_op jit(solution)/shard_map/mlp_forward/pallas_call | solution.py:439
  265.5 36.5 %mlp_forward.3 = (bf16[1536,2048]{1,0:T(8,128)(2,1)}, f32[1536,1024]{1,0:T(8,128)}, bf16[1024,1024]{1,0:T(8,128)(2,1)}, bf16[1024,1024]{1,0:T(8,128)(2,1)}) custom-call(bf16[1536,1024]{1,0:T(8,128)(2,1)} %get-tuple-element.238.refs_0_.x_ref, bf16[1536,1024]{1,0:T(8,128)(2,1)} %fusion.cot_ref.refs_1_.refs_0_, ...), custom_call_target="tpu_custom_call", output_to_operand_aliasing={{1}: (8, {})} | custom-call | flops 301989888 | bytes 1572864 | tf_op jit(solution)/shard_map/mlp_forward/pallas_call | solution.py:439
  302.6 13.5 %mlp_backward.2 = (bf16[1536,4096]{1,0:T(8,128)(2,1)}, f32[1536,1024]{1,0:T(8,128)}, f32[1,2048]{1,0:T(1,128)}) custom-call(bf16[1536,2048]{1,0:T(8,128)(2,1)} %cot_back.1.refs_0_, bf16[1536,2048]{1,0:T(8,128)(2,1)} %get-tuple-element.256.refs_1_, bf16[1024,1024]{1,0:T(8,128)(2,1)} %refs_2_.1, bf16[1024,1024]{1,0:T(8,128)(2,1)} %collective-permute-done.2.refs_3_), custom_call_target="tpu_custom_call" | custom-call | flops 201326592 | bytes 1572864 | tf_op jit(solution)/shard_map/mlp_backward/pallas_call | solution.py:525
  320.3 21.4 %mlp_backward.3 = (bf16[1536,4096]{1,0:T(8,128)(2,1)}, f32[1536,1024]{1,0:T(8,128)}, f32[1,2048]{1,0:T(1,128)}) custom-call(bf16[1536,1024]{1,0:T(8,128)(2,1)} %fusion.cot_ref.refs_1_.refs_0_, bf16[1536,2048]{1,0:T(8,128)(2,1)} %get-tuple-element.254.refs_1_, bf16[1024,1024]{1,0:T(8,128)(2,1)} %copy-done.6, ...), custom_call_target="tpu_custom_call", output_to_operand_aliasing={{0}: (6, {}), {1}: (7, {})} | custom-call | flops 201326592 | bytes 1572864 | tf_op jit(solution)/shard_map/mlp_backward/pallas_call | solution.py:525
  341.8 14.9 %residual_back.1 = (f32[1536,1024]{1,0:T(8,128)}, bf16[1536,1024]{1,0:T(8,128)(2,1)}, f32[8,1024]{1,0:T(8,128)}, bf16[4,1536,256]{2,1,0:T(8,128)(2,1)}) custom-call(s32[1]{0:T(128)} %bitcast.refs_0_.place_ref, f32[1536,1024]{1,0:T(8,128)} %get-tuple-element.265.refs_1_, f32[1536,1024]{1,0:T(8,128)} %get-tuple-element.237.refs_2_, ...), custom_call_target="tpu_custom_call" | custom-call | flops 50331648 | bytes 524288 | tf_op jit(solution)/shard_map/residual_back/pallas_call | solution.py:301
  356.6 11.3 %collective-permute-done.16 = bf16[1024,1024]{1,0:T(8,128)(2,1)} collective-permute-done((bf16[1024,1024]{1,0:T(8,128)(2,1)}, bf16[1024,1024]{1,0:T(8,128)(2,1)}, u32[]{:S(2)}, u32[]{:S(2)}) %collective-permute-start.16) | collective-permute-done | bytes 2097184 | tf_op jit(solution)/shard_map/ppermute | solution.py:715
  371.7 26.4 %weight_back.1 = (bf16[1024,1024]{1,0:T(8,128)(2,1)}, bf16[1024,1024]{1,0:T(8,128)(2,1)}, bf16[1024,1024]{1,0:T(8,128)(2,1)}, bf16[1024,1024]{1,0:T(8,128)(2,1)}...) custom-call(bf16[1536,1024]{1,0:T(8,128)(2,1)} %get-tuple-element.23, ...), custom_call_target="tpu_custom_call" | custom-call | flops 251658240 | bytes 1572864 | tf_op jit(solution)/shard_map/weight_back/pallas_call | solution.py:580
  398.1 10.4 %all-to-all-done.3.grad_ref = bf16[4,1536,256]{2,1,0:T(8,128)(2,1)S(1)} async-done(((bf16[4,1536,256]{2,1,0:T(8,128)(2,1)}), bf16[4,1536,256]{2,1,0:T(8,128)(2,1)S(1)}, u32[]{:S(2)}, u32[]{:S(2)}) %all-to-all-start.3) | async-done | bytes 3145760 | tf_op jit(solution)/shard_map/all_to_all | solution.py:726
  429.0 47.0 %attend_back.4.refs_2_ = bf16[3,2048,256]{2,1,0:T(8,128)(2,1)} custom-call(bf16[3,2048,256]{2,1,0:T(8,128)(2,1)} %fusion.9.q_ref.k_ref.v_ref, bf16[3,2048,256]{2,1,0:T(8,128)(2,1)} %fusion.9.q_ref.k_ref.v_ref, bf16[3,2048,256]{2,1,0:T(8,128)(2,1)} %fusion.9.q_ref.k_ref.v_ref, bf16[2048,256]{1,0:T(8,128)(2,1)} %get-tuple-element.209.out_ref, ...), custom_call_target="tpu_custom_call" | custom-call | flops 335544320 | bytes 524288 | tf_op jit(solution)/shard_map/attend_back/pallas_call | solution.py:169
  484.6 13.2 %project_back.3 = (bf16[512,1024]{1,0:T(8,128)(2,1)}, bf16[512,1024]{1,0:T(8,128)(2,1)}, bf16[512,1024]{1,0:T(8,128)(2,1)}, bf16[512,1024]{1,0:T(8,128)(2,1)}, f...) custom-call(s32[1]{0:T(128)} %bitcast.refs_0_.place_ref, bf16[2048,1024]{1,0:T(8,128)(2,1)} %all-gather.4.cloned.1.call-done.refs_1_, ...), custom_call_target="tpu_custom_call" | custom-call | flops 100663296 | bytes 524288 | tf_op jit(solution)/shard_map/project_back/pallas_call | solution.py:662
  509.7 47.3 %attend_back.5.refs_2_ = bf16[3,2048,256]{2,1,0:T(8,128)(2,1)} custom-call(bf16[3,2048,256]{2,1,0:T(8,128)(2,1)} %fusion.10.q_ref.k_ref.v_ref, bf16[3,2048,256]{2,1,0:T(8,128)(2,1)} %fusion.10.q_ref.k_ref.v_ref, bf16[3,2048,256]{2,1,0:T(8,128)(2,1)} %fusion.10.q_ref.k_ref.v_ref, bf16[2048,256]{1,0:T(8,128)(2,1)} %get-tuple-element.215.out_ref, ...), custom_call_target="tpu_custom_call" | custom-call | flops 335544320 | bytes 524288 | tf_op jit(solution)/shard_map/attend_back/pallas_call | solution.py:169
  562.7 14.0 %project_back.4 = (bf16[512,1024]{1,0:T(8,128)(2,1)}, bf16[512,1024]{1,0:T(8,128)(2,1)}, bf16[512,1024]{1,0:T(8,128)(2,1)}, bf16[512,1024]{1,0:T(8,128)(2,1)}, f...) custom-call(s32[1]{0:T(128)} %bitcast.refs_0_.place_ref, ...), custom_call_target="tpu_custom_call", output_to_operand_aliasing={{4}: (4, {}), {5}: (5, {})} | custom-call | flops 100663296 | bytes 524288 | tf_op jit(solution)/shard_map/project_back/pallas_call | solution.py:662
  585.2 47.0 %attend_back.3.refs_2_.dqkv_ref = bf16[3,2048,256]{2,1,0:T(8,128)(2,1)} custom-call(bf16[3,2048,256]{2,1,0:T(8,128)(2,1)} %fusion.11.q_ref.k_ref.v_ref, bf16[3,2048,256]{2,1,0:T(8,128)(2,1)} %fusion.11.q_ref.k_ref.v_ref, bf16[3,2048,256]{2,1,0:T(8,128)(2,1)} %fusion.11.q_ref.k_ref.v_ref, bf16[2048,256]{1,0:T(8,128)(2,1)} %get-tuple-element.227.out_ref, ...), custom_call_target="tpu_custom_call" | custom-call | flops 335544320 | bytes 524288 | tf_op jit(solution)/shard_map/attend_back/pallas_call | solution.py:169
  637.0 10.9 %project_back.5 = (f32[3,1024,256]{2,1,0:T(8,128)}, f32[8,256]{1,0:T(8,128)}, bf16[3,1040,256]{2,1,0:T(8,128)(2,1)}) custom-call(s32[1]{0:T(128)} %bitcast.refs_0_.place_ref, bf16[2048,1024]{1,0:T(8,128)(2,1)} %all-gather.8.cloned.1.call-done.refs_1_, ...), custom_call_target="tpu_custom_call", output_to_operand_aliasing={{0}: (4, {}), {1}: (5, {})} | custom-call | flops 100663296 | bytes 524288 | tf_op jit(solution)/shard_map/project_back/pallas_call | solution.py:662
  654.7 8.3 %project_rows.1 = (bf16[512,1024]{1,0:T(8,128)(2,1)}, bf16[512,1024]{1,0:T(8,128)(2,1)}, bf16[512,1024]{1,0:T(8,128)(2,1)}, bf16[512,1024]{1,0:T(8,128)(2,1)}) custom-call(s32[1]{0:T(128)} %bitcast.refs_0_.place_ref, bf16[3,2048,256]{2,1,0:T(8,128)(2,1)} %attend_back.3.refs_2_.dqkv_ref, bf16[3,1024,256]{2,1,0:T(8,128)(2,1)} %weight_ref.1), custom_call_target="tpu_custom_call" | custom-call | flops 50331648 | bytes 524288 | tf_op jit(solution)/shard_map/project_rows/pallas_call | solution.py:695
  684.0 8.1 %collective-permute-done.37.refs_5_ = bf16[512,1024]{1,0:T(8,128)(2,1)} collective-permute-done((bf16[512,1024]{1,0:T(8,128)(2,1)}, bf16[512,1024]{1,0:T(8,128)(2,1)}, u32[]{:S(2)}, u32[]{:S(2)}) %collective-permute-start.37) | collective-permute-done | bytes 1048608 | tf_op jit(solution)/shard_map/ppermute | solution.py:715
  724.9 15.9 %all-reduce.4.cloned.1.call-done = bf16[3,1040,256]{2,1,0:T(8,128)(2,1)} async-done(((bf16[3,1040,256]{2,1,0:T(8,128)(2,1)}), bf16[3,1040,256]{2,1,0:T(8,128)(2,1)}) %all-reduce.4.cloned.1.call-update) | async-done | bytes 1597456 | tf_op jit(solution)/shard_map/psum | solution.py:1011
  (299 shorter events, 237.6 us)
Async XLA Ops:
  7.2 40.2 %all-gather.4.cloned.1.call-start = ((), (), s32[]{:S(2)}) async-start(), calls=%async_computation.4 | async-start | bytes 5242880 | tf_op jit(solution)/shard_map/all_gather | solution.py:865
  10.1 74.0 %all-gather.6.cloned.1.call-start = ((), (), s32[]{:S(2)}) async-start(), calls=%async_computation.5 | async-start | bytes 5242880 | tf_op jit(solution)/shard_map/all_gather | solution.py:865
  47.4 78.7 %all-gather.8.cloned.1.call-start = ((), (), s32[]{:S(2)}) async-start(), calls=%async_computation.6 | async-start | bytes 5242880 | tf_op jit(solution)/shard_map/all_gather | solution.py:865
  84.1 42.0 %all-to-all-start = ((bf16[4,512,256]{2,1,0:T(8,128)(2,1)}), bf16[4,512,256]{2,1,0:T(8,128)(2,1)S(1)}, u32[]{:S(2)}, u32[]{:S(2)}) async-start(bf16[4,512,256]{2,1,0:T(8,128)(2,1)} %bitcast.59), calls=%async_computation | async-start | bytes 2097152 | tf_op jit(solution)/shard_map/all_to_all | solution.py:726
  128.8 48.8 %collective-permute-start.5 = (bf16[512,1024]{1,0:T(8,128)(2,1)}, bf16[512,1024]{1,0:T(8,128)(2,1)}, u32[]{:S(2)}, u32[]{:S(2)}) collective-permute-start(bf16[512,1024]{1,0:T(8,128)(2,1)} %constant_dynamic-slice_fusion.8), channel_id=1, source_target_pairs={{0,2},{1,3},{2,0},{3,1},{4,6},{5,7},{6,4},{7,5},{8,10},{9,11},{10,... | collective-permute-start | bytes 3145736 | tf_op jit(solution)/shard_map/ppermute | solution.py:715
  129.1 39.2 %all-to-all-start.1 = ((bf16[4,512,256]{2,1,0:T(8,128)(2,1)}), bf16[4,512,256]{2,1,0:T(8,128)(2,1)S(1)}, u32[]{:S(2)}, u32[]{:S(2)}) async-start(bf16[4,512,256]{2,1,0:T(8,128)(2,1)} %bitcast.58), calls=%async_computation.1 | async-start | bytes 2097152 | tf_op jit(solution)/shard_map/all_to_all | solution.py:726
  132.8 44.7 %collective-permute-start.4 = (bf16[256,1024]{1,0:T(8,128)(2,1)S(1)}, bf16[256,1024]{1,0:T(8,128)(2,1)}, u32[]{:S(2)}, u32[]{:S(2)}) collective-permute-start(bf16[256,1024]{1,0:T(8,128)(2,1)S(1)} %copy-done.19), channel_id=1, source_target_pairs={{0,2},{1,3},{2,0},{3,1},{4,6},{5,7},{6,4},{7,5},{8,10},{9,11},{10,... | collective-permute-start | bytes 1572872 | tf_op jit(solution)/shard_map/ppermute | solution.py:715
  137.2 63.9 %collective-permute-start.7 = (bf16[512,1024]{1,0:T(8,128)(2,1)}, bf16[512,1024]{1,0:T(8,128)(2,1)}, u32[]{:S(2)}, u32[]{:S(2)}) collective-permute-start(bf16[512,1024]{1,0:T(8,128)(2,1)} %constant_dynamic-slice_fusion.7), channel_id=1, source_target_pairs={{0,2},{1,3},{2,0},{3,1},{4,6},{5,7},{6,4},{7,5},{8,10},{9,11},{10,... | collective-permute-start | bytes 3145736 | tf_op jit(solution)/shard_map/ppermute | solution.py:715
  177.6 38.2 %collective-permute-start.8 = (bf16[512,1024]{1,0:T(8,128)(2,1)}, bf16[512,1024]{1,0:T(8,128)(2,1)}, u32[]{:S(2)}, u32[]{:S(2)}) collective-permute-start(bf16[512,1024]{1,0:T(8,128)(2,1)} %collective-permute-done.5), channel_id=1, source_target_pairs={{0,4},{4,0},{8,12},{12,8},{16,20},{20,16},{24,28},{28,24},{1,5},{5... | collective-permute-start | bytes 3145736 | tf_op jit(solution)/shard_map/ppermute | solution.py:801
  217.1 41.2 %collective-permute-start.10 = (bf16[1024,1024]{1,0:T(8,128)(2,1)S(1)}, bf16[1024,1024]{1,0:T(8,128)(2,1)}, u32[]{:S(2)}, u32[]{:S(2)}) collective-permute-start(bf16[1024,1024]{1,0:T(8,128)(2,1)S(1)} %constant_dynamic-update-slice_fusion.14.refs_2_), channel_id=1, source_target_pairs={{0,1},{1,0},{2,3},{3,2},{4,5},{5,4},{6,7},{7,6},{8,9},{9,8},{10,11... | collective-permute-start | bytes 6291464 | tf_op jit(solution)/shard_map/ppermute | solution.py:715
  217.2 41.1 %collective-permute-start.11 = (bf16[512,1024]{1,0:T(8,128)(2,1)}, bf16[512,1024]{1,0:T(8,128)(2,1)S(1)}, u32[]{:S(2)}, u32[]{:S(2)}) collective-permute-start(bf16[512,1024]{1,0:T(8,128)(2,1)} %collective-permute-done.7), channel_id=1, source_target_pairs={{0,4},{4,0},{8,12},{12,8},{16,20},{20,16},{24,28},{28,24},{1,5},{5... | collective-permute-start | bytes 3145736 | tf_op jit(solution)/shard_map/ppermute | solution.py:801
  320.0 48.0 %collective-permute-start.16 = (bf16[1024,1024]{1,0:T(8,128)(2,1)}, bf16[1024,1024]{1,0:T(8,128)(2,1)}, u32[]{:S(2)}, u32[]{:S(2)}) collective-permute-start(bf16[1024,1024]{1,0:T(8,128)(2,1)} %add_convert_fusion.6), channel_id=1, source_target_pairs={{0,2},{1,3},{2,0},{3,1},{4,6},{5,7},{6,4},{7,5},{8,10},{9,11},{10,... | collective-permute-start | bytes 6291464 | tf_op jit(solution)/shard_map/ppermute | solution.py:715
  368.0 40.6 %all-to-all-start.3 = ((bf16[4,1536,256]{2,1,0:T(8,128)(2,1)}), bf16[4,1536,256]{2,1,0:T(8,128)(2,1)S(1)}, u32[]{:S(2)}, u32[]{:S(2)}) async-start(bf16[4,1536,256]{2,1,0:T(8,128)(2,1)} %get-tuple-element.278), calls=%async_computation.3 | async-start | bytes 6291456 | tf_op jit(solution)/shard_map/all_to_all | solution.py:726
  371.7 264.0 %all-reduce.6.cloned.1.call-start = ((), (), s32[]{:S(2)}) async-start(), calls=%async_computation.8 | async-start | bytes 5242880 | tf_op jit(solution)/shard_map/psum | solution.py:994
  421.4 54.7 %collective-permute-start.21 = (bf16[1024,1024]{1,0:T(8,128)(2,1)}, bf16[1024,1024]{1,0:T(8,128)(2,1)}, u32[]{:S(2)}, u32[]{:S(2)}) collective-permute-start(bf16[1024,1024]{1,0:T(8,128)(2,1)} %add_convert_fusion.5), channel_id=1, source_target_pairs={{0,2},{1,3},{2,0},{3,1},{4,6},{5,7},{6,4},{7,5},{8,10},{9,11},{10,... | collective-permute-start | bytes 6291464 | tf_op jit(solution)/shard_map/ppermute | solution.py:715
  425.5 55.1 %collective-permute-start.23 = (bf16[512,1024]{1,0:T(8,128)(2,1)S(1)}, bf16[512,1024]{1,0:T(8,128)(2,1)}, u32[]{:S(2)}, u32[]{:S(2)}) collective-permute-start(bf16[512,1024]{1,0:T(8,128)(2,1)S(1)} %constant_dynamic-slice_fusion.6), channel_id=1, source_target_pairs={{0,4},{4,0},{8,12},{12,8},{16,20},{20,16},{24,28},{28,24},{1,5},{5... | collective-permute-start | bytes 3145736 | tf_op jit(solution)/shard_map/ppermute | solution.py:783
  427.2 53.4 %collective-permute-start.22 = (bf16[256,1024]{1,0:T(8,128)(2,1)}, bf16[256,1024]{1,0:T(8,128)(2,1)}, u32[]{:S(2)}, u32[]{:S(2)}) collective-permute-start(bf16[256,1024]{1,0:T(8,128)(2,1)} %add_convert_fusion.13), channel_id=1, source_target_pairs={{0,2},{1,3},{2,0},{3,1},{4,6},{5,7},{6,4},{7,5},{8,10},{9,11},{10,... | collective-permute-start | bytes 1572872 | tf_op jit(solution)/shard_map/ppermute | solution.py:715
  503.0 54.0 %collective-permute-start.26 = (bf16[512,1024]{1,0:T(8,128)(2,1)}, bf16[512,1024]{1,0:T(8,128)(2,1)S(1)}, u32[]{:S(2)}, u32[]{:S(2)}) collective-permute-start(bf16[512,1024]{1,0:T(8,128)(2,1)} %get-tuple-element.311), channel_id=1, source_target_pairs={{0,1},{1,0},{2,3},{3,2},{4,5},{5,4},{6,7},{7,6},{8,9},{9,8},{10,11... | collective-permute-start | bytes 3145736 | tf_op jit(solution)/shard_map/ppermute | solution.py:715
  503.3 53.6 %collective-permute-start.27 = (bf16[512,1024]{1,0:T(8,128)(2,1)}, bf16[512,1024]{1,0:T(8,128)(2,1)}, u32[]{:S(2)}, u32[]{:S(2)}) collective-permute-start(bf16[512,1024]{1,0:T(8,128)(2,1)} %get-tuple-element.312), channel_id=1, source_target_pairs={{0,1},{1,0},{2,3},{3,2},{4,5},{5,4},{6,7},{7,6},{8,9},{9,8},{10,11... | collective-permute-start | bytes 3145736 | tf_op jit(solution)/shard_map/ppermute | solution.py:715
  505.6 235.1 %all-reduce.4.cloned.1.call-start = ((), (), s32[]{:S(2)}) async-start(), calls=%async_computation.7 | async-start | bytes 3194880 | tf_op jit(solution)/shard_map/psum | solution.py:1011
  506.0 51.0 %collective-permute-start.30 = (bf16[128,1024]{1,0:T(8,128)(2,1)S(1)}, bf16[128,1024]{1,0:T(8,128)(2,1)S(1)}, u32[]{:S(2)}, u32[]{:S(2)}) collective-permute-start(bf16[128,1024]{1,0:T(8,128)(2,1)S(1)} %constant_dynamic-slice_fusion), channel_id=1, source_target_pairs={{0,16},{4,20},{8,24},{12,28},{16,0},{20,4},{24,8},{28,12},{1,17},{... | collective-permute-start | bytes 786440 | tf_op jit(solution)/shard_map/ppermute | solution.py:783
  508.4 48.5 %collective-permute-start.29 = (f32[64,128]{1,0:T(8,128)S(1)}, f32[64,128]{1,0:T(8,128)S(1)}, u32[]{:S(2)}, u32[]{:S(2)}) collective-permute-start(f32[64,128]{1,0:T(8,128)S(1)} %add.239), channel_id=1, source_target_pairs={{0,2},{1,3},{2,0},{3,1},{4,6},{5,7},{6,4},{7,5},{8,10},{9,11},{10,... | collective-permute-start | bytes 98312 | tf_op jit(solution)/shard_map/ppermute | solution.py:769
  560.9 74.0 %collective-permute-start.28 = (bf16[512,1024]{1,0:T(8,128)(2,1)S(1)}, bf16[512,1024]{1,0:T(8,128)(2,1)}, u32[]{:S(2)}, u32[]{:S(2)}) collective-permute-start(bf16[512,1024]{1,0:T(8,128)(2,1)S(1)} %add_convert_fusion.9), channel_id=1, source_target_pairs={{0,2},{1,3},{2,0},{3,1},{4,6},{5,7},{6,4},{7,5},{8,10},{9,11},{10,... | collective-permute-start | bytes 3145736 | tf_op jit(solution)/shard_map/ppermute | solution.py:715
  577.8 58.4 %collective-permute-start.34 = (bf16[256,1024]{1,0:T(8,128)(2,1)S(1)}, bf16[256,1024]{1,0:T(8,128)(2,1)S(1)}, u32[]{:S(2)}, u32[]{:S(2)}) collective-permute-start(bf16[256,1024]{1,0:T(8,128)(2,1)S(1)} %constant_dynamic-update-slice_fusion.10), channel_id=1, source_target_pairs={{0,8},{4,12},{8,0},{12,4},{16,24},{20,28},{24,16},{28,20},{1,9},{5... | collective-permute-start | bytes 1572872 | tf_op jit(solution)/shard_map/ppermute | solution.py:786
  (76 other events, 1150.8 us)
Sparse Core Ops, SparseCore 0:
  10.2 37.1 all-gather.3
  49.5 34.4 all-gather.5
  86.2 39.9 all-gather.7
  505.8 129.8 all-reduce.5
  648.0 92.7 all-reduce.3

commit v6 on v5

--- a/solution.py
+++ b/solution.py
@@ -370,6 +370,33 @@
         cost_estimate=hint(0, rows * model),
         name="input_back",
     )(*operands)
+
+
+def layer_out(total, residual, down_bias, valid, shape):
+    slots, rows, model = shape
+    block = largest_block(rows, 256)
+    steps = rows // block
+
+    def body(total_ref, residual_ref, bias_ref, valid_ref, out_ref):
+        value = residual_ref[...] + total_ref[...] + bias_ref[...]
+        out_ref[...] = (value * valid_ref[pl.program_id(0) // steps]).astype(bf16)
+
+    row_spec = pl.BlockSpec((block, model), lambda i: (i, 0))
+    return pl.pallas_call(
+        body,
+        grid=(slots * steps,),
+        in_specs=[
+            row_spec,
+            row_spec,
+            pl.BlockSpec((1, model), lambda i: (0, 0)),
+            pl.BlockSpec(memory_space=pltpu.SMEM),
+        ],
+        out_specs=pl.BlockSpec((None, block, model), lambda i: (i // steps, i % steps, 0)),
+        out_shape=jax.ShapeDtypeStruct(shape, bf16),
+        compiler_params=params(),
+        cost_estimate=hint(0, rows * model),
+        name="layer_out",
+    )(total, residual, down_bias, valid)
 
 
 def mlp_forward(normed, cot, ups, biases, downs, total):
@@ -843,7 +870,6 @@
         own_valid = lax.dynamic_slice_in_dim(valid_all, own_start, slot_count)
         all_rows = slot_count * own_rows
         row_scale = jnp.repeat(own_scale, own_rows)[:, None]
-        row_valid = jnp.repeat(own_valid, own_rows)[:, None]
         gain_row, shift_row, mlp_gain_row, mlp_shift_row, out_bias_row = (
             value[None, :] for value in (attn_gain, attn_shift, mlp_gain, mlp_shift, out_bias)
         )
@@ -871,7 +897,7 @@
         early = None
         if square:
             early = cot_back(cot_low, [down_projection_weight, weights_near[2]])
-            every, early = tie(every, early)
+            every, (early, normed) = tie(every, (early, normed))
         qkvs, attended, lses, heads_own, normed_every = [], [], [], [], []
         for i in range(slot_count):
             last = i == slot_count - 1
@@ -945,7 +971,7 @@
             )
             slopes.append(slope)
             down_grads += grads
-        output = ((residual + total + down_bias) * row_valid).astype(bf16)
+        layer_sum = total
 
         cot_late, down_grads = tie(cot_low, down_grads)
         before = None
@@ -970,7 +996,8 @@
         down_sum, pieces = sum_far(down_stage, pieces)
         grad_attended = exchange(pieces)
         weight_grads = weight_back(normed_mlp, pre_grad, attended_rows, grad_low, tensor_size)
-        weight_grads, grad_attended = tie(weight_grads, grad_attended)
+        weight_grads = list(weight_grads)
+        weight_grads[0], grad_attended = tie(weight_grads[0], grad_attended)
         up_grads, out_grads = weight_grads[:tensor_size], weight_grads[tensor_size:]
 
         (up_stage, out_stage), grad_attended = sums_near([up_grads, out_grads], grad_attended)
@@ -1007,8 +1034,9 @@
                     down_sum, partial = ring_step(down_sum, ring.pop(0), partial)
             else:
                 *sums, qkv_low = results
-                qkv_low, (dqkv, grad_residual) = tie(qkv_low, (dqkv, grad_residual))
+                qkv_low, (dqkv, grad_residual, layer_sum) = tie(qkv_low, (dqkv, grad_residual, layer_sum))
                 qkv_all = lax.psum(qkv_low, "dp")
+                output = layer_out(layer_sum, residual, down_bias[None, :], own_valid, patches.shape)
                 partial = project_rows(place, dqkv, query_key_value_weight, tensor_size)
                 if i >= 1:
                     grad_normed[i - 1], partial = sum_near(grad_normed[i - 1], partial)
@@ -1047,7 +1075,7 @@
         gain_all = (raw[0] * inverse - attn_shift * shift_all) / attn_gain
         columns = columns * inverse
         return (
-            output.reshape(patches.shape),
+            output,
             grad_inputs,
             weight_grad * inverse,
             jnp.stack([columns[0], columns[2]]),

time: 760 us -> 754 us (level)
  Pallas kernels: 457 us -> 465 us
  waiting for transfers between devices: 124 us -> 116 us
    ppermute x30, waiting for transfers between devices: 52.1 us -> 17.9 us  [swap(): lax.ppermute(value, 'tensor', [(i, i ^ bits) for i in range(tensor_size)])]
    ppermute x3, waiting for transfers between devices: 7.17 us -> 20.5 us  [ring_step(): anchor, received = tie(anchor, lax.ppermute(value, 'dp', pairs))]
  transfers between devices with their start and end apart: 57 -> 57, of which waited for: 21 -> 16; matrix products, arithmetic and copies ran while one was open for 11% -> 10% of each run, Pallas kernels for 56% -> 57%
where the time goes in v6:
time: 754 us; the launch traced here: 746 us
  Pallas kernels  465 us (62%)
  waiting for transfers between devices  116 us (15%)
  other arithmetic  52.1 us (7%)
  starting transfers between devices  50.6 us (7%)
  local copies, waits for them, and re-layouts  24.5 us (3%)
  matrix products  21.9 us (3%)
  between operations  15.5 us (2%)
    pallas_call x3, Pallas kernels, attend_back(): pl.pallas_call(body, grid=(pairs, kblocks), in_specs=[pl.BlockSpec((None,...  141 us
    pallas_call x3, Pallas kernels, attend(): pl.pallas_call(body, grid=(pairs, length // qblock), in_specs=[pl.BlockSp...  72.5 us
    pallas_call x2, Pallas kernels, mlp_forward(): pl.pallas_call(body, grid=(steps,), in_specs=in_specs, out_specs=[slope_s...  71.4 us
    pallas_call x3, Pallas kernels, project_back(): pl.pallas_call(kernel, grid=(steps,), in_specs=in_specs, out_specs=out_sp...  38.7 us
    pallas_call x2, Pallas kernels, mlp_backward(): pl.pallas_call(body, grid=(rows // block,), in_specs=in_specs, out_specs=...  35 us
    pallas_call x1, Pallas kernels, weight_back(): pl.pallas_call(body, grid=(steps,), in_specs=[row_spec, pl.BlockSpec((blo...  26.4 us
    all_to_all x4, waiting for transfers between devices, exchange(): return lax.all_to_all(stacked, 'tensor', 0, 0)  26.4 us
    all_gather x3, waiting for transfers between devices, gather_rows(): return lax.all_gather(own, 'tensor', axis=0, tiled=True)  25.5 us
  transfers between devices with their start and end apart: 57, of which 16 were waited for; matrix products, arithmetic and copies ran while one was open for 10% of the time, Pallas kernels for 57%

profile of v6, /device:TPU:0, one launch (start us, length us, event | category | flops | bytes accessed | tf_op | source)
XLA Modules:
  0.0 746.2 jit_solution(16972598990393691540)
XLA Ops:
  21.3 11.5 %cot_back.1.refs_0_ = bf16[1536,2048]{1,0:T(8,128)(2,1)} custom-call(bf16[1536,1024]{1,0:T(8,128)(2,1)} %fusion.cot_ref.refs_1_.refs_0_, bf16[1024,1024]{1,0:T(8,128)(2,1)} %refs_6_, bf16[1024,1024]{1,0:T(8,128)(2,1)} %collective-permute-done.refs_1_.refs_7_), custom_call_target="tpu_custom_call" | custom-call | flops 100663296 | bytes 1572864 | tf_op jit(solution)/shard_map/cot_back/pallas_call | solution.py:494
  32.8 14.6 %all-gather.4.cloned.1.call-done.refs_1_ = bf16[2048,1024]{1,0:T(8,128)(2,1)} async-done(((bf16[512,1024]{1,0:T(8,128)(2,1)}), bf16[2048,1024]{1,0:T(8,128)(2,1)}) %all-gather.4.cloned.1.call-update) | async-done | bytes 4194320 | tf_op jit(solution)/shard_map/all_gather | solution.py:891
  55.6 24.6 %attend.3 = (bf16[2048,256]{1,0:T(8,128)(2,1)}, f32[2,2,2048]{2,1,0:T(2,128)}) custom-call(bf16[3,2048,256]{2,1,0:T(8,128)(2,1)} %fusion.9.q_ref.k_ref.v_ref, bf16[3,2048,256]{2,1,0:T(8,128)(2,1)} %fusion.9.q_ref.k_ref.v_ref, bf16[3,2048,256]{2,1,0:T(8,128)(2,1)} %fusion.9.q_ref.k_ref.v_ref), custom_call_target="tpu_custom_call" | custom-call | flops 134217728 | bytes 524288 | tf_op jit(solution)/shard_map/attend/pallas_call | solution.py:76
  94.9 24.1 %attend.4 = (bf16[2048,256]{1,0:T(8,128)(2,1)}, f32[2,2,2048]{2,1,0:T(2,128)}) custom-call(bf16[3,2048,256]{2,1,0:T(8,128)(2,1)} %fusion.10.q_ref.k_ref.v_ref, bf16[3,2048,256]{2,1,0:T(8,128)(2,1)} %fusion.10.q_ref.k_ref.v_ref, bf16[3,2048,256]{2,1,0:T(8,128)(2,1)} %fusion.10.q_ref.k_ref.v_ref), custom_call_target="tpu_custom_call" | custom-call | flops 134217728 | bytes 524288 | tf_op jit(solution)/shard_map/attend/pallas_call | solution.py:76
  146.1 23.8 %attend.5 = (bf16[2048,256]{1,0:T(8,128)(2,1)}, f32[2,2,2048]{2,1,0:T(2,128)}) custom-call(bf16[3,2048,256]{2,1,0:T(8,128)(2,1)} %fusion.11.q_ref.k_ref.v_ref, bf16[3,2048,256]{2,1,0:T(8,128)(2,1)} %fusion.11.q_ref.k_ref.v_ref, bf16[3,2048,256]{2,1,0:T(8,128)(2,1)} %fusion.11.q_ref.k_ref.v_ref), custom_call_target="tpu_custom_call" | custom-call | flops 134217728 | bytes 524288 | tf_op jit(solution)/shard_map/attend/pallas_call | solution.py:76
  201.1 9.5 %all-to-all-done.2.refs_6_ = bf16[4,512,256]{2,1,0:T(8,128)(2,1)} async-done(((bf16[4,512,256]{2,1,0:T(8,128)(2,1)}), bf16[4,512,256]{2,1,0:T(8,128)(2,1)}, u32[]{:S(2)}, u32[]{:S(2)}) %all-to-all-start.2) | async-done | bytes 1048608 | tf_op jit(solution)/shard_map/all_to_all | solution.py:753
  223.3 34.9 %mlp_forward.2 = (bf16[1536,2048]{1,0:T(8,128)(2,1)}, f32[1536,1024]{1,0:T(8,128)}, bf16[1024,1024]{1,0:T(8,128)(2,1)}, bf16[1024,1024]{1,0:T(8,128)(2,1)}) custom-call(bf16[1536,1024]{1,0:T(8,128)(2,1)} %get-tuple-element.235.refs_0_.x_ref, bf16[1536,1024]{1,0:T(8,128)(2,1)} %fusion.cot_ref.refs_1_.refs_0_, bf16[1024,1024]{1,0:T(8,128)(2,1)} %refs_2_.1, ...), custom_call_target="tpu_custom_call" | custom-call | flops 301989888 | bytes 1572864 | tf_op jit(solution)/shard_map/mlp_forward/pallas_call | solution.py:466
  265.5 36.5 %mlp_forward.3 = (bf16[1536,2048]{1,0:T(8,128)(2,1)}, f32[1536,1024]{1,0:T(8,128)}, bf16[1024,1024]{1,0:T(8,128)(2,1)}, bf16[1024,1024]{1,0:T(8,128)(2,1)}) custom-call(bf16[1536,1024]{1,0:T(8,128)(2,1)} %get-tuple-element.235.refs_0_.x_ref, bf16[1536,1024]{1,0:T(8,128)(2,1)} %fusion.cot_ref.refs_1_.refs_0_, ...), custom_call_target="tpu_custom_call", output_to_operand_aliasing={{1}: (8, {})} | custom-call | flops 301989888 | bytes 1572864 | tf_op jit(solution)/shard_map/mlp_forward/pallas_call | solution.py:466
  302.5 13.5 %mlp_backward.2 = (bf16[1536,4096]{1,0:T(8,128)(2,1)}, f32[1536,1024]{1,0:T(8,128)}, f32[1,2048]{1,0:T(1,128)}) custom-call(bf16[1536,2048]{1,0:T(8,128)(2,1)} %cot_back.1.refs_0_, bf16[1536,2048]{1,0:T(8,128)(2,1)} %get-tuple-element.252.refs_1_, bf16[1024,1024]{1,0:T(8,128)(2,1)} %refs_2_.1, bf16[1024,1024]{1,0:T(8,128)(2,1)} %collective-permute-done.2.refs_3_), custom_call_target="tpu_custom_call" | custom-call | flops 201326592 | bytes 1572864 | tf_op jit(solution)/shard_map/mlp_backward/pallas_call | solution.py:552
  320.3 21.5 %mlp_backward.3 = (bf16[1536,4096]{1,0:T(8,128)(2,1)}, f32[1536,1024]{1,0:T(8,128)}, f32[1,2048]{1,0:T(1,128)}) custom-call(bf16[1536,1024]{1,0:T(8,128)(2,1)} %fusion.cot_ref.refs_1_.refs_0_, bf16[1536,2048]{1,0:T(8,128)(2,1)} %get-tuple-element.250.refs_1_, bf16[1024,1024]{1,0:T(8,128)(2,1)} %copy-done.6, ...), custom_call_target="tpu_custom_call", output_to_operand_aliasing={{0}: (6, {}), {1}: (7, {})} | custom-call | flops 201326592 | bytes 1572864 | tf_op jit(solution)/shard_map/mlp_backward/pallas_call | solution.py:552
  341.8 14.9 %residual_back.1 = (f32[1536,1024]{1,0:T(8,128)}, bf16[1536,1024]{1,0:T(8,128)(2,1)}, f32[8,1024]{1,0:T(8,128)}, bf16[4,1536,256]{2,1,0:T(8,128)(2,1)}) custom-call(s32[1]{0:T(128)} %bitcast.refs_0_.place_ref, f32[1536,1024]{1,0:T(8,128)} %get-tuple-element.261.refs_1_, f32[1536,1024]{1,0:T(8,128)} %get-tuple-element.262.refs_2_.residual_ref, ...), custom_call_target="tpu_custom_call" | custom-call | flops 50331648 | bytes 524288 | tf_op jit(solution)/shard_map/residual_back/pallas_call | solution.py:301
  356.7 11.3 %collective-permute-done.16 = bf16[1024,1024]{1,0:T(8,128)(2,1)} collective-permute-done((bf16[1024,1024]{1,0:T(8,128)(2,1)}, bf16[1024,1024]{1,0:T(8,128)(2,1)}, u32[]{:S(2)}, u32[]{:S(2)}) %collective-permute-start.16) | collective-permute-done | bytes 2097184 | tf_op jit(solution)/shard_map/ppermute | solution.py:742
  371.7 26.4 %weight_back.1 = (bf16[1024,1024]{1,0:T(8,128)(2,1)}, bf16[1024,1024]{1,0:T(8,128)(2,1)}, bf16[1024,1024]{1,0:T(8,128)(2,1)}, bf16[1024,1024]{1,0:T(8,128)(2,1)}...) custom-call(bf16[1536,1024]{1,0:T(8,128)(2,1)} %get-tuple-element.23, ...), custom_call_target="tpu_custom_call" | custom-call | flops 251658240 | bytes 1572864 | tf_op jit(solution)/shard_map/weight_back/pallas_call | solution.py:607
  399.1 9.4 %all-to-all-done.3.grad_ref = bf16[4,1536,256]{2,1,0:T(8,128)(2,1)S(1)} async-done(((bf16[4,1536,256]{2,1,0:T(8,128)(2,1)}), bf16[4,1536,256]{2,1,0:T(8,128)(2,1)S(1)}, u32[]{:S(2)}, u32[]{:S(2)}) %all-to-all-start.3) | async-done | bytes 3145760 | tf_op jit(solution)/shard_map/all_to_all | solution.py:753
  423.3 47.0 %attend_back.4.refs_2_ = bf16[3,2048,256]{2,1,0:T(8,128)(2,1)} custom-call(bf16[3,2048,256]{2,1,0:T(8,128)(2,1)} %fusion.9.q_ref.k_ref.v_ref, bf16[3,2048,256]{2,1,0:T(8,128)(2,1)} %fusion.9.q_ref.k_ref.v_ref, bf16[3,2048,256]{2,1,0:T(8,128)(2,1)} %fusion.9.q_ref.k_ref.v_ref, bf16[2048,256]{1,0:T(8,128)(2,1)} %get-tuple-element.209.out_ref, ...), custom_call_target="tpu_custom_call" | custom-call | flops 335544320 | bytes 524288 | tf_op jit(solution)/shard_map/attend_back/pallas_call | solution.py:169
  483.8 13.4 %project_back.3 = (bf16[512,1024]{1,0:T(8,128)(2,1)}, bf16[512,1024]{1,0:T(8,128)(2,1)}, bf16[512,1024]{1,0:T(8,128)(2,1)}, bf16[512,1024]{1,0:T(8,128)(2,1)}, f...) custom-call(s32[1]{0:T(128)} %bitcast.refs_0_.place_ref, bf16[2048,1024]{1,0:T(8,128)(2,1)} %all-gather.4.cloned.1.call-done.refs_1_, ...), custom_call_target="tpu_custom_call" | custom-call | flops 100663296 | bytes 524288 | tf_op jit(solution)/shard_map/project_back/pallas_call | solution.py:689
  501.1 46.9 %attend_back.5.refs_2_ = bf16[3,2048,256]{2,1,0:T(8,128)(2,1)} custom-call(bf16[3,2048,256]{2,1,0:T(8,128)(2,1)} %fusion.10.q_ref.k_ref.v_ref, bf16[3,2048,256]{2,1,0:T(8,128)(2,1)} %fusion.10.q_ref.k_ref.v_ref, bf16[3,2048,256]{2,1,0:T(8,128)(2,1)} %fusion.10.q_ref.k_ref.v_ref, bf16[2048,256]{1,0:T(8,128)(2,1)} %get-tuple-element.211.out_ref, ...), custom_call_target="tpu_custom_call" | custom-call | flops 335544320 | bytes 524288 | tf_op jit(solution)/shard_map/attend_back/pallas_call | solution.py:169
  553.7 14.6 %project_back.4 = (bf16[512,1024]{1,0:T(8,128)(2,1)}, bf16[512,1024]{1,0:T(8,128)(2,1)}, bf16[512,1024]{1,0:T(8,128)(2,1)}, bf16[512,1024]{1,0:T(8,128)(2,1)}, f...) custom-call(s32[1]{0:T(128)} %bitcast.refs_0_.place_ref, ...), custom_call_target="tpu_custom_call", output_to_operand_aliasing={{4}: (4, {}), {5}: (5, {})} | custom-call | flops 100663296 | bytes 524288 | tf_op jit(solution)/shard_map/project_back/pallas_call | solution.py:689
  575.6 47.1 %attend_back.3.refs_2_.dqkv_ref = bf16[3,2048,256]{2,1,0:T(8,128)(2,1)} custom-call(bf16[3,2048,256]{2,1,0:T(8,128)(2,1)} %fusion.11.q_ref.k_ref.v_ref, bf16[3,2048,256]{2,1,0:T(8,128)(2,1)} %fusion.11.q_ref.k_ref.v_ref, bf16[3,2048,256]{2,1,0:T(8,128)(2,1)} %fusion.11.q_ref.k_ref.v_ref, bf16[2048,256]{1,0:T(8,128)(2,1)} %get-tuple-element.215.out_ref, ...), custom_call_target="tpu_custom_call" | custom-call | flops 335544320 | bytes 524288 | tf_op jit(solution)/shard_map/attend_back/pallas_call | solution.py:169
  626.7 10.7 %project_back.5 = (f32[3,1024,256]{2,1,0:T(8,128)}, f32[8,256]{1,0:T(8,128)}, bf16[3,1040,256]{2,1,0:T(8,128)(2,1)}) custom-call(s32[1]{0:T(128)} %bitcast.refs_0_.place_ref, bf16[2048,1024]{1,0:T(8,128)(2,1)} %all-gather.8.cloned.1.call-done.refs_1_, ...), custom_call_target="tpu_custom_call", output_to_operand_aliasing={{0}: (4, {}), {1}: (5, {})} | custom-call | flops 100663296 | bytes 524288 | tf_op jit(solution)/shard_map/project_back/pallas_call | solution.py:689
  643.0 8.6 %project_rows.1 = (bf16[512,1024]{1,0:T(8,128)(2,1)}, bf16[512,1024]{1,0:T(8,128)(2,1)}, bf16[512,1024]{1,0:T(8,128)(2,1)}, bf16[512,1024]{1,0:T(8,128)(2,1)}) custom-call(s32[1]{0:T(128)} %bitcast.refs_0_.place_ref, bf16[3,2048,256]{2,1,0:T(8,128)(2,1)} %attend_back.3.refs_2_.dqkv_ref, bf16[3,1024,256]{2,1,0:T(8,128)(2,1)} %weight_ref.1), custom_call_target="tpu_custom_call" | custom-call | flops 50331648 | bytes 524288 | tf_op jit(solution)/shard_map/project_rows/pallas_call | solution.py:722
  657.8 7.5 %layer_out.1 = bf16[3,512,1024]{2,1,0:T(8,128)(2,1)} custom-call(f32[1536,1024]{1,0:T(8,128)} %get-tuple-element.338.total_ref, f32[1536,1024]{1,0:T(8,128)} %get-tuple-element.262.refs_2_.residual_ref, f32[1,1024]{1,0:T(1,128)} %bitcast.90, f32[3]{0:T(128)} %dynamic_slice.58.valid_ref), custom_call_target="tpu_custom_call" | custom-call | bytes 524288 | tf_op jit(solution)/shard_map/layer_out/pallas_call | solution.py:385
  685.0 14.7 %collective-permute-done.42 = bf16[512,1024]{1,0:T(8,128)(2,1)S(1)} collective-permute-done((bf16[512,1024]{1,0:T(8,128)(2,1)S(1)}, bf16[512,1024]{1,0:T(8,128)(2,1)S(1)}, u32[]{:S(2)}, u32[]{:S(2)}) %collective-permute-start.42) | collective-permute-done | bytes 1048608 | tf_op jit(solution)/shard_map/ppermute | solution.py:813
  713.9 20.9 %all-reduce.4.cloned.1.call-done = bf16[3,1040,256]{2,1,0:T(8,128)(2,1)} async-done(((bf16[3,1040,256]{2,1,0:T(8,128)(2,1)}), bf16[3,1040,256]{2,1,0:T(8,128)(2,1)}) %all-reduce.4.cloned.1.call-update) | async-done | bytes 1597456 | tf_op jit(solution)/shard_map/psum | solution.py:1038
  (293 shorter events, 222.8 us)
Async XLA Ops:
  7.2 40.2 %all-gather.4.cloned.1.call-start = ((), (), s32[]{:S(2)}) async-start(), calls=%async_computation.4 | async-start | bytes 5242880 | tf_op jit(solution)/shard_map/all_gather | solution.py:891
  9.9 74.1 %all-gather.6.cloned.1.call-start = ((), (), s32[]{:S(2)}) async-start(), calls=%async_computation.5 | async-start | bytes 5242880 | tf_op jit(solution)/shard_map/all_gather | solution.py:891
  47.4 78.7 %all-gather.8.cloned.1.call-start = ((), (), s32[]{:S(2)}) async-start(), calls=%async_computation.6 | async-start | bytes 5242880 | tf_op jit(solution)/shard_map/all_gather | solution.py:891
  84.1 42.0 %all-to-all-start = ((bf16[4,512,256]{2,1,0:T(8,128)(2,1)}), bf16[4,512,256]{2,1,0:T(8,128)(2,1)S(1)}, u32[]{:S(2)}, u32[]{:S(2)}) async-start(bf16[4,512,256]{2,1,0:T(8,128)(2,1)} %bitcast.58), calls=%async_computation | async-start | bytes 2097152 | tf_op jit(solution)/shard_map/all_to_all | solution.py:753
  128.8 48.7 %collective-permute-start.5 = (bf16[512,1024]{1,0:T(8,128)(2,1)}, bf16[512,1024]{1,0:T(8,128)(2,1)}, u32[]{:S(2)}, u32[]{:S(2)}) collective-permute-start(bf16[512,1024]{1,0:T(8,128)(2,1)} %constant_dynamic-slice_fusion.8), channel_id=1, source_target_pairs={{0,2},{1,3},{2,0},{3,1},{4,6},{5,7},{6,4},{7,5},{8,10},{9,11},{10,... | collective-permute-start | bytes 3145736 | tf_op jit(solution)/shard_map/ppermute | solution.py:742
  129.1 48.3 %collective-permute-start.4 = (bf16[256,1024]{1,0:T(8,128)(2,1)S(1)}, bf16[256,1024]{1,0:T(8,128)(2,1)}, u32[]{:S(2)}, u32[]{:S(2)}) collective-permute-start(bf16[256,1024]{1,0:T(8,128)(2,1)S(1)} %copy-done.20), channel_id=1, source_target_pairs={{0,2},{1,3},{2,0},{3,1},{4,6},{5,7},{6,4},{7,5},{8,10},{9,11},{10,... | collective-permute-start | bytes 1572872 | tf_op jit(solution)/shard_map/ppermute | solution.py:742
  130.8 46.6 %all-to-all-start.1 = ((bf16[4,512,256]{2,1,0:T(8,128)(2,1)}), bf16[4,512,256]{2,1,0:T(8,128)(2,1)S(1)}, u32[]{:S(2)}, u32[]{:S(2)}) async-start(bf16[4,512,256]{2,1,0:T(8,128)(2,1)} %bitcast.12), calls=%async_computation.1 | async-start | bytes 2097152 | tf_op jit(solution)/shard_map/all_to_all | solution.py:753
  136.8 64.2 %collective-permute-start.7 = (bf16[512,1024]{1,0:T(8,128)(2,1)}, bf16[512,1024]{1,0:T(8,128)(2,1)}, u32[]{:S(2)}, u32[]{:S(2)}) collective-permute-start(bf16[512,1024]{1,0:T(8,128)(2,1)} %constant_dynamic-slice_fusion.7), channel_id=1, source_target_pairs={{0,2},{1,3},{2,0},{3,1},{4,6},{5,7},{6,4},{7,5},{8,10},{9,11},{10,... | collective-permute-start | bytes 3145736 | tf_op jit(solution)/shard_map/ppermute | solution.py:742
  177.4 38.3 %collective-permute-start.8 = (bf16[512,1024]{1,0:T(8,128)(2,1)}, bf16[512,1024]{1,0:T(8,128)(2,1)}, u32[]{:S(2)}, u32[]{:S(2)}) collective-permute-start(bf16[512,1024]{1,0:T(8,128)(2,1)} %collective-permute-done.5), channel_id=1, source_target_pairs={{0,4},{4,0},{8,12},{12,8},{16,20},{20,16},{24,28},{28,24},{1,5},{5... | collective-permute-start | bytes 3145736 | tf_op jit(solution)/shard_map/ppermute | solution.py:828
  217.1 41.2 %collective-permute-start.10 = (bf16[1024,1024]{1,0:T(8,128)(2,1)S(1)}, bf16[1024,1024]{1,0:T(8,128)(2,1)}, u32[]{:S(2)}, u32[]{:S(2)}) collective-permute-start(bf16[1024,1024]{1,0:T(8,128)(2,1)S(1)} %constant_dynamic-update-slice_fusion.14.refs_2_), channel_id=1, source_target_pairs={{0,1},{1,0},{2,3},{3,2},{4,5},{5,4},{6,7},{7,6},{8,9},{9,8},{10,11... | collective-permute-start | bytes 6291464 | tf_op jit(solution)/shard_map/ppermute | solution.py:742
  217.2 41.1 %collective-permute-start.11 = (bf16[512,1024]{1,0:T(8,128)(2,1)}, bf16[512,1024]{1,0:T(8,128)(2,1)S(1)}, u32[]{:S(2)}, u32[]{:S(2)}) collective-permute-start(bf16[512,1024]{1,0:T(8,128)(2,1)} %collective-permute-done.7), channel_id=1, source_target_pairs={{0,4},{4,0},{8,12},{12,8},{16,20},{20,16},{24,28},{28,24},{1,5},{5... | collective-permute-start | bytes 3145736 | tf_op jit(solution)/shard_map/ppermute | solution.py:828
  319.9 48.0 %collective-permute-start.16 = (bf16[1024,1024]{1,0:T(8,128)(2,1)}, bf16[1024,1024]{1,0:T(8,128)(2,1)}, u32[]{:S(2)}, u32[]{:S(2)}) collective-permute-start(bf16[1024,1024]{1,0:T(8,128)(2,1)} %add_convert_fusion.6), channel_id=1, source_target_pairs={{0,2},{1,3},{2,0},{3,1},{4,6},{5,7},{6,4},{7,5},{8,10},{9,11},{10,... | collective-permute-start | bytes 6291464 | tf_op jit(solution)/shard_map/ppermute | solution.py:742
  367.9 40.6 %all-to-all-start.3 = ((bf16[4,1536,256]{2,1,0:T(8,128)(2,1)}), bf16[4,1536,256]{2,1,0:T(8,128)(2,1)S(1)}, u32[]{:S(2)}, u32[]{:S(2)}) async-start(bf16[4,1536,256]{2,1,0:T(8,128)(2,1)} %get-tuple-element.268), calls=%async_computation.3 | async-start | bytes 6291456 | tf_op jit(solution)/shard_map/all_to_all | solution.py:753
  371.6 253.9 %all-reduce.6.cloned.1.call-start = ((), (), s32[]{:S(2)}) async-start(), calls=%async_computation.8 | async-start | bytes 5242880 | tf_op jit(solution)/shard_map/psum | solution.py:1021
  414.3 56.1 %collective-permute-start.21 = (bf16[1024,1024]{1,0:T(8,128)(2,1)}, bf16[1024,1024]{1,0:T(8,128)(2,1)}, u32[]{:S(2)}, u32[]{:S(2)}) collective-permute-start(bf16[1024,1024]{1,0:T(8,128)(2,1)} %add_convert_fusion.5), channel_id=1, source_target_pairs={{0,2},{1,3},{2,0},{3,1},{4,6},{5,7},{6,4},{7,5},{8,10},{9,11},{10,... | collective-permute-start | bytes 6291464 | tf_op jit(solution)/shard_map/ppermute | solution.py:742
  418.4 54.6 %collective-permute-start.23 = (bf16[512,1024]{1,0:T(8,128)(2,1)S(1)}, bf16[512,1024]{1,0:T(8,128)(2,1)}, u32[]{:S(2)}, u32[]{:S(2)}) collective-permute-start(bf16[512,1024]{1,0:T(8,128)(2,1)S(1)} %constant_dynamic-slice_fusion.6), channel_id=1, source_target_pairs={{0,4},{4,0},{8,12},{12,8},{16,20},{20,16},{24,28},{28,24},{1,5},{5... | collective-permute-start | bytes 3145736 | tf_op jit(solution)/shard_map/ppermute | solution.py:810
  421.4 51.6 %collective-permute-start.22 = (bf16[256,1024]{1,0:T(8,128)(2,1)}, bf16[256,1024]{1,0:T(8,128)(2,1)}, u32[]{:S(2)}, u32[]{:S(2)}) collective-permute-start(bf16[256,1024]{1,0:T(8,128)(2,1)} %add_convert_fusion.13), channel_id=1, source_target_pairs={{0,2},{1,3},{2,0},{3,1},{4,6},{5,7},{6,4},{7,5},{8,10},{9,11},{10,... | collective-permute-start | bytes 1572872 | tf_op jit(solution)/shard_map/ppermute | solution.py:742
  483.6 251.2 %all-reduce.4.cloned.1.call-start = ((), (), s32[]{:S(2)}) async-start(), calls=%async_computation.7 | async-start | bytes 3194880 | tf_op jit(solution)/shard_map/psum | solution.py:1038
  497.2 50.9 %collective-permute-start.26 = (bf16[512,1024]{1,0:T(8,128)(2,1)}, bf16[512,1024]{1,0:T(8,128)(2,1)S(1)}, u32[]{:S(2)}, u32[]{:S(2)}) collective-permute-start(bf16[512,1024]{1,0:T(8,128)(2,1)} %get-tuple-element.301), channel_id=1, source_target_pairs={{0,1},{1,0},{2,3},{3,2},{4,5},{5,4},{6,7},{7,6},{8,9},{9,8},{10,11... | collective-permute-start | bytes 3145736 | tf_op jit(solution)/shard_map/ppermute | solution.py:742
  497.7 50.3 %collective-permute-start.27 = (bf16[512,1024]{1,0:T(8,128)(2,1)}, bf16[512,1024]{1,0:T(8,128)(2,1)}, u32[]{:S(2)}, u32[]{:S(2)}) collective-permute-start(bf16[512,1024]{1,0:T(8,128)(2,1)} %get-tuple-element.302), channel_id=1, source_target_pairs={{0,1},{1,0},{2,3},{3,2},{4,5},{5,4},{6,7},{7,6},{8,9},{9,8},{10,11... | collective-permute-start | bytes 3145736 | tf_op jit(solution)/shard_map/ppermute | solution.py:742
  498.0 50.0 %collective-permute-start.30 = (bf16[128,1024]{1,0:T(8,128)(2,1)S(1)}, bf16[128,1024]{1,0:T(8,128)(2,1)S(1)}, u32[]{:S(2)}, u32[]{:S(2)}) collective-permute-start(bf16[128,1024]{1,0:T(8,128)(2,1)S(1)} %constant_dynamic-slice_fusion), channel_id=1, source_target_pairs={{0,16},{4,20},{8,24},{12,28},{16,0},{20,4},{24,8},{28,12},{1,17},{... | collective-permute-start | bytes 786440 | tf_op jit(solution)/shard_map/ppermute | solution.py:810
  500.5 47.6 %collective-permute-start.29 = (f32[64,128]{1,0:T(8,128)S(1)}, f32[64,128]{1,0:T(8,128)S(1)}, u32[]{:S(2)}, u32[]{:S(2)}) collective-permute-start(f32[64,128]{1,0:T(8,128)S(1)} %add.225), channel_id=1, source_target_pairs={{0,2},{1,3},{2,0},{3,1},{4,6},{5,7},{6,4},{7,5},{8,10},{9,11},{10,... | collective-permute-start | bytes 98312 | tf_op jit(solution)/shard_map/ppermute | solution.py:796
  551.0 74.4 %collective-permute-start.28 = (bf16[512,1024]{1,0:T(8,128)(2,1)}, bf16[512,1024]{1,0:T(8,128)(2,1)S(1)}, u32[]{:S(2)}, u32[]{:S(2)}) collective-permute-start(bf16[512,1024]{1,0:T(8,128)(2,1)} %add_convert_fusion.9), channel_id=1, source_target_pairs={{0,2},{1,3},{2,0},{3,1},{4,6},{5,7},{6,4},{7,5},{8,10},{9,11},{10,... | collective-permute-start | bytes 3145736 | tf_op jit(solution)/shard_map/ppermute | solution.py:742
  574.2 52.5 %collective-permute-start.34 = (bf16[256,1024]{1,0:T(8,128)(2,1)S(1)}, bf16[256,1024]{1,0:T(8,128)(2,1)S(1)}, u32[]{:S(2)}, u32[]{:S(2)}) collective-permute-start(bf16[256,1024]{1,0:T(8,128)(2,1)S(1)} %constant_dynamic-update-slice_fusion.10), channel_id=1, source_target_pairs={{0,8},{4,12},{8,0},{12,4},{16,24},{20,28},{24,16},{28,20},{1,9},{5... | collective-permute-start | bytes 1572872 | tf_op jit(solution)/shard_map/ppermute | solution.py:813
  (74 other events, 1106.8 us)
Sparse Core Ops, SparseCore 0:
  10.1 37.1 all-gather.3
  49.5 34.4 all-gather.5
  86.2 39.9 all-gather.7
  483.8 133.0 all-reduce.5
  642.0 92.8 all-reduce.3

commit v7 on v6

--- a/solution.py
+++ b/solution.py
@@ -570,53 +570,72 @@
     )(*operands)
 
 
-def weight_back(normed, pre_grad, attended, grad_low, pieces):
+def weight_back(normed, pre_grad, picks, attended, grad_low, pieces):
     rows, model = normed.shape
-    every = pre_grad.shape[1]
-    units = every // pieces
+    units = pre_grad.shape[1] // pieces
     piece = model // pieces
     block = largest_block(rows, 512)
     steps = rows // block
-
-    def body(x_ref, pre_ref, attended_ref, grad_ref, *refs):
-        up_refs, out_refs = refs[:pieces], refs[pieces : 2 * pieces]
-        up_acc, out_acc = refs[2 * pieces :]
+    count = len(picks)
+    outs = 0 if attended is None else pieces
+
+    def body(x_ref, *refs):
+        pre_refs = refs[:count]
+        rest = refs[count:]
+        if outs:
+            attended_ref, grad_ref = rest[:2]
+            rest = rest[2:]
+        up_refs, out_refs = rest[:count], rest[count : count + outs]
+        up_acc = rest[count + outs]
         step = pl.program_id(0)
 
-        @pl.when(step == 0)
-        def _():
-            up_acc[...] = jnp.zeros_like(up_acc)
-            out_acc[...] = jnp.zeros_like(out_acc)
-
-        part = largest_block(every, 512)
-        for j in range(every // part):
-            cols = slice(j * part, (j + 1) * part)
-            up_acc[:, cols] += tn(x_ref[...], pre_ref[:, cols])
-        part = largest_block(model, 512)
-        for j in range(model // part):
-            cols = slice(j * part, (j + 1) * part)
-            out_acc[:, cols] += tn(attended_ref[...], grad_ref[:, cols])
+        def add(acc, place, value):
+            @pl.when(step == 0)
+            def _():
+                acc[place] = value
+
+            @pl.when(step > 0)
+            def _():
+                acc[place] += value
+
+        for k in range(count):
+            add(up_acc, (slice(None), slice(k * units, (k + 1) * units)), tn(x_ref[...], pre_refs[k][...]))
+        if outs:
+            out_acc = rest[-1]
+            add(out_acc, (slice(None), slice(None)), tn(attended_ref[...], grad_ref[...]))
 
         @pl.when(step == steps - 1)
         def _():
-            for k in range(pieces):
+            for k in range(count):
                 up_refs[k][...] = up_acc[:, k * units : (k + 1) * units].astype(bf16)
+            for k in range(outs):
                 out_refs[k][...] = out_acc[k * piece : (k + 1) * piece, :].astype(bf16)
 
     row_spec = pl.BlockSpec((block, model), lambda i: (i, 0))
+
+    def columns_of(pick):
+        return pl.BlockSpec((block, units), lambda i: (i, pick))
+
+    operands = [normed] + [pre_grad] * count
+    in_specs = [row_spec] + [columns_of(pick) for pick in picks]
+    scratch = [pltpu.VMEM((model, count * units), f32)]
+    if outs:
+        operands += [attended, grad_low]
+        in_specs += [row_spec, row_spec]
+        scratch.append(pltpu.VMEM((model, model), f32))
     return pl.pallas_call(
         body,
         grid=(steps,),
-        in_specs=[row_spec, pl.BlockSpec((block, every), lambda i: (i, 0)), row_spec, row_spec],
-        out_specs=[pl.BlockSpec((model, units), lambda i: (0, 0))] * pieces
-        + [pl.BlockSpec((piece, model), lambda i: (0, 0))] * pieces,
-        out_shape=[jax.ShapeDtypeStruct((model, units), bf16)] * pieces
-        + [jax.ShapeDtypeStruct((piece, model), bf16)] * pieces,
-        scratch_shapes=[pltpu.VMEM((model, every), f32), pltpu.VMEM((model, model), f32)],
+        in_specs=in_specs,
+        out_specs=[pl.BlockSpec((model, units), lambda i: (0, 0))] * count
+        + [pl.BlockSpec((piece, model), lambda i: (0, 0))] * outs,
+        out_shape=[jax.ShapeDtypeStruct((model, units), bf16)] * count
+        + [jax.ShapeDtypeStruct((piece, model), bf16)] * outs,
+        scratch_shapes=scratch,
         compiler_params=params(),
-        cost_estimate=hint(2 * rows * model * (every + model), rows * model),
+        cost_estimate=hint(2 * rows * model * units * count, rows * model),
         name="weight_back",
-    )(normed, pre_grad, attended, grad_low)
+    )(*operands)
 
 
 def project_back(place, normed, dqkv, weight, before, last, pieces):
@@ -758,16 +777,6 @@
         anchor, (near_own, near_far) = tie(anchor, (swap(blocks[1], 1), swap(blocks[3], 1)))
         far = (blocks[2].astype(f32) + near_far.astype(f32)).astype(blocks[2].dtype)
         return (blocks[0], near_own, far), anchor
-
-    def sums_near(lists, anchor):
-        if not square:
-            return [sum_near(blocks, anchor)[0] for blocks in lists], anchor
-        moved = [(swap(blocks[1], 1), swap(blocks[3], 1)) for blocks in lists]
-        anchor, moved = tie(anchor, moved)
-        return [
-            (blocks[0], own, (blocks[2].astype(f32) + far.astype(f32)).astype(blocks[2].dtype))
-            for blocks, (own, far) in zip(lists, moved, strict=True)
-        ], anchor
 
     def terms_far(stage, anchor):
         if not square:
@@ -990,21 +999,34 @@
         ring = ring_plan()
         pre_grad, total = before
 
+        if square:
+            ahead = weight_back(normed_mlp, pre_grad, [1, 3], None, None, tensor_size)
+            total, ahead = tie(total, ahead)
         grad_residual, grad_low, small_rows, pieces = residual_back(
             total, residual, cotangent, own_scale, place, out_weight, mlp_gain_row, tensor_size
         )
         down_sum, pieces = sum_far(down_stage, pieces)
         grad_attended = exchange(pieces)
-        weight_grads = weight_back(normed_mlp, pre_grad, attended_rows, grad_low, tensor_size)
-        weight_grads = list(weight_grads)
-        weight_grads[0], grad_attended = tie(weight_grads[0], grad_attended)
-        up_grads, out_grads = weight_grads[:tensor_size], weight_grads[tensor_size:]
-
-        (up_stage, out_stage), grad_attended = sums_near([up_grads, out_grads], grad_attended)
+        if square:
+            up_near, up_diag_near = swap(ahead[0], 1), swap(ahead[1], 1)
+            first, second, *out_grads = weight_back(
+                normed_mlp, pre_grad, [2, 0], attended_rows, grad_low, tensor_size
+            )
+            second, (up_near, up_diag_near) = tie(second, (up_near, up_diag_near))
+            up_far_sum = (first.astype(f32) + up_diag_near.astype(f32)).astype(bf16)
+            out_stage, up_far_sum = sum_near(out_grads, up_far_sum)
+            up_far_sum, grad_attended = tie(up_far_sum, grad_attended)
+            up_stage = (second, up_near, up_far_sum)
+        else:
+            weight_grads = weight_back(
+                normed_mlp, pre_grad, list(range(tensor_size)), attended_rows, grad_low, tensor_size
+            )
+            up_stage, grad_attended = sum_near(weight_grads[:tensor_size], grad_attended)
+            out_stage, grad_attended = sum_near(weight_grads[tensor_size:], grad_attended)
         bias_rows = in_order(jnp.concatenate(bias_grads, axis=1).reshape(tensor_size, -1))
         smalls = jnp.concatenate([small_rows[:4].reshape(-1), bias_rows.reshape(-1)]).reshape(-1, 128)
+
         waiting = list(steps)
-
         weights_wide = query_key_value_weight.astype(f32)
         sums = None
         grad_normed = []
@@ -1046,8 +1068,8 @@
                         jnp.sum(sums[1][:3, None, :] * weights_wide, axis=(0, 2)),
                     ]
                 )
-                for step in steps:
-                    raw = raw + lax.ppermute(raw, step[0], step[1])
+                for axis, pairs in steps:
+                    raw = raw + lax.ppermute(raw, axis, pairs)
             grad_normed.append(partial)
         grad_inputs = None
         for i in range(slot_count):
@@ -1068,11 +1090,12 @@
         down_all = down_sum.astype(f32)
         inverse = 1.0 / total_items
         smalls = smalls.reshape(-1) * inverse
+        raw = raw * inverse
         small_rows = smalls[: 4 * model].reshape(4, model)
         units = up_bias.shape[0]
         bias_all = lax.dynamic_slice_in_dim(smalls[4 * model :], lax.axis_index("tensor") * units, units)
-        shift_all = raw[1] * inverse
-        gain_all = (raw[0] * inverse - attn_shift * shift_all) / attn_gain
+        shift_all = raw[1]
+        gain_all = (raw[0] - attn_shift * shift_all) / attn_gain
         columns = columns * inverse
         return (
             output,

time: 754 us -> 750 us (level)
  waiting for transfers between devices: 116 us -> 104 us
  Pallas kernels: 465 us -> 473 us
    ppermute x30, waiting for transfers between devices: 17.9 us -> 5.28 us  [swap(): lax.ppermute(value, 'tensor', [(i, i ^ bits) for i in range(tensor_size)])]
    pallas_call x1 -> x2, Pallas kernels: 26.4 us -> 35.2 us  [weight_back(): pl.pallas_call(body, grid=(steps,), in_specs=in_specs, out_specs=[pl.Bloc...]
  transfers between devices with their start and end apart: 57 -> 57, of which waited for: 16 -> 15; matrix products, arithmetic and copies ran while one was open for 10% -> 10% of each run, Pallas kernels for 57% -> 58%
where the time goes in v7:
time: 750 us; the launch traced here: 743 us
  Pallas kernels  473 us (63%)
  waiting for transfers between devices  104 us (14%)
  starting transfers between devices  50.6 us (7%)
  other arithmetic  49.2 us (7%)
  local copies, waits for them, and re-layouts  27.9 us (4%)
  matrix products  21.9 us (3%)
  between operations  15.5 us (2%)
    pallas_call x3, Pallas kernels, attend_back(): pl.pallas_call(body, grid=(pairs, kblocks), in_specs=[pl.BlockSpec((None,...  141 us
    pallas_call x3, Pallas kernels, attend(): pl.pallas_call(body, grid=(pairs, length // qblock), in_specs=[pl.BlockSp...  72.5 us
    pallas_call x2, Pallas kernels, mlp_forward(): pl.pallas_call(body, grid=(steps,), in_specs=in_specs, out_specs=[slope_s...  71.4 us
    pallas_call x3, Pallas kernels, project_back(): pl.pallas_call(kernel, grid=(steps,), in_specs=in_specs, out_specs=out_sp...  38.5 us
    pallas_call x2, Pallas kernels, weight_back(): pl.pallas_call(body, grid=(steps,), in_specs=in_specs, out_specs=[pl.Bloc...  35.2 us
    pallas_call x2, Pallas kernels, mlp_backward(): pl.pallas_call(body, grid=(rows // block,), in_specs=in_specs, out_specs=...  34.6 us
    all_to_all x4, waiting for transfers between devices, exchange(): return lax.all_to_all(stacked, 'tensor', 0, 0)  26.9 us
    all_gather x3, waiting for transfers between devices, gather_rows(): return lax.all_gather(own, 'tensor', axis=0, tiled=True)  25.5 us
  transfers between devices with their start and end apart: 57, of which 15 were waited for; matrix products, arithmetic and copies ran while one was open for 10% of the time, Pallas kernels for 58%

profile of v7, /device:TPU:0, one launch (start us, length us, event | category | flops | bytes accessed | tf_op | source)
XLA Modules:
  0.0 742.6 jit_solution(5151003081315167903)
XLA Ops:
  21.3 11.4 %cot_back.1.refs_0_ = bf16[1536,2048]{1,0:T(8,128)(2,1)} custom-call(bf16[1536,1024]{1,0:T(8,128)(2,1)} %fusion.cot_ref.refs_1_.refs_0_, bf16[1024,1024]{1,0:T(8,128)(2,1)} %refs_6_, bf16[1024,1024]{1,0:T(8,128)(2,1)} %collective-permute-done.refs_1_.refs_7_), custom_call_target="tpu_custom_call" | custom-call | flops 100663296 | bytes 1572864 | tf_op jit(solution)/shard_map/cot_back/pallas_call | solution.py:494
  32.8 14.6 %all-gather.4.cloned.1.call-done.refs_1_ = bf16[2048,1024]{1,0:T(8,128)(2,1)} async-done(((bf16[512,1024]{1,0:T(8,128)(2,1)}), bf16[2048,1024]{1,0:T(8,128)(2,1)}) %all-gather.4.cloned.1.call-update) | async-done | bytes 4194320 | tf_op jit(solution)/shard_map/all_gather | solution.py:900
  55.6 24.5 %attend.3 = (bf16[2048,256]{1,0:T(8,128)(2,1)}, f32[2,2,2048]{2,1,0:T(2,128)}) custom-call(bf16[3,2048,256]{2,1,0:T(8,128)(2,1)} %fusion.9.q_ref.k_ref.v_ref, bf16[3,2048,256]{2,1,0:T(8,128)(2,1)} %fusion.9.q_ref.k_ref.v_ref, bf16[3,2048,256]{2,1,0:T(8,128)(2,1)} %fusion.9.q_ref.k_ref.v_ref), custom_call_target="tpu_custom_call" | custom-call | flops 134217728 | bytes 524288 | tf_op jit(solution)/shard_map/attend/pallas_call | solution.py:76
  94.9 24.1 %attend.4 = (bf16[2048,256]{1,0:T(8,128)(2,1)}, f32[2,2,2048]{2,1,0:T(2,128)}) custom-call(bf16[3,2048,256]{2,1,0:T(8,128)(2,1)} %fusion.10.q_ref.k_ref.v_ref, bf16[3,2048,256]{2,1,0:T(8,128)(2,1)} %fusion.10.q_ref.k_ref.v_ref, bf16[3,2048,256]{2,1,0:T(8,128)(2,1)} %fusion.10.q_ref.k_ref.v_ref), custom_call_target="tpu_custom_call" | custom-call | flops 134217728 | bytes 524288 | tf_op jit(solution)/shard_map/attend/pallas_call | solution.py:76
  146.1 23.8 %attend.5 = (bf16[2048,256]{1,0:T(8,128)(2,1)}, f32[2,2,2048]{2,1,0:T(2,128)}) custom-call(bf16[3,2048,256]{2,1,0:T(8,128)(2,1)} %fusion.11.q_ref.k_ref.v_ref, bf16[3,2048,256]{2,1,0:T(8,128)(2,1)} %fusion.11.q_ref.k_ref.v_ref, bf16[3,2048,256]{2,1,0:T(8,128)(2,1)} %fusion.11.q_ref.k_ref.v_ref), custom_call_target="tpu_custom_call" | custom-call | flops 134217728 | bytes 524288 | tf_op jit(solution)/shard_map/attend/pallas_call | solution.py:76
  201.1 9.5 %all-to-all-done.2.refs_6_ = bf16[4,512,256]{2,1,0:T(8,128)(2,1)} async-done(((bf16[4,512,256]{2,1,0:T(8,128)(2,1)}), bf16[4,512,256]{2,1,0:T(8,128)(2,1)}, u32[]{:S(2)}, u32[]{:S(2)}) %all-to-all-start.2) | async-done | bytes 1048608 | tf_op jit(solution)/shard_map/all_to_all | solution.py:772
  223.4 34.9 %mlp_forward.2 = (bf16[1536,2048]{1,0:T(8,128)(2,1)}, f32[1536,1024]{1,0:T(8,128)}, bf16[1024,1024]{1,0:T(8,128)(2,1)}, bf16[1024,1024]{1,0:T(8,128)(2,1)}) custom-call(bf16[1536,1024]{1,0:T(8,128)(2,1)} %get-tuple-element.239.refs_0_.x_ref, bf16[1536,1024]{1,0:T(8,128)(2,1)} %fusion.cot_ref.refs_1_.refs_0_, bf16[1024,1024]{1,0:T(8,128)(2,1)} %refs_2_.1, ...), custom_call_target="tpu_custom_call" | custom-call | flops 301989888 | bytes 1572864 | tf_op jit(solution)/shard_map/mlp_forward/pallas_call | solution.py:466
  265.5 36.5 %mlp_forward.3 = (bf16[1536,2048]{1,0:T(8,128)(2,1)}, f32[1536,1024]{1,0:T(8,128)}, bf16[1024,1024]{1,0:T(8,128)(2,1)}, bf16[1024,1024]{1,0:T(8,128)(2,1)}) custom-call(bf16[1536,1024]{1,0:T(8,128)(2,1)} %get-tuple-element.239.refs_0_.x_ref, bf16[1536,1024]{1,0:T(8,128)(2,1)} %fusion.cot_ref.refs_1_.refs_0_, ...), custom_call_target="tpu_custom_call", output_to_operand_aliasing={{1}: (8, {})} | custom-call | flops 301989888 | bytes 1572864 | tf_op jit(solution)/shard_map/mlp_forward/pallas_call | solution.py:466
  302.5 13.4 %mlp_backward.2 = (bf16[1536,4096]{1,0:T(8,128)(2,1)}, f32[1536,1024]{1,0:T(8,128)}, f32[1,2048]{1,0:T(1,128)}) custom-call(bf16[1536,2048]{1,0:T(8,128)(2,1)} %cot_back.1.refs_0_, bf16[1536,2048]{1,0:T(8,128)(2,1)} %get-tuple-element.256.refs_1_, bf16[1024,1024]{1,0:T(8,128)(2,1)} %refs_2_.1, bf16[1024,1024]{1,0:T(8,128)(2,1)} %collective-permute-done.2.refs_3_), custom_call_target="tpu_custom_call" | custom-call | flops 201326592 | bytes 1572864 | tf_op jit(solution)/shard_map/mlp_backward/pallas_call | solution.py:552
  320.9 21.2 %mlp_backward.3 = (bf16[1536,4096]{1,0:T(8,128)(2,1)}, f32[1536,1024]{1,0:T(8,128)}, f32[1,2048]{1,0:T(1,128)}) custom-call(bf16[1536,1024]{1,0:T(8,128)(2,1)} %fusion.cot_ref.refs_1_.refs_0_, bf16[1536,2048]{1,0:T(8,128)(2,1)} %get-tuple-element.254.refs_1_, bf16[1024,1024]{1,0:T(8,128)(2,1)} %copy-done.6, ...), custom_call_target="tpu_custom_call", output_to_operand_aliasing={{0}: (6, {}), {1}: (7, {})} | custom-call | flops 201326592 | bytes 1572864 | tf_op jit(solution)/shard_map/mlp_backward/pallas_call | solution.py:552
  342.1 14.1 %weight_back.2 = (bf16[1024,1024]{1,0:T(8,128)(2,1)}, bf16[1024,1024]{1,0:T(8,128)(2,1)}) custom-call(bf16[1536,1024]{1,0:T(8,128)(2,1)} %get-tuple-element.239.refs_0_.x_ref, bf16[1536,4096]{1,0:T(8,128)(2,1)} %get-tuple-element.263.refs_0_.refs_1_, bf16[1536,4096]{1,0:T(8,128)(2,1)} %get-tuple-element.263.refs_0_.refs_1_), custom_call_target="tpu_custom_call" | custom-call | flops 100663296 | bytes 1572864 | tf_op jit(solution)/shard_map/weight_back/pallas_call | solution.py:626
  356.8 14.9 %residual_back.1 = (f32[1536,1024]{1,0:T(8,128)}, bf16[1536,1024]{1,0:T(8,128)(2,1)}, f32[8,1024]{1,0:T(8,128)}, bf16[4,1536,256]{2,1,0:T(8,128)(2,1)}) custom-call(s32[1]{0:T(128)} %bitcast.refs_0_.place_ref, f32[1536,1024]{1,0:T(8,128)} %get-tuple-element.268.refs_1_, f32[1536,1024]{1,0:T(8,128)} %get-tuple-element.269.refs_2_.residual_ref, ...), custom_call_target="tpu_custom_call" | custom-call | flops 50331648 | bytes 524288 | tf_op jit(solution)/shard_map/residual_back/pallas_call | solution.py:301
  375.4 21.1 %weight_back.3 = (bf16[1024,1024]{1,0:T(8,128)(2,1)}, bf16[1024,1024]{1,0:T(8,128)(2,1)}, bf16[256,1024]{1,0:T(8,128)(2,1)}, bf16[256,1024]{1,0:T(8,128)(2,1)}, ...) custom-call(bf16[1536,1024]{1,0:T(8,128)(2,1)} %get-tuple-element.239.refs_0_.x_ref, ...), custom_call_target="tpu_custom_call" | custom-call | flops 100663296 | bytes 1572864 | tf_op jit(solution)/shard_map/weight_back/pallas_call | solution.py:626
  402.3 9.9 %all-to-all-done.3.grad_ref = bf16[4,1536,256]{2,1,0:T(8,128)(2,1)S(1)} async-done(((bf16[4,1536,256]{2,1,0:T(8,128)(2,1)}), bf16[4,1536,256]{2,1,0:T(8,128)(2,1)S(1)}, u32[]{:S(2)}, u32[]{:S(2)}) %all-to-all-start.3) | async-done | bytes 3145760 | tf_op jit(solution)/shard_map/all_to_all | solution.py:772
  422.4 47.1 %attend_back.4.refs_2_ = bf16[3,2048,256]{2,1,0:T(8,128)(2,1)} custom-call(bf16[3,2048,256]{2,1,0:T(8,128)(2,1)} %fusion.9.q_ref.k_ref.v_ref, bf16[3,2048,256]{2,1,0:T(8,128)(2,1)} %fusion.9.q_ref.k_ref.v_ref, bf16[3,2048,256]{2,1,0:T(8,128)(2,1)} %fusion.9.q_ref.k_ref.v_ref, bf16[2048,256]{1,0:T(8,128)(2,1)} %get-tuple-element.213.out_ref, ...), custom_call_target="tpu_custom_call" | custom-call | flops 335544320 | bytes 524288 | tf_op jit(solution)/shard_map/attend_back/pallas_call | solution.py:169
  480.5 13.3 %project_back.3 = (bf16[512,1024]{1,0:T(8,128)(2,1)}, bf16[512,1024]{1,0:T(8,128)(2,1)}, bf16[512,1024]{1,0:T(8,128)(2,1)}, bf16[512,1024]{1,0:T(8,128)(2,1)}, f...) custom-call(s32[1]{0:T(128)} %bitcast.refs_0_.place_ref, bf16[2048,1024]{1,0:T(8,128)(2,1)} %all-gather.4.cloned.1.call-done.refs_1_, ...), custom_call_target="tpu_custom_call" | custom-call | flops 100663296 | bytes 524288 | tf_op jit(solution)/shard_map/project_back/pallas_call | solution.py:708
  497.8 46.9 %attend_back.5.refs_2_ = bf16[3,2048,256]{2,1,0:T(8,128)(2,1)} custom-call(bf16[3,2048,256]{2,1,0:T(8,128)(2,1)} %fusion.10.q_ref.k_ref.v_ref, bf16[3,2048,256]{2,1,0:T(8,128)(2,1)} %fusion.10.q_ref.k_ref.v_ref, bf16[3,2048,256]{2,1,0:T(8,128)(2,1)} %fusion.10.q_ref.k_ref.v_ref, bf16[2048,256]{1,0:T(8,128)(2,1)} %get-tuple-element.215.out_ref, ...), custom_call_target="tpu_custom_call" | custom-call | flops 335544320 | bytes 524288 | tf_op jit(solution)/shard_map/attend_back/pallas_call | solution.py:169
  550.0 14.5 %project_back.4 = (bf16[512,1024]{1,0:T(8,128)(2,1)}, bf16[512,1024]{1,0:T(8,128)(2,1)}, bf16[512,1024]{1,0:T(8,128)(2,1)}, bf16[512,1024]{1,0:T(8,128)(2,1)}, f...) custom-call(s32[1]{0:T(128)} %bitcast.refs_0_.place_ref, ...), custom_call_target="tpu_custom_call", output_to_operand_aliasing={{4}: (4, {}), {5}: (5, {})} | custom-call | flops 100663296 | bytes 524288 | tf_op jit(solution)/shard_map/project_back/pallas_call | solution.py:708
  571.8 47.0 %attend_back.3.refs_2_.dqkv_ref = bf16[3,2048,256]{2,1,0:T(8,128)(2,1)} custom-call(bf16[3,2048,256]{2,1,0:T(8,128)(2,1)} %fusion.11.q_ref.k_ref.v_ref, bf16[3,2048,256]{2,1,0:T(8,128)(2,1)} %fusion.11.q_ref.k_ref.v_ref, bf16[3,2048,256]{2,1,0:T(8,128)(2,1)} %fusion.11.q_ref.k_ref.v_ref, bf16[2048,256]{1,0:T(8,128)(2,1)} %get-tuple-element.219.out_ref, ...), custom_call_target="tpu_custom_call" | custom-call | flops 335544320 | bytes 524288 | tf_op jit(solution)/shard_map/attend_back/pallas_call | solution.py:169
  622.9 10.7 %project_back.5 = (f32[3,1024,256]{2,1,0:T(8,128)}, f32[8,256]{1,0:T(8,128)}, bf16[3,1040,256]{2,1,0:T(8,128)(2,1)}) custom-call(s32[1]{0:T(128)} %bitcast.refs_0_.place_ref, bf16[2048,1024]{1,0:T(8,128)(2,1)} %all-gather.8.cloned.1.call-done.refs_1_, ...), custom_call_target="tpu_custom_call", output_to_operand_aliasing={{0}: (4, {}), {1}: (5, {})} | custom-call | flops 100663296 | bytes 524288 | tf_op jit(solution)/shard_map/project_back/pallas_call | solution.py:708
  639.2 8.5 %project_rows.1 = (bf16[512,1024]{1,0:T(8,128)(2,1)}, bf16[512,1024]{1,0:T(8,128)(2,1)}, bf16[512,1024]{1,0:T(8,128)(2,1)}, bf16[512,1024]{1,0:T(8,128)(2,1)}) custom-call(s32[1]{0:T(128)} %bitcast.refs_0_.place_ref, bf16[3,2048,256]{2,1,0:T(8,128)(2,1)} %attend_back.3.refs_2_.dqkv_ref, bf16[3,1024,256]{2,1,0:T(8,128)(2,1)} %weight_ref.1), custom_call_target="tpu_custom_call" | custom-call | flops 50331648 | bytes 524288 | tf_op jit(solution)/shard_map/project_rows/pallas_call | solution.py:741
  653.8 7.6 %layer_out.1 = bf16[3,512,1024]{2,1,0:T(8,128)(2,1)} custom-call(f32[1536,1024]{1,0:T(8,128)} %get-tuple-element.346.total_ref, f32[1536,1024]{1,0:T(8,128)} %get-tuple-element.269.refs_2_.residual_ref, f32[1,1024]{1,0:T(1,128)} %bitcast.90, f32[3]{0:T(128)} %dynamic_slice.58.valid_ref), custom_call_target="tpu_custom_call" | custom-call | bytes 524288 | tf_op jit(solution)/shard_map/layer_out/pallas_call | solution.py:385
  681.1 14.3 %collective-permute-done.42 = bf16[512,1024]{1,0:T(8,128)(2,1)S(1)} collective-permute-done((bf16[512,1024]{1,0:T(8,128)(2,1)S(1)}, bf16[512,1024]{1,0:T(8,128)(2,1)S(1)}, u32[]{:S(2)}, u32[]{:S(2)}) %collective-permute-start.42) | collective-permute-done | bytes 1048608 | tf_op jit(solution)/shard_map/ppermute | solution.py:822
  709.7 21.5 %all-reduce.4.cloned.1.call-done = bf16[3,1040,256]{2,1,0:T(8,128)(2,1)} async-done(((bf16[3,1040,256]{2,1,0:T(8,128)(2,1)}), bf16[3,1040,256]{2,1,0:T(8,128)(2,1)}) %all-reduce.4.cloned.1.call-update) | async-done | bytes 1597456 | tf_op jit(solution)/shard_map/psum | solution.py:1060
  (298 shorter events, 221.5 us)
Async XLA Ops:
  9.9 74.1 %all-gather.6.cloned.1.call-start = ((), (), s32[]{:S(2)}) async-start(), calls=%async_computation.5 | async-start | bytes 5242880 | tf_op jit(solution)/shard_map/all_gather | solution.py:900
  47.4 78.7 %all-gather.8.cloned.1.call-start = ((), (), s32[]{:S(2)}) async-start(), calls=%async_computation.6 | async-start | bytes 5242880 | tf_op jit(solution)/shard_map/all_gather | solution.py:900
  84.1 42.0 %all-to-all-start = ((bf16[4,512,256]{2,1,0:T(8,128)(2,1)}), bf16[4,512,256]{2,1,0:T(8,128)(2,1)S(1)}, u32[]{:S(2)}, u32[]{:S(2)}) async-start(bf16[4,512,256]{2,1,0:T(8,128)(2,1)} %bitcast.58), calls=%async_computation | async-start | bytes 2097152 | tf_op jit(solution)/shard_map/all_to_all | solution.py:772
  128.8 48.7 %collective-permute-start.5 = (bf16[512,1024]{1,0:T(8,128)(2,1)}, bf16[512,1024]{1,0:T(8,128)(2,1)}, u32[]{:S(2)}, u32[]{:S(2)}) collective-permute-start(bf16[512,1024]{1,0:T(8,128)(2,1)} %constant_dynamic-slice_fusion.8), channel_id=1, source_target_pairs={{0,2},{1,3},{2,0},{3,1},{4,6},{5,7},{6,4},{7,5},{8,10},{9,11},{10,... | collective-permute-start | bytes 3145736 | tf_op jit(solution)/shard_map/ppermute | solution.py:761
  129.1 48.3 %collective-permute-start.4 = (bf16[256,1024]{1,0:T(8,128)(2,1)S(1)}, bf16[256,1024]{1,0:T(8,128)(2,1)}, u32[]{:S(2)}, u32[]{:S(2)}) collective-permute-start(bf16[256,1024]{1,0:T(8,128)(2,1)S(1)} %copy-done.20), channel_id=1, source_target_pairs={{0,2},{1,3},{2,0},{3,1},{4,6},{5,7},{6,4},{7,5},{8,10},{9,11},{10,... | collective-permute-start | bytes 1572872 | tf_op jit(solution)/shard_map/ppermute | solution.py:761
  130.8 46.6 %all-to-all-start.1 = ((bf16[4,512,256]{2,1,0:T(8,128)(2,1)}), bf16[4,512,256]{2,1,0:T(8,128)(2,1)S(1)}, u32[]{:S(2)}, u32[]{:S(2)}) async-start(bf16[4,512,256]{2,1,0:T(8,128)(2,1)} %bitcast.12), calls=%async_computation.1 | async-start | bytes 2097152 | tf_op jit(solution)/shard_map/all_to_all | solution.py:772
  136.8 64.3 %collective-permute-start.7 = (bf16[512,1024]{1,0:T(8,128)(2,1)}, bf16[512,1024]{1,0:T(8,128)(2,1)}, u32[]{:S(2)}, u32[]{:S(2)}) collective-permute-start(bf16[512,1024]{1,0:T(8,128)(2,1)} %constant_dynamic-slice_fusion.7), channel_id=1, source_target_pairs={{0,2},{1,3},{2,0},{3,1},{4,6},{5,7},{6,4},{7,5},{8,10},{9,11},{10,... | collective-permute-start | bytes 3145736 | tf_op jit(solution)/shard_map/ppermute | solution.py:761
  217.1 41.2 %collective-permute-start.10 = (bf16[1024,1024]{1,0:T(8,128)(2,1)S(1)}, bf16[1024,1024]{1,0:T(8,128)(2,1)}, u32[]{:S(2)}, u32[]{:S(2)}) collective-permute-start(bf16[1024,1024]{1,0:T(8,128)(2,1)S(1)} %constant_dynamic-update-slice_fusion.14.refs_2_), channel_id=1, source_target_pairs={{0,1},{1,0},{2,3},{3,2},{4,5},{5,4},{6,7},{7,6},{8,9},{9,8},{10,11... | collective-permute-start | bytes 6291464 | tf_op jit(solution)/shard_map/ppermute | solution.py:761
  217.2 41.1 %collective-permute-start.11 = (bf16[512,1024]{1,0:T(8,128)(2,1)}, bf16[512,1024]{1,0:T(8,128)(2,1)S(1)}, u32[]{:S(2)}, u32[]{:S(2)}) collective-permute-start(bf16[512,1024]{1,0:T(8,128)(2,1)} %collective-permute-done.7), channel_id=1, source_target_pairs={{0,4},{4,0},{8,12},{12,8},{16,20},{20,16},{24,28},{28,24},{1,5},{5... | collective-permute-start | bytes 3145736 | tf_op jit(solution)/shard_map/ppermute | solution.py:837
  320.4 51.2 %collective-permute-start.20 = (bf16[1024,1024]{1,0:T(8,128)(2,1)S(1)}, bf16[1024,1024]{1,0:T(8,128)(2,1)}, u32[]{:S(2)}, u32[]{:S(2)}) collective-permute-start(bf16[1024,1024]{1,0:T(8,128)(2,1)S(1)} %add_convert_fusion.5), channel_id=1, source_target_pairs={{0,2},{1,3},{2,0},{3,1},{4,6},{5,7},{6,4},{7,5},{8,10},{9,11},{10,... | collective-permute-start | bytes 6291464 | tf_op jit(solution)/shard_map/ppermute | solution.py:761
  356.2 40.8 %collective-permute-start.16 = (bf16[1024,1024]{1,0:T(8,128)(2,1)}, bf16[1024,1024]{1,0:T(8,128)(2,1)}, u32[]{:S(2)}, u32[]{:S(2)}) collective-permute-start(bf16[1024,1024]{1,0:T(8,128)(2,1)} %get-tuple-element.273), channel_id=1, source_target_pairs={{0,1},{1,0},{2,3},{3,2},{4,5},{5,4},{6,7},{7,6},{8,9},{9,8},{10,11... | collective-permute-start | bytes 6291464 | tf_op jit(solution)/shard_map/ppermute | solution.py:761
  356.2 40.8 %collective-permute-start.17 = (bf16[1024,1024]{1,0:T(8,128)(2,1)}, bf16[1024,1024]{1,0:T(8,128)(2,1)}, u32[]{:S(2)}, u32[]{:S(2)}) collective-permute-start(bf16[1024,1024]{1,0:T(8,128)(2,1)} %get-tuple-element.274), channel_id=1, source_target_pairs={{0,1},{1,0},{2,3},{3,2},{4,5},{5,4},{6,7},{7,6},{8,9},{9,8},{10,11... | collective-permute-start | bytes 6291464 | tf_op jit(solution)/shard_map/ppermute | solution.py:761
  371.6 40.6 %all-to-all-start.3 = ((bf16[4,1536,256]{2,1,0:T(8,128)(2,1)}), bf16[4,1536,256]{2,1,0:T(8,128)(2,1)S(1)}, u32[]{:S(2)}, u32[]{:S(2)}) async-start(bf16[4,1536,256]{2,1,0:T(8,128)(2,1)} %get-tuple-element.282), calls=%async_computation.3 | async-start | bytes 6291456 | tf_op jit(solution)/shard_map/all_to_all | solution.py:772
  375.4 246.4 %all-reduce.6.cloned.1.call-start = ((), (), s32[]{:S(2)}) async-start(), calls=%async_computation.8 | async-start | bytes 5242880 | tf_op jit(solution)/shard_map/psum | solution.py:1043
  412.3 57.3 %collective-permute-start.21 = (bf16[1024,1024]{1,0:T(8,128)(2,1)}, bf16[1024,1024]{1,0:T(8,128)(2,1)}, u32[]{:S(2)}, u32[]{:S(2)}) collective-permute-start(bf16[1024,1024]{1,0:T(8,128)(2,1)} %add_convert_fusion.6), channel_id=1, source_target_pairs={{0,2},{1,3},{2,0},{3,1},{4,6},{5,7},{6,4},{7,5},{8,10},{9,11},{10,... | collective-permute-start | bytes 6291464 | tf_op jit(solution)/shard_map/ppermute | solution.py:761
  419.4 51.5 %collective-permute-start.23 = (bf16[512,1024]{1,0:T(8,128)(2,1)}, bf16[512,1024]{1,0:T(8,128)(2,1)}, u32[]{:S(2)}, u32[]{:S(2)}) collective-permute-start(bf16[512,1024]{1,0:T(8,128)(2,1)} %constant_dynamic-slice_fusion.6), channel_id=1, source_target_pairs={{0,4},{4,0},{8,12},{12,8},{16,20},{20,16},{24,28},{28,24},{1,5},{5... | collective-permute-start | bytes 3145736 | tf_op jit(solution)/shard_map/ppermute | solution.py:819
  421.2 49.7 %collective-permute-start.22 = (bf16[256,1024]{1,0:T(8,128)(2,1)S(1)}, bf16[256,1024]{1,0:T(8,128)(2,1)S(1)}, u32[]{:S(2)}, u32[]{:S(2)}) collective-permute-start(bf16[256,1024]{1,0:T(8,128)(2,1)S(1)} %add_convert_fusion.13), channel_id=1, source_target_pairs={{0,2},{1,3},{2,0},{3,1},{4,6},{5,7},{6,4},{7,5},{8,10},{9,11},{10,... | collective-permute-start | bytes 1572872 | tf_op jit(solution)/shard_map/ppermute | solution.py:761
  480.3 250.9 %all-reduce.4.cloned.1.call-start = ((), (), s32[]{:S(2)}) async-start(), calls=%async_computation.7 | async-start | bytes 3194880 | tf_op jit(solution)/shard_map/psum | solution.py:1060
  493.8 51.0 %collective-permute-start.26 = (bf16[512,1024]{1,0:T(8,128)(2,1)}, bf16[512,1024]{1,0:T(8,128)(2,1)}, u32[]{:S(2)}, u32[]{:S(2)}) collective-permute-start(bf16[512,1024]{1,0:T(8,128)(2,1)} %get-tuple-element.309), channel_id=1, source_target_pairs={{0,1},{1,0},{2,3},{3,2},{4,5},{5,4},{6,7},{7,6},{8,9},{9,8},{10,11... | collective-permute-start | bytes 3145736 | tf_op jit(solution)/shard_map/ppermute | solution.py:761
  494.3 50.4 %collective-permute-start.27 = (bf16[512,1024]{1,0:T(8,128)(2,1)}, bf16[512,1024]{1,0:T(8,128)(2,1)}, u32[]{:S(2)}, u32[]{:S(2)}) collective-permute-start(bf16[512,1024]{1,0:T(8,128)(2,1)} %get-tuple-element.310), channel_id=1, source_target_pairs={{0,1},{1,0},{2,3},{3,2},{4,5},{5,4},{6,7},{7,6},{8,9},{9,8},{10,11... | collective-permute-start | bytes 3145736 | tf_op jit(solution)/shard_map/ppermute | solution.py:761
  494.6 50.1 %collective-permute-start.30 = (bf16[128,1024]{1,0:T(8,128)(2,1)S(1)}, bf16[128,1024]{1,0:T(8,128)(2,1)S(1)}, u32[]{:S(2)}, u32[]{:S(2)}) collective-permute-start(bf16[128,1024]{1,0:T(8,128)(2,1)S(1)} %constant_dynamic-slice_fusion), channel_id=1, source_target_pairs={{0,16},{4,20},{8,24},{12,28},{16,0},{20,4},{24,8},{28,12},{1,17},{... | collective-permute-start | bytes 786440 | tf_op jit(solution)/shard_map/ppermute | solution.py:819
  497.1 47.6 %collective-permute-start.29 = (f32[64,128]{1,0:T(8,128)S(1)}, f32[64,128]{1,0:T(8,128)S(1)}, u32[]{:S(2)}, u32[]{:S(2)}) collective-permute-start(f32[64,128]{1,0:T(8,128)S(1)} %add.225), channel_id=1, source_target_pairs={{0,2},{1,3},{2,0},{3,1},{4,6},{5,7},{6,4},{7,5},{8,10},{9,11},{10,... | collective-permute-start | bytes 98312 | tf_op jit(solution)/shard_map/ppermute | solution.py:805
  547.4 74.4 %collective-permute-start.28 = (bf16[512,1024]{1,0:T(8,128)(2,1)}, bf16[512,1024]{1,0:T(8,128)(2,1)S(1)}, u32[]{:S(2)}, u32[]{:S(2)}) collective-permute-start(bf16[512,1024]{1,0:T(8,128)(2,1)} %add_convert_fusion.9), channel_id=1, source_target_pairs={{0,2},{1,3},{2,0},{3,1},{4,6},{5,7},{6,4},{7,5},{8,10},{9,11},{10,... | collective-permute-start | bytes 3145736 | tf_op jit(solution)/shard_map/ppermute | solution.py:761
  570.5 52.4 %collective-permute-start.34 = (bf16[256,1024]{1,0:T(8,128)(2,1)S(1)}, bf16[256,1024]{1,0:T(8,128)(2,1)S(1)}, u32[]{:S(2)}, u32[]{:S(2)}) collective-permute-start(bf16[256,1024]{1,0:T(8,128)(2,1)S(1)} %constant_dynamic-update-slice_fusion.10), channel_id=1, source_target_pairs={{0,8},{4,12},{8,0},{12,4},{16,24},{20,28},{24,16},{28,20},{1,9},{5... | collective-permute-start | bytes 1572872 | tf_op jit(solution)/shard_map/ppermute | solution.py:822
  (76 other events, 1180.1 us)
Sparse Core Ops, SparseCore 0:
  10.1 37.1 all-gather.3
  49.5 34.4 all-gather.5
  86.2 39.9 all-gather.7
  480.4 132.5 all-reduce.5
  638.1 93.0 all-reduce.3

commit v8 on v7

--- a/solution.py
+++ b/solution.py
@@ -196,6 +196,77 @@
 
 def params():
     return pltpu.CompilerParams(vmem_limit_bytes=VMEM_LIMIT)
+
+
+def add_terms(*terms):
+    rows, columns = terms[0].shape
+    block = largest_block(rows, 256)
+
+    def body(*refs):
+        total = refs[0][...].astype(f32)
+        for ref in refs[1:-1]:
+            total = total + ref[...].astype(f32)
+        refs[-1][...] = total.astype(refs[-1].dtype)
+
+    spec = pl.BlockSpec((block, columns), lambda i: (i, 0))
+    return pl.pallas_call(
+        body,
+        grid=(rows // block,),
+        in_specs=[spec] * len(terms),
+        out_specs=spec,
+        out_shape=jax.ShapeDtypeStruct((rows, columns), terms[0].dtype),
+        compiler_params=params(),
+        cost_estimate=hint(0, rows * columns),
+        name="add_terms",
+    )(*terms)
+
+
+def join_halves(side, own, other):
+    half, columns = own.shape
+
+    def body(side_ref, own_ref, other_ref, out_ref):
+        first = pl.multiple_of(side_ref[0] * half, half)
+        second = pl.multiple_of((1 - side_ref[0]) * half, half)
+        out_ref[pl.ds(first, half), :] = own_ref[...]
+        out_ref[pl.ds(second, half), :] = other_ref[...]
+
+    width = largest_block(columns, 256)
+    spec = pl.BlockSpec((half, width), lambda i: (0, i))
+    return pl.pallas_call(
+        body,
+        grid=(columns // width,),
+        in_specs=[pl.BlockSpec(memory_space=pltpu.SMEM), spec, spec],
+        out_specs=pl.BlockSpec((2 * half, width), lambda i: (0, i)),
+        out_shape=jax.ShapeDtypeStruct((2 * half, columns), own.dtype),
+        compiler_params=params(),
+        cost_estimate=hint(0, half * columns),
+        name="join_halves",
+    )(side, own, other)
+
+
+def project(rows_in, weight, bias):
+    rows, model = rows_in.shape
+    width = weight.shape[2]
+    block = largest_block(rows, 512)
+
+    def body(x_ref, weight_ref, bias_ref, out_ref):
+        for c in range(3):
+            out_ref[c] = (nn(x_ref[...], weight_ref[c]) + bias_ref[c]).astype(bf16)
+
+    return pl.pallas_call(
+        body,
+        grid=(rows // block,),
+        in_specs=[
+            pl.BlockSpec((block, model), lambda i: (i, 0)),
+            pl.BlockSpec((3, model, width), lambda i: (0, 0, 0)),
+            pl.BlockSpec((3, 1, width), lambda i: (0, 0, 0)),
+        ],
+        out_specs=pl.BlockSpec((3, block, width), lambda i: (0, i, 0)),
+        out_shape=jax.ShapeDtypeStruct((3, rows, width), bf16),
+        compiler_params=params(),
+        cost_estimate=hint(6 * rows * model * width, rows * width),
+        name="project",
+    )(rows_in, weight, bias)
 
 
 def norm_item(patches, item, norm_gain, norm_shift):
@@ -771,11 +842,14 @@
     def exchange(stacked):
         return lax.all_to_all(stacked, "tensor", 0, 0)
 
-    def sum_near(blocks, anchor):
+    def sum_near(blocks, anchor, plain=False):
         if not square:
             return (jnp.stack(blocks),), anchor
         anchor, (near_own, near_far) = tie(anchor, (swap(blocks[1], 1), swap(blocks[3], 1)))
-        far = (blocks[2].astype(f32) + near_far.astype(f32)).astype(blocks[2].dtype)
+        if plain:
+            far = (blocks[2].astype(f32) + near_far.astype(f32)).astype(blocks[2].dtype)
+        else:
+            far = add_terms(blocks[2], near_far)
         return (blocks[0], near_own, far), anchor
 
     def terms_far(stage, anchor):
@@ -789,10 +863,7 @@
 
     def sum_far(stage, anchor):
         terms, anchor = terms_far(stage, anchor)
-        total = terms[0].astype(f32)
-        for term in terms[1:]:
-            total = total + term.astype(f32)
-        return total.astype(terms[0].dtype), anchor
+        return (add_terms(*terms) if len(terms) > 1 else terms[0]), anchor
 
     steps = []
     for axis, size in (("tensor", tensor_size), ("dp", group_size)):
@@ -823,10 +894,7 @@
         return in_halves(value, received, side), anchor
 
     def in_halves(own, other, side):
-        rows = own.shape[0]
-        whole = jnp.zeros((2 * rows,) + own.shape[1:], own.dtype)
-        whole = lax.dynamic_update_slice_in_dim(whole, own, side * rows, axis=0)
-        return lax.dynamic_update_slice_in_dim(whole, other, (1 - side) * rows, axis=0)
+        return join_halves(side.reshape(1).astype(jnp.int32), own, other)
 
     def fetch_half(own):
         half = own.shape[0] // 2
@@ -915,9 +983,7 @@
             if not last:
                 every, following = tie(every, normed[i + 1])
                 following = gather_rows(following)
-            qkv = (
-                jnp.einsum("wz,gzh->gwh", every, query_key_value_weight, preferred_element_type=f32) + proj_bias
-            ).astype(bf16)
+            qkv = project(every, query_key_value_weight, proj_bias)
             if i == 0:
                 qkv, (weights_near, bias_far) = tie(qkv, (weights_near, bias_far))
             out, lse = attend(qkv)
@@ -1013,7 +1079,7 @@
                 normed_mlp, pre_grad, [2, 0], attended_rows, grad_low, tensor_size
             )
             second, (up_near, up_diag_near) = tie(second, (up_near, up_diag_near))
-            up_far_sum = (first.astype(f32) + up_diag_near.astype(f32)).astype(bf16)
+            up_far_sum = add_terms(first, up_diag_near)
             out_stage, up_far_sum = sum_near(out_grads, up_far_sum)
             up_far_sum, grad_attended = tie(up_far_sum, grad_attended)
             up_stage = (second, up_near, up_far_sum)
@@ -1061,7 +1127,7 @@
                 output = layer_out(layer_sum, residual, down_bias[None, :], own_valid, patches.shape)
                 partial = project_rows(place, dqkv, query_key_value_weight, tensor_size)
                 if i >= 1:
-                    grad_normed[i - 1], partial = sum_near(grad_normed[i - 1], partial)
+                    grad_normed[i - 1], partial = sum_near(grad_normed[i - 1], partial, True)
                 raw = jnp.stack(
                     [
                         jnp.sum(sums[0] * weights_wide, axis=(0, 2)),
@@ -1074,7 +1140,7 @@
         grad_inputs = None
         for i in range(slot_count):
             if i == slot_count - 1:
-                grad_normed[i], grad_residual = sum_near(grad_normed[i], grad_residual)
+                grad_normed[i], grad_residual = sum_near(grad_normed[i], grad_residual, True)
             terms = grad_normed[i]
             if i >= slot_count - 2:
                 terms, grad_residual = terms_far(terms, grad_residual)

time: 750 us -> 759 us (1.012)
  Pallas kernels: 473 us -> 539 us
  matrix products: 21.9 us -> 0 us
  other arithmetic: 49.2 us -> 30.7 us
    pallas_call x0 -> x15, Pallas kernels: none -> 66.1 us  [the longest x7 26.2 us: add_terms(): pl.pallas_call(body, grid=(rows // block,), in_specs=[spec] * len(terms),...]
    dot_general x3 -> x0, matrix products: 21.9 us -> none  [shards(): jnp.einsum('wz,gzh->gwh', every, query_key_value_weight, preferred_elemen...]
    convert_element_type x4 -> x0, other arithmetic: 15.7 us -> none  [the longest x3 11.2 us: sum_far(): return (total.astype(terms[0].dtype), anchor)]
    ppermute x30, waiting for transfers between devices: 5.28 us -> 18.2 us  [swap(): lax.ppermute(value, 'tensor', [(i, i ^ bits) for i in range(tensor_size)])]
    psum x1, waiting for transfers between devices: 21.5 us -> 12.9 us  [shards(): qkv_all = lax.psum(qkv_low, 'dp')]
  transfers between devices with their start and end apart: 57 -> 57, of which waited for: 15 -> 14; matrix products, arithmetic and copies ran while one was open for 10% -> 5% of each run, Pallas kernels for 58% -> 65%
where the time goes in v8:
time: 759 us; the launch traced here: 753 us
  Pallas kernels  539 us (71%)
  waiting for transfers between devices  97.8 us (13%)
  starting transfers between devices  49.5 us (7%)
  other arithmetic  30.7 us (4%)
  local copies, waits for them, and re-layouts  20.5 us (3%)
  between operations  15.6 us (2%)
    pallas_call x3, Pallas kernels, attend_back(): pl.pallas_call(body, grid=(pairs, kblocks), in_specs=[pl.BlockSpec((None,...  141 us
    pallas_call x3, Pallas kernels, attend(): pl.pallas_call(body, grid=(pairs, length // qblock), in_specs=[pl.BlockSp...  71.9 us
    pallas_call x2, Pallas kernels, mlp_forward(): pl.pallas_call(body, grid=(steps,), in_specs=in_specs, out_specs=[slope_s...  71.8 us
    pallas_call x3, Pallas kernels, project_back(): pl.pallas_call(kernel, grid=(steps,), in_specs=in_specs, out_specs=out_sp...  38.1 us
    pallas_call x2, Pallas kernels, weight_back(): pl.pallas_call(body, grid=(steps,), in_specs=in_specs, out_specs=[pl.Bloc...  34.9 us
    pallas_call x2, Pallas kernels, mlp_backward(): pl.pallas_call(body, grid=(rows // block,), in_specs=in_specs, out_specs=...  34.6 us
    pallas_call x7, Pallas kernels, add_terms(): pl.pallas_call(body, grid=(rows // block,), in_specs=[spec] * len(terms),...  26.2 us
    all_gather x3, waiting for transfers between devices, gather_rows(): return lax.all_gather(own, 'tensor', axis=0, tiled=True)  22.6 us
  transfers between devices with their start and end apart: 57, of which 14 were waited for; matrix products, arithmetic and copies ran while one was open for 5% of the time, Pallas kernels for 65%

profile of v8, /device:TPU:0, one launch (start us, length us, event | category | flops | bytes accessed | tf_op | source)
XLA Modules:
  0.0 753.0 jit_solution(225007376076953472)
XLA Ops:
  23.5 11.2 %cot_back.1.refs_0_ = bf16[1536,2048]{1,0:T(8,128)(2,1)} custom-call(bf16[1536,1024]{1,0:T(8,128)(2,1)} %fusion.cot_ref.refs_1_.refs_0_, bf16[1024,1024]{1,0:T(8,128)(2,1)} %refs_6_, bf16[1024,1024]{1,0:T(8,128)(2,1)} %collective-permute-done.refs_1_.refs_7_), custom_call_target="tpu_custom_call" | custom-call | flops 100663296 | bytes 1572864 | tf_op jit(solution)/shard_map/cot_back/pallas_call | solution.py:565
  34.7 12.7 %all-gather.4.cloned.1.call-done.x_ref.refs_1_ = bf16[2048,1024]{1,0:T(8,128)(2,1)} async-done(((bf16[512,1024]{1,0:T(8,128)(2,1)}), bf16[2048,1024]{1,0:T(8,128)(2,1)}) %all-gather.4.cloned.1.call-update) | async-done | bytes 4194320 | tf_op jit(solution)/shard_map/all_gather | solution.py:968
  57.3 24.1 %attend.3 = (bf16[2048,256]{1,0:T(8,128)(2,1)}, f32[2,2,2048]{2,1,0:T(2,128)}) custom-call(bf16[3,2048,256]{2,1,0:T(8,128)(2,1)} %project.3.q_ref.k_ref.v_ref, bf16[3,2048,256]{2,1,0:T(8,128)(2,1)} %project.3.q_ref.k_ref.v_ref, bf16[3,2048,256]{2,1,0:T(8,128)(2,1)} %project.3.q_ref.k_ref.v_ref), custom_call_target="tpu_custom_call" | custom-call | flops 134217728 | bytes 524288 | tf_op jit(solution)/shard_map/attend/pallas_call | solution.py:76
  95.3 24.0 %attend.4 = (bf16[2048,256]{1,0:T(8,128)(2,1)}, f32[2,2,2048]{2,1,0:T(2,128)}) custom-call(bf16[3,2048,256]{2,1,0:T(8,128)(2,1)} %project.4.q_ref.k_ref.v_ref, bf16[3,2048,256]{2,1,0:T(8,128)(2,1)} %project.4.q_ref.k_ref.v_ref, bf16[3,2048,256]{2,1,0:T(8,128)(2,1)} %project.4.q_ref.k_ref.v_ref), custom_call_target="tpu_custom_call" | custom-call | flops 134217728 | bytes 524288 | tf_op jit(solution)/shard_map/attend/pallas_call | solution.py:76
  143.5 23.9 %attend.5 = (bf16[2048,256]{1,0:T(8,128)(2,1)}, f32[2,2,2048]{2,1,0:T(2,128)}) custom-call(bf16[3,2048,256]{2,1,0:T(8,128)(2,1)} %project.5.q_ref.k_ref.v_ref, bf16[3,2048,256]{2,1,0:T(8,128)(2,1)} %project.5.q_ref.k_ref.v_ref, bf16[3,2048,256]{2,1,0:T(8,128)(2,1)} %project.5.q_ref.k_ref.v_ref), custom_call_target="tpu_custom_call" | custom-call | flops 134217728 | bytes 524288 | tf_op jit(solution)/shard_map/attend/pallas_call | solution.py:76
  167.4 10.5 %collective-permute-done.4 = bf16[256,1024]{1,0:T(8,128)(2,1)} collective-permute-done((bf16[256,1024]{1,0:T(8,128)(2,1)}, bf16[256,1024]{1,0:T(8,128)(2,1)}, u32[]{:S(2)}, u32[]{:S(2)}) %collective-permute-start.4) | collective-permute-done | bytes 524320 | tf_op jit(solution)/shard_map/ppermute | solution.py:832
  200.4 10.6 %all-to-all-done.2.refs_6_ = bf16[4,512,256]{2,1,0:T(8,128)(2,1)} async-done(((bf16[4,512,256]{2,1,0:T(8,128)(2,1)}), bf16[4,512,256]{2,1,0:T(8,128)(2,1)}, u32[]{:S(2)}, u32[]{:S(2)}) %all-to-all-start.2) | async-done | bytes 1048608 | tf_op jit(solution)/shard_map/all_to_all | solution.py:843
  224.7 35.0 %mlp_forward.2 = (bf16[1536,2048]{1,0:T(8,128)(2,1)}, f32[1536,1024]{1,0:T(8,128)}, bf16[1024,1024]{1,0:T(8,128)(2,1)}, bf16[1024,1024]{1,0:T(8,128)(2,1)}) custom-call(bf16[1536,1024]{1,0:T(8,128)(2,1)} %get-tuple-element.239.refs_0_.x_ref, bf16[1536,1024]{1,0:T(8,128)(2,1)} %fusion.cot_ref.refs_1_.refs_0_, bf16[1024,1024]{1,0:T(8,128)(2,1)} %refs_2_.1, ...), custom_call_target="tpu_custom_call" | custom-call | flops 301989888 | bytes 1572864 | tf_op jit(solution)/shard_map/mlp_forward/pallas_call | solution.py:537
  269.1 36.8 %mlp_forward.3 = (bf16[1536,2048]{1,0:T(8,128)(2,1)}, f32[1536,1024]{1,0:T(8,128)}, bf16[1024,1024]{1,0:T(8,128)(2,1)}, bf16[1024,1024]{1,0:T(8,128)(2,1)}) custom-call(bf16[1536,1024]{1,0:T(8,128)(2,1)} %get-tuple-element.239.refs_0_.x_ref, bf16[1536,1024]{1,0:T(8,128)(2,1)} %fusion.cot_ref.refs_1_.refs_0_, ...), custom_call_target="tpu_custom_call", output_to_operand_aliasing={{1}: (8, {})} | custom-call | flops 301989888 | bytes 1572864 | tf_op jit(solution)/shard_map/mlp_forward/pallas_call | solution.py:537
  306.5 13.4 %mlp_backward.2 = (bf16[1536,4096]{1,0:T(8,128)(2,1)}, f32[1536,1024]{1,0:T(8,128)}, f32[1,2048]{1,0:T(1,128)}) custom-call(bf16[1536,2048]{1,0:T(8,128)(2,1)} %cot_back.1.refs_0_, bf16[1536,2048]{1,0:T(8,128)(2,1)} %get-tuple-element.256.refs_1_, bf16[1024,1024]{1,0:T(8,128)(2,1)} %refs_2_.1, bf16[1024,1024]{1,0:T(8,128)(2,1)} %collective-permute-done.2.refs_3_), custom_call_target="tpu_custom_call" | custom-call | flops 201326592 | bytes 1572864 | tf_op jit(solution)/shard_map/mlp_backward/pallas_call | solution.py:623
  325.9 21.2 %mlp_backward.3 = (bf16[1536,4096]{1,0:T(8,128)(2,1)}, f32[1536,1024]{1,0:T(8,128)}, f32[1,2048]{1,0:T(1,128)}) custom-call(bf16[1536,1024]{1,0:T(8,128)(2,1)} %fusion.cot_ref.refs_1_.refs_0_, bf16[1536,2048]{1,0:T(8,128)(2,1)} %get-tuple-element.254.refs_1_, bf16[1024,1024]{1,0:T(8,128)(2,1)} %join_halves.5.refs_2_, ...), custom_call_target="tpu_custom_call", output_to_operand_aliasing={{0}: (6, {}), {1}: (7, {})} | custom-call | flops 201326592 | bytes 1572864 | tf_op jit(solution)/shard_map/mlp_backward/pallas_call | solution.py:623
  347.1 14.2 %weight_back.2 = (bf16[1024,1024]{1,0:T(8,128)(2,1)}, bf16[1024,1024]{1,0:T(8,128)(2,1)}) custom-call(bf16[1536,1024]{1,0:T(8,128)(2,1)} %get-tuple-element.239.refs_0_.x_ref, bf16[1536,4096]{1,0:T(8,128)(2,1)} %get-tuple-element.263.refs_0_.refs_1_, bf16[1536,4096]{1,0:T(8,128)(2,1)} %get-tuple-element.263.refs_0_.refs_1_), custom_call_target="tpu_custom_call" | custom-call | flops 100663296 | bytes 1572864 | tf_op jit(solution)/shard_map/weight_back/pallas_call | solution.py:697
  361.3 14.9 %residual_back.1 = (f32[1536,1024]{1,0:T(8,128)}, bf16[1536,1024]{1,0:T(8,128)(2,1)}, f32[8,1024]{1,0:T(8,128)}, bf16[4,1536,256]{2,1,0:T(8,128)(2,1)}) custom-call(s32[1]{0:T(128)} %bitcast.refs_0_.place_ref, f32[1536,1024]{1,0:T(8,128)} %get-tuple-element.268.refs_1_, f32[1536,1024]{1,0:T(8,128)} %get-tuple-element.269.refs_2_.residual_ref, ...), custom_call_target="tpu_custom_call" | custom-call | flops 50331648 | bytes 524288 | tf_op jit(solution)/shard_map/residual_back/pallas_call | solution.py:372
  380.5 20.8 %weight_back.3 = (bf16[1024,1024]{1,0:T(8,128)(2,1)}, bf16[1024,1024]{1,0:T(8,128)(2,1)}, bf16[256,1024]{1,0:T(8,128)(2,1)}, bf16[256,1024]{1,0:T(8,128)(2,1)}, ...) custom-call(bf16[1536,1024]{1,0:T(8,128)(2,1)} %get-tuple-element.239.refs_0_.x_ref, ...), custom_call_target="tpu_custom_call" | custom-call | flops 100663296 | bytes 1572864 | tf_op jit(solution)/shard_map/weight_back/pallas_call | solution.py:697
  407.0 9.8 %all-to-all-done.3.grad_ref = bf16[4,1536,256]{2,1,0:T(8,128)(2,1)S(1)} async-done(((bf16[4,1536,256]{2,1,0:T(8,128)(2,1)}), bf16[4,1536,256]{2,1,0:T(8,128)(2,1)S(1)}, u32[]{:S(2)}, u32[]{:S(2)}) %all-to-all-start.3) | async-done | bytes 3145760 | tf_op jit(solution)/shard_map/all_to_all | solution.py:843
  429.6 47.4 %attend_back.4.refs_2_ = bf16[3,2048,256]{2,1,0:T(8,128)(2,1)} custom-call(bf16[3,2048,256]{2,1,0:T(8,128)(2,1)} %project.3.q_ref.k_ref.v_ref, bf16[3,2048,256]{2,1,0:T(8,128)(2,1)} %project.3.q_ref.k_ref.v_ref, bf16[3,2048,256]{2,1,0:T(8,128)(2,1)} %project.3.q_ref.k_ref.v_ref, bf16[2048,256]{1,0:T(8,128)(2,1)} %get-tuple-element.213.out_ref, ...), custom_call_target="tpu_custom_call" | custom-call | flops 335544320 | bytes 524288 | tf_op jit(solution)/shard_map/attend_back/pallas_call | solution.py:169
  488.2 13.4 %project_back.3 = (bf16[512,1024]{1,0:T(8,128)(2,1)}, bf16[512,1024]{1,0:T(8,128)(2,1)}, bf16[512,1024]{1,0:T(8,128)(2,1)}, bf16[512,1024]{1,0:T(8,128)(2,1)}, f...) custom-call(s32[1]{0:T(128)} %bitcast.refs_0_.place_ref, bf16[2048,1024]{1,0:T(8,128)(2,1)} %all-gather.4.cloned.1.call-done.x_ref.refs_1_, ...), custom_call_target="tpu_custom_call" | custom-call | flops 100663296 | bytes 524288 | tf_op jit(solution)/shard_map/project_back/pallas_call | solution.py:779
  506.0 47.0 %attend_back.5.refs_2_ = bf16[3,2048,256]{2,1,0:T(8,128)(2,1)} custom-call(bf16[3,2048,256]{2,1,0:T(8,128)(2,1)} %project.4.q_ref.k_ref.v_ref, bf16[3,2048,256]{2,1,0:T(8,128)(2,1)} %project.4.q_ref.k_ref.v_ref, bf16[3,2048,256]{2,1,0:T(8,128)(2,1)} %project.4.q_ref.k_ref.v_ref, bf16[2048,256]{1,0:T(8,128)(2,1)} %get-tuple-element.215.out_ref, ...), custom_call_target="tpu_custom_call" | custom-call | flops 335544320 | bytes 524288 | tf_op jit(solution)/shard_map/attend_back/pallas_call | solution.py:169
  557.7 14.1 %project_back.4 = (bf16[512,1024]{1,0:T(8,128)(2,1)}, bf16[512,1024]{1,0:T(8,128)(2,1)}, bf16[512,1024]{1,0:T(8,128)(2,1)}, bf16[512,1024]{1,0:T(8,128)(2,1)}, f...) custom-call(s32[1]{0:T(128)} %bitcast.refs_0_.place_ref, ...), custom_call_target="tpu_custom_call", output_to_operand_aliasing={{4}: (4, {}), {5}: (5, {})} | custom-call | flops 100663296 | bytes 524288 | tf_op jit(solution)/shard_map/project_back/pallas_call | solution.py:779
  584.5 46.8 %attend_back.3.refs_2_.dqkv_ref = bf16[3,2048,256]{2,1,0:T(8,128)(2,1)} custom-call(bf16[3,2048,256]{2,1,0:T(8,128)(2,1)} %project.5.q_ref.k_ref.v_ref, bf16[3,2048,256]{2,1,0:T(8,128)(2,1)} %project.5.q_ref.k_ref.v_ref, bf16[3,2048,256]{2,1,0:T(8,128)(2,1)} %project.5.q_ref.k_ref.v_ref, bf16[2048,256]{1,0:T(8,128)(2,1)} %get-tuple-element.219.out_ref, ...), custom_call_target="tpu_custom_call" | custom-call | flops 335544320 | bytes 524288 | tf_op jit(solution)/shard_map/attend_back/pallas_call | solution.py:169
  632.3 10.6 %project_back.5 = (f32[3,1024,256]{2,1,0:T(8,128)}, f32[8,256]{1,0:T(8,128)}, bf16[3,1040,256]{2,1,0:T(8,128)(2,1)}) custom-call(s32[1]{0:T(128)} %bitcast.refs_0_.place_ref, bf16[2048,1024]{1,0:T(8,128)(2,1)} %all-gather.8.cloned.1.call-done.x_ref.refs_1_, ...), custom_call_target="tpu_custom_call", output_to_operand_aliasing={{0}: (4, {}), {1}: (5, {})} | custom-call | flops 100663296 | bytes 524288 | tf_op jit(solution)/shard_map/project_back/pallas_call | solution.py:779
  647.7 8.7 %project_rows.1 = (bf16[512,1024]{1,0:T(8,128)(2,1)}, bf16[512,1024]{1,0:T(8,128)(2,1)}, bf16[512,1024]{1,0:T(8,128)(2,1)}, bf16[512,1024]{1,0:T(8,128)(2,1)}) custom-call(s32[1]{0:T(128)} %bitcast.refs_0_.place_ref, bf16[3,2048,256]{2,1,0:T(8,128)(2,1)} %attend_back.3.refs_2_.dqkv_ref, bf16[3,1024,256]{2,1,0:T(8,128)(2,1)} %weight_ref.7), custom_call_target="tpu_custom_call" | custom-call | flops 50331648 | bytes 524288 | tf_op jit(solution)/shard_map/project_rows/pallas_call | solution.py:812
  693.0 15.8 %collective-permute-done.42.other_ref = bf16[512,1024]{1,0:T(8,128)(2,1)} collective-permute-done((bf16[512,1024]{1,0:T(8,128)(2,1)S(1)}, bf16[512,1024]{1,0:T(8,128)(2,1)}, u32[]{:S(2)}, u32[]{:S(2)}) %collective-permute-start.42) | collective-permute-done | bytes 1048608 | tf_op jit(solution)/shard_map/ppermute | solution.py:893
  728.5 12.9 %all-reduce.4.cloned.1.call-done = bf16[3,1040,256]{2,1,0:T(8,128)(2,1)} async-done(((bf16[3,1040,256]{2,1,0:T(8,128)(2,1)}), bf16[3,1040,256]{2,1,0:T(8,128)(2,1)}) %all-reduce.4.cloned.1.call-update) | async-done | bytes 1597456 | tf_op jit(solution)/shard_map/psum | solution.py:1126
  (286 shorter events, 237.8 us)
Async XLA Ops:
  7.2 40.2 %all-gather.4.cloned.1.call-start = ((), (), s32[]{:S(2)}) async-start(), calls=%async_computation.4 | async-start | bytes 5242880 | tf_op jit(solution)/shard_map/all_gather | solution.py:968
  10.0 74.0 %all-gather.6.cloned.1.call-start = ((), (), s32[]{:S(2)}) async-start(), calls=%async_computation.5 | async-start | bytes 5242880 | tf_op jit(solution)/shard_map/all_gather | solution.py:968
  47.4 79.1 %all-gather.8.cloned.1.call-start = ((), (), s32[]{:S(2)}) async-start(), calls=%async_computation.6 | async-start | bytes 5242880 | tf_op jit(solution)/shard_map/all_gather | solution.py:968
  84.1 42.4 %all-to-all-start = ((bf16[4,512,256]{2,1,0:T(8,128)(2,1)}), bf16[4,512,256]{2,1,0:T(8,128)(2,1)S(1)}, u32[]{:S(2)}, u32[]{:S(2)}) async-start(bf16[4,512,256]{2,1,0:T(8,128)(2,1)} %bitcast.38), calls=%async_computation | async-start | bytes 2097152 | tf_op jit(solution)/shard_map/all_to_all | solution.py:843
  129.1 48.8 %collective-permute-start.5 = (bf16[512,1024]{1,0:T(8,128)(2,1)}, bf16[512,1024]{1,0:T(8,128)(2,1)}, u32[]{:S(2)}, u32[]{:S(2)}) collective-permute-start(bf16[512,1024]{1,0:T(8,128)(2,1)} %constant_dynamic-slice_fusion.8), channel_id=1, source_target_pairs={{0,2},{1,3},{2,0},{3,1},{4,6},{5,7},{6,4},{7,5},{8,10},{9,11},{10,... | collective-permute-start | bytes 3145736 | tf_op jit(solution)/shard_map/ppermute | solution.py:832
  133.2 44.7 %collective-permute-start.4 = (bf16[256,1024]{1,0:T(8,128)(2,1)}, bf16[256,1024]{1,0:T(8,128)(2,1)}, u32[]{:S(2)}, u32[]{:S(2)}) collective-permute-start(bf16[256,1024]{1,0:T(8,128)(2,1)} %param.24), channel_id=1, source_target_pairs={{0,2},{1,3},{2,0},{3,1},{4,6},{5,7},{6,4},{7,5},{8,10},{9,11},{10,... | collective-permute-start | bytes 1572872 | tf_op jit(solution)/shard_map/ppermute | solution.py:832
  136.3 64.1 %collective-permute-start.7 = (bf16[512,1024]{1,0:T(8,128)(2,1)}, bf16[512,1024]{1,0:T(8,128)(2,1)}, u32[]{:S(2)}, u32[]{:S(2)}) collective-permute-start(bf16[512,1024]{1,0:T(8,128)(2,1)} %constant_dynamic-slice_fusion.7), channel_id=1, source_target_pairs={{0,2},{1,3},{2,0},{3,1},{4,6},{5,7},{6,4},{7,5},{8,10},{9,11},{10,... | collective-permute-start | bytes 3145736 | tf_op jit(solution)/shard_map/ppermute | solution.py:832
  219.9 39.8 %collective-permute-start.10 = (bf16[1024,1024]{1,0:T(8,128)(2,1)}, bf16[1024,1024]{1,0:T(8,128)(2,1)S(1)}, u32[]{:S(2)}, u32[]{:S(2)}) collective-permute-start(bf16[1024,1024]{1,0:T(8,128)(2,1)} %join_halves.5.refs_2_), channel_id=1, source_target_pairs={{0,1},{1,0},{2,3},{3,2},{4,5},{5,4},{6,7},{7,6},{8,9},{9,8},{10,11... | collective-permute-start | bytes 6291464 | tf_op jit(solution)/shard_map/ppermute | solution.py:832
  325.5 50.7 %collective-permute-start.20 = (bf16[1024,1024]{1,0:T(8,128)(2,1)}, bf16[1024,1024]{1,0:T(8,128)(2,1)}, u32[]{:S(2)}, u32[]{:S(2)}) collective-permute-start(bf16[1024,1024]{1,0:T(8,128)(2,1)} %add_terms.8), channel_id=1, source_target_pairs={{0,2},{1,3},{2,0},{3,1},{4,6},{5,7},{6,4},{7,5},{8,10},{9,11},{10,... | collective-permute-start | bytes 6291464 | tf_op jit(solution)/shard_map/ppermute | solution.py:832
  376.2 40.6 %all-to-all-start.3 = ((bf16[4,1536,256]{2,1,0:T(8,128)(2,1)}), bf16[4,1536,256]{2,1,0:T(8,128)(2,1)S(1)}, u32[]{:S(2)}, u32[]{:S(2)}) async-start(bf16[4,1536,256]{2,1,0:T(8,128)(2,1)} %get-tuple-element.282), calls=%async_computation.3 | async-start | bytes 6291456 | tf_op jit(solution)/shard_map/all_to_all | solution.py:843
  379.9 251.4 %all-reduce.6.cloned.1.call-start = ((), (), s32[]{:S(2)}) async-start(), calls=%async_computation.8 | async-start | bytes 5242880 | tf_op jit(solution)/shard_map/psum | solution.py:1109
  416.8 60.2 %collective-permute-start.21 = (bf16[1024,1024]{1,0:T(8,128)(2,1)}, bf16[1024,1024]{1,0:T(8,128)(2,1)}, u32[]{:S(2)}, u32[]{:S(2)}) collective-permute-start(bf16[1024,1024]{1,0:T(8,128)(2,1)} %add_terms.7), channel_id=1, source_target_pairs={{0,2},{1,3},{2,0},{3,1},{4,6},{5,7},{6,4},{7,5},{8,10},{9,11},{10,... | collective-permute-start | bytes 6291464 | tf_op jit(solution)/shard_map/ppermute | solution.py:832
  425.1 51.9 %collective-permute-start.23 = (bf16[512,1024]{1,0:T(8,128)(2,1)}, bf16[512,1024]{1,0:T(8,128)(2,1)}, u32[]{:S(2)}, u32[]{:S(2)}) collective-permute-start(bf16[512,1024]{1,0:T(8,128)(2,1)} %constant_dynamic-slice_fusion.6), channel_id=1, source_target_pairs={{0,4},{4,0},{8,12},{12,8},{16,20},{20,16},{24,28},{28,24},{1,5},{5... | collective-permute-start | bytes 3145736 | tf_op jit(solution)/shard_map/ppermute | solution.py:890
  428.7 48.3 %collective-permute-start.22 = (bf16[256,1024]{1,0:T(8,128)(2,1)}, bf16[256,1024]{1,0:T(8,128)(2,1)S(1)}, u32[]{:S(2)}, u32[]{:S(2)}) collective-permute-start(bf16[256,1024]{1,0:T(8,128)(2,1)} %add_terms.9), channel_id=1, source_target_pairs={{0,2},{1,3},{2,0},{3,1},{4,6},{5,7},{6,4},{7,5},{8,10},{9,11},{10,... | collective-permute-start | bytes 1572872 | tf_op jit(solution)/shard_map/ppermute | solution.py:832
  487.8 253.6 %all-reduce.4.cloned.1.call-start = ((), (), s32[]{:S(2)}) async-start(), calls=%async_computation.7 | async-start | bytes 3194880 | tf_op jit(solution)/shard_map/psum | solution.py:1126
  501.6 51.5 %collective-permute-start.26 = (bf16[512,1024]{1,0:T(8,128)(2,1)}, bf16[512,1024]{1,0:T(8,128)(2,1)}, u32[]{:S(2)}, u32[]{:S(2)}) collective-permute-start(bf16[512,1024]{1,0:T(8,128)(2,1)} %get-tuple-element.309), channel_id=1, source_target_pairs={{0,1},{1,0},{2,3},{3,2},{4,5},{5,4},{6,7},{7,6},{8,9},{9,8},{10,11... | collective-permute-start | bytes 3145736 | tf_op jit(solution)/shard_map/ppermute | solution.py:832
  502.1 51.0 %collective-permute-start.27 = (bf16[512,1024]{1,0:T(8,128)(2,1)}, bf16[512,1024]{1,0:T(8,128)(2,1)}, u32[]{:S(2)}, u32[]{:S(2)}) collective-permute-start(bf16[512,1024]{1,0:T(8,128)(2,1)} %get-tuple-element.310), channel_id=1, source_target_pairs={{0,1},{1,0},{2,3},{3,2},{4,5},{5,4},{6,7},{7,6},{8,9},{9,8},{10,11... | collective-permute-start | bytes 3145736 | tf_op jit(solution)/shard_map/ppermute | solution.py:832
  502.4 54.0 %collective-permute-start.30 = (bf16[128,1024]{1,0:T(8,128)(2,1)S(1)}, bf16[128,1024]{1,0:T(8,128)(2,1)S(1)}, u32[]{:S(2)}, u32[]{:S(2)}) collective-permute-start(bf16[128,1024]{1,0:T(8,128)(2,1)S(1)} %constant_dynamic-slice_fusion), channel_id=1, source_target_pairs={{0,16},{4,20},{8,24},{12,28},{16,0},{20,4},{24,8},{28,12},{1,17},{... | collective-permute-start | bytes 786440 | tf_op jit(solution)/shard_map/ppermute | solution.py:890
  504.9 51.5 %collective-permute-start.29 = (f32[64,128]{1,0:T(8,128)S(1)}, f32[64,128]{1,0:T(8,128)S(1)}, u32[]{:S(2)}, u32[]{:S(2)}) collective-permute-start(f32[64,128]{1,0:T(8,128)S(1)} %add.148), channel_id=1, source_target_pairs={{0,2},{1,3},{2,0},{3,1},{4,6},{5,7},{6,4},{7,5},{8,10},{9,11},{10,... | collective-permute-start | bytes 98312 | tf_op jit(solution)/shard_map/ppermute | solution.py:876
  555.5 75.8 %collective-permute-start.28 = (bf16[512,1024]{1,0:T(8,128)(2,1)}, bf16[512,1024]{1,0:T(8,128)(2,1)S(1)}, u32[]{:S(2)}, u32[]{:S(2)}) collective-permute-start(bf16[512,1024]{1,0:T(8,128)(2,1)} %add_terms.11), channel_id=1, source_target_pairs={{0,2},{1,3},{2,0},{3,1},{4,6},{5,7},{6,4},{7,5},{8,10},{9,11},{10,... | collective-permute-start | bytes 3145736 | tf_op jit(solution)/shard_map/ppermute | solution.py:832
  581.9 49.4 %collective-permute-start.34 = (bf16[256,1024]{1,0:T(8,128)(2,1)}, bf16[256,1024]{1,0:T(8,128)(2,1)S(1)}, u32[]{:S(2)}, u32[]{:S(2)}) collective-permute-start(bf16[256,1024]{1,0:T(8,128)(2,1)} %join_halves.7.own_ref), channel_id=1, source_target_pairs={{0,8},{4,12},{8,0},{12,4},{16,24},{20,28},{24,16},{28,20},{1,9},{5... | collective-permute-start | bytes 1572872 | tf_op jit(solution)/shard_map/ppermute | solution.py:893
  581.9 75.7 %collective-permute-start.35 = (bf16[512,1024]{1,0:T(8,128)(2,1)}, bf16[512,1024]{1,0:T(8,128)(2,1)S(1)}, u32[]{:S(2)}, u32[]{:S(2)}) collective-permute-start(bf16[512,1024]{1,0:T(8,128)(2,1)} %get-tuple-element.354), channel_id=1, source_target_pairs={{0,1},{1,0},{2,3},{3,2},{4,5},{5,4},{6,7},{7,6},{8,9},{9,8},{10,11... | collective-permute-start | bytes 3145736 | tf_op jit(solution)/shard_map/ppermute | solution.py:832
  582.0 75.6 %collective-permute-start.36 = (bf16[512,1024]{1,0:T(8,128)(2,1)}, bf16[512,1024]{1,0:T(8,128)(2,1)}, u32[]{:S(2)}, u32[]{:S(2)}) collective-permute-start(bf16[512,1024]{1,0:T(8,128)(2,1)} %get-tuple-element.355), channel_id=1, source_target_pairs={{0,1},{1,0},{2,3},{3,2},{4,5},{5,4},{6,7},{7,6},{8,9},{9,8},{10,11... | collective-permute-start | bytes 3145736 | tf_op jit(solution)/shard_map/ppermute | solution.py:832
  582.5 48.9 %collective-permute-start.32 = (f32[64,128]{1,0:T(8,128)S(1)}, f32[64,128]{1,0:T(8,128)S(1)}, u32[]{:S(2)}, u32[]{:S(2)}) collective-permute-start(f32[64,128]{1,0:T(8,128)S(1)} %add.154), channel_id=1, source_target_pairs={{0,8},{4,12},{8,0},{12,4},{16,24},{20,28},{24,16},{28,20},{1,9},{5... | collective-permute-start | bytes 98312 | tf_op jit(solution)/shard_map/ppermute | solution.py:876
  (74 other events, 1223.0 us)
Sparse Core Ops, SparseCore 0:
  10.2 37.1 all-gather.3
  49.5 34.4 all-gather.5
  86.2 40.2 all-gather.7
  487.9 137.0 all-reduce.5
  647.8 93.5 all-reduce.3

commit v9 on v7

--- a/solution.py
+++ b/solution.py
@@ -926,12 +926,9 @@
             if i > 0:
                 out, heads_own[-1] = tie(out, heads_own[-1])
             if i == min(1, slot_count - 1):
-                out, (up_own, down_own, out_own) = tie(
-                    out, (up_projection_weight, down_projection_weight, output_projection_weight)
-                )
+                out, (up_own, out_own) = tie(out, (up_projection_weight, output_projection_weight))
                 out_far = gather_far(out_own)
                 up_far = fetch(up_own)
-                down_far = fetch(down_own)
             if last:
                 out, (out_far, up_far) = tie(out, (out_far, up_far))
             heads_own.append(exchange(out.reshape(tensor_size, own_rows, width)))
@@ -947,12 +944,13 @@
         rows_done = None
         for i in range(slot_count):
             if i == slot_count - 1:
-                rows_done, (heads_own[i], down_far) = tie(rows_done, (heads_own[i], down_far))
+                rows_done, heads_own[i] = tie(rows_done, heads_own[i])
+                heads_own[i], down_own = tie(heads_own[i], down_projection_weight)
+                down_far = gather_far(down_own)
             rows_done = out_project(
                 patches, i, place, heads_own[i], out_weight, out_bias_row, mlp_gain_row, mlp_shift_row, rows_done
             )
         if square:
-            down_rest = fetch_rest(down_far)
             rows_done, up_rest = tie(rows_done, up_rest)
             up_far = in_halves(up_far, up_rest, dp_side)
             up_diag = swap(up_far, 1)
@@ -971,8 +969,7 @@
         for c in range(calls):
             pair = slice(2 * c, 2 * c + 2)
             if c == 1 and square:
-                total, (up_diag, down_rest) = tie(total, (up_diag, down_rest))
-                down_far = in_halves(down_far, down_rest, dp_side)
+                total, (up_diag, down_far) = tie(total, (up_diag, down_far))
                 up_blocks += [up_far, up_diag]
                 down_blocks += [down_far, swap(down_far, 1)]
             slope, total, *grads = mlp_forward(

time: 750 us -> 739 us (0.985)
  local copies, waits for them, and re-layouts: 27.9 us -> 19 us
  transfers between devices with their start and end apart: 57 -> 56, of which waited for: 15 -> 16; matrix products, arithmetic and copies ran while one was open for 10% -> 10% of each run, Pallas kernels for 58% -> 59%
where the time goes in v9:
time: 739 us; the launch traced here: 732 us
  Pallas kernels  473 us (64%)
  waiting for transfers between devices  102 us (14%)
  starting transfers between devices  50.8 us (7%)
  other arithmetic  49.2 us (7%)
  matrix products  21.9 us (3%)
  local copies, waits for them, and re-layouts  19 us (3%)
  between operations  15.5 us (2%)
    pallas_call x3, Pallas kernels, attend_back(): pl.pallas_call(body, grid=(pairs, kblocks), in_specs=[pl.BlockSpec((None,...  141 us
    pallas_call x3, Pallas kernels, attend(): pl.pallas_call(body, grid=(pairs, length // qblock), in_specs=[pl.BlockSp...  72.4 us
    pallas_call x2, Pallas kernels, mlp_forward(): pl.pallas_call(body, grid=(steps,), in_specs=in_specs, out_specs=[slope_s...  71.6 us
    pallas_call x3, Pallas kernels, project_back(): pl.pallas_call(kernel, grid=(steps,), in_specs=in_specs, out_specs=out_sp...  38.6 us
    pallas_call x2, Pallas kernels, weight_back(): pl.pallas_call(body, grid=(steps,), in_specs=in_specs, out_specs=[pl.Bloc...  35.3 us
    pallas_call x2, Pallas kernels, mlp_backward(): pl.pallas_call(body, grid=(rows // block,), in_specs=in_specs, out_specs=...  34.6 us
    all_gather x3, waiting for transfers between devices, gather_rows(): return lax.all_gather(own, 'tensor', axis=0, tiled=True)  25.6 us
    psum x1, waiting for transfers between devices, shards(): qkv_all = lax.psum(qkv_low, 'dp')  22.2 us
  transfers between devices with their start and end apart: 56, of which 16 were waited for; matrix products, arithmetic and copies ran while one was open for 10% of the time, Pallas kernels for 59%

profile of v9, /device:TPU:0, one launch (start us, length us, event | category | flops | bytes accessed | tf_op | source)
XLA Modules:
  0.0 732.1 jit_solution(10552077348449432350)
XLA Ops:
  21.3 11.5 %cot_back.1.refs_0_ = bf16[1536,2048]{1,0:T(8,128)(2,1)} custom-call(bf16[1536,1024]{1,0:T(8,128)(2,1)} %fusion.cot_ref.refs_1_.refs_0_, bf16[1024,1024]{1,0:T(8,128)(2,1)} %refs_6_, bf16[1024,1024]{1,0:T(8,128)(2,1)} %collective-permute-done.refs_1_.refs_7_), custom_call_target="tpu_custom_call" | custom-call | flops 100663296 | bytes 1572864 | tf_op jit(solution)/shard_map/cot_back/pallas_call | solution.py:494
  32.8 14.6 %all-gather.4.cloned.1.call-done.refs_1_ = bf16[2048,1024]{1,0:T(8,128)(2,1)} async-done(((bf16[512,1024]{1,0:T(8,128)(2,1)}), bf16[2048,1024]{1,0:T(8,128)(2,1)}) %all-gather.4.cloned.1.call-update) | async-done | bytes 4194320 | tf_op jit(solution)/shard_map/all_gather | solution.py:900
  55.6 24.3 %attend.3 = (bf16[2048,256]{1,0:T(8,128)(2,1)}, f32[2,2,2048]{2,1,0:T(2,128)}) custom-call(bf16[3,2048,256]{2,1,0:T(8,128)(2,1)} %fusion.9.q_ref.k_ref.v_ref, bf16[3,2048,256]{2,1,0:T(8,128)(2,1)} %fusion.9.q_ref.k_ref.v_ref, bf16[3,2048,256]{2,1,0:T(8,128)(2,1)} %fusion.9.q_ref.k_ref.v_ref), custom_call_target="tpu_custom_call" | custom-call | flops 134217728 | bytes 524288 | tf_op jit(solution)/shard_map/attend/pallas_call | solution.py:76
  94.9 24.4 %attend.4 = (bf16[2048,256]{1,0:T(8,128)(2,1)}, f32[2,2,2048]{2,1,0:T(2,128)}) custom-call(bf16[3,2048,256]{2,1,0:T(8,128)(2,1)} %fusion.10.q_ref.k_ref.v_ref, bf16[3,2048,256]{2,1,0:T(8,128)(2,1)} %fusion.10.q_ref.k_ref.v_ref, bf16[3,2048,256]{2,1,0:T(8,128)(2,1)} %fusion.10.q_ref.k_ref.v_ref), custom_call_target="tpu_custom_call" | custom-call | flops 134217728 | bytes 524288 | tf_op jit(solution)/shard_map/attend/pallas_call | solution.py:76
  141.8 23.8 %attend.5 = (bf16[2048,256]{1,0:T(8,128)(2,1)}, f32[2,2,2048]{2,1,0:T(2,128)}) custom-call(bf16[3,2048,256]{2,1,0:T(8,128)(2,1)} %fusion.11.q_ref.k_ref.v_ref, bf16[3,2048,256]{2,1,0:T(8,128)(2,1)} %fusion.11.q_ref.k_ref.v_ref, bf16[3,2048,256]{2,1,0:T(8,128)(2,1)} %fusion.11.q_ref.k_ref.v_ref), custom_call_target="tpu_custom_call" | custom-call | flops 134217728 | bytes 524288 | tf_op jit(solution)/shard_map/attend/pallas_call | solution.py:76
  165.6 11.1 %all-to-all-done.1.refs_6_ = bf16[4,512,256]{2,1,0:T(8,128)(2,1)S(1)} async-done(((bf16[4,512,256]{2,1,0:T(8,128)(2,1)}), bf16[4,512,256]{2,1,0:T(8,128)(2,1)S(1)}, u32[]{:S(2)}, u32[]{:S(2)}) %all-to-all-start.1) | async-done | bytes 1048608 | tf_op jit(solution)/shard_map/all_to_all | solution.py:772
  213.0 35.1 %mlp_forward.2 = (bf16[1536,2048]{1,0:T(8,128)(2,1)}, f32[1536,1024]{1,0:T(8,128)}, bf16[1024,1024]{1,0:T(8,128)(2,1)}, bf16[1024,1024]{1,0:T(8,128)(2,1)}) custom-call(bf16[1536,1024]{1,0:T(8,128)(2,1)} %get-tuple-element.239.refs_0_.x_ref, bf16[1536,1024]{1,0:T(8,128)(2,1)} %fusion.cot_ref.refs_1_.refs_0_, bf16[1024,1024]{1,0:T(8,128)(2,1)} %refs_2_.1, ...), custom_call_target="tpu_custom_call" | custom-call | flops 301989888 | bytes 1572864 | tf_op jit(solution)/shard_map/mlp_forward/pallas_call | solution.py:466
  253.0 36.5 %mlp_forward.3 = (bf16[1536,2048]{1,0:T(8,128)(2,1)}, f32[1536,1024]{1,0:T(8,128)}, bf16[1024,1024]{1,0:T(8,128)(2,1)}, bf16[1024,1024]{1,0:T(8,128)(2,1)}) custom-call(bf16[1536,1024]{1,0:T(8,128)(2,1)} %get-tuple-element.239.refs_0_.x_ref, bf16[1536,1024]{1,0:T(8,128)(2,1)} %fusion.cot_ref.refs_1_.refs_0_, ...), custom_call_target="tpu_custom_call", output_to_operand_aliasing={{1}: (8, {})} | custom-call | flops 301989888 | bytes 1572864 | tf_op jit(solution)/shard_map/mlp_forward/pallas_call | solution.py:466
  290.1 13.4 %mlp_backward.2 = (bf16[1536,4096]{1,0:T(8,128)(2,1)}, f32[1536,1024]{1,0:T(8,128)}, f32[1,2048]{1,0:T(1,128)}) custom-call(bf16[1536,2048]{1,0:T(8,128)(2,1)} %cot_back.1.refs_0_, bf16[1536,2048]{1,0:T(8,128)(2,1)} %get-tuple-element.256.refs_1_, bf16[1024,1024]{1,0:T(8,128)(2,1)} %refs_2_.1, bf16[1024,1024]{1,0:T(8,128)(2,1)} %collective-permute-done.2.refs_3_), custom_call_target="tpu_custom_call" | custom-call | flops 201326592 | bytes 1572864 | tf_op jit(solution)/shard_map/mlp_backward/pallas_call | solution.py:552
  309.9 21.3 %mlp_backward.3 = (bf16[1536,4096]{1,0:T(8,128)(2,1)}, f32[1536,1024]{1,0:T(8,128)}, f32[1,2048]{1,0:T(1,128)}) custom-call(bf16[1536,1024]{1,0:T(8,128)(2,1)} %fusion.cot_ref.refs_1_.refs_0_, bf16[1536,2048]{1,0:T(8,128)(2,1)} %get-tuple-element.254.refs_1_, bf16[1024,1024]{1,0:T(8,128)(2,1)} %copy-done.6, ...), custom_call_target="tpu_custom_call", output_to_operand_aliasing={{0}: (6, {}), {1}: (7, {})} | custom-call | flops 201326592 | bytes 1572864 | tf_op jit(solution)/shard_map/mlp_backward/pallas_call | solution.py:552
  331.1 14.1 %weight_back.2 = (bf16[1024,1024]{1,0:T(8,128)(2,1)}, bf16[1024,1024]{1,0:T(8,128)(2,1)}) custom-call(bf16[1536,1024]{1,0:T(8,128)(2,1)} %get-tuple-element.239.refs_0_.x_ref, bf16[1536,4096]{1,0:T(8,128)(2,1)} %get-tuple-element.263.refs_0_.refs_1_, bf16[1536,4096]{1,0:T(8,128)(2,1)} %get-tuple-element.263.refs_0_.refs_1_), custom_call_target="tpu_custom_call" | custom-call | flops 100663296 | bytes 1572864 | tf_op jit(solution)/shard_map/weight_back/pallas_call | solution.py:626
  345.8 14.9 %residual_back.1 = (f32[1536,1024]{1,0:T(8,128)}, bf16[1536,1024]{1,0:T(8,128)(2,1)}, f32[8,1024]{1,0:T(8,128)}, bf16[4,1536,256]{2,1,0:T(8,128)(2,1)}) custom-call(s32[1]{0:T(128)} %bitcast.refs_0_.place_ref, f32[1536,1024]{1,0:T(8,128)} %get-tuple-element.268.refs_1_, f32[1536,1024]{1,0:T(8,128)} %get-tuple-element.269.refs_2_.residual_ref, ...), custom_call_target="tpu_custom_call" | custom-call | flops 50331648 | bytes 524288 | tf_op jit(solution)/shard_map/residual_back/pallas_call | solution.py:301
  364.4 21.2 %weight_back.3 = (bf16[1024,1024]{1,0:T(8,128)(2,1)}, bf16[1024,1024]{1,0:T(8,128)(2,1)}, bf16[256,1024]{1,0:T(8,128)(2,1)}, bf16[256,1024]{1,0:T(8,128)(2,1)}, ...) custom-call(bf16[1536,1024]{1,0:T(8,128)(2,1)} %get-tuple-element.239.refs_0_.x_ref, ...), custom_call_target="tpu_custom_call" | custom-call | flops 100663296 | bytes 1572864 | tf_op jit(solution)/shard_map/weight_back/pallas_call | solution.py:626
  391.4 9.9 %all-to-all-done.3.grad_ref = bf16[4,1536,256]{2,1,0:T(8,128)(2,1)S(1)} async-done(((bf16[4,1536,256]{2,1,0:T(8,128)(2,1)}), bf16[4,1536,256]{2,1,0:T(8,128)(2,1)S(1)}, u32[]{:S(2)}, u32[]{:S(2)}) %all-to-all-start.3) | async-done | bytes 3145760 | tf_op jit(solution)/shard_map/all_to_all | solution.py:772
  411.4 47.1 %attend_back.4.refs_2_ = bf16[3,2048,256]{2,1,0:T(8,128)(2,1)} custom-call(bf16[3,2048,256]{2,1,0:T(8,128)(2,1)} %fusion.9.q_ref.k_ref.v_ref, bf16[3,2048,256]{2,1,0:T(8,128)(2,1)} %fusion.9.q_ref.k_ref.v_ref, bf16[3,2048,256]{2,1,0:T(8,128)(2,1)} %fusion.9.q_ref.k_ref.v_ref, bf16[2048,256]{1,0:T(8,128)(2,1)} %get-tuple-element.213.out_ref, ...), custom_call_target="tpu_custom_call" | custom-call | flops 335544320 | bytes 524288 | tf_op jit(solution)/shard_map/attend_back/pallas_call | solution.py:169
  469.5 13.5 %project_back.3 = (bf16[512,1024]{1,0:T(8,128)(2,1)}, bf16[512,1024]{1,0:T(8,128)(2,1)}, bf16[512,1024]{1,0:T(8,128)(2,1)}, bf16[512,1024]{1,0:T(8,128)(2,1)}, f...) custom-call(s32[1]{0:T(128)} %bitcast.refs_0_.place_ref, bf16[2048,1024]{1,0:T(8,128)(2,1)} %all-gather.4.cloned.1.call-done.refs_1_, ...), custom_call_target="tpu_custom_call" | custom-call | flops 100663296 | bytes 524288 | tf_op jit(solution)/shard_map/project_back/pallas_call | solution.py:708
  487.2 46.9 %attend_back.5.refs_2_ = bf16[3,2048,256]{2,1,0:T(8,128)(2,1)} custom-call(bf16[3,2048,256]{2,1,0:T(8,128)(2,1)} %fusion.10.q_ref.k_ref.v_ref, bf16[3,2048,256]{2,1,0:T(8,128)(2,1)} %fusion.10.q_ref.k_ref.v_ref, bf16[3,2048,256]{2,1,0:T(8,128)(2,1)} %fusion.10.q_ref.k_ref.v_ref, bf16[2048,256]{1,0:T(8,128)(2,1)} %get-tuple-element.215.out_ref, ...), custom_call_target="tpu_custom_call" | custom-call | flops 335544320 | bytes 524288 | tf_op jit(solution)/shard_map/attend_back/pallas_call | solution.py:169
  539.5 14.3 %project_back.4 = (bf16[512,1024]{1,0:T(8,128)(2,1)}, bf16[512,1024]{1,0:T(8,128)(2,1)}, bf16[512,1024]{1,0:T(8,128)(2,1)}, bf16[512,1024]{1,0:T(8,128)(2,1)}, f...) custom-call(s32[1]{0:T(128)} %bitcast.refs_0_.place_ref, ...), custom_call_target="tpu_custom_call", output_to_operand_aliasing={{4}: (4, {}), {5}: (5, {})} | custom-call | flops 100663296 | bytes 524288 | tf_op jit(solution)/shard_map/project_back/pallas_call | solution.py:708
  561.0 46.8 %attend_back.3.refs_2_.dqkv_ref = bf16[3,2048,256]{2,1,0:T(8,128)(2,1)} custom-call(bf16[3,2048,256]{2,1,0:T(8,128)(2,1)} %fusion.11.q_ref.k_ref.v_ref, bf16[3,2048,256]{2,1,0:T(8,128)(2,1)} %fusion.11.q_ref.k_ref.v_ref, bf16[3,2048,256]{2,1,0:T(8,128)(2,1)} %fusion.11.q_ref.k_ref.v_ref, bf16[2048,256]{1,0:T(8,128)(2,1)} %get-tuple-element.219.out_ref, ...), custom_call_target="tpu_custom_call" | custom-call | flops 335544320 | bytes 524288 | tf_op jit(solution)/shard_map/attend_back/pallas_call | solution.py:169
  611.9 10.9 %project_back.5 = (f32[3,1024,256]{2,1,0:T(8,128)}, f32[8,256]{1,0:T(8,128)}, bf16[3,1040,256]{2,1,0:T(8,128)(2,1)}) custom-call(s32[1]{0:T(128)} %bitcast.refs_0_.place_ref, bf16[2048,1024]{1,0:T(8,128)(2,1)} %all-gather.8.cloned.1.call-done.refs_1_, ...), custom_call_target="tpu_custom_call", output_to_operand_aliasing={{0}: (4, {}), {1}: (5, {})} | custom-call | flops 100663296 | bytes 524288 | tf_op jit(solution)/shard_map/project_back/pallas_call | solution.py:708
  628.3 8.4 %project_rows.1 = (bf16[512,1024]{1,0:T(8,128)(2,1)}, bf16[512,1024]{1,0:T(8,128)(2,1)}, bf16[512,1024]{1,0:T(8,128)(2,1)}, bf16[512,1024]{1,0:T(8,128)(2,1)}) custom-call(s32[1]{0:T(128)} %bitcast.refs_0_.place_ref, bf16[3,2048,256]{2,1,0:T(8,128)(2,1)} %attend_back.3.refs_2_.dqkv_ref, bf16[3,1024,256]{2,1,0:T(8,128)(2,1)} %weight_ref.1), custom_call_target="tpu_custom_call" | custom-call | flops 50331648 | bytes 524288 | tf_op jit(solution)/shard_map/project_rows/pallas_call | solution.py:741
  643.3 7.6 %layer_out.1 = bf16[3,512,1024]{2,1,0:T(8,128)(2,1)} custom-call(f32[1536,1024]{1,0:T(8,128)} %get-tuple-element.346.total_ref, f32[1536,1024]{1,0:T(8,128)} %get-tuple-element.269.refs_2_.residual_ref, f32[1,1024]{1,0:T(1,128)} %bitcast.91, f32[3]{0:T(128)} %dynamic_slice.54.valid_ref), custom_call_target="tpu_custom_call" | custom-call | bytes 524288 | tf_op jit(solution)/shard_map/layer_out/pallas_call | solution.py:385
  670.4 13.9 %collective-permute-done.41 = bf16[512,1024]{1,0:T(8,128)(2,1)S(1)} collective-permute-done((bf16[512,1024]{1,0:T(8,128)(2,1)S(1)}, bf16[512,1024]{1,0:T(8,128)(2,1)S(1)}, u32[]{:S(2)}, u32[]{:S(2)}) %collective-permute-start.41) | collective-permute-done | bytes 1048608 | tf_op jit(solution)/shard_map/ppermute | solution.py:822
  698.5 22.2 %all-reduce.4.cloned.1.call-done = bf16[3,1040,256]{2,1,0:T(8,128)(2,1)} async-done(((bf16[3,1040,256]{2,1,0:T(8,128)(2,1)}), bf16[3,1040,256]{2,1,0:T(8,128)(2,1)}) %all-reduce.4.cloned.1.call-update) | async-done | bytes 1597456 | tf_op jit(solution)/shard_map/psum | solution.py:1057
  (284 shorter events, 209.1 us)
Async XLA Ops:
  7.2 40.2 %all-gather.4.cloned.1.call-start = ((), (), s32[]{:S(2)}) async-start(), calls=%async_computation.4 | async-start | bytes 5242880 | tf_op jit(solution)/shard_map/all_gather | solution.py:900
  9.9 74.1 %all-gather.6.cloned.1.call-start = ((), (), s32[]{:S(2)}) async-start(), calls=%async_computation.5 | async-start | bytes 5242880 | tf_op jit(solution)/shard_map/all_gather | solution.py:900
  47.4 78.7 %all-gather.8.cloned.1.call-start = ((), (), s32[]{:S(2)}) async-start(), calls=%async_computation.6 | async-start | bytes 5242880 | tf_op jit(solution)/shard_map/all_gather | solution.py:900
  84.1 42.0 %all-to-all-start = ((bf16[4,512,256]{2,1,0:T(8,128)(2,1)}), bf16[4,512,256]{2,1,0:T(8,128)(2,1)S(1)}, u32[]{:S(2)}, u32[]{:S(2)}) async-start(bf16[4,512,256]{2,1,0:T(8,128)(2,1)} %bitcast.59), calls=%async_computation | async-start | bytes 2097152 | tf_op jit(solution)/shard_map/all_to_all | solution.py:772
  128.8 48.0 %collective-permute-start.5 = (bf16[512,1024]{1,0:T(8,128)(2,1)}, bf16[512,1024]{1,0:T(8,128)(2,1)}, u32[]{:S(2)}, u32[]{:S(2)}) collective-permute-start(bf16[512,1024]{1,0:T(8,128)(2,1)} %constant_dynamic-slice_fusion.7), channel_id=1, source_target_pairs={{0,2},{1,3},{2,0},{3,1},{4,6},{5,7},{6,4},{7,5},{8,10},{9,11},{10,... | collective-permute-start | bytes 3145736 | tf_op jit(solution)/shard_map/ppermute | solution.py:761
  129.1 47.6 %collective-permute-start.4 = (bf16[256,1024]{1,0:T(8,128)(2,1)S(1)}, bf16[256,1024]{1,0:T(8,128)(2,1)}, u32[]{:S(2)}, u32[]{:S(2)}) collective-permute-start(bf16[256,1024]{1,0:T(8,128)(2,1)S(1)} %copy-done.18), channel_id=1, source_target_pairs={{0,2},{1,3},{2,0},{3,1},{4,6},{5,7},{6,4},{7,5},{8,10},{9,11},{10,... | collective-permute-start | bytes 1572872 | tf_op jit(solution)/shard_map/ppermute | solution.py:761
  130.8 46.0 %all-to-all-start.1 = ((bf16[4,512,256]{2,1,0:T(8,128)(2,1)}), bf16[4,512,256]{2,1,0:T(8,128)(2,1)S(1)}, u32[]{:S(2)}, u32[]{:S(2)}) async-start(bf16[4,512,256]{2,1,0:T(8,128)(2,1)} %bitcast.58), calls=%async_computation.1 | async-start | bytes 2097152 | tf_op jit(solution)/shard_map/all_to_all | solution.py:772
  200.3 48.2 %collective-permute-start.10 = (bf16[1024,1024]{1,0:T(8,128)(2,1)}, bf16[1024,1024]{1,0:T(8,128)(2,1)}, u32[]{:S(2)}, u32[]{:S(2)}) collective-permute-start(bf16[1024,1024]{1,0:T(8,128)(2,1)} %refs_6_), channel_id=1, source_target_pairs={{0,2},{1,3},{2,0},{3,1},{4,6},{5,7},{6,4},{7,5},{8,10},{9,11},{10,... | collective-permute-start | bytes 6291464 | tf_op jit(solution)/shard_map/ppermute | solution.py:761
  208.5 40.1 %collective-permute-start.9 = (bf16[1024,1024]{1,0:T(8,128)(2,1)S(1)}, bf16[1024,1024]{1,0:T(8,128)(2,1)}, u32[]{:S(2)}, u32[]{:S(2)}) collective-permute-start(bf16[1024,1024]{1,0:T(8,128)(2,1)S(1)} %constant_dynamic-update-slice_fusion.12.refs_2_), channel_id=1, source_target_pairs={{0,1},{1,0},{2,3},{3,2},{4,5},{5,4},{6,7},{7,6},{8,9},{9,8},{10,11... | collective-permute-start | bytes 6291464 | tf_op jit(solution)/shard_map/ppermute | solution.py:761
  308.1 52.6 %collective-permute-start.19 = (bf16[1024,1024]{1,0:T(8,128)(2,1)S(1)}, bf16[1024,1024]{1,0:T(8,128)(2,1)}, u32[]{:S(2)}, u32[]{:S(2)}) collective-permute-start(bf16[1024,1024]{1,0:T(8,128)(2,1)S(1)} %add_convert_fusion.5), channel_id=1, source_target_pairs={{0,2},{1,3},{2,0},{3,1},{4,6},{5,7},{6,4},{7,5},{8,10},{9,11},{10,... | collective-permute-start | bytes 6291464 | tf_op jit(solution)/shard_map/ppermute | solution.py:761
  345.3 40.9 %collective-permute-start.15 = (bf16[1024,1024]{1,0:T(8,128)(2,1)}, bf16[1024,1024]{1,0:T(8,128)(2,1)}, u32[]{:S(2)}, u32[]{:S(2)}) collective-permute-start(bf16[1024,1024]{1,0:T(8,128)(2,1)} %get-tuple-element.273), channel_id=1, source_target_pairs={{0,1},{1,0},{2,3},{3,2},{4,5},{5,4},{6,7},{7,6},{8,9},{9,8},{10,11... | collective-permute-start | bytes 6291464 | tf_op jit(solution)/shard_map/ppermute | solution.py:761
  345.3 40.9 %collective-permute-start.16 = (bf16[1024,1024]{1,0:T(8,128)(2,1)}, bf16[1024,1024]{1,0:T(8,128)(2,1)}, u32[]{:S(2)}, u32[]{:S(2)}) collective-permute-start(bf16[1024,1024]{1,0:T(8,128)(2,1)} %get-tuple-element.274), channel_id=1, source_target_pairs={{0,1},{1,0},{2,3},{3,2},{4,5},{5,4},{6,7},{7,6},{8,9},{9,8},{10,11... | collective-permute-start | bytes 6291464 | tf_op jit(solution)/shard_map/ppermute | solution.py:761
  360.7 40.6 %all-to-all-start.3 = ((bf16[4,1536,256]{2,1,0:T(8,128)(2,1)}), bf16[4,1536,256]{2,1,0:T(8,128)(2,1)S(1)}, u32[]{:S(2)}, u32[]{:S(2)}) async-start(bf16[4,1536,256]{2,1,0:T(8,128)(2,1)} %get-tuple-element.282), calls=%async_computation.3 | async-start | bytes 6291456 | tf_op jit(solution)/shard_map/all_to_all | solution.py:772
  364.4 246.3 %all-reduce.6.cloned.1.call-start = ((), (), s32[]{:S(2)}) async-start(), calls=%async_computation.8 | async-start | bytes 5242880 | tf_op jit(solution)/shard_map/psum | solution.py:1040
  401.3 57.3 %collective-permute-start.20 = (bf16[1024,1024]{1,0:T(8,128)(2,1)}, bf16[1024,1024]{1,0:T(8,128)(2,1)}, u32[]{:S(2)}, u32[]{:S(2)}) collective-permute-start(bf16[1024,1024]{1,0:T(8,128)(2,1)} %add_convert_fusion.6), channel_id=1, source_target_pairs={{0,2},{1,3},{2,0},{3,1},{4,6},{5,7},{6,4},{7,5},{8,10},{9,11},{10,... | collective-permute-start | bytes 6291464 | tf_op jit(solution)/shard_map/ppermute | solution.py:761
  408.6 51.3 %collective-permute-start.22 = (bf16[512,1024]{1,0:T(8,128)(2,1)}, bf16[512,1024]{1,0:T(8,128)(2,1)}, u32[]{:S(2)}, u32[]{:S(2)}) collective-permute-start(bf16[512,1024]{1,0:T(8,128)(2,1)} %constant_dynamic-slice_fusion.6), channel_id=1, source_target_pairs={{0,4},{4,0},{8,12},{12,8},{16,20},{20,16},{24,28},{28,24},{1,5},{5... | collective-permute-start | bytes 3145736 | tf_op jit(solution)/shard_map/ppermute | solution.py:819
  410.4 49.5 %collective-permute-start.21 = (bf16[256,1024]{1,0:T(8,128)(2,1)S(1)}, bf16[256,1024]{1,0:T(8,128)(2,1)S(1)}, u32[]{:S(2)}, u32[]{:S(2)}) collective-permute-start(bf16[256,1024]{1,0:T(8,128)(2,1)S(1)} %add_convert_fusion.13), channel_id=1, source_target_pairs={{0,2},{1,3},{2,0},{3,1},{4,6},{5,7},{6,4},{7,5},{8,10},{9,11},{10,... | collective-permute-start | bytes 1572872 | tf_op jit(solution)/shard_map/ppermute | solution.py:761
  469.4 251.3 %all-reduce.4.cloned.1.call-start = ((), (), s32[]{:S(2)}) async-start(), calls=%async_computation.7 | async-start | bytes 3194880 | tf_op jit(solution)/shard_map/psum | solution.py:1057
  483.0 51.2 %collective-permute-start.25 = (bf16[512,1024]{1,0:T(8,128)(2,1)}, bf16[512,1024]{1,0:T(8,128)(2,1)}, u32[]{:S(2)}, u32[]{:S(2)}) collective-permute-start(bf16[512,1024]{1,0:T(8,128)(2,1)} %get-tuple-element.309), channel_id=1, source_target_pairs={{0,1},{1,0},{2,3},{3,2},{4,5},{5,4},{6,7},{7,6},{8,9},{9,8},{10,11... | collective-permute-start | bytes 3145736 | tf_op jit(solution)/shard_map/ppermute | solution.py:761
  483.5 50.6 %collective-permute-start.26 = (bf16[512,1024]{1,0:T(8,128)(2,1)}, bf16[512,1024]{1,0:T(8,128)(2,1)}, u32[]{:S(2)}, u32[]{:S(2)}) collective-permute-start(bf16[512,1024]{1,0:T(8,128)(2,1)} %get-tuple-element.310), channel_id=1, source_target_pairs={{0,1},{1,0},{2,3},{3,2},{4,5},{5,4},{6,7},{7,6},{8,9},{9,8},{10,11... | collective-permute-start | bytes 3145736 | tf_op jit(solution)/shard_map/ppermute | solution.py:761
  483.8 50.3 %collective-permute-start.29 = (bf16[128,1024]{1,0:T(8,128)(2,1)S(1)}, bf16[128,1024]{1,0:T(8,128)(2,1)S(1)}, u32[]{:S(2)}, u32[]{:S(2)}) collective-permute-start(bf16[128,1024]{1,0:T(8,128)(2,1)S(1)} %constant_dynamic-slice_fusion), channel_id=1, source_target_pairs={{0,16},{4,20},{8,24},{12,28},{16,0},{20,4},{24,8},{28,12},{1,17},{... | collective-permute-start | bytes 786440 | tf_op jit(solution)/shard_map/ppermute | solution.py:819
  486.3 47.8 %collective-permute-start.28 = (f32[64,128]{1,0:T(8,128)S(1)}, f32[64,128]{1,0:T(8,128)S(1)}, u32[]{:S(2)}, u32[]{:S(2)}) collective-permute-start(f32[64,128]{1,0:T(8,128)S(1)} %add.221), channel_id=1, source_target_pairs={{0,2},{1,3},{2,0},{3,1},{4,6},{5,7},{6,4},{7,5},{8,10},{9,11},{10,... | collective-permute-start | bytes 98312 | tf_op jit(solution)/shard_map/ppermute | solution.py:805
  536.8 73.9 %collective-permute-start.27 = (bf16[512,1024]{1,0:T(8,128)(2,1)}, bf16[512,1024]{1,0:T(8,128)(2,1)}, u32[]{:S(2)}, u32[]{:S(2)}) collective-permute-start(bf16[512,1024]{1,0:T(8,128)(2,1)} %add_convert_fusion.9), channel_id=1, source_target_pairs={{0,2},{1,3},{2,0},{3,1},{4,6},{5,7},{6,4},{7,5},{8,10},{9,11},{10,... | collective-permute-start | bytes 3145736 | tf_op jit(solution)/shard_map/ppermute | solution.py:761
  559.7 52.2 %collective-permute-start.33 = (bf16[256,1024]{1,0:T(8,128)(2,1)S(1)}, bf16[256,1024]{1,0:T(8,128)(2,1)S(1)}, u32[]{:S(2)}, u32[]{:S(2)}) collective-permute-start(bf16[256,1024]{1,0:T(8,128)(2,1)S(1)} %constant_dynamic-update-slice_fusion.10), channel_id=1, source_target_pairs={{0,8},{4,12},{8,0},{12,4},{16,24},{20,28},{24,16},{28,20},{1,9},{5... | collective-permute-start | bytes 1572872 | tf_op jit(solution)/shard_map/ppermute | solution.py:822
  (71 other events, 1119.3 us)
Sparse Core Ops, SparseCore 0:
  10.1 37.1 all-gather.3
  49.5 34.4 all-gather.5
  86.2 39.9 all-gather.7
  469.5 132.7 all-reduce.5
  627.3 93.3 all-reduce.3

commit v10 on v9

--- a/solution.py
+++ b/solution.py
@@ -930,30 +930,27 @@
                 out_far = gather_far(out_own)
                 up_far = fetch(up_own)
             if last:
-                out, (out_far, up_far) = tie(out, (out_far, up_far))
+                out, out_far = tie(out, out_far)
             heads_own.append(exchange(out.reshape(tensor_size, own_rows, width)))
             qkvs.append(qkv)
             attended.append(out)
             lses.append(lse)
             every = following
         if square:
-            up_rest = fetch_rest(up_far)
             out_weight = jnp.concatenate([out_own, weights_near[0], out_far, swap(out_far, 1)], axis=0)
         else:
             out_weight = jnp.concatenate(gather_near(out_own, out_far), axis=0)
         rows_done = None
         for i in range(slot_count):
             if i == slot_count - 1:
-                rows_done, heads_own[i] = tie(rows_done, heads_own[i])
+                rows_done, (heads_own[i], up_far) = tie(rows_done, (heads_own[i], up_far))
                 heads_own[i], down_own = tie(heads_own[i], down_projection_weight)
                 down_far = gather_far(down_own)
             rows_done = out_project(
                 patches, i, place, heads_own[i], out_weight, out_bias_row, mlp_gain_row, mlp_shift_row, rows_done
             )
         if square:
-            rows_done, up_rest = tie(rows_done, up_rest)
-            up_far = in_halves(up_far, up_rest, dp_side)
-            up_diag = swap(up_far, 1)
+            up_rest = fetch_rest(up_far)
         attended_rows, residual, normed_mlp = rows_done
 
         bias_blocks = gather_near(bias_row, bias_far)
@@ -969,8 +966,9 @@
         for c in range(calls):
             pair = slice(2 * c, 2 * c + 2)
             if c == 1 and square:
-                total, (up_diag, down_far) = tie(total, (up_diag, down_far))
-                up_blocks += [up_far, up_diag]
+                total, (up_rest, down_far) = tie(total, (up_rest, down_far))
+                up_far = in_halves(up_far, up_rest, dp_side)
+                up_blocks += [up_far, swap(up_far, 1)]
                 down_blocks += [down_far, swap(down_far, 1)]
             slope, total, *grads = mlp_forward(
                 normed_mlp, cot_low, up_blocks[pair], bias_blocks[pair], down_blocks[pair], total

time: 739 us -> 731 us (0.989)
  waiting for transfers between devices: 102 us -> 91.1 us
    all_to_all x4, waiting for transfers between devices: 21 us -> 9.88 us  [exchange(): return lax.all_to_all(stacked, 'tensor', 0, 0)]
  transfers between devices with their start and end apart: 56 -> 56, of which waited for: 16 -> 13; matrix products, arithmetic and copies ran while one was open for 10% -> 10% of each run, Pallas kernels for 59% -> 60%
where the time goes in v10:
time: 731 us; the launch traced here: 723 us
  Pallas kernels  474 us (65%)
  waiting for transfers between devices  91.1 us (12%)
  starting transfers between devices  50.9 us (7%)
  other arithmetic  49.5 us (7%)
  matrix products  21.9 us (3%)
  local copies, waits for them, and re-layouts  21.1 us (3%)
  between operations  15.5 us (2%)
    pallas_call x3, Pallas kernels, attend_back(): pl.pallas_call(body, grid=(pairs, kblocks), in_specs=[pl.BlockSpec((None,...  141 us
    pallas_call x3, Pallas kernels, attend(): pl.pallas_call(body, grid=(pairs, length // qblock), in_specs=[pl.BlockSp...  72.4 us
    pallas_call x2, Pallas kernels, mlp_forward(): pl.pallas_call(body, grid=(steps,), in_specs=in_specs, out_specs=[slope_s...  71.6 us
    pallas_call x3, Pallas kernels, project_back(): pl.pallas_call(kernel, grid=(steps,), in_specs=in_specs, out_specs=out_sp...  38.6 us
    pallas_call x2, Pallas kernels, weight_back(): pl.pallas_call(body, grid=(steps,), in_specs=in_specs, out_specs=[pl.Bloc...  35.3 us
    pallas_call x2, Pallas kernels, mlp_backward(): pl.pallas_call(body, grid=(rows // block,), in_specs=in_specs, out_specs=...  34.6 us
    all_gather x3, waiting for transfers between devices, gather_rows(): return lax.all_gather(own, 'tensor', axis=0, tiled=True)  25.6 us
    psum x1, waiting for transfers between devices, shards(): qkv_all = lax.psum(qkv_low, 'dp')  22 us
  transfers between devices with their start and end apart: 56, of which 13 were waited for; matrix products, arithmetic and copies ran while one was open for 10% of the time, Pallas kernels for 60%

profile of v10, /device:TPU:0, one launch (start us, length us, event | category | flops | bytes accessed | tf_op | source)
XLA Modules:
  0.0 723.4 jit_solution(15418054313251729996)
XLA Ops:
  21.3 11.5 %cot_back.1.refs_0_ = bf16[1536,2048]{1,0:T(8,128)(2,1)} custom-call(bf16[1536,1024]{1,0:T(8,128)(2,1)} %fusion.cot_ref.refs_1_.refs_0_, bf16[1024,1024]{1,0:T(8,128)(2,1)} %refs_6_, bf16[1024,1024]{1,0:T(8,128)(2,1)} %collective-permute-done.refs_1_.refs_7_), custom_call_target="tpu_custom_call" | custom-call | flops 100663296 | bytes 1572864 | tf_op jit(solution)/shard_map/cot_back/pallas_call | solution.py:494
  32.8 14.6 %all-gather.4.cloned.1.call-done.refs_1_ = bf16[2048,1024]{1,0:T(8,128)(2,1)} async-done(((bf16[512,1024]{1,0:T(8,128)(2,1)}), bf16[2048,1024]{1,0:T(8,128)(2,1)}) %all-gather.4.cloned.1.call-update) | async-done | bytes 4194320 | tf_op jit(solution)/shard_map/all_gather | solution.py:900
  55.6 24.2 %attend.3 = (bf16[2048,256]{1,0:T(8,128)(2,1)}, f32[2,2,2048]{2,1,0:T(2,128)}) custom-call(bf16[3,2048,256]{2,1,0:T(8,128)(2,1)} %fusion.9.q_ref.k_ref.v_ref, bf16[3,2048,256]{2,1,0:T(8,128)(2,1)} %fusion.9.q_ref.k_ref.v_ref, bf16[3,2048,256]{2,1,0:T(8,128)(2,1)} %fusion.9.q_ref.k_ref.v_ref), custom_call_target="tpu_custom_call" | custom-call | flops 134217728 | bytes 524288 | tf_op jit(solution)/shard_map/attend/pallas_call | solution.py:76
  87.6 7.3 %fusion.10.q_ref.k_ref.v_ref = bf16[3,2048,256]{2,1,0:T(8,128)(2,1)} fusion(f32[3,256]{1,0:T(4,128)S(1)} %pad_maximum_fusion.2, bf16[3,1024,256]{2,1,0:T(8,128)(2,1)S(1)} %copy-done.1, bf16[2048,1024]{1,0:T(8,128)(2,1)} %all-gather.6.cloned.1.call-done.refs_1_), kind=kOutput, calls=%fused_computation.22 | convolution fusion | flops 3224371200 | bytes 8915968 | tf_op jit(solution)/shard_map/wz,gzh->gwh/dot_general | solution.py:919
  94.9 24.4 %attend.4 = (bf16[2048,256]{1,0:T(8,128)(2,1)}, f32[2,2,2048]{2,1,0:T(2,128)}) custom-call(bf16[3,2048,256]{2,1,0:T(8,128)(2,1)} %fusion.10.q_ref.k_ref.v_ref, bf16[3,2048,256]{2,1,0:T(8,128)(2,1)} %fusion.10.q_ref.k_ref.v_ref, bf16[3,2048,256]{2,1,0:T(8,128)(2,1)} %fusion.10.q_ref.k_ref.v_ref), custom_call_target="tpu_custom_call" | custom-call | flops 134217728 | bytes 524288 | tf_op jit(solution)/shard_map/attend/pallas_call | solution.py:76
  142.4 23.8 %attend.5 = (bf16[2048,256]{1,0:T(8,128)(2,1)}, f32[2,2,2048]{2,1,0:T(2,128)}) custom-call(bf16[3,2048,256]{2,1,0:T(8,128)(2,1)} %fusion.11.q_ref.k_ref.v_ref, bf16[3,2048,256]{2,1,0:T(8,128)(2,1)} %fusion.11.q_ref.k_ref.v_ref, bf16[3,2048,256]{2,1,0:T(8,128)(2,1)} %fusion.11.q_ref.k_ref.v_ref), custom_call_target="tpu_custom_call" | custom-call | flops 134217728 | bytes 524288 | tf_op jit(solution)/shard_map/attend/pallas_call | solution.py:76
  195.3 35.1 %mlp_forward.2 = (bf16[1536,2048]{1,0:T(8,128)(2,1)}, f32[1536,1024]{1,0:T(8,128)}, bf16[1024,1024]{1,0:T(8,128)(2,1)}, bf16[1024,1024]{1,0:T(8,128)(2,1)}) custom-call(bf16[1536,1024]{1,0:T(8,128)(2,1)} %get-tuple-element.231.refs_0_.x_ref, bf16[1536,1024]{1,0:T(8,128)(2,1)} %fusion.cot_ref.refs_1_.refs_0_, bf16[1024,1024]{1,0:T(8,128)(2,1)} %refs_2_.1, ...), custom_call_target="tpu_custom_call" | custom-call | flops 301989888 | bytes 1572864 | tf_op jit(solution)/shard_map/mlp_forward/pallas_call | solution.py:466
  243.7 36.5 %mlp_forward.3 = (bf16[1536,2048]{1,0:T(8,128)(2,1)}, f32[1536,1024]{1,0:T(8,128)}, bf16[1024,1024]{1,0:T(8,128)(2,1)}, bf16[1024,1024]{1,0:T(8,128)(2,1)}) custom-call(bf16[1536,1024]{1,0:T(8,128)(2,1)} %get-tuple-element.231.refs_0_.x_ref, bf16[1536,1024]{1,0:T(8,128)(2,1)} %fusion.cot_ref.refs_1_.refs_0_, ...), custom_call_target="tpu_custom_call", output_to_operand_aliasing={{1}: (8, {})} | custom-call | flops 301989888 | bytes 1572864 | tf_op jit(solution)/shard_map/mlp_forward/pallas_call | solution.py:466
  280.8 13.4 %mlp_backward.2 = (bf16[1536,4096]{1,0:T(8,128)(2,1)}, f32[1536,1024]{1,0:T(8,128)}, f32[1,2048]{1,0:T(1,128)}) custom-call(bf16[1536,2048]{1,0:T(8,128)(2,1)} %cot_back.1.refs_0_, bf16[1536,2048]{1,0:T(8,128)(2,1)} %get-tuple-element.248.refs_1_, bf16[1024,1024]{1,0:T(8,128)(2,1)} %refs_2_.1, bf16[1024,1024]{1,0:T(8,128)(2,1)} %collective-permute-done.2.refs_3_), custom_call_target="tpu_custom_call" | custom-call | flops 201326592 | bytes 1572864 | tf_op jit(solution)/shard_map/mlp_backward/pallas_call | solution.py:552
  300.6 21.3 %mlp_backward.3 = (bf16[1536,4096]{1,0:T(8,128)(2,1)}, f32[1536,1024]{1,0:T(8,128)}, f32[1,2048]{1,0:T(1,128)}) custom-call(bf16[1536,1024]{1,0:T(8,128)(2,1)} %fusion.cot_ref.refs_1_.refs_0_, bf16[1536,2048]{1,0:T(8,128)(2,1)} %get-tuple-element.246.refs_1_, bf16[1024,1024]{1,0:T(8,128)(2,1)} %copy-done.4, ...), custom_call_target="tpu_custom_call", output_to_operand_aliasing={{0}: (6, {}), {1}: (7, {})} | custom-call | flops 201326592 | bytes 1572864 | tf_op jit(solution)/shard_map/mlp_backward/pallas_call | solution.py:552
  321.9 14.1 %weight_back.2 = (bf16[1024,1024]{1,0:T(8,128)(2,1)}, bf16[1024,1024]{1,0:T(8,128)(2,1)}) custom-call(bf16[1536,1024]{1,0:T(8,128)(2,1)} %get-tuple-element.231.refs_0_.x_ref, bf16[1536,4096]{1,0:T(8,128)(2,1)} %get-tuple-element.255.refs_0_.refs_1_, bf16[1536,4096]{1,0:T(8,128)(2,1)} %get-tuple-element.255.refs_0_.refs_1_), custom_call_target="tpu_custom_call" | custom-call | flops 100663296 | bytes 1572864 | tf_op jit(solution)/shard_map/weight_back/pallas_call | solution.py:626
  336.5 14.9 %residual_back.1 = (f32[1536,1024]{1,0:T(8,128)}, bf16[1536,1024]{1,0:T(8,128)(2,1)}, f32[8,1024]{1,0:T(8,128)}, bf16[4,1536,256]{2,1,0:T(8,128)(2,1)}) custom-call(s32[1]{0:T(128)} %bitcast.refs_0_.place_ref, f32[1536,1024]{1,0:T(8,128)} %get-tuple-element.260.refs_1_, f32[1536,1024]{1,0:T(8,128)} %get-tuple-element.261.refs_2_.residual_ref, ...), custom_call_target="tpu_custom_call" | custom-call | flops 50331648 | bytes 524288 | tf_op jit(solution)/shard_map/residual_back/pallas_call | solution.py:301
  355.2 21.2 %weight_back.3 = (bf16[1024,1024]{1,0:T(8,128)(2,1)}, bf16[1024,1024]{1,0:T(8,128)(2,1)}, bf16[256,1024]{1,0:T(8,128)(2,1)}, bf16[256,1024]{1,0:T(8,128)(2,1)}, ...) custom-call(bf16[1536,1024]{1,0:T(8,128)(2,1)} %get-tuple-element.231.refs_0_.x_ref, ...), custom_call_target="tpu_custom_call" | custom-call | flops 100663296 | bytes 1572864 | tf_op jit(solution)/shard_map/weight_back/pallas_call | solution.py:626
  382.1 9.9 %all-to-all-done.3.grad_ref = bf16[4,1536,256]{2,1,0:T(8,128)(2,1)S(1)} async-done(((bf16[4,1536,256]{2,1,0:T(8,128)(2,1)}), bf16[4,1536,256]{2,1,0:T(8,128)(2,1)S(1)}, u32[]{:S(2)}, u32[]{:S(2)}) %all-to-all-start.3) | async-done | bytes 3145760 | tf_op jit(solution)/shard_map/all_to_all | solution.py:772
  403.1 47.1 %attend_back.4.refs_2_ = bf16[3,2048,256]{2,1,0:T(8,128)(2,1)} custom-call(bf16[3,2048,256]{2,1,0:T(8,128)(2,1)} %fusion.9.q_ref.k_ref.v_ref, bf16[3,2048,256]{2,1,0:T(8,128)(2,1)} %fusion.9.q_ref.k_ref.v_ref, bf16[3,2048,256]{2,1,0:T(8,128)(2,1)} %fusion.9.q_ref.k_ref.v_ref, bf16[2048,256]{1,0:T(8,128)(2,1)} %get-tuple-element.209.out_ref, ...), custom_call_target="tpu_custom_call" | custom-call | flops 335544320 | bytes 524288 | tf_op jit(solution)/shard_map/attend_back/pallas_call | solution.py:169
  460.4 13.5 %project_back.3 = (bf16[512,1024]{1,0:T(8,128)(2,1)}, bf16[512,1024]{1,0:T(8,128)(2,1)}, bf16[512,1024]{1,0:T(8,128)(2,1)}, bf16[512,1024]{1,0:T(8,128)(2,1)}, f...) custom-call(s32[1]{0:T(128)} %bitcast.refs_0_.place_ref, bf16[2048,1024]{1,0:T(8,128)(2,1)} %all-gather.4.cloned.1.call-done.refs_1_, ...), custom_call_target="tpu_custom_call" | custom-call | flops 100663296 | bytes 524288 | tf_op jit(solution)/shard_map/project_back/pallas_call | solution.py:708
  478.1 46.9 %attend_back.5.refs_2_ = bf16[3,2048,256]{2,1,0:T(8,128)(2,1)} custom-call(bf16[3,2048,256]{2,1,0:T(8,128)(2,1)} %fusion.10.q_ref.k_ref.v_ref, bf16[3,2048,256]{2,1,0:T(8,128)(2,1)} %fusion.10.q_ref.k_ref.v_ref, bf16[3,2048,256]{2,1,0:T(8,128)(2,1)} %fusion.10.q_ref.k_ref.v_ref, bf16[2048,256]{1,0:T(8,128)(2,1)} %get-tuple-element.211.out_ref, ...), custom_call_target="tpu_custom_call" | custom-call | flops 335544320 | bytes 524288 | tf_op jit(solution)/shard_map/attend_back/pallas_call | solution.py:169
  530.9 14.3 %project_back.4 = (bf16[512,1024]{1,0:T(8,128)(2,1)}, bf16[512,1024]{1,0:T(8,128)(2,1)}, bf16[512,1024]{1,0:T(8,128)(2,1)}, bf16[512,1024]{1,0:T(8,128)(2,1)}, f...) custom-call(s32[1]{0:T(128)} %bitcast.refs_0_.place_ref, ...), custom_call_target="tpu_custom_call", output_to_operand_aliasing={{4}: (4, {}), {5}: (5, {})} | custom-call | flops 100663296 | bytes 524288 | tf_op jit(solution)/shard_map/project_back/pallas_call | solution.py:708
  552.0 46.8 %attend_back.3.refs_2_.dqkv_ref = bf16[3,2048,256]{2,1,0:T(8,128)(2,1)} custom-call(bf16[3,2048,256]{2,1,0:T(8,128)(2,1)} %fusion.11.q_ref.k_ref.v_ref, bf16[3,2048,256]{2,1,0:T(8,128)(2,1)} %fusion.11.q_ref.k_ref.v_ref, bf16[3,2048,256]{2,1,0:T(8,128)(2,1)} %fusion.11.q_ref.k_ref.v_ref, bf16[2048,256]{1,0:T(8,128)(2,1)} %get-tuple-element.214.out_ref, ...), custom_call_target="tpu_custom_call" | custom-call | flops 335544320 | bytes 524288 | tf_op jit(solution)/shard_map/attend_back/pallas_call | solution.py:169
  602.8 10.9 %project_back.5 = (f32[3,1024,256]{2,1,0:T(8,128)}, f32[8,256]{1,0:T(8,128)}, bf16[3,1040,256]{2,1,0:T(8,128)(2,1)}) custom-call(s32[1]{0:T(128)} %bitcast.refs_0_.place_ref, bf16[2048,1024]{1,0:T(8,128)(2,1)} %all-gather.8.cloned.1.call-done.refs_1_, ...), custom_call_target="tpu_custom_call", output_to_operand_aliasing={{0}: (4, {}), {1}: (5, {})} | custom-call | flops 100663296 | bytes 524288 | tf_op jit(solution)/shard_map/project_back/pallas_call | solution.py:708
  619.1 8.6 %project_rows.1 = (bf16[512,1024]{1,0:T(8,128)(2,1)}, bf16[512,1024]{1,0:T(8,128)(2,1)}, bf16[512,1024]{1,0:T(8,128)(2,1)}, bf16[512,1024]{1,0:T(8,128)(2,1)}) custom-call(s32[1]{0:T(128)} %bitcast.refs_0_.place_ref, bf16[3,2048,256]{2,1,0:T(8,128)(2,1)} %attend_back.3.refs_2_.dqkv_ref, bf16[3,1024,256]{2,1,0:T(8,128)(2,1)} %weight_ref.1), custom_call_target="tpu_custom_call" | custom-call | flops 50331648 | bytes 524288 | tf_op jit(solution)/shard_map/project_rows/pallas_call | solution.py:741
  634.7 7.6 %layer_out.1 = bf16[3,512,1024]{2,1,0:T(8,128)(2,1)} custom-call(f32[1536,1024]{1,0:T(8,128)} %get-tuple-element.338.total_ref, f32[1536,1024]{1,0:T(8,128)} %get-tuple-element.261.refs_2_.residual_ref, f32[1,1024]{1,0:T(1,128)} %bitcast.91, f32[3]{0:T(128)} %dynamic_slice.54.valid_ref), custom_call_target="tpu_custom_call" | custom-call | bytes 524288 | tf_op jit(solution)/shard_map/layer_out/pallas_call | solution.py:385
  661.2 14.6 %collective-permute-done.41 = bf16[512,1024]{1,0:T(8,128)(2,1)S(1)} collective-permute-done((bf16[512,1024]{1,0:T(8,128)(2,1)S(1)}, bf16[512,1024]{1,0:T(8,128)(2,1)S(1)}, u32[]{:S(2)}, u32[]{:S(2)}) %collective-permute-start.41) | collective-permute-done | bytes 1048608 | tf_op jit(solution)/shard_map/ppermute | solution.py:822
  690.0 22.0 %all-reduce.4.cloned.1.call-done = bf16[3,1040,256]{2,1,0:T(8,128)(2,1)} async-done(((bf16[3,1040,256]{2,1,0:T(8,128)(2,1)}), bf16[3,1040,256]{2,1,0:T(8,128)(2,1)}) %all-reduce.4.cloned.1.call-update) | async-done | bytes 1597456 | tf_op jit(solution)/shard_map/psum | solution.py:1055
  (284 shorter events, 203.6 us)
Async XLA Ops:
  7.2 40.2 %all-gather.4.cloned.1.call-start = ((), (), s32[]{:S(2)}) async-start(), calls=%async_computation.4 | async-start | bytes 5242880 | tf_op jit(solution)/shard_map/all_gather | solution.py:900
  9.9 74.1 %all-gather.6.cloned.1.call-start = ((), (), s32[]{:S(2)}) async-start(), calls=%async_computation.5 | async-start | bytes 5242880 | tf_op jit(solution)/shard_map/all_gather | solution.py:900
  47.4 78.7 %all-gather.8.cloned.1.call-start = ((), (), s32[]{:S(2)}) async-start(), calls=%async_computation.6 | async-start | bytes 5242880 | tf_op jit(solution)/shard_map/all_gather | solution.py:900
  84.1 42.0 %all-to-all-start = ((bf16[4,512,256]{2,1,0:T(8,128)(2,1)}), bf16[4,512,256]{2,1,0:T(8,128)(2,1)S(1)}, u32[]{:S(2)}, u32[]{:S(2)}) async-start(bf16[4,512,256]{2,1,0:T(8,128)(2,1)} %bitcast.59), calls=%async_computation | async-start | bytes 2097152 | tf_op jit(solution)/shard_map/all_to_all | solution.py:772
  126.1 40.1 %collective-permute-start.4 = (bf16[256,1024]{1,0:T(8,128)(2,1)S(1)}, bf16[256,1024]{1,0:T(8,128)(2,1)}, u32[]{:S(2)}, u32[]{:S(2)}) collective-permute-start(bf16[256,1024]{1,0:T(8,128)(2,1)S(1)} %copy-done.18), channel_id=1, source_target_pairs={{0,2},{1,3},{2,0},{3,1},{4,6},{5,7},{6,4},{7,5},{8,10},{9,11},{10,... | collective-permute-start | bytes 1572872 | tf_op jit(solution)/shard_map/ppermute | solution.py:761
  127.1 39.1 %all-to-all-start.1 = ((bf16[4,512,256]{2,1,0:T(8,128)(2,1)}), bf16[4,512,256]{2,1,0:T(8,128)(2,1)S(1)}, u32[]{:S(2)}, u32[]{:S(2)}) async-start(bf16[4,512,256]{2,1,0:T(8,128)(2,1)} %bitcast.58), calls=%async_computation.1 | async-start | bytes 2097152 | tf_op jit(solution)/shard_map/all_to_all | solution.py:772
  133.1 53.3 %collective-permute-start.6 = (bf16[512,1024]{1,0:T(8,128)(2,1)}, bf16[512,1024]{1,0:T(8,128)(2,1)}, u32[]{:S(2)}, u32[]{:S(2)}) collective-permute-start(bf16[512,1024]{1,0:T(8,128)(2,1)} %constant_dynamic-slice_fusion.7), channel_id=1, source_target_pairs={{0,2},{1,3},{2,0},{3,1},{4,6},{5,7},{6,4},{7,5},{8,10},{9,11},{10,... | collective-permute-start | bytes 3145736 | tf_op jit(solution)/shard_map/ppermute | solution.py:761
  186.4 48.2 %collective-permute-start.9 = (bf16[1024,1024]{1,0:T(8,128)(2,1)}, bf16[1024,1024]{1,0:T(8,128)(2,1)}, u32[]{:S(2)}, u32[]{:S(2)}) collective-permute-start(bf16[1024,1024]{1,0:T(8,128)(2,1)} %refs_6_), channel_id=1, source_target_pairs={{0,2},{1,3},{2,0},{3,1},{4,6},{5,7},{6,4},{7,5},{8,10},{9,11},{10,... | collective-permute-start | bytes 6291464 | tf_op jit(solution)/shard_map/ppermute | solution.py:761
  188.2 43.8 %collective-permute-start.8 = (bf16[512,1024]{1,0:T(8,128)(2,1)}, bf16[512,1024]{1,0:T(8,128)(2,1)}, u32[]{:S(2)}, u32[]{:S(2)}) collective-permute-start(bf16[512,1024]{1,0:T(8,128)(2,1)} %collective-permute-done.6), channel_id=1, source_target_pairs={{0,4},{4,0},{8,12},{12,8},{16,20},{20,16},{24,28},{28,24},{1,5},{5... | collective-permute-start | bytes 3145736 | tf_op jit(solution)/shard_map/ppermute | solution.py:837
  298.8 52.6 %collective-permute-start.19 = (bf16[1024,1024]{1,0:T(8,128)(2,1)S(1)}, bf16[1024,1024]{1,0:T(8,128)(2,1)}, u32[]{:S(2)}, u32[]{:S(2)}) collective-permute-start(bf16[1024,1024]{1,0:T(8,128)(2,1)S(1)} %add_convert_fusion.5), channel_id=1, source_target_pairs={{0,2},{1,3},{2,0},{3,1},{4,6},{5,7},{6,4},{7,5},{8,10},{9,11},{10,... | collective-permute-start | bytes 6291464 | tf_op jit(solution)/shard_map/ppermute | solution.py:761
  336.0 40.9 %collective-permute-start.15 = (bf16[1024,1024]{1,0:T(8,128)(2,1)}, bf16[1024,1024]{1,0:T(8,128)(2,1)}, u32[]{:S(2)}, u32[]{:S(2)}) collective-permute-start(bf16[1024,1024]{1,0:T(8,128)(2,1)} %get-tuple-element.265), channel_id=1, source_target_pairs={{0,1},{1,0},{2,3},{3,2},{4,5},{5,4},{6,7},{7,6},{8,9},{9,8},{10,11... | collective-permute-start | bytes 6291464 | tf_op jit(solution)/shard_map/ppermute | solution.py:761
  336.0 40.9 %collective-permute-start.16 = (bf16[1024,1024]{1,0:T(8,128)(2,1)}, bf16[1024,1024]{1,0:T(8,128)(2,1)}, u32[]{:S(2)}, u32[]{:S(2)}) collective-permute-start(bf16[1024,1024]{1,0:T(8,128)(2,1)} %get-tuple-element.266), channel_id=1, source_target_pairs={{0,1},{1,0},{2,3},{3,2},{4,5},{5,4},{6,7},{7,6},{8,9},{9,8},{10,11... | collective-permute-start | bytes 6291464 | tf_op jit(solution)/shard_map/ppermute | solution.py:761
  351.4 40.6 %all-to-all-start.3 = ((bf16[4,1536,256]{2,1,0:T(8,128)(2,1)}), bf16[4,1536,256]{2,1,0:T(8,128)(2,1)S(1)}, u32[]{:S(2)}, u32[]{:S(2)}) async-start(bf16[4,1536,256]{2,1,0:T(8,128)(2,1)} %get-tuple-element.274), calls=%async_computation.3 | async-start | bytes 6291456 | tf_op jit(solution)/shard_map/all_to_all | solution.py:772
  355.1 246.6 %all-reduce.6.cloned.1.call-start = ((), (), s32[]{:S(2)}) async-start(), calls=%async_computation.8 | async-start | bytes 5242880 | tf_op jit(solution)/shard_map/psum | solution.py:1038
  392.0 58.2 %collective-permute-start.20 = (bf16[1024,1024]{1,0:T(8,128)(2,1)}, bf16[1024,1024]{1,0:T(8,128)(2,1)}, u32[]{:S(2)}, u32[]{:S(2)}) collective-permute-start(bf16[1024,1024]{1,0:T(8,128)(2,1)} %add_convert_fusion.6), channel_id=1, source_target_pairs={{0,2},{1,3},{2,0},{3,1},{4,6},{5,7},{6,4},{7,5},{8,10},{9,11},{10,... | collective-permute-start | bytes 6291464 | tf_op jit(solution)/shard_map/ppermute | solution.py:761
  399.3 51.3 %collective-permute-start.22 = (bf16[512,1024]{1,0:T(8,128)(2,1)}, bf16[512,1024]{1,0:T(8,128)(2,1)}, u32[]{:S(2)}, u32[]{:S(2)}) collective-permute-start(bf16[512,1024]{1,0:T(8,128)(2,1)} %constant_dynamic-slice_fusion.6), channel_id=1, source_target_pairs={{0,4},{4,0},{8,12},{12,8},{16,20},{20,16},{24,28},{28,24},{1,5},{5... | collective-permute-start | bytes 3145736 | tf_op jit(solution)/shard_map/ppermute | solution.py:819
  402.1 48.6 %collective-permute-start.21 = (bf16[256,1024]{1,0:T(8,128)(2,1)S(1)}, bf16[256,1024]{1,0:T(8,128)(2,1)S(1)}, u32[]{:S(2)}, u32[]{:S(2)}) collective-permute-start(bf16[256,1024]{1,0:T(8,128)(2,1)S(1)} %add_convert_fusion.13), channel_id=1, source_target_pairs={{0,2},{1,3},{2,0},{3,1},{4,6},{5,7},{6,4},{7,5},{8,10},{9,11},{10,... | collective-permute-start | bytes 1572872 | tf_op jit(solution)/shard_map/ppermute | solution.py:761
  460.3 251.7 %all-reduce.4.cloned.1.call-start = ((), (), s32[]{:S(2)}) async-start(), calls=%async_computation.7 | async-start | bytes 3194880 | tf_op jit(solution)/shard_map/psum | solution.py:1055
  473.9 51.1 %collective-permute-start.25 = (bf16[512,1024]{1,0:T(8,128)(2,1)}, bf16[512,1024]{1,0:T(8,128)(2,1)}, u32[]{:S(2)}, u32[]{:S(2)}) collective-permute-start(bf16[512,1024]{1,0:T(8,128)(2,1)} %get-tuple-element.301), channel_id=1, source_target_pairs={{0,1},{1,0},{2,3},{3,2},{4,5},{5,4},{6,7},{7,6},{8,9},{9,8},{10,11... | collective-permute-start | bytes 3145736 | tf_op jit(solution)/shard_map/ppermute | solution.py:761
  474.5 50.6 %collective-permute-start.26 = (bf16[512,1024]{1,0:T(8,128)(2,1)}, bf16[512,1024]{1,0:T(8,128)(2,1)}, u32[]{:S(2)}, u32[]{:S(2)}) collective-permute-start(bf16[512,1024]{1,0:T(8,128)(2,1)} %get-tuple-element.302), channel_id=1, source_target_pairs={{0,1},{1,0},{2,3},{3,2},{4,5},{5,4},{6,7},{7,6},{8,9},{9,8},{10,11... | collective-permute-start | bytes 3145736 | tf_op jit(solution)/shard_map/ppermute | solution.py:761
  474.8 50.3 %collective-permute-start.29 = (bf16[128,1024]{1,0:T(8,128)(2,1)S(1)}, bf16[128,1024]{1,0:T(8,128)(2,1)S(1)}, u32[]{:S(2)}, u32[]{:S(2)}) collective-permute-start(bf16[128,1024]{1,0:T(8,128)(2,1)S(1)} %constant_dynamic-slice_fusion), channel_id=1, source_target_pairs={{0,16},{4,20},{8,24},{12,28},{16,0},{20,4},{24,8},{28,12},{1,17},{... | collective-permute-start | bytes 786440 | tf_op jit(solution)/shard_map/ppermute | solution.py:819
  477.3 47.8 %collective-permute-start.28 = (f32[64,128]{1,0:T(8,128)S(1)}, f32[64,128]{1,0:T(8,128)S(1)}, u32[]{:S(2)}, u32[]{:S(2)}) collective-permute-start(f32[64,128]{1,0:T(8,128)S(1)} %add.221), channel_id=1, source_target_pairs={{0,2},{1,3},{2,0},{3,1},{4,6},{5,7},{6,4},{7,5},{8,10},{9,11},{10,... | collective-permute-start | bytes 98312 | tf_op jit(solution)/shard_map/ppermute | solution.py:805
  527.7 74.0 %collective-permute-start.27 = (bf16[512,1024]{1,0:T(8,128)(2,1)}, bf16[512,1024]{1,0:T(8,128)(2,1)}, u32[]{:S(2)}, u32[]{:S(2)}) collective-permute-start(bf16[512,1024]{1,0:T(8,128)(2,1)} %add_convert_fusion.9), channel_id=1, source_target_pairs={{0,2},{1,3},{2,0},{3,1},{4,6},{5,7},{6,4},{7,5},{8,10},{9,11},{10,... | collective-permute-start | bytes 3145736 | tf_op jit(solution)/shard_map/ppermute | solution.py:761
  550.6 52.2 %collective-permute-start.33 = (bf16[256,1024]{1,0:T(8,128)(2,1)S(1)}, bf16[256,1024]{1,0:T(8,128)(2,1)S(1)}, u32[]{:S(2)}, u32[]{:S(2)}) collective-permute-start(bf16[256,1024]{1,0:T(8,128)(2,1)S(1)} %constant_dynamic-update-slice_fusion.10), channel_id=1, source_target_pairs={{0,8},{4,12},{8,0},{12,4},{16,24},{20,28},{24,16},{28,20},{1,9},{5... | collective-permute-start | bytes 1572872 | tf_op jit(solution)/shard_map/ppermute | solution.py:822
  (71 other events, 1035.4 us)
Sparse Core Ops, SparseCore 0:
  10.1 37.1 all-gather.3
  49.5 34.4 all-gather.5
  86.2 39.9 all-gather.7
  460.4 132.7 all-reduce.5
  618.1 93.8 all-reduce.3
